TPU v7x, 32 devices: a whole 2x2x4 slice. The times are simulated.
32 devices in a mesh: tm: 8 (over y, x, core), rows: 4 (over z).
Axes of the slice: x: 2, y: 2, z: 4, core: 2. Of those that a mesh axis runs over, the one named last changes fastest.
Arguments:
- event_slices: bfloat16 [8, 32, 160, 256], P('tm', 'rows'), may hold values from -6 to 6
- frame_features: bfloat16 [8, 32, 160, 256], P('tm', 'rows'), may hold values from -6 to 6
- exposure_start: int32 [8], P('tm'), may hold values from 0 to 7, as said below
- exposure_end: int32 [8], P('tm'), may hold values from 0 to 7, as said below
- intersection_us: int32 [8, 5], P('tm'), may hold values from 1 to 1000
- conv_first: bfloat16 [3, 3, 256, 256], replicated, may hold values from -0.125 to 0.125
- conv_second: bfloat16 [3, 3, 256, 256], replicated, may hold values from -0.125 to 0.125
- conv_frame: bfloat16 [3, 3, 256, 256], replicated, may hold values from -0.125 to 0.125
Outputs:
- frame_out: bfloat16 [8, 32, 160, 256], P('tm', 'rows')
Inputs may be any that keep to these rules, and one draw needn't show every extreme that they name: exposure_start[f] lies between f - 2 and f. exposure_end[f] lies between f and f + 2.
All inputs are finite; a program needn't handle non-finite values.
Results may differ from a plain program's by a relative error of at most 0.014.
Values may be sent and summed in bfloat16 or wider, within the bound.
No kernel may reach another device: no remote copies, remote signals or barrier semaphores. Data moves between devices by JAX's collectives and lax.ppermute only.
A program may use at most 128 MiB of HBM per device.

v0:
```python
import jax
import jax.numpy as jnp
from jax import lax
from jax.sharding import PartitionSpec as P


def extended(block, sides, width):
    for axis, dim in sides:
        count = lax.axis_size(axis)
        forward = [(i, i + 1) for i in range(count - 1)]
        backward = [(target, source) for source, target in forward]
        low = lax.ppermute(
            lax.slice_in_dim(block, block.shape[dim] - width, None, axis=dim), axis, forward
        )
        high = lax.ppermute(lax.slice_in_dim(block, 0, width, axis=dim), axis, backward)
        block = jnp.concatenate([low, block, high], axis=dim)
    return block


def passed_along(value, axis, steps):
    count = lax.axis_size(axis)
    initial, last = (max(0, -steps), min(count, count - steps))
    return lax.ppermute(value, axis, [(source, source + steps) for source in range(initial, last)])


def local_conv(padded, kernel):
    return lax.conv_general_dilated(
        padded[None],
        kernel,
        (1, 1),
        ((0, 0), (1, 1)),
        dimension_numbers=("NHWC", "HWIO", "NHWC"),
        preferred_element_type=jnp.float32,
    )[0]


def rimmed(image):
    return extended(image, (("rows", 0),), 1)


def shards(
    event_slices,
    frame_features,
    exposure_start,
    exposure_end,
    intersection_us,
    conv_first,
    conv_second,
    conv_frame,
):
    image = event_slices[0]
    first_layer = jax.nn.gelu(local_conv(rimmed(image), conv_first), approximate=True).astype(
        jnp.bfloat16
    )
    second = jax.nn.gelu(local_conv(rimmed(first_layer), conv_second), approximate=True).astype(
        jnp.bfloat16
    )
    frame_index = lax.axis_index("tm")
    intersection = intersection_us[0].astype(jnp.float32)
    window = intersection.shape[0]
    radius = (window - 1) // 2
    slice_index = frame_index + jnp.arange(window, dtype=jnp.int32) - radius
    valid = (slice_index >= exposure_start[0]) & (slice_index <= exposure_end[0])
    frame_weights = jnp.where(valid, intersection, jnp.float32(0.0))
    weight_total = jnp.sum(frame_weights)
    summed = frame_weights[radius] * second.astype(jnp.float32)
    for offset in range(window):
        if offset != radius:
            arrived = passed_along(second, "tm", radius - offset)
            summed = summed + frame_weights[offset] * arrived.astype(jnp.float32)
    mixed_frame = (summed / weight_total * frame_features[0].astype(jnp.float32)).astype(
        jnp.bfloat16
    )
    padded_frame = extended(mixed_frame, (("rows", 0),), 1)
    result = local_conv(padded_frame, conv_frame).astype(jnp.bfloat16)
    return result[None]


def solution(mesh):
    return jax.shard_map(
        shards,
        mesh=mesh,
        in_specs=(
            P("tm", "rows", None, None),
            P("tm", "rows", None, None),
            P("tm"),
            P("tm"),
            P("tm", None),
            P(),
            P(),
            P(),
        ),
        out_specs=P("tm", "rows", None, None),
        check_vma=False,
    )
```

profile of v0, /device:TPU:0, one launch (start us, length us, event | category | flops | bytes accessed | tf_op | source)
XLA Modules:
  0.0 100.8 jit_solution(12429596573554316207)
XLA Ops:
  0.0 1.0 %slice_bitcast_fusion.4 = (bf16[1,160,256]{2,1,0:T(8,128)(2,1)S(1)}, bf16[1,160,256]{2,1,0:T(8,128)(2,1)S(1)}) fusion(bf16[1,8,160,256]{3,2,1,0:T(8,128)(2,1)} %param.8), kind=kLoop, calls=%fused_computation.52 | loop fusion | bytes 327680 | tf_op jit(solution)/shard_map/slice | solution.py:13
  1.0 4.9 %collective-permute-start = (bf16[1,160,256]{2,1,0:T(8,128)(2,1)S(1)}, bf16[1,160,256]{2,1,0:T(8,128)(2,1)S(1)}, u32[]{:S(2)}, u32[]{:S(2)}) collective-permute-start(bf16[1,160,256]{2,1,0:T(8,128)(2,1)S(1)} %get-tuple-element.11), channel_id=1, source_target_pairs={{0,1},{1,2},{2,3},{4,5},{5,6},{6,7},{8,9},{9,10},{10,11},{12,13},{... | collective-permute-start | bytes 245768 | tf_op jit(solution)/shard_map/ppermute | solution.py:12
  6.0 1.3 %collective-permute-start.1 = (bf16[1,160,256]{2,1,0:T(8,128)(2,1)S(1)}, bf16[1,160,256]{2,1,0:T(8,128)(2,1)S(1)}, u32[]{:S(2)}, u32[]{:S(2)}) collective-permute-start(bf16[1,160,256]{2,1,0:T(8,128)(2,1)S(1)} %get-tuple-element.12), channel_id=1, source_target_pairs={{1,0},{2,1},{3,2},{5,4},{6,5},{7,6},{9,8},{10,9},{11,10},{13,12},{... | collective-permute-start | bytes 245768 | tf_op jit(solution)/shard_map/ppermute | solution.py:15
  7.3 0.7 collective-permute-done
  8.0 4.3 %collective-permute-done.1 = bf16[1,160,256]{2,1,0:T(8,128)(2,1)S(1)} collective-permute-done((bf16[1,160,256]{2,1,0:T(8,128)(2,1)S(1)}, bf16[1,160,256]{2,1,0:T(8,128)(2,1)S(1)}, u32[]{:S(2)}, u32[]{:S(2)}) %collective-permute-start.1) | collective-permute-done | bytes 81952 | tf_op jit(solution)/shard_map/ppermute | solution.py:15
  12.3 1.2 %maximum_bitcast_fusion.2 = bf16[10,1,160,256]{3,2,0,1:T(8,128)(2,1)S(1)} fusion(bf16[1,160,256]{2,1,0:T(8,128)(2,1)S(1)} %collective-permute-done.1, bf16[8,160,256]{2,1,0:T(8,128)(2,1)} %bitcast.65, bf16[1,160,256]{2,1,0:T(8,128)(2,1)S(1)} %collective-permute-done), kind=kLoop, calls=%fused_computation.46 | loop fusion | flops 819200 | bytes 1638400 | tf_op jit(solution)/shard_map/broadcast_in_dim | solution.py:28
  13.5 0.2 pad
  13.7 0.3 reshape.7
  14.0 0.0 copy-start.4
  14.0 0.2 copy.10
  14.2 0.4 copy-done.4
  14.7 1.8 %convolution_select_fusion.1 = f32[8,8,21,256]{3,1,2,0:T(8,128)S(1)} fusion(bf16[3,3,256,256]{3,2,1,0:T(8,128)(2,1)S(1)} %copy-done, bf16[10,1,7,2,256]{4,2,3,0,1:T(8,128)(2,1)S(1)} %slice.58, bf16[10,1,8,21,256]{4,2,3,0,1:T(8,128)(2,1)S(1)} %copy.10, pred[8,21]{0,1:T(8,128)(4,1)S(1)} %copy-done.4), kind=kOutput, calls=%fused_computation.8 | convolution fusion | flops 1588617216 | bytes 3487912 | tf_op jit(solution)/shard_map/conv_general_dilated | solution.py:27
  16.5 0.4 copy.11
  16.9 0.4 fusion.10
  17.4 0.2 fusion.52
  17.6 3.5 %collective-permute-start.2 = (bf16[1,160,256]{2,0,1:T(2,128)(2,1)S(1)}, bf16[1,160,256]{2,0,1:T(2,128)(2,1)S(1)}, u32[]{:S(2)}, u32[]{:S(2)}) collective-permute-start(bf16[1,160,256]{2,0,1:T(2,128)(2,1)S(1)} %get-tuple-element.9), channel_id=1, source_target_pairs={{0,1},{1,2},{2,3},{4,5},{5,6},{6,7},{8,9},{9,10},{10,11},{12,13},{... | collective-permute-start | bytes 245768 | tf_op jit(solution)/shard_map/ppermute | solution.py:12
  21.1 1.3 %collective-permute-start.3 = (bf16[1,160,256]{2,0,1:T(2,128)(2,1)S(1)}, bf16[1,160,256]{2,0,1:T(2,128)(2,1)S(1)}, u32[]{:S(2)}, u32[]{:S(2)}) collective-permute-start(bf16[1,160,256]{2,0,1:T(2,128)(2,1)S(1)} %get-tuple-element.10), channel_id=1, source_target_pairs={{1,0},{2,1},{3,2},{5,4},{6,5},{7,6},{9,8},{10,9},{11,10},{13,12},{... | collective-permute-start | bytes 245768 | tf_op jit(solution)/shard_map/ppermute | solution.py:15
  22.4 1.5 %collective-permute-done.2 = bf16[1,160,256]{2,0,1:T(2,128)(2,1)S(1)} collective-permute-done((bf16[1,160,256]{2,0,1:T(2,128)(2,1)S(1)}, bf16[1,160,256]{2,0,1:T(2,128)(2,1)S(1)}, u32[]{:S(2)}, u32[]{:S(2)}) %collective-permute-start.2) | collective-permute-done | bytes 81952 | tf_op jit(solution)/shard_map/ppermute | solution.py:12
  23.9 4.4 %collective-permute-done.3 = bf16[1,160,256]{2,0,1:T(2,128)(2,1)S(1)} collective-permute-done((bf16[1,160,256]{2,0,1:T(2,128)(2,1)S(1)}, bf16[1,160,256]{2,0,1:T(2,128)(2,1)S(1)}, u32[]{:S(2)}, u32[]{:S(2)}) %collective-permute-start.3) | collective-permute-done | bytes 81952 | tf_op jit(solution)/shard_map/ppermute | solution.py:15
  28.3 0.8 maximum_bitcast_fusion
  29.1 0.2 pad.2
  29.3 0.0 copy-start.2
  29.3 0.3 copy.14
  29.6 0.9 copy-done.2
  30.6 1.8 %convolution_select_fusion = f32[8,8,21,256]{3,1,2,0:T(8,128)S(1)} fusion(bf16[3,3,256,256]{3,2,1,0:T(8,128)(2,1)S(1)} %copy-done.2, bf16[10,1,7,2,256]{4,2,3,0,1:T(8,128)(2,1)S(1)} %slice.62, bf16[10,1,8,21,256]{4,2,3,0,1:T(8,128)(2,1)S(1)} %copy.14, pred[8,21]{0,1:T(8,128)(4,1)S(1)} %copy-done.4), kind=kOutput, calls=%fused_computation.7 | convolution fusion | flops 1588617216 | bytes 3487912 | tf_op jit(solution)/shard_map/conv_general_dilated | solution.py:27
  32.4 0.4 copy.15
  32.9 0.4 fusion.18
  33.3 4.3 %collective-permute-start.4 = (bf16[8,160,256]{2,0,1:T(8,128)(2,1)S(1)}, bf16[8,160,256]{2,0,1:T(8,128)(2,1)}, u32[]{:S(2)}, u32[]{:S(2)}) collective-permute-start(bf16[8,160,256]{2,0,1:T(8,128)(2,1)S(1)} %fusion.18), channel_id=1, source_target_pairs={{0,8},{4,12},{8,16},{12,20},{16,24},{20,28},{1,9},{5,13},{9,17},{1... | collective-permute-start | bytes 1966088 | tf_op jit(solution)/shard_map/ppermute | solution.py:23
  37.5 2.1 %collective-permute-start.5 = (bf16[8,160,256]{2,0,1:T(8,128)(2,1)S(1)}, bf16[8,160,256]{2,0,1:T(8,128)(2,1)}, u32[]{:S(2)}, u32[]{:S(2)}) collective-permute-start(bf16[8,160,256]{2,0,1:T(8,128)(2,1)S(1)} %fusion.18), channel_id=1, source_target_pairs={{0,4},{4,8},{8,12},{12,16},{16,20},{20,24},{24,28},{1,5},{5,9},{9,... | collective-permute-start | bytes 1966088 | tf_op jit(solution)/shard_map/ppermute | solution.py:23
  39.7 1.3 %collective-permute-start.6 = (bf16[8,160,256]{2,0,1:T(8,128)(2,1)S(1)}, bf16[8,160,256]{2,0,1:T(8,128)(2,1)}, u32[]{:S(2)}, u32[]{:S(2)}) collective-permute-start(bf16[8,160,256]{2,0,1:T(8,128)(2,1)S(1)} %fusion.18), channel_id=1, source_target_pairs={{4,0},{8,4},{12,8},{16,12},{20,16},{24,20},{28,24},{5,1},{9,5},{13... | collective-permute-start | bytes 1966088 | tf_op jit(solution)/shard_map/ppermute | solution.py:23
  41.0 1.3 %collective-permute-start.7 = (bf16[8,160,256]{2,0,1:T(8,128)(2,1)S(1)}, bf16[8,160,256]{2,0,1:T(8,128)(2,1)}, u32[]{:S(2)}, u32[]{:S(2)}) collective-permute-start(bf16[8,160,256]{2,0,1:T(8,128)(2,1)S(1)} %fusion.18), channel_id=1, source_target_pairs={{8,0},{12,4},{16,8},{20,12},{24,16},{28,20},{9,1},{13,5},{17,9},{2... | collective-permute-start | bytes 1966088 | tf_op jit(solution)/shard_map/ppermute | solution.py:23
  43.6 0.7 fusion.50
  44.2 0.6 fusion.53
  44.8 7.0 %collective-permute-done.4 = bf16[8,160,256]{2,0,1:T(8,128)(2,1)} collective-permute-done((bf16[8,160,256]{2,0,1:T(8,128)(2,1)S(1)}, bf16[8,160,256]{2,0,1:T(8,128)(2,1)}, u32[]{:S(2)}, u32[]{:S(2)}) %collective-permute-start.4) | collective-permute-done | bytes 655392 | tf_op jit(solution)/shard_map/ppermute | solution.py:23
  51.9 26.1 %collective-permute-done.7 = bf16[8,160,256]{2,0,1:T(8,128)(2,1)} collective-permute-done((bf16[8,160,256]{2,0,1:T(8,128)(2,1)S(1)}, bf16[8,160,256]{2,0,1:T(8,128)(2,1)}, u32[]{:S(2)}, u32[]{:S(2)}) %collective-permute-start.7) | collective-permute-done | bytes 655392 | tf_op jit(solution)/shard_map/ppermute | solution.py:23
  77.9 6.7 %fusion.19 = bf16[8,160,256]{2,0,1:T(8,128)(2,1)S(1)} fusion(bf16[8,160,256]{2,0,1:T(8,128)(2,1)} %collective-permute-done.7, bf16[8,160,256]{2,0,1:T(8,128)(2,1)} %collective-permute-done.6, bf16[8,160,256]{2,0,1:T(8,128)(2,1)} %collective-permute-done.5, bf16[8,160,256]{2,0,1:T(8,128)(2,1)} %collective-permute-done.4, bf16[1,8,160,256]{3,2,1,0:T(8,128)(2,1)} %param.9, ...), kind=kLoop, calls=%fused_computation.30 | loop fusion | flops 8847360 | bytes 5242904 | tf_op jit(solution)/shard_map/convert_element_type | solution.py:71
  84.7 0.2 fusion.51
  84.9 3.5 %collective-permute-start.8 = (bf16[1,160,256]{2,0,1:T(2,128)(2,1)S(1)}, bf16[1,160,256]{2,0,1:T(2,128)(2,1)S(1)}, u32[]{:S(2)}, u32[]{:S(2)}) collective-permute-start(bf16[1,160,256]{2,0,1:T(2,128)(2,1)S(1)} %get-tuple-element.7), channel_id=1, source_target_pairs={{0,1},{1,2},{2,3},{4,5},{5,6},{6,7},{8,9},{9,10},{10,11},{12,13},{... | collective-permute-start | bytes 245768 | tf_op jit(solution)/shard_map/ppermute | solution.py:12
  88.4 1.5 %collective-permute-start.9 = (bf16[1,160,256]{2,0,1:T(2,128)(2,1)S(1)}, bf16[1,160,256]{2,0,1:T(2,128)(2,1)S(1)}, u32[]{:S(2)}, u32[]{:S(2)}) collective-permute-start(bf16[1,160,256]{2,0,1:T(2,128)(2,1)S(1)} %get-tuple-element.8), channel_id=1, source_target_pairs={{1,0},{2,1},{3,2},{5,4},{6,5},{7,6},{9,8},{10,9},{11,10},{13,12},{... | collective-permute-start | bytes 245768 | tf_op jit(solution)/shard_map/ppermute | solution.py:15
  89.9 1.3 %collective-permute-done.8 = bf16[1,160,256]{2,0,1:T(2,128)(2,1)S(1)} collective-permute-done((bf16[1,160,256]{2,0,1:T(2,128)(2,1)S(1)}, bf16[1,160,256]{2,0,1:T(2,128)(2,1)S(1)}, u32[]{:S(2)}, u32[]{:S(2)}) %collective-permute-start.8) | collective-permute-done | bytes 81952 | tf_op jit(solution)/shard_map/ppermute | solution.py:12
  91.2 4.4 %collective-permute-done.9 = bf16[1,160,256]{2,0,1:T(2,128)(2,1)S(1)} collective-permute-done((bf16[1,160,256]{2,0,1:T(2,128)(2,1)S(1)}, bf16[1,160,256]{2,0,1:T(2,128)(2,1)S(1)}, u32[]{:S(2)}, u32[]{:S(2)}) %collective-permute-start.9) | collective-permute-done | bytes 81952 | tf_op jit(solution)/shard_map/ppermute | solution.py:15
  95.6 0.8 maximum_bitcast_fusion.1
  96.4 0.2 pad.4
  96.6 0.3 copy.19
  96.9 0.9 copy-done.3
  97.9 1.8 %select_convert_fusion = bf16[8,8,21,256]{3,1,2,0:T(8,128)(2,1)S(1)} fusion(bf16[3,3,256,256]{3,2,1,0:T(8,128)(2,1)S(1)} %copy-done.3, bf16[10,1,7,2,256]{4,2,3,0,1:T(8,128)(2,1)S(1)} %slice.66, bf16[10,1,8,21,256]{4,2,3,0,1:T(8,128)(2,1)S(1)} %copy.19, pred[8,21]{0,1:T(8,128)(4,1)S(1)} %copy-done.4), kind=kOutput, calls=%fused_computation.6 | convolution fusion | flops 1588961280 | bytes 2799784 | tf_op jit(solution)/shard_map/conv_general_dilated | solution.py:27
  99.7 0.1 copy.20
  99.9 1.0 copy.21
  (11 shorter events, 0.1 us)
Async XLA Ops:
  0.0 14.2 %copy-start = (bf16[3,3,256,256]{3,2,1,0:T(8,128)(2,1)S(1)}, bf16[3,3,256,256]{3,2,1,0:T(8,128)(2,1)}, u32[]{:S(2)}) copy-start(bf16[3,3,256,256]{3,2,1,0:T(8,128)(2,1)} %param.13) | copy-start | bytes 3538948
  1.0 7.0 %collective-permute-start = (bf16[1,160,256]{2,1,0:T(8,128)(2,1)S(1)}, bf16[1,160,256]{2,1,0:T(8,128)(2,1)S(1)}, u32[]{:S(2)}, u32[]{:S(2)}) collective-permute-start(bf16[1,160,256]{2,1,0:T(8,128)(2,1)S(1)} %get-tuple-element.11), channel_id=1, source_target_pairs={{0,1},{1,2},{2,3},{4,5},{5,6},{6,7},{8,9},{9,10},{10,11},{12,13},{... | collective-permute-start | bytes 245768 | tf_op jit(solution)/shard_map/ppermute | solution.py:12
  6.0 6.3 %collective-permute-start.1 = (bf16[1,160,256]{2,1,0:T(8,128)(2,1)S(1)}, bf16[1,160,256]{2,1,0:T(8,128)(2,1)S(1)}, u32[]{:S(2)}, u32[]{:S(2)}) collective-permute-start(bf16[1,160,256]{2,1,0:T(8,128)(2,1)S(1)} %get-tuple-element.12), channel_id=1, source_target_pairs={{1,0},{2,1},{3,2},{5,4},{6,5},{7,6},{9,8},{10,9},{11,10},{13,12},{... | collective-permute-start | bytes 245768 | tf_op jit(solution)/shard_map/ppermute | solution.py:15
  14.0 0.7 copy-start.4
  17.6 6.3 %collective-permute-start.2 = (bf16[1,160,256]{2,0,1:T(2,128)(2,1)S(1)}, bf16[1,160,256]{2,0,1:T(2,128)(2,1)S(1)}, u32[]{:S(2)}, u32[]{:S(2)}) collective-permute-start(bf16[1,160,256]{2,0,1:T(2,128)(2,1)S(1)} %get-tuple-element.9), channel_id=1, source_target_pairs={{0,1},{1,2},{2,3},{4,5},{5,6},{6,7},{8,9},{9,10},{10,11},{12,13},{... | collective-permute-start | bytes 245768 | tf_op jit(solution)/shard_map/ppermute | solution.py:12
  21.1 7.2 %collective-permute-start.3 = (bf16[1,160,256]{2,0,1:T(2,128)(2,1)S(1)}, bf16[1,160,256]{2,0,1:T(2,128)(2,1)S(1)}, u32[]{:S(2)}, u32[]{:S(2)}) collective-permute-start(bf16[1,160,256]{2,0,1:T(2,128)(2,1)S(1)} %get-tuple-element.10), channel_id=1, source_target_pairs={{1,0},{2,1},{3,2},{5,4},{6,5},{7,6},{9,8},{10,9},{11,10},{13,12},{... | collective-permute-start | bytes 245768 | tf_op jit(solution)/shard_map/ppermute | solution.py:15
  29.3 1.3 %copy-start.2 = (bf16[3,3,256,256]{3,2,1,0:T(8,128)(2,1)S(1)}, bf16[3,3,256,256]{3,2,1,0:T(8,128)(2,1)}, u32[]{:S(2)}) copy-start(bf16[3,3,256,256]{3,2,1,0:T(8,128)(2,1)} %param.14) | copy-start | bytes 3538948
  32.8 10.7 %copy-start.1 = (s32[1,5]{1,0:T(1,128)S(1)}, s32[1,5]{1,0:T(1,128)}, u32[]{:S(2)}) copy-start(s32[1,5]{1,0:T(1,128)} %param.12) | copy-start | bytes 64
  33.3 18.6 %collective-permute-start.4 = (bf16[8,160,256]{2,0,1:T(8,128)(2,1)S(1)}, bf16[8,160,256]{2,0,1:T(8,128)(2,1)}, u32[]{:S(2)}, u32[]{:S(2)}) collective-permute-start(bf16[8,160,256]{2,0,1:T(8,128)(2,1)S(1)} %fusion.18), channel_id=1, source_target_pairs={{0,8},{4,12},{8,16},{12,20},{16,24},{20,28},{1,9},{5,13},{9,17},{1... | collective-permute-start | bytes 1966088 | tf_op jit(solution)/shard_map/ppermute | solution.py:23
  37.5 14.3 %collective-permute-start.5 = (bf16[8,160,256]{2,0,1:T(8,128)(2,1)S(1)}, bf16[8,160,256]{2,0,1:T(8,128)(2,1)}, u32[]{:S(2)}, u32[]{:S(2)}) collective-permute-start(bf16[8,160,256]{2,0,1:T(8,128)(2,1)S(1)} %fusion.18), channel_id=1, source_target_pairs={{0,4},{4,8},{8,12},{12,16},{16,20},{20,24},{24,28},{1,5},{5,9},{9,... | collective-permute-start | bytes 1966088 | tf_op jit(solution)/shard_map/ppermute | solution.py:23
  39.7 12.2 %collective-permute-start.6 = (bf16[8,160,256]{2,0,1:T(8,128)(2,1)S(1)}, bf16[8,160,256]{2,0,1:T(8,128)(2,1)}, u32[]{:S(2)}, u32[]{:S(2)}) collective-permute-start(bf16[8,160,256]{2,0,1:T(8,128)(2,1)S(1)} %fusion.18), channel_id=1, source_target_pairs={{4,0},{8,4},{12,8},{16,12},{20,16},{24,20},{28,24},{5,1},{9,5},{13... | collective-permute-start | bytes 1966088 | tf_op jit(solution)/shard_map/ppermute | solution.py:23
  41.0 37.0 %collective-permute-start.7 = (bf16[8,160,256]{2,0,1:T(8,128)(2,1)S(1)}, bf16[8,160,256]{2,0,1:T(8,128)(2,1)}, u32[]{:S(2)}, u32[]{:S(2)}) collective-permute-start(bf16[8,160,256]{2,0,1:T(8,128)(2,1)S(1)} %fusion.18), channel_id=1, source_target_pairs={{8,0},{12,4},{16,8},{20,12},{24,16},{28,20},{9,1},{13,5},{17,9},{2... | collective-permute-start | bytes 1966088 | tf_op jit(solution)/shard_map/ppermute | solution.py:23
  84.9 6.3 %collective-permute-start.8 = (bf16[1,160,256]{2,0,1:T(2,128)(2,1)S(1)}, bf16[1,160,256]{2,0,1:T(2,128)(2,1)S(1)}, u32[]{:S(2)}, u32[]{:S(2)}) collective-permute-start(bf16[1,160,256]{2,0,1:T(2,128)(2,1)S(1)} %get-tuple-element.7), channel_id=1, source_target_pairs={{0,1},{1,2},{2,3},{4,5},{5,6},{6,7},{8,9},{9,10},{10,11},{12,13},{... | collective-permute-start | bytes 245768 | tf_op jit(solution)/shard_map/ppermute | solution.py:12
  88.4 7.2 %collective-permute-start.9 = (bf16[1,160,256]{2,0,1:T(2,128)(2,1)S(1)}, bf16[1,160,256]{2,0,1:T(2,128)(2,1)S(1)}, u32[]{:S(2)}, u32[]{:S(2)}) collective-permute-start(bf16[1,160,256]{2,0,1:T(2,128)(2,1)S(1)} %get-tuple-element.8), channel_id=1, source_target_pairs={{1,0},{2,1},{3,2},{5,4},{6,5},{7,6},{9,8},{10,9},{11,10},{13,12},{... | collective-permute-start | bytes 245768 | tf_op jit(solution)/shard_map/ppermute | solution.py:15
  96.6 1.3 %copy-start.3 = (bf16[3,3,256,256]{3,2,1,0:T(8,128)(2,1)S(1)}, bf16[3,3,256,256]{3,2,1,0:T(8,128)(2,1)}, u32[]{:S(2)}) copy-start(bf16[3,3,256,256]{3,2,1,0:T(8,128)(2,1)} %param.15) | copy-start | bytes 3538948
where the time goes:
time: 101 us
  waiting for transfers between devices  49.8 us (49%)
  starting transfers between devices  24.9 us (25%)
  other arithmetic  11.1 us (11%)
  local copies, waits for them, and re-layouts  8.09 us (8%)
  matrix products  5.41 us (5%)
  between operations  1.58 us (2%)
    ppermute x4, waiting for transfers between devices, passed_along(): lax.ppermute(value, axis, [(source, source + steps) for source in range(i...  33.1 us
    ppermute x3, waiting for transfers between devices, extended(): lax.ppermute(lax.slice_in_dim(block, 0, width, axis=dim), axis, backward)  13.1 us
    ppermute x3, starting transfers between devices, extended(): lax.ppermute(lax.slice_in_dim(block, block.shape[dim] - width, None, axis...  11.9 us
    ppermute x4, starting transfers between devices, passed_along(): lax.ppermute(value, axis, [(source, source + steps) for source in range(i...  8.96 us
    convert_element_type x1, other arithmetic, shards(): (summed / weight_total * frame_features[0].astype(jnp.float32)).astype(jn...  6.75 us
    conv_general_dilated x3, matrix products, local_conv(): lax.conv_general_dilated(padded[None], kernel, (1, 1), ((0, 0), (1, 1)),...  5.41 us
    ppermute x3, starting transfers between devices, extended(): lax.ppermute(lax.slice_in_dim(block, 0, width, axis=dim), axis, backward)  4.06 us
    ppermute x3, waiting for transfers between devices, extended(): lax.ppermute(lax.slice_in_dim(block, block.shape[dim] - width, None, axis...  3.58 us
  transfers between devices with their start and end apart: 10, of which 8 were waited for; matrix products, arithmetic and copies ran while one was open for 1% of the time, Pallas kernels for 0%

commit v1 on v0

v1 whole, which is shorter than its diff:
```python
import jax
import jax.numpy as jnp
from jax import lax
from jax.sharding import PartitionSpec as P


def shifted(value, axis, steps):
    count = lax.axis_size(axis)
    initial, last = (max(0, -steps), min(count, count - steps))
    pairs = [(source, source + steps) for source in range(initial, last)]
    if not pairs:
        return jnp.zeros_like(value)
    return lax.ppermute(value, axis, pairs)


def local_conv(padded, kernel):
    return lax.conv_general_dilated(
        padded[None],
        kernel,
        (1, 1),
        ((0, 0), (1, 1)),
        dimension_numbers=("NHWC", "HWIO", "NHWC"),
        preferred_element_type=jnp.float32,
    )[0]


def inside_rows(count, first_row, height):
    rows = first_row + jnp.arange(count, dtype=jnp.int32)
    return ((rows >= 0) & (rows < height))[:, None, None]


def shards(
    event_slices,
    frame_features,
    exposure_start,
    exposure_end,
    intersection_us,
    conv_first,
    conv_second,
    conv_frame,
):
    image = event_slices[0]
    frame = frame_features[0]
    block = image.shape[0]
    height = block * lax.axis_size("rows")
    row0 = lax.axis_index("rows") * block

    down = jnp.concatenate([image[block - 3 :], frame[block - 1 :]], axis=0)
    up = jnp.concatenate([image[:3], frame[:1]], axis=0)
    from_above = shifted(down, "rows", 1)
    from_below = shifted(up, "rows", -1)
    image_ext = jnp.concatenate([from_above[:3], image, from_below[:3]], axis=0)
    frame_ext = jnp.concatenate([from_above[3:], frame, from_below[3:]], axis=0)

    first = jax.nn.gelu(local_conv(image_ext, conv_first), approximate=True)
    first = jnp.where(inside_rows(block + 4, row0 - 2, height), first, 0.0).astype(jnp.bfloat16)
    second = jax.nn.gelu(local_conv(first, conv_second), approximate=True).astype(jnp.bfloat16)

    frame_index = lax.axis_index("tm")
    intersection = intersection_us[0].astype(jnp.float32)
    window = intersection.shape[0]
    radius = (window - 1) // 2
    slice_index = frame_index + jnp.arange(window, dtype=jnp.int32) - radius
    valid = (slice_index >= exposure_start[0]) & (slice_index <= exposure_end[0])
    frame_weights = jnp.where(valid, intersection, jnp.float32(0.0))
    scaled = frame_weights / jnp.sum(frame_weights)

    summed = scaled[radius] * second.astype(jnp.float32)
    for offset in range(window):
        if offset != radius:
            arrived = shifted(second, "tm", radius - offset)
            summed = summed + scaled[offset] * arrived.astype(jnp.float32)
    mixed = (summed * frame_ext.astype(jnp.float32)).astype(jnp.bfloat16)
    result = local_conv(mixed, conv_frame).astype(jnp.bfloat16)
    return result[None]


def solution(mesh):
    return jax.shard_map(
        shards,
        mesh=mesh,
        in_specs=(
            P("tm", "rows", None, None),
            P("tm", "rows", None, None),
            P("tm"),
            P("tm"),
            P("tm", None),
            P(),
            P(),
            P(),
        ),
        out_specs=P("tm", "rows", None, None),
        check_vma=False,
    )
```

time: 101 us -> 101 us (level)
  the two profiles are of different devices: /device:TPU:0 before, /device:TPU:25 now
where the time goes in v1:
time: 101 us; the launch traced here: 100 us
  waiting for transfers between devices  49.8 us (49%)
  local copies, waits for them, and re-layouts  15.9 us (16%)
  starting transfers between devices  15.7 us (16%)
  other arithmetic  9.84 us (10%)
  matrix products  7.23 us (7%)
  between operations  1.58 us (2%)
    ppermute x6, waiting for transfers between devices, shifted(): return lax.ppermute(value, axis, pairs)  49.8 us
    ppermute x6, starting transfers between devices, shifted(): return lax.ppermute(value, axis, pairs)  15.7 us
    conv_general_dilated x3, matrix products, local_conv(): lax.conv_general_dilated(padded[None], kernel, (1, 1), ((0, 0), (1, 1)),...  7.23 us
    conv_general_dilated x8, local copies, waits for them, and re-layouts, local_conv(): lax.conv_general_dilated(padded[None], kernel, (1, 1), ((0, 0), (1, 1)),...  6.47 us
    broadcast_in_dim x2, other arithmetic, local_conv(): padded[None]  6.36 us
    slice x2, local copies, waits for them, and re-layouts, shards(): down = jnp.concatenate([image[block - 3:], frame[block - 1:]], axis=0)  2.19 us
  transfers between devices with their start and end apart: 6, of which 6 were waited for; matrix products, arithmetic and copies ran while one was open for 4% of the time, Pallas kernels for 0%

profile of v1, /device:TPU:25, one launch (start us, length us, event | category | flops | bytes accessed | tf_op | source)
XLA Modules:
  0.0 100.0 jit_solution(11429518441259676751)
XLA Ops:
  0.0 0.0 copy-start
  0.0 1.0 %slice_bitcast_fusion.5 = (bf16[1,160,256]{2,1,0:T(8,128)(2,1)S(1)}, bf16[1,160,256]{2,1,0:T(8,128)(2,1)S(1)}) fusion(bf16[1,8,160,256]{3,2,1,0:T(8,128)(2,1)} %param.9), kind=kLoop, calls=%fused_computation.62 | loop fusion | bytes 327680 | tf_op jit(solution)/shard_map/slice | solution.py:48
  1.0 0.0 copy-start.1
  1.1 1.2 %slice_bitcast_fusion.3 = (bf16[3,160,256]{2,1,0:T(8,128)(2,1)S(1)}, bf16[3,160,256]{2,1,0:T(8,128)(2,1)S(1)}) fusion(bf16[1,8,160,256]{3,2,1,0:T(8,128)(2,1)} %param.8), kind=kLoop, calls=%fused_computation.60 | loop fusion | bytes 983040 | tf_op jit(solution)/shard_map/slice | solution.py:48
  2.3 2.1 %collective-permute-start.1 = (bf16[4,160,256]{2,1,0:T(8,128)(2,1)S(1)}, bf16[4,160,256]{2,1,0:T(8,128)(2,1)S(1)}, u32[]{:S(2)}, u32[]{:S(2)}) collective-permute-start(bf16[4,160,256]{2,1,0:T(8,128)(2,1)S(1)} %pad_maximum_fusion.1), channel_id=1, source_target_pairs={{1,0},{2,1},{3,2},{5,4},{6,5},{7,6},{9,8},{10,9},{11,10},{13,12},{... | collective-permute-start | bytes 983048 | tf_op jit(solution)/shard_map/ppermute | solution.py:13
  4.4 1.3 %collective-permute-start = (bf16[4,160,256]{2,1,0:T(8,128)(2,1)S(1)}, bf16[4,160,256]{2,1,0:T(8,128)(2,1)S(1)}, u32[]{:S(2)}, u32[]{:S(2)}) collective-permute-start(bf16[4,160,256]{2,1,0:T(8,128)(2,1)S(1)} %pad_maximum_fusion), channel_id=1, source_target_pairs={{0,1},{1,2},{2,3},{4,5},{5,6},{6,7},{8,9},{9,10},{10,11},{12,13},{... | collective-permute-start | bytes 983048 | tf_op jit(solution)/shard_map/ppermute | solution.py:13
  5.7 5.0 %collective-permute-done.1 = bf16[4,160,256]{2,1,0:T(8,128)(2,1)S(1)} collective-permute-done((bf16[4,160,256]{2,1,0:T(8,128)(2,1)S(1)}, bf16[4,160,256]{2,1,0:T(8,128)(2,1)S(1)}, u32[]{:S(2)}, u32[]{:S(2)}) %collective-permute-start.1) | collective-permute-done | bytes 327712 | tf_op jit(solution)/shard_map/ppermute | solution.py:13
  10.7 3.8 %collective-permute-done = bf16[4,160,256]{2,1,0:T(8,128)(2,1)S(1)} collective-permute-done((bf16[4,160,256]{2,1,0:T(8,128)(2,1)S(1)}, bf16[4,160,256]{2,1,0:T(8,128)(2,1)S(1)}, u32[]{:S(2)}, u32[]{:S(2)}) %collective-permute-start) | collective-permute-done | bytes 327712 | tf_op jit(solution)/shard_map/ppermute | solution.py:13
  14.6 0.0 copy-done.1
  14.6 0.1 maximum_bitcast_fusion
  14.7 0.0 copy-done.3
  14.7 0.5 copy-done.4
  15.3 1.4 %pad = bf16[14,1,168,256]{3,2,0,1:T(8,128)(2,1)} pad(bf16[14,1,160,256]{3,2,0,1:T(8,128)(2,1)S(1)} %maximum_bitcast_fusion, bf16[]{:T(256)} %constant.39), padding=0_0x0_0x1_7x0_0 | pad | bytes 2351106 | tf_op jit(solution)/shard_map/broadcast_in_dim | solution.py:18
  16.7 2.2 %reshape.14 = bf16[14,1,8,21,256]{4,3,2,0,1:T(8,128)(2,1)S(1)} reshape(bf16[14,1,168,256]{3,2,0,1:T(8,128)(2,1)} %pad) | data formatting | bytes 2408448 | tf_op jit(solution)/shard_map/conv_general_dilated | solution.py:17
  18.9 0.0 copy-start.7
  18.9 0.3 copy.10
  19.3 0.0 copy-done
  19.3 0.3 copy-done.7
  19.6 3.1 %fusion.22 = bf16[12,1,8,21,256]{4,2,3,0,1:T(8,128)(2,1)S(1)} fusion(bf16[3,3,256,256]{3,2,1,0:T(8,128)(2,1)S(1)} %copy-done, bf16[14,1,7,2,256]{4,2,3,0,1:T(8,128)(2,1)S(1)} %slice.76, bf16[14,1,8,21,256]{4,2,3,0,1:T(8,128)(2,1)S(1)} %copy.10, pred[12]{0:T(512)(128)(4,1)S(1)} %compare_and_fusion, pred[8,21]{0,1:T(8,128)(4,1)S(1)} %copy-done.7), kind=kOutput, calls=%fused_computation.31 | convolution fusion | flops 2388320256 | bytes 3516596 | tf_op jit(solution)/shard_map/conv_general_dilated | solution.py:17
  22.8 2.3 %fusion.31 = f32[10,8,21,256]{3,1,2,0:T(8,128)S(1)} fusion(bf16[3,3,256,256]{3,2,1,0:T(8,128)(2,1)S(1)} %copy-done.5, bf16[12,1,7,1,256]{4,2,3,0,1:T(8,128)(2,1)S(1)} %get-tuple-element.8, bf16[12,1,7,1,256]{4,2,3,0,1:T(8,128)(2,1)S(1)} %get-tuple-element.7, bf16[12,1,8,21,256]{4,2,3,0,1:T(8,128)(2,1)S(1)} %fusion.22), kind=kOutput, calls=%fused_computation.40 | convolution fusion | flops 1987461120 | bytes 4018176 | tf_op jit(solution)/shard_map/conv_general_dilated | solution.py:17
  25.1 1.9 %copy.11 = f32[10,8,21,256]{3,2,1,0:T(8,128)} copy(f32[10,8,21,256]{3,1,2,0:T(8,128)S(1)} %fusion.31) | data formatting | bytes 3440640 | tf_op jit(solution)/shard_map/conv_general_dilated | solution.py:17
  27.0 1.6 %reshape.21 = f32[10,1,168,256]{3,2,0,1:T(8,128)S(1)} reshape(f32[10,8,21,256]{3,2,1,0:T(8,128)} %copy.11) | data formatting | bytes 3440640 | tf_op jit(solution)/shard_map/conv_general_dilated | solution.py:17
  28.6 0.0 copy-start.2
  28.6 1.4 %fusion.20 = bf16[10,160,256]{2,1,0:T(8,128)(2,1)} fusion(f32[10,1,168,256]{3,2,0,1:T(8,128)S(1)} %reshape.21), kind=kLoop, calls=%fused_computation.26 | loop fusion | flops 3686400 | bytes 2457600 | tf_op jit(solution)/shard_map/convert_element_type | solution.py:57
  30.0 3.8 %collective-permute-start.4 = (bf16[10,160,256]{2,1,0:T(8,128)(2,1)}, bf16[10,160,256]{2,1,0:T(8,128)(2,1)}, u32[]{:S(2)}, u32[]{:S(2)}) collective-permute-start(bf16[10,160,256]{2,1,0:T(8,128)(2,1)} %fusion.20), channel_id=1, source_target_pairs={{4,0},{8,4},{12,8},{16,12},{20,16},{24,20},{28,24},{5,1},{9,5},{13... | collective-permute-start | bytes 2457608 | tf_op jit(solution)/shard_map/ppermute | solution.py:13
  33.7 3.0 %collective-permute-start.3 = (bf16[10,160,256]{2,1,0:T(8,128)(2,1)}, bf16[10,160,256]{2,1,0:T(8,128)(2,1)}, u32[]{:S(2)}, u32[]{:S(2)}) collective-permute-start(bf16[10,160,256]{2,1,0:T(8,128)(2,1)} %fusion.20), channel_id=1, source_target_pairs={{0,4},{4,8},{8,12},{12,16},{16,20},{20,24},{24,28},{1,5},{5,9},{9,... | collective-permute-start | bytes 2457608 | tf_op jit(solution)/shard_map/ppermute | solution.py:13
  36.8 4.0 %collective-permute-start.2 = (bf16[10,160,256]{2,1,0:T(8,128)(2,1)}, bf16[10,160,256]{2,1,0:T(8,128)(2,1)}, u32[]{:S(2)}, u32[]{:S(2)}) collective-permute-start(bf16[10,160,256]{2,1,0:T(8,128)(2,1)} %fusion.20), channel_id=1, source_target_pairs={{0,8},{4,12},{8,16},{12,20},{16,24},{20,28},{1,9},{5,13},{9,17},{1... | collective-permute-start | bytes 2457608 | tf_op jit(solution)/shard_map/ppermute | solution.py:13
  40.8 1.5 %collective-permute-start.5 = (bf16[10,160,256]{2,1,0:T(8,128)(2,1)}, bf16[10,160,256]{2,1,0:T(8,128)(2,1)}, u32[]{:S(2)}, u32[]{:S(2)}) collective-permute-start(bf16[10,160,256]{2,1,0:T(8,128)(2,1)} %fusion.20), channel_id=1, source_target_pairs={{8,0},{12,4},{16,8},{20,12},{24,16},{28,20},{9,1},{13,5},{17,9},{2... | collective-permute-start | bytes 2457608 | tf_op jit(solution)/shard_map/ppermute | solution.py:13
  43.6 1.3 %fusion.60 = (f32[]{:T(128)}, f32[5]{0:T(128)S(1)}) fusion(s32[1,5]{1,0:T(1,128)} %param.12, s32[]{:T(128)} %bitcast.56, s32[]{:T(128)} %bitcast.55, s32[]{:T(128)S(6)} %axis_index.23), kind=kLoop, calls=%fused_computation.76 | loop fusion | flops 39 | bytes 56 | tf_op jit(solution)/shard_map/reduce_sum | solution.py:66
  44.9 0.7 broadcast_divide_fusion
  45.6 0.7 fusion.62
  46.2 0.9 slice.81
  47.1 0.9 slice.80
  48.0 3.0 %collective-permute-done.4 = bf16[10,160,256]{2,1,0:T(8,128)(2,1)} collective-permute-done((bf16[10,160,256]{2,1,0:T(8,128)(2,1)}, bf16[10,160,256]{2,1,0:T(8,128)(2,1)}, u32[]{:S(2)}, u32[]{:S(2)}) %collective-permute-start.4) | collective-permute-done | bytes 819232 | tf_op jit(solution)/shard_map/ppermute | solution.py:13
  51.1 1.0 %collective-permute-done.3 = bf16[10,160,256]{2,1,0:T(8,128)(2,1)} collective-permute-done((bf16[10,160,256]{2,1,0:T(8,128)(2,1)}, bf16[10,160,256]{2,1,0:T(8,128)(2,1)}, u32[]{:S(2)}, u32[]{:S(2)}) %collective-permute-start.3) | collective-permute-done | bytes 819232 | tf_op jit(solution)/shard_map/ppermute | solution.py:13
  52.1 11.8 %collective-permute-done.2 = bf16[10,160,256]{2,1,0:T(8,128)(2,1)} collective-permute-done((bf16[10,160,256]{2,1,0:T(8,128)(2,1)}, bf16[10,160,256]{2,1,0:T(8,128)(2,1)}, u32[]{:S(2)}, u32[]{:S(2)}) %collective-permute-start.2) | collective-permute-done | bytes 819232 | tf_op jit(solution)/shard_map/ppermute | solution.py:13
  63.9 25.1 %collective-permute-done.5 = bf16[10,160,256]{2,1,0:T(8,128)(2,1)} collective-permute-done((bf16[10,160,256]{2,1,0:T(8,128)(2,1)}, bf16[10,160,256]{2,1,0:T(8,128)(2,1)}, u32[]{:S(2)}, u32[]{:S(2)}) %collective-permute-start.5) | collective-permute-done | bytes 819232 | tf_op jit(solution)/shard_map/ppermute | solution.py:13
  89.1 6.2 %fusion.46 = bf16[10,1,160,256]{3,2,0,1:T(8,128)(2,1)S(1)} fusion(bf16[1,160,256]{2,1,0:T(8,128)(2,1)S(1)} %slice.81, bf16[8,160,256]{2,1,0:T(8,128)(2,1)S(1)} %bitcast.59, bf16[1,160,256]{2,1,0:T(8,128)(2,1)S(1)} %slice.80, bf16[10,160,256]{2,1,0:T(8,128)(2,1)} %collective-permute-done.5, f32[]{:T(128)} %bitcast.17, ...), kind=kLoop, calls=%fused_computation.52 | loop fusion | flops 11468800 | bytes 6553620 | tf_op jit(solution)/shard_map/broadcast_in_dim | solution.py:18
  95.3 0.2 pad.4
  95.5 0.0 copy-start.8
  95.5 0.3 reshape.24
  95.8 0.0 copy-start.6
  95.8 0.2 copy.13
  96.0 0.2 copy-done.8
  96.2 0.9 copy-done.6
  97.1 1.8 %select_convert_fusion = bf16[8,8,21,256]{3,1,2,0:T(8,128)(2,1)S(1)} fusion(bf16[3,3,256,256]{3,2,1,0:T(8,128)(2,1)S(1)} %copy-done.6, bf16[10,1,7,2,256]{4,2,3,0,1:T(8,128)(2,1)S(1)} %slice.82, bf16[10,1,8,21,256]{4,2,3,0,1:T(8,128)(2,1)S(1)} %copy.13, pred[8,21]{0,1:T(8,128)(4,1)S(1)} %copy-done.8), kind=kOutput, calls=%fused_computation.30 | convolution fusion | flops 1588961280 | bytes 2799784 | tf_op jit(solution)/shard_map/conv_general_dilated | solution.py:17
  98.9 0.1 copy.14
  99.1 1.0 copy.15
  (14 shorter events, 0.2 us)
Async XLA Ops:
  0.0 19.3 %copy-start = (bf16[3,3,256,256]{3,2,1,0:T(8,128)(2,1)S(1)}, bf16[3,3,256,256]{3,2,1,0:T(8,128)(2,1)}, u32[]{:S(2)}) copy-start(bf16[3,3,256,256]{3,2,1,0:T(8,128)(2,1)} %param.13) | copy-start | bytes 3538948
  1.0 13.5 %copy-start.1 = (bf16[1,8,160,256]{3,2,1,0:T(8,128)(2,1)S(1)}, bf16[1,8,160,256]{3,2,1,0:T(8,128)(2,1)}, u32[]{:S(2)}) copy-start(bf16[1,8,160,256]{3,2,1,0:T(8,128)(2,1)} %param.8) | copy-start | bytes 1966084
  2.3 8.4 %collective-permute-start.1 = (bf16[4,160,256]{2,1,0:T(8,128)(2,1)S(1)}, bf16[4,160,256]{2,1,0:T(8,128)(2,1)S(1)}, u32[]{:S(2)}, u32[]{:S(2)}) collective-permute-start(bf16[4,160,256]{2,1,0:T(8,128)(2,1)S(1)} %pad_maximum_fusion.1), channel_id=1, source_target_pairs={{1,0},{2,1},{3,2},{5,4},{6,5},{7,6},{9,8},{10,9},{11,10},{13,12},{... | collective-permute-start | bytes 983048 | tf_op jit(solution)/shard_map/ppermute | solution.py:13
  4.4 10.2 %collective-permute-start = (bf16[4,160,256]{2,1,0:T(8,128)(2,1)S(1)}, bf16[4,160,256]{2,1,0:T(8,128)(2,1)S(1)}, u32[]{:S(2)}, u32[]{:S(2)}) collective-permute-start(bf16[4,160,256]{2,1,0:T(8,128)(2,1)S(1)} %pad_maximum_fusion), channel_id=1, source_target_pairs={{0,1},{1,2},{2,3},{4,5},{5,6},{6,7},{8,9},{9,10},{10,11},{12,13},{... | collective-permute-start | bytes 983048 | tf_op jit(solution)/shard_map/ppermute | solution.py:13
  10.7 4.0 %copy-start.3 = (bf16[4,160,256]{2,1,0:T(8,128)(2,1)}, bf16[4,160,256]{2,1,0:T(8,128)(2,1)S(1)}, u32[]{:S(2)}) copy-start(bf16[4,160,256]{2,1,0:T(8,128)(2,1)S(1)} %collective-permute-done.1) | copy-start | bytes 983044
  14.6 0.7 copy-start.4
  18.9 0.7 copy-start.7
  19.6 3.2 %copy-start.5 = (bf16[3,3,256,256]{3,2,1,0:T(8,128)(2,1)S(1)}, bf16[3,3,256,256]{3,2,1,0:T(8,128)(2,1)}, u32[]{:S(2)}) copy-start(bf16[3,3,256,256]{3,2,1,0:T(8,128)(2,1)} %param.14) | copy-start | bytes 3538948
  28.6 60.5 %copy-start.2 = (bf16[1,8,160,256]{3,2,1,0:T(8,128)(2,1)S(1)}, bf16[1,8,160,256]{3,2,1,0:T(8,128)(2,1)}, u32[]{:S(2)}) copy-start(bf16[1,8,160,256]{3,2,1,0:T(8,128)(2,1)} %param.9) | copy-start | bytes 1966084
  30.0 21.1 %collective-permute-start.4 = (bf16[10,160,256]{2,1,0:T(8,128)(2,1)}, bf16[10,160,256]{2,1,0:T(8,128)(2,1)}, u32[]{:S(2)}, u32[]{:S(2)}) collective-permute-start(bf16[10,160,256]{2,1,0:T(8,128)(2,1)} %fusion.20), channel_id=1, source_target_pairs={{4,0},{8,4},{12,8},{16,12},{20,16},{24,20},{28,24},{5,1},{9,5},{13... | collective-permute-start | bytes 2457608 | tf_op jit(solution)/shard_map/ppermute | solution.py:13
  33.7 18.3 %collective-permute-start.3 = (bf16[10,160,256]{2,1,0:T(8,128)(2,1)}, bf16[10,160,256]{2,1,0:T(8,128)(2,1)}, u32[]{:S(2)}, u32[]{:S(2)}) collective-permute-start(bf16[10,160,256]{2,1,0:T(8,128)(2,1)} %fusion.20), channel_id=1, source_target_pairs={{0,4},{4,8},{8,12},{12,16},{16,20},{20,24},{24,28},{1,5},{5,9},{9,... | collective-permute-start | bytes 2457608 | tf_op jit(solution)/shard_map/ppermute | solution.py:13
  36.8 27.1 %collective-permute-start.2 = (bf16[10,160,256]{2,1,0:T(8,128)(2,1)}, bf16[10,160,256]{2,1,0:T(8,128)(2,1)}, u32[]{:S(2)}, u32[]{:S(2)}) collective-permute-start(bf16[10,160,256]{2,1,0:T(8,128)(2,1)} %fusion.20), channel_id=1, source_target_pairs={{0,8},{4,12},{8,16},{12,20},{16,24},{20,28},{1,9},{5,13},{9,17},{1... | collective-permute-start | bytes 2457608 | tf_op jit(solution)/shard_map/ppermute | solution.py:13
  40.8 48.3 %collective-permute-start.5 = (bf16[10,160,256]{2,1,0:T(8,128)(2,1)}, bf16[10,160,256]{2,1,0:T(8,128)(2,1)}, u32[]{:S(2)}, u32[]{:S(2)}) collective-permute-start(bf16[10,160,256]{2,1,0:T(8,128)(2,1)} %fusion.20), channel_id=1, source_target_pairs={{8,0},{12,4},{16,8},{20,12},{24,16},{28,20},{9,1},{13,5},{17,9},{2... | collective-permute-start | bytes 2457608 | tf_op jit(solution)/shard_map/ppermute | solution.py:13
  95.5 0.7 copy-start.8
  95.8 1.3 %copy-start.6 = (bf16[3,3,256,256]{3,2,1,0:T(8,128)(2,1)S(1)}, bf16[3,3,256,256]{3,2,1,0:T(8,128)(2,1)}, u32[]{:S(2)}) copy-start(bf16[3,3,256,256]{3,2,1,0:T(8,128)(2,1)} %param.15) | copy-start | bytes 3538948

commit v2 on v1

--- a/solution.py
+++ b/solution.py
@@ -56,20 +56,35 @@
     first = jnp.where(inside_rows(block + 4, row0 - 2, height), first, 0.0).astype(jnp.bfloat16)
     second = jax.nn.gelu(local_conv(first, conv_second), approximate=True).astype(jnp.bfloat16)
 
-    frame_index = lax.axis_index("tm")
-    intersection = intersection_us[0].astype(jnp.float32)
-    window = intersection.shape[0]
+    count = lax.axis_size("tm")
+    t = lax.axis_index("tm")
+    window = intersection_us.shape[1]
     radius = (window - 1) // 2
-    slice_index = frame_index + jnp.arange(window, dtype=jnp.int32) - radius
-    valid = (slice_index >= exposure_start[0]) & (slice_index <= exposure_end[0])
-    frame_weights = jnp.where(valid, intersection, jnp.float32(0.0))
-    scaled = frame_weights / jnp.sum(frame_weights)
+    frames = jnp.arange(count, dtype=jnp.int32)[:, None]
+    slice_index = frames + jnp.arange(window, dtype=jnp.int32)[None, :] - radius
+    valid = (slice_index >= exposure_start[:, None]) & (slice_index <= exposure_end[:, None])
+    weights = jnp.where(valid, intersection_us.astype(jnp.float32), jnp.float32(0.0))
+    weights = weights / jnp.sum(weights, axis=1, keepdims=True)
 
-    summed = scaled[radius] * second.astype(jnp.float32)
-    for offset in range(window):
-        if offset != radius:
-            arrived = shifted(second, "tm", radius - offset)
-            summed = summed + scaled[offset] * arrived.astype(jnp.float32)
+    partner = lax.ppermute(second, "tm", [(i, i ^ 1) for i in range(count)])
+    odd = (t % 2).astype(jnp.float32)
+    even = 1.0 - odd
+    own32 = second.astype(jnp.float32)
+    partner32 = partner.astype(jnp.float32)
+    ahead = weights[jnp.minimum(t + 2, count - 1)]
+    behind = weights[jnp.maximum(t - 2, 0)]
+    to_ahead = (ahead[0] * own32 + (even * ahead[1]) * partner32).astype(jnp.bfloat16)
+    to_behind = (behind[4] * own32 + (odd * behind[3]) * partner32).astype(jnp.bfloat16)
+    from_behind = shifted(to_ahead, "tm", 2)
+    from_ahead = shifted(to_behind, "tm", -2)
+    mine = weights[t]
+    partner_weight = odd * mine[1] + even * mine[3]
+    summed = (
+        mine[2] * own32
+        + partner_weight * partner32
+        + from_behind.astype(jnp.float32)
+        + from_ahead.astype(jnp.float32)
+    )
     mixed = (summed * frame_ext.astype(jnp.float32)).astype(jnp.bfloat16)
     result = local_conv(mixed, conv_frame).astype(jnp.bfloat16)
     return result[None]
@@ -82,9 +97,9 @@
         in_specs=(
             P("tm", "rows", None, None),
             P("tm", "rows", None, None),
-            P("tm"),
-            P("tm"),
-            P("tm", None),
+            P(),
+            P(),
+            P(),
             P(),
             P(),
             P(),

time: 101 us -> 111 us (1.099)
  the two profiles are of different devices: /device:TPU:25 before, /device:TPU:0 now
where the time goes in v2:
time: 111 us
  waiting for transfers between devices  38.4 us (35%)
  local copies, waits for them, and re-layouts  21.5 us (19%)
  blocking collectives  16.2 us (15%)
  starting transfers between devices  12.3 us (11%)
  other arithmetic  11.1 us (10%)
  matrix products  7.1 us (6%)
  between operations  4.05 us (4%)
    ppermute x4, waiting for transfers between devices, shifted(): return lax.ppermute(value, axis, pairs)  38.4 us
    unnamed x2, blocking collectives  16.2 us
    ppermute x4, starting transfers between devices, shifted(): return lax.ppermute(value, axis, pairs)  12.3 us
    conv_general_dilated x8, local copies, waits for them, and re-layouts, local_conv(): lax.conv_general_dilated(padded[None], kernel, (1, 1), ((0, 0), (1, 1)),...  7.57 us
    conv_general_dilated x3, matrix products, local_conv(): lax.conv_general_dilated(padded[None], kernel, (1, 1), ((0, 0), (1, 1)),...  7.1 us
    unnamed x29, local copies, waits for them, and re-layouts  4.93 us
    convert_element_type x1, other arithmetic, shards(): (ahead[0] * own32 + even * ahead[1] * partner32).astype(jnp.bfloat16)  4.57 us
    broadcast_in_dim x2, other arithmetic, local_conv(): padded[None]  3.48 us
  transfers between devices with their start and end apart: 5, of which 4 were waited for; matrix products, arithmetic and copies ran while one was open for 6% of the time, Pallas kernels for 0%

profile of v2, /device:TPU:0, one launch (start us, length us, event | category | flops | bytes accessed | tf_op | source)
XLA Modules:
  0.0 110.7 jit_solution(18353961254256994497)
XLA Ops:
  0.0 1.0 slice_bitcast_fusion.5
  1.0 0.0 copy-start.1
  1.1 1.2 %slice_bitcast_fusion.3 = (bf16[3,160,256]{2,1,0:T(8,128)(2,1)S(1)}, bf16[3,160,256]{2,1,0:T(8,128)(2,1)S(1)}) fusion(bf16[1,8,160,256]{3,2,1,0:T(8,128)(2,1)} %param.8), kind=kLoop, calls=%fused_computation.74 | loop fusion | bytes 983040 | tf_op jit(solution)/shard_map/slice | solution.py:48
  2.3 1.3 %collective-permute-start.1 = (bf16[4,160,256]{2,1,0:T(8,128)(2,1)S(1)}, bf16[4,160,256]{2,1,0:T(8,128)(2,1)S(1)}, u32[]{:S(2)}, u32[]{:S(2)}) collective-permute-start(bf16[4,160,256]{2,1,0:T(8,128)(2,1)S(1)} %pad_maximum_fusion.1), channel_id=1, source_target_pairs={{1,0},{2,1},{3,2},{5,4},{6,5},{7,6},{9,8},{10,9},{11,10},{13,12},{... | collective-permute-start | bytes 983048 | tf_op jit(solution)/shard_map/ppermute | solution.py:13
  3.6 0.8 pad_maximum_fusion
  4.3 5.6 %collective-permute-start = (bf16[4,160,256]{2,1,0:T(8,128)(2,1)}, bf16[4,160,256]{2,1,0:T(8,128)(2,1)S(1)}, u32[]{:S(2)}, u32[]{:S(2)}) collective-permute-start(bf16[4,160,256]{2,1,0:T(8,128)(2,1)} %pad_maximum_fusion), channel_id=1, source_target_pairs={{0,1},{1,2},{2,3},{4,5},{5,6},{6,7},{8,9},{9,10},{10,11},{12,13},{... | collective-permute-start | bytes 983048 | tf_op jit(solution)/shard_map/ppermute | solution.py:13
  9.9 0.5 compare_and_fusion
  10.4 4.5 %collective-permute-done.1 = bf16[4,160,256]{2,1,0:T(8,128)(2,1)S(1)} collective-permute-done((bf16[4,160,256]{2,1,0:T(8,128)(2,1)S(1)}, bf16[4,160,256]{2,1,0:T(8,128)(2,1)S(1)}, u32[]{:S(2)}, u32[]{:S(2)}) %collective-permute-start.1) | collective-permute-done | bytes 327712 | tf_op jit(solution)/shard_map/ppermute | solution.py:13
  14.9 0.7 copy-done.3
  15.6 1.5 %collective-permute-done = bf16[4,160,256]{2,1,0:T(8,128)(2,1)S(1)} collective-permute-done((bf16[4,160,256]{2,1,0:T(8,128)(2,1)}, bf16[4,160,256]{2,1,0:T(8,128)(2,1)S(1)}, u32[]{:S(2)}, u32[]{:S(2)}) %collective-permute-start) | collective-permute-done | bytes 327712 | tf_op jit(solution)/shard_map/ppermute | solution.py:13
  17.2 0.7 copy-done.4
  17.9 0.1 maximum_bitcast_fusion
  18.0 1.4 %pad = bf16[14,1,168,256]{3,2,0,1:T(8,128)(2,1)} pad(bf16[14,1,160,256]{3,2,0,1:T(8,128)(2,1)S(1)} %maximum_bitcast_fusion, bf16[]{:T(256)} %constant.53), padding=0_0x0_0x1_7x0_0 | pad | bytes 2351106 | tf_op jit(solution)/shard_map/broadcast_in_dim | solution.py:18
  19.4 2.2 %reshape.30 = bf16[14,1,8,21,256]{4,3,2,0,1:T(8,128)(2,1)S(1)} reshape(bf16[14,1,168,256]{3,2,0,1:T(8,128)(2,1)} %pad) | data formatting | bytes 2408448 | tf_op jit(solution)/shard_map/conv_general_dilated | solution.py:17
  21.6 0.0 copy-start.9
  21.6 0.3 copy.18
  22.0 0.3 copy-done.9
  22.3 3.1 %fusion.31 = bf16[12,1,8,21,256]{4,2,3,0,1:T(8,128)(2,1)S(1)} fusion(bf16[3,3,256,256]{3,2,1,0:T(8,128)(2,1)S(1)} %copy-done, bf16[14,1,7,2,256]{4,2,3,0,1:T(8,128)(2,1)S(1)} %slice.91, bf16[14,1,8,21,256]{4,2,3,0,1:T(8,128)(2,1)S(1)} %copy.18, pred[12]{0:T(512)(128)(4,1)S(1)} %copy-done.11, pred[8,21]{0,1:T(8,128)(4,1)S(1)} %copy-done.9), kind=kOutput, calls=%fused_computation.45 | convolution fusion | flops 2388320256 | bytes 3516596 | tf_op jit(solution)/shard_map/conv_general_dilated | solution.py:17
  25.5 2.2 %fusion.40 = f32[10,8,21,256]{3,1,2,0:T(8,128)S(1)} fusion(bf16[3,3,256,256]{3,2,1,0:T(8,128)(2,1)S(1)} %copy-done.6, bf16[12,1,7,1,256]{4,2,3,0,1:T(8,128)(2,1)S(1)} %get-tuple-element.10, bf16[12,1,7,1,256]{4,2,3,0,1:T(8,128)(2,1)S(1)} %get-tuple-element.9, bf16[12,1,8,21,256]{4,2,3,0,1:T(8,128)(2,1)S(1)} %fusion.31), kind=kOutput, calls=%fused_computation.54 | convolution fusion | flops 1987461120 | bytes 4018176 | tf_op jit(solution)/shard_map/conv_general_dilated | solution.py:17
  27.7 1.9 %copy.19 = f32[10,8,21,256]{3,2,1,0:T(8,128)} copy(f32[10,8,21,256]{3,1,2,0:T(8,128)S(1)} %fusion.40) | data formatting | bytes 3440640 | tf_op jit(solution)/shard_map/conv_general_dilated | solution.py:17
  29.5 1.6 %reshape.37 = f32[10,1,168,256]{3,2,0,1:T(8,128)S(1)} reshape(f32[10,8,21,256]{3,2,1,0:T(8,128)} %copy.19) | data formatting | bytes 3440640 | tf_op jit(solution)/shard_map/conv_general_dilated | solution.py:17
  31.1 0.0 copy-start.8
  31.1 0.0 copy-start.5
  31.1 1.4 %fusion.20 = bf16[10,160,256]{2,1,0:T(8,128)(2,1)} fusion(f32[10,1,168,256]{3,2,0,1:T(8,128)S(1)} %reshape.37), kind=kLoop, calls=%fused_computation.32 | loop fusion | flops 3686400 | bytes 2457600 | tf_op jit(solution)/shard_map/convert_element_type | solution.py:57
  33.9 0.6 dynamic-slice
  34.5 0.7 dynamic-update-slice.1
  35.2 0.7 dynamic-update-slice
  36.0 8.2 %all-reduce.2 = (s32[8]{0:T(128)S(1)}, s32[8]{0:T(128)S(1)}) all-reduce(s32[8]{0:T(128)S(1)} %dynamic-update-slice.1, s32[8]{0:T(128)S(1)} %dynamic-update-slice), channel_id=3, replica_groups=mesh['tm'=8,'rows'=4] {'tm'}, use_global_device_ids=true, to_apply=%add.1 | all-reduce | flops 16 | bytes 128
  44.2 8.1 %all-gather.3 = s32[8,1,5]{2,1,0:T(1,128)S(1)} all-gather(s32[1,1,5]{2,1,0:T(1,128)S(1)} %bitcast.68), channel_id=4, replica_groups=mesh['tm'=8,'rows'=4] {'tm'}, dimensions={0}, use_global_device_ids=true | all-gather | bytes 180 | tf_op args[4]
  52.2 0.2 fusion.63
  52.4 0.1 fusion.62
  52.5 0.7 fusion.77
  53.8 0.7 fusion.75
  55.1 4.6 %fusion.27 = (bf16[10,160,256]{2,1,0:T(8,128)(2,1)}, bf16[10,160,256]{2,1,0:T(8,128)(2,1)}) fusion(bf16[10,160,256]{2,1,0:T(8,128)(2,1)} %collective-permute-done.2, f32[]{:T(128)S(6)} %mul.123, f32[]{:T(128)} %bitcast.17, f32[]{:T(128)S(6)} %mul.128, f32[]{:T(128)} %bitcast.19, f32[10,1,168,256]{3,2,0,1:T(8,128)S(1)} %reshape.37), kind=kLoop, calls=%fused_computation.39 | loop fusion | flops 7782400 | bytes 4096016 | tf_op jit(solution)/shard_map/convert_element_type | solution.py:76
  59.7 4.0 %collective-permute-start.3 = (bf16[10,160,256]{2,1,0:T(8,128)(2,1)}, bf16[10,160,256]{2,1,0:T(8,128)(2,1)}, u32[]{:S(2)}, u32[]{:S(2)}) collective-permute-start(bf16[10,160,256]{2,1,0:T(8,128)(2,1)} %get-tuple-element.7), channel_id=1, source_target_pairs={{0,8},{4,12},{8,16},{12,20},{16,24},{20,28},{1,9},{5,13},{9,17},{1... | collective-permute-start | bytes 2457608 | tf_op jit(solution)/shard_map/ppermute | solution.py:13
  63.7 1.5 %collective-permute-start.4 = (bf16[10,160,256]{2,1,0:T(8,128)(2,1)}, bf16[10,160,256]{2,1,0:T(8,128)(2,1)}, u32[]{:S(2)}, u32[]{:S(2)}) collective-permute-start(bf16[10,160,256]{2,1,0:T(8,128)(2,1)} %get-tuple-element.8), channel_id=1, source_target_pairs={{8,0},{12,4},{16,8},{20,12},{24,16},{28,20},{9,1},{13,5},{17,9},{2... | collective-permute-start | bytes 2457608 | tf_op jit(solution)/shard_map/ppermute | solution.py:13
  66.4 0.9 slice.96
  67.3 0.9 slice.95
  68.2 12.9 %collective-permute-done.3 = bf16[10,160,256]{2,1,0:T(8,128)(2,1)} collective-permute-done((bf16[10,160,256]{2,1,0:T(8,128)(2,1)}, bf16[10,160,256]{2,1,0:T(8,128)(2,1)}, u32[]{:S(2)}, u32[]{:S(2)}) %collective-permute-start.3) | collective-permute-done | bytes 819232 | tf_op jit(solution)/shard_map/ppermute | solution.py:13
  81.1 19.5 %collective-permute-done.4 = bf16[10,160,256]{2,1,0:T(8,128)(2,1)} collective-permute-done((bf16[10,160,256]{2,1,0:T(8,128)(2,1)}, bf16[10,160,256]{2,1,0:T(8,128)(2,1)}, u32[]{:S(2)}, u32[]{:S(2)}) %collective-permute-start.4) | collective-permute-done | bytes 819232 | tf_op jit(solution)/shard_map/ppermute | solution.py:13
  100.6 3.3 %fusion.55 = bf16[10,1,160,256]{3,2,0,1:T(8,128)(2,1)S(1)} fusion(bf16[10,160,256]{2,1,0:T(8,128)(2,1)} %collective-permute-done.4, bf16[10,160,256]{2,1,0:T(8,128)(2,1)} %collective-permute-done.3, bf16[10,160,256]{2,1,0:T(8,128)(2,1)} %collective-permute-done.2, bf16[1,160,256]{2,1,0:T(8,128)(2,1)S(1)} %slice.96, bf16[8,160,256]{2,1,0:T(8,128)(2,1)S(1)} %bitcast.65, ...), kind=kLoop, calls=%fused_computation.66 | loop fusion | flops 9420800 | bytes 5734408 | tf_op jit(solution)/shard_map/broadcast_in_dim | solution.py:18
  103.9 1.1 %pad.4 = bf16[10,1,168,256]{3,2,0,1:T(8,128)(2,1)} pad(bf16[10,1,160,256]{3,2,0,1:T(8,128)(2,1)S(1)} %fusion.55, bf16[]{:T(256)} %constant.53), padding=0_0x0_0x1_7x0_0 | pad | bytes 1679362 | tf_op jit(solution)/shard_map/broadcast_in_dim | solution.py:18
  105.0 1.4 %reshape.40 = bf16[10,1,8,21,256]{4,3,2,0,1:T(8,128)(2,1)S(1)} reshape(bf16[10,1,168,256]{3,2,0,1:T(8,128)(2,1)} %pad.4) | data formatting | bytes 1720320 | tf_op jit(solution)/shard_map/conv_general_dilated | solution.py:17
  106.4 0.2 copy.21
  106.7 1.0 copy-done.7
  107.7 1.8 %select_convert_fusion = bf16[8,8,21,256]{3,1,2,0:T(8,128)(2,1)S(1)} fusion(bf16[3,3,256,256]{3,2,1,0:T(8,128)(2,1)S(1)} %copy-done.7, bf16[10,1,7,2,256]{4,2,3,0,1:T(8,128)(2,1)S(1)} %slice.97, bf16[10,1,8,21,256]{4,2,3,0,1:T(8,128)(2,1)S(1)} %copy.21, pred[8,21]{0,1:T(8,128)(4,1)S(1)} %copy-done.10), kind=kOutput, calls=%fused_computation.44 | convolution fusion | flops 1588961280 | bytes 2799784 | tf_op jit(solution)/shard_map/conv_general_dilated | solution.py:17
  109.5 0.1 copy.22
  109.7 1.0 copy.23
  (28 shorter events, 0.2 us)
Async XLA Ops:
  0.0 22.0 %copy-start = (bf16[3,3,256,256]{3,2,1,0:T(8,128)(2,1)S(1)}, bf16[3,3,256,256]{3,2,1,0:T(8,128)(2,1)}, u32[]{:S(2)}) copy-start(bf16[3,3,256,256]{3,2,1,0:T(8,128)(2,1)} %param.13) | copy-start | bytes 3538948
  1.0 16.8 %copy-start.1 = (bf16[1,8,160,256]{3,2,1,0:T(8,128)(2,1)S(1)}, bf16[1,8,160,256]{3,2,1,0:T(8,128)(2,1)}, u32[]{:S(2)}) copy-start(bf16[1,8,160,256]{3,2,1,0:T(8,128)(2,1)} %param.8) | copy-start | bytes 1966084
  2.3 12.6 %collective-permute-start.1 = (bf16[4,160,256]{2,1,0:T(8,128)(2,1)S(1)}, bf16[4,160,256]{2,1,0:T(8,128)(2,1)S(1)}, u32[]{:S(2)}, u32[]{:S(2)}) collective-permute-start(bf16[4,160,256]{2,1,0:T(8,128)(2,1)S(1)} %pad_maximum_fusion.1), channel_id=1, source_target_pairs={{1,0},{2,1},{3,2},{5,4},{6,5},{7,6},{9,8},{10,9},{11,10},{13,12},{... | collective-permute-start | bytes 983048 | tf_op jit(solution)/shard_map/ppermute | solution.py:13
  4.3 12.8 %collective-permute-start = (bf16[4,160,256]{2,1,0:T(8,128)(2,1)}, bf16[4,160,256]{2,1,0:T(8,128)(2,1)S(1)}, u32[]{:S(2)}, u32[]{:S(2)}) collective-permute-start(bf16[4,160,256]{2,1,0:T(8,128)(2,1)} %pad_maximum_fusion), channel_id=1, source_target_pairs={{0,1},{1,2},{2,3},{4,5},{5,6},{6,7},{8,9},{9,10},{10,11},{12,13},{... | collective-permute-start | bytes 983048 | tf_op jit(solution)/shard_map/ppermute | solution.py:13
  14.9 0.7 copy-start.3
  17.1 0.7 copy-start.4
  21.6 0.7 copy-start.9
  21.6 0.7 copy-start.11
  22.3 3.2 %copy-start.6 = (bf16[3,3,256,256]{3,2,1,0:T(8,128)(2,1)S(1)}, bf16[3,3,256,256]{3,2,1,0:T(8,128)(2,1)}, u32[]{:S(2)}) copy-start(bf16[3,3,256,256]{3,2,1,0:T(8,128)(2,1)} %param.14) | copy-start | bytes 3538948
  31.1 2.8 %copy-start.8 = (u32[32]{0:T(128)S(1)}, u32[32]{0:T(128)}, u32[]{:S(2)}) copy-start(u32[32]{0:T(128)} %constant.69) | copy-start | bytes 388
  31.1 13.1 %copy-start.5 = (s32[1,5]{1,0:T(1,128)S(1)}, s32[1,5]{1,0:T(1,128)}, u32[]{:S(2)}) copy-start(s32[1,5]{1,0:T(1,128)} %param.12) | copy-start | bytes 64
  32.6 22.5 %collective-permute-start.2 = (bf16[10,160,256]{2,1,0:T(8,128)(2,1)}, bf16[10,160,256]{2,1,0:T(8,128)(2,1)}, u32[]{:S(2)}, u32[]{:S(2)}) collective-permute-start(bf16[10,160,256]{2,1,0:T(8,128)(2,1)} %fusion.20), channel_id=1, source_target_pairs={{0,4},{4,0},{8,12},{12,8},{16,20},{20,16},{24,28},{28,24},{1,5},{5... | collective-permute-start | bytes 2457608 | tf_op jit(solution)/shard_map/ppermute | solution.py:69
  55.1 45.4 %copy-start.2 = (bf16[1,8,160,256]{3,2,1,0:T(8,128)(2,1)S(1)}, bf16[1,8,160,256]{3,2,1,0:T(8,128)(2,1)}, u32[]{:S(2)}) copy-start(bf16[1,8,160,256]{3,2,1,0:T(8,128)(2,1)} %param.9) | copy-start | bytes 1966084
  59.7 21.4 %collective-permute-start.3 = (bf16[10,160,256]{2,1,0:T(8,128)(2,1)}, bf16[10,160,256]{2,1,0:T(8,128)(2,1)}, u32[]{:S(2)}, u32[]{:S(2)}) collective-permute-start(bf16[10,160,256]{2,1,0:T(8,128)(2,1)} %get-tuple-element.7), channel_id=1, source_target_pairs={{0,8},{4,12},{8,16},{12,20},{16,24},{20,28},{1,9},{5,13},{9,17},{1... | collective-permute-start | bytes 2457608 | tf_op jit(solution)/shard_map/ppermute | solution.py:13
  63.7 36.9 %collective-permute-start.4 = (bf16[10,160,256]{2,1,0:T(8,128)(2,1)}, bf16[10,160,256]{2,1,0:T(8,128)(2,1)}, u32[]{:S(2)}, u32[]{:S(2)}) collective-permute-start(bf16[10,160,256]{2,1,0:T(8,128)(2,1)} %get-tuple-element.8), channel_id=1, source_target_pairs={{8,0},{12,4},{16,8},{20,12},{24,16},{28,20},{9,1},{13,5},{17,9},{2... | collective-permute-start | bytes 2457608 | tf_op jit(solution)/shard_map/ppermute | solution.py:13
  105.0 1.6 %copy-start.10 = (pred[8,21]{0,1:T(8,128)(4,1)S(1)}, pred[8,21]{0,1:T(8,128)(4,1)}, u32[]{:S(2)}) copy-start(pred[8,21]{0,1:T(8,128)(4,1)} %constant.64) | copy-start | bytes 508
  106.4 1.3 %copy-start.7 = (bf16[3,3,256,256]{3,2,1,0:T(8,128)(2,1)S(1)}, bf16[3,3,256,256]{3,2,1,0:T(8,128)(2,1)}, u32[]{:S(2)}) copy-start(bf16[3,3,256,256]{3,2,1,0:T(8,128)(2,1)} %param.15) | copy-start | bytes 3538948

commit v3 on v1

--- a/solution.py
+++ b/solution.py
@@ -56,20 +56,32 @@
     first = jnp.where(inside_rows(block + 4, row0 - 2, height), first, 0.0).astype(jnp.bfloat16)
     second = jax.nn.gelu(local_conv(first, conv_second), approximate=True).astype(jnp.bfloat16)
 
-    frame_index = lax.axis_index("tm")
+    count = lax.axis_size("tm")
+    t = lax.axis_index("tm")
     intersection = intersection_us[0].astype(jnp.float32)
     window = intersection.shape[0]
     radius = (window - 1) // 2
-    slice_index = frame_index + jnp.arange(window, dtype=jnp.int32) - radius
+    slice_index = t + jnp.arange(window, dtype=jnp.int32) - radius
     valid = (slice_index >= exposure_start[0]) & (slice_index <= exposure_end[0])
-    frame_weights = jnp.where(valid, intersection, jnp.float32(0.0))
-    scaled = frame_weights / jnp.sum(frame_weights)
+    weights = jnp.where(valid, intersection, jnp.float32(0.0))
+    weights = weights / jnp.sum(weights)
 
-    summed = scaled[radius] * second.astype(jnp.float32)
-    for offset in range(window):
-        if offset != radius:
-            arrived = shifted(second, "tm", radius - offset)
-            summed = summed + scaled[offset] * arrived.astype(jnp.float32)
+    swap = [(i, i ^ 1) for i in range(count)]
+    partner = lax.ppermute(second, "tm", swap)
+    from_behind = shifted(second, "tm", 2)
+    from_ahead = shifted(second, "tm", -2)
+    odd = t % 2
+    forward = jnp.where(odd == 1, from_behind, from_ahead)
+    relayed = lax.ppermute(forward, "tm", swap)
+    even_f = (1 - odd).astype(jnp.float32)
+    odd_f = odd.astype(jnp.float32)
+    summed = (
+        weights[0] * from_behind.astype(jnp.float32)
+        + (even_f * weights[1] + odd_f * weights[3]) * relayed.astype(jnp.float32)
+        + weights[2] * second.astype(jnp.float32)
+        + (even_f * weights[3] + odd_f * weights[1]) * partner.astype(jnp.float32)
+        + weights[4] * from_ahead.astype(jnp.float32)
+    )
     mixed = (summed * frame_ext.astype(jnp.float32)).astype(jnp.bfloat16)
     result = local_conv(mixed, conv_frame).astype(jnp.bfloat16)
     return result[None]

time: 101 us -> 91.4 us (0.905)
  the two profiles are of different devices: /device:TPU:25 before, /device:TPU:22 now
where the time goes in v3:
time: 91.4 us; the launch traced here: 90 us
  waiting for transfers between devices  41.1 us (45%)
  local copies, waits for them, and re-layouts  15.9 us (17%)
  other arithmetic  10.9 us (12%)
  starting transfers between devices  10.9 us (12%)
  matrix products  7.23 us (8%)
  between operations  3.97 us (4%)
    ppermute x4, waiting for transfers between devices, shifted(): return lax.ppermute(value, axis, pairs)  41.1 us
    ppermute x4, starting transfers between devices, shifted(): return lax.ppermute(value, axis, pairs)  10.8 us
    conv_general_dilated x3, matrix products, local_conv(): lax.conv_general_dilated(padded[None], kernel, (1, 1), ((0, 0), (1, 1)),...  7.23 us
    conv_general_dilated x8, local copies, waits for them, and re-layouts, local_conv(): lax.conv_general_dilated(padded[None], kernel, (1, 1), ((0, 0), (1, 1)),...  6.47 us
    broadcast_in_dim x2, other arithmetic, local_conv(): padded[None]  5.25 us
    slice x2, local copies, waits for them, and re-layouts, shards(): down = jnp.concatenate([image[block - 3:], frame[block - 1:]], axis=0)  2.19 us
    select_n x1, other arithmetic, shards(): forward = jnp.where(odd == 1, from_behind, from_ahead)  2.13 us
    unnamed x18, local copies, waits for them, and re-layouts  1.97 us
  transfers between devices with their start and end apart: 6, of which 4 were waited for; matrix products, arithmetic and copies ran while one was open for 7% of the time, Pallas kernels for 0%

profile of v3, /device:TPU:22, one launch (start us, length us, event | category | flops | bytes accessed | tf_op | source)
XLA Modules:
  0.0 90.0 jit_solution(13172936381280306544)
XLA Ops:
  0.0 0.0 copy-start
  0.0 1.0 %slice_bitcast_fusion.5 = (bf16[1,160,256]{2,1,0:T(8,128)(2,1)S(1)}, bf16[1,160,256]{2,1,0:T(8,128)(2,1)S(1)}) fusion(bf16[1,8,160,256]{3,2,1,0:T(8,128)(2,1)} %param.9), kind=kLoop, calls=%fused_computation.63 | loop fusion | bytes 327680 | tf_op jit(solution)/shard_map/slice | solution.py:48
  1.0 0.0 copy-start.1
  1.1 1.2 %slice_bitcast_fusion.3 = (bf16[3,160,256]{2,1,0:T(8,128)(2,1)S(1)}, bf16[3,160,256]{2,1,0:T(8,128)(2,1)S(1)}) fusion(bf16[1,8,160,256]{3,2,1,0:T(8,128)(2,1)} %param.8), kind=kLoop, calls=%fused_computation.61 | loop fusion | bytes 983040 | tf_op jit(solution)/shard_map/slice | solution.py:48
  2.3 2.4 %collective-permute-start.1 = (bf16[4,160,256]{2,1,0:T(8,128)(2,1)S(1)}, bf16[4,160,256]{2,1,0:T(8,128)(2,1)S(1)}, u32[]{:S(2)}, u32[]{:S(2)}) collective-permute-start(bf16[4,160,256]{2,1,0:T(8,128)(2,1)S(1)} %pad_maximum_fusion.1), channel_id=1, source_target_pairs={{1,0},{2,1},{3,2},{5,4},{6,5},{7,6},{9,8},{10,9},{11,10},{13,12},{... | collective-permute-start | bytes 983048 | tf_op jit(solution)/shard_map/ppermute | solution.py:13
  4.7 3.5 %collective-permute-start = (bf16[4,160,256]{2,1,0:T(8,128)(2,1)S(1)}, bf16[4,160,256]{2,1,0:T(8,128)(2,1)S(1)}, u32[]{:S(2)}, u32[]{:S(2)}) collective-permute-start(bf16[4,160,256]{2,1,0:T(8,128)(2,1)S(1)} %pad_maximum_fusion), channel_id=1, source_target_pairs={{0,1},{1,2},{2,3},{4,5},{5,6},{6,7},{8,9},{9,10},{10,11},{12,13},{... | collective-permute-start | bytes 983048 | tf_op jit(solution)/shard_map/ppermute | solution.py:13
  8.2 5.4 %collective-permute-done.1 = bf16[4,160,256]{2,1,0:T(8,128)(2,1)S(1)} collective-permute-done((bf16[4,160,256]{2,1,0:T(8,128)(2,1)S(1)}, bf16[4,160,256]{2,1,0:T(8,128)(2,1)S(1)}, u32[]{:S(2)}, u32[]{:S(2)}) %collective-permute-start.1) | collective-permute-done | bytes 327712 | tf_op jit(solution)/shard_map/ppermute | solution.py:13
  13.6 2.1 %collective-permute-done = bf16[4,160,256]{2,1,0:T(8,128)(2,1)S(1)} collective-permute-done((bf16[4,160,256]{2,1,0:T(8,128)(2,1)S(1)}, bf16[4,160,256]{2,1,0:T(8,128)(2,1)S(1)}, u32[]{:S(2)}, u32[]{:S(2)}) %collective-permute-start) | collective-permute-done | bytes 327712 | tf_op jit(solution)/shard_map/ppermute | solution.py:13
  15.7 0.0 copy-done.1
  15.8 0.1 maximum_bitcast_fusion
  15.9 0.0 copy-done.3
  15.9 0.6 copy-done.4
  16.5 1.4 %pad = bf16[14,1,168,256]{3,2,0,1:T(8,128)(2,1)} pad(bf16[14,1,160,256]{3,2,0,1:T(8,128)(2,1)S(1)} %maximum_bitcast_fusion, bf16[]{:T(256)} %constant.51), padding=0_0x0_0x1_7x0_0 | pad | bytes 2351106 | tf_op jit(solution)/shard_map/broadcast_in_dim | solution.py:18
  17.9 2.2 %reshape.14 = bf16[14,1,8,21,256]{4,3,2,0,1:T(8,128)(2,1)S(1)} reshape(bf16[14,1,168,256]{3,2,0,1:T(8,128)(2,1)} %pad) | data formatting | bytes 2408448 | tf_op jit(solution)/shard_map/conv_general_dilated | solution.py:17
  20.1 0.0 copy-start.7
  20.1 0.3 copy.10
  20.4 0.0 copy-done
  20.5 0.3 copy-done.7
  20.8 3.1 %fusion.22 = bf16[12,1,8,21,256]{4,2,3,0,1:T(8,128)(2,1)S(1)} fusion(bf16[3,3,256,256]{3,2,1,0:T(8,128)(2,1)S(1)} %copy-done, bf16[14,1,7,2,256]{4,2,3,0,1:T(8,128)(2,1)S(1)} %slice.78, bf16[14,1,8,21,256]{4,2,3,0,1:T(8,128)(2,1)S(1)} %copy.10, pred[12]{0:T(512)(128)(4,1)S(1)} %compare_and_fusion, pred[8,21]{0,1:T(8,128)(4,1)S(1)} %copy-done.7), kind=kOutput, calls=%fused_computation.31 | convolution fusion | flops 2388320256 | bytes 3516596 | tf_op jit(solution)/shard_map/conv_general_dilated | solution.py:17
  24.0 2.3 %fusion.31 = f32[10,8,21,256]{3,1,2,0:T(8,128)S(1)} fusion(bf16[3,3,256,256]{3,2,1,0:T(8,128)(2,1)S(1)} %copy-done.5, bf16[12,1,7,1,256]{4,2,3,0,1:T(8,128)(2,1)S(1)} %get-tuple-element.8, bf16[12,1,7,1,256]{4,2,3,0,1:T(8,128)(2,1)S(1)} %get-tuple-element.7, bf16[12,1,8,21,256]{4,2,3,0,1:T(8,128)(2,1)S(1)} %fusion.22), kind=kOutput, calls=%fused_computation.40 | convolution fusion | flops 1987461120 | bytes 4018176 | tf_op jit(solution)/shard_map/conv_general_dilated | solution.py:17
  26.3 1.9 %copy.11 = f32[10,8,21,256]{3,2,1,0:T(8,128)} copy(f32[10,8,21,256]{3,1,2,0:T(8,128)S(1)} %fusion.31) | data formatting | bytes 3440640 | tf_op jit(solution)/shard_map/conv_general_dilated | solution.py:17
  28.1 1.6 %reshape.21 = f32[10,1,168,256]{3,2,0,1:T(8,128)S(1)} reshape(f32[10,8,21,256]{3,2,1,0:T(8,128)} %copy.11) | data formatting | bytes 3440640 | tf_op jit(solution)/shard_map/conv_general_dilated | solution.py:17
  29.7 1.4 %fusion.20 = bf16[10,160,256]{2,1,0:T(8,128)(2,1)} fusion(f32[10,1,168,256]{3,2,0,1:T(8,128)S(1)} %reshape.21), kind=kLoop, calls=%fused_computation.26 | loop fusion | flops 3686400 | bytes 2457600 | tf_op jit(solution)/shard_map/convert_element_type | solution.py:57
  31.2 3.5 %collective-permute-start.3 = (bf16[10,160,256]{2,1,0:T(8,128)(2,1)}, bf16[10,160,256]{2,1,0:T(8,128)(2,1)}, u32[]{:S(2)}, u32[]{:S(2)}) collective-permute-start(bf16[10,160,256]{2,1,0:T(8,128)(2,1)} %fusion.20), channel_id=1, source_target_pairs={{8,0},{12,4},{16,8},{20,12},{24,16},{28,20},{9,1},{13,5},{17,9},{2... | collective-permute-start | bytes 2457608 | tf_op jit(solution)/shard_map/ppermute | solution.py:13
  34.6 1.5 %collective-permute-start.2 = (bf16[10,160,256]{2,1,0:T(8,128)(2,1)}, bf16[10,160,256]{2,1,0:T(8,128)(2,1)}, u32[]{:S(2)}, u32[]{:S(2)}) collective-permute-start(bf16[10,160,256]{2,1,0:T(8,128)(2,1)} %fusion.20), channel_id=1, source_target_pairs={{0,8},{4,12},{8,16},{12,20},{16,24},{20,28},{1,9},{5,13},{9,17},{1... | collective-permute-start | bytes 2457608 | tf_op jit(solution)/shard_map/ppermute | solution.py:13
  36.1 0.1 collective-permute-start.5
  36.2 14.1 %collective-permute-done.3 = bf16[10,160,256]{2,1,0:T(8,128)(2,1)} collective-permute-done((bf16[10,160,256]{2,1,0:T(8,128)(2,1)}, bf16[10,160,256]{2,1,0:T(8,128)(2,1)}, u32[]{:S(2)}, u32[]{:S(2)}) %collective-permute-start.3) | collective-permute-done | bytes 819232 | tf_op jit(solution)/shard_map/ppermute | solution.py:13
  50.3 19.4 %collective-permute-done.2 = bf16[10,160,256]{2,1,0:T(8,128)(2,1)} collective-permute-done((bf16[10,160,256]{2,1,0:T(8,128)(2,1)}, bf16[10,160,256]{2,1,0:T(8,128)(2,1)}, u32[]{:S(2)}, u32[]{:S(2)}) %collective-permute-start.2) | collective-permute-done | bytes 819232 | tf_op jit(solution)/shard_map/ppermute | solution.py:13
  69.8 2.1 %broadcast_select_fusion = bf16[10,160,256]{2,1,0:T(8,128)(2,1)} fusion(bf16[10,160,256]{2,1,0:T(8,128)(2,1)} %collective-permute-done.2, bf16[10,160,256]{2,1,0:T(8,128)(2,1)} %collective-permute-done.3, pred[]{:T(512)S(6)} %eq.5), kind=kLoop, calls=%fused_computation.52 | loop fusion | flops 409600 | bytes 2457601 | tf_op jit(solution)/shard_map/jit(_where)/select_n | solution.py:74
  71.9 0.0 collective-permute-start.4
  73.2 1.3 %fusion.60 = (f32[]{:T(128)}, f32[5]{0:T(128)S(1)}) fusion(s32[1,5]{1,0:T(1,128)} %param.12, s32[]{:T(128)} %bitcast.56, s32[]{:T(128)} %bitcast.55, s32[]{:T(128)S(6)} %axis_index.23), kind=kLoop, calls=%fused_computation.77 | loop fusion | flops 39 | bytes 56 | tf_op jit(solution)/shard_map/reduce_sum | solution.py:67
  74.6 0.7 broadcast_divide_fusion
  75.3 0.7 fusion.62
  78.3 0.9 slice.83
  79.2 0.9 slice.82
  80.1 0.0 collective-permute-done.5
  80.1 0.0 collective-permute-done.4
  80.1 5.1 %fusion.46 = bf16[10,1,160,256]{3,2,0,1:T(8,128)(2,1)S(1)} fusion(bf16[1,160,256]{2,1,0:T(8,128)(2,1)S(1)} %slice.83, bf16[8,160,256]{2,1,0:T(8,128)(2,1)S(1)} %bitcast.59, bf16[1,160,256]{2,1,0:T(8,128)(2,1)S(1)} %slice.82, bf16[10,160,256]{2,1,0:T(8,128)(2,1)} %collective-permute-done.3, f32[]{:T(128)} %bitcast.17, ...), kind=kLoop, calls=%fused_computation.53 | loop fusion | flops 11468800 | bytes 6553620 | tf_op jit(solution)/shard_map/broadcast_in_dim | solution.py:18
  85.2 0.2 pad.4
  85.4 0.0 copy-start.8
  85.5 0.3 reshape.24
  85.7 0.0 copy-start.6
  85.7 0.2 copy.13
  86.0 0.2 copy-done.8
  86.1 0.9 copy-done.6
  87.0 1.8 %select_convert_fusion = bf16[8,8,21,256]{3,1,2,0:T(8,128)(2,1)S(1)} fusion(bf16[3,3,256,256]{3,2,1,0:T(8,128)(2,1)S(1)} %copy-done.6, bf16[10,1,7,2,256]{4,2,3,0,1:T(8,128)(2,1)S(1)} %slice.84, bf16[10,1,8,21,256]{4,2,3,0,1:T(8,128)(2,1)S(1)} %copy.13, pred[8,21]{0,1:T(8,128)(4,1)S(1)} %copy-done.8), kind=kOutput, calls=%fused_computation.30 | convolution fusion | flops 1588961280 | bytes 2799784 | tf_op jit(solution)/shard_map/conv_general_dilated | solution.py:17
  88.8 0.1 copy.14
  89.0 1.0 %copy.15 = bf16[1,8,160,256]{3,2,1,0:T(8,128)(2,1)} copy(bf16[1,8,160,256]{3,1,2,0:T(8,128)(2,1)S(1)} %slice_bitcast_fusion.1) | data formatting | bytes 1310720 | tf_op jit(solution)/shard_map/convert_element_type | solution.py:86
  (15 shorter events, 0.2 us)
Async XLA Ops:
  0.0 20.4 %copy-start = (bf16[3,3,256,256]{3,2,1,0:T(8,128)(2,1)S(1)}, bf16[3,3,256,256]{3,2,1,0:T(8,128)(2,1)}, u32[]{:S(2)}) copy-start(bf16[3,3,256,256]{3,2,1,0:T(8,128)(2,1)} %param.13) | copy-start | bytes 3538948
  1.0 14.7 %copy-start.1 = (bf16[1,8,160,256]{3,2,1,0:T(8,128)(2,1)S(1)}, bf16[1,8,160,256]{3,2,1,0:T(8,128)(2,1)}, u32[]{:S(2)}) copy-start(bf16[1,8,160,256]{3,2,1,0:T(8,128)(2,1)} %param.8) | copy-start | bytes 1966084
  2.3 11.3 %collective-permute-start.1 = (bf16[4,160,256]{2,1,0:T(8,128)(2,1)S(1)}, bf16[4,160,256]{2,1,0:T(8,128)(2,1)S(1)}, u32[]{:S(2)}, u32[]{:S(2)}) collective-permute-start(bf16[4,160,256]{2,1,0:T(8,128)(2,1)S(1)} %pad_maximum_fusion.1), channel_id=1, source_target_pairs={{1,0},{2,1},{3,2},{5,4},{6,5},{7,6},{9,8},{10,9},{11,10},{13,12},{... | collective-permute-start | bytes 983048 | tf_op jit(solution)/shard_map/ppermute | solution.py:13
  4.7 11.1 %collective-permute-start = (bf16[4,160,256]{2,1,0:T(8,128)(2,1)S(1)}, bf16[4,160,256]{2,1,0:T(8,128)(2,1)S(1)}, u32[]{:S(2)}, u32[]{:S(2)}) collective-permute-start(bf16[4,160,256]{2,1,0:T(8,128)(2,1)S(1)} %pad_maximum_fusion), channel_id=1, source_target_pairs={{0,1},{1,2},{2,3},{4,5},{5,6},{6,7},{8,9},{9,10},{10,11},{12,13},{... | collective-permute-start | bytes 983048 | tf_op jit(solution)/shard_map/ppermute | solution.py:13
  13.6 2.3 %copy-start.3 = (bf16[4,160,256]{2,1,0:T(8,128)(2,1)}, bf16[4,160,256]{2,1,0:T(8,128)(2,1)S(1)}, u32[]{:S(2)}) copy-start(bf16[4,160,256]{2,1,0:T(8,128)(2,1)S(1)} %collective-permute-done.1) | copy-start | bytes 983044
  15.7 0.7 copy-start.4
  20.1 0.7 copy-start.7
  20.8 3.2 %copy-start.5 = (bf16[3,3,256,256]{3,2,1,0:T(8,128)(2,1)S(1)}, bf16[3,3,256,256]{3,2,1,0:T(8,128)(2,1)}, u32[]{:S(2)}) copy-start(bf16[3,3,256,256]{3,2,1,0:T(8,128)(2,1)} %param.14) | copy-start | bytes 3538948
  31.2 48.9 %copy-start.2 = (bf16[1,8,160,256]{3,2,1,0:T(8,128)(2,1)S(1)}, bf16[1,8,160,256]{3,2,1,0:T(8,128)(2,1)}, u32[]{:S(2)}) copy-start(bf16[1,8,160,256]{3,2,1,0:T(8,128)(2,1)} %param.9) | copy-start | bytes 1966084
  31.2 19.2 %collective-permute-start.3 = (bf16[10,160,256]{2,1,0:T(8,128)(2,1)}, bf16[10,160,256]{2,1,0:T(8,128)(2,1)}, u32[]{:S(2)}, u32[]{:S(2)}) collective-permute-start(bf16[10,160,256]{2,1,0:T(8,128)(2,1)} %fusion.20), channel_id=1, source_target_pairs={{8,0},{12,4},{16,8},{20,12},{24,16},{28,20},{9,1},{13,5},{17,9},{2... | collective-permute-start | bytes 2457608 | tf_op jit(solution)/shard_map/ppermute | solution.py:13
  34.6 35.1 %collective-permute-start.2 = (bf16[10,160,256]{2,1,0:T(8,128)(2,1)}, bf16[10,160,256]{2,1,0:T(8,128)(2,1)}, u32[]{:S(2)}, u32[]{:S(2)}) collective-permute-start(bf16[10,160,256]{2,1,0:T(8,128)(2,1)} %fusion.20), channel_id=1, source_target_pairs={{0,8},{4,12},{8,16},{12,20},{16,24},{20,28},{1,9},{5,13},{9,17},{1... | collective-permute-start | bytes 2457608 | tf_op jit(solution)/shard_map/ppermute | solution.py:13
  36.1 44.0 %collective-permute-start.5 = (bf16[10,160,256]{2,1,0:T(8,128)(2,1)}, bf16[10,160,256]{2,1,0:T(8,128)(2,1)}, u32[]{:S(2)}, u32[]{:S(2)}) collective-permute-start(bf16[10,160,256]{2,1,0:T(8,128)(2,1)} %fusion.20), channel_id=1, source_target_pairs={{0,4},{4,0},{8,12},{12,8},{16,20},{20,16},{24,28},{28,24},{1,5},{5... | collective-permute-start | bytes 2457608 | tf_op jit(solution)/shard_map/ppermute | solution.py:70
  71.9 8.2 %collective-permute-start.4 = (bf16[10,160,256]{2,1,0:T(8,128)(2,1)}, bf16[10,160,256]{2,1,0:T(8,128)(2,1)}, u32[]{:S(2)}, u32[]{:S(2)}) collective-permute-start(bf16[10,160,256]{2,1,0:T(8,128)(2,1)} %broadcast_select_fusion), channel_id=1, source_target_pairs={{0,4},{4,0},{8,12},{12,8},{16,20},{20,16},{24,28},{28,24},{1,5},{5... | collective-permute-start | bytes 2457608 | tf_op jit(solution)/shard_map/ppermute | solution.py:75
  85.4 0.7 copy-start.8
  85.7 1.3 %copy-start.6 = (bf16[3,3,256,256]{3,2,1,0:T(8,128)(2,1)S(1)}, bf16[3,3,256,256]{3,2,1,0:T(8,128)(2,1)}, u32[]{:S(2)}) copy-start(bf16[3,3,256,256]{3,2,1,0:T(8,128)(2,1)} %param.15) | copy-start | bytes 3538948

commit v4 on v3

v4 whole, which is shorter than its diff:
```python
import numpy as np
import jax
import jax.numpy as jnp
from jax import lax
from jax.experimental import pallas as pl
from jax.experimental.pallas import tpu as pltpu
from jax.sharding import PartitionSpec as P


def shifted(value, axis, steps):
    count = lax.axis_size(axis)
    initial, last = (max(0, -steps), min(count, count - steps))
    pairs = [(source, source + steps) for source in range(initial, last)]
    if not pairs:
        return jnp.zeros_like(value)
    return lax.ppermute(value, axis, pairs)


def gelu(v):
    c = np.float32(np.sqrt(2 / np.pi))
    return v * (0.5 * (1.0 + jnp.tanh(c * (v + 0.044715 * (v * v * v)))))


def conv_rows(x, w_ref, rows_out):
    cols, cin = x.shape[1], x.shape[2]
    cout = w_ref.shape[3]
    m = rows_out * cols
    taps = []
    for b in range(3):
        acc = None
        for a in range(3):
            d = jnp.dot(x[a : a + rows_out].reshape(m, cin), w_ref[a, b],
                        preferred_element_type=jnp.float32)
            acc = d if acc is None else acc + d
        taps.append(acc)
    col = lax.broadcasted_iota(jnp.int32, (rows_out, cols, cout), 1).reshape(m, cout)
    left = pltpu.roll(taps[0], shift=1, axis=0)
    right = pltpu.roll(taps[2], shift=m - 1, axis=0)
    out = taps[1] + jnp.where(col == 0, 0.0, left) + jnp.where(col == cols - 1, 0.0, right)
    return out.reshape(rows_out, cols, cout)


def layers_kernel(bounds_ref, above_ref, image_ref, below_ref, w1_ref, w2_ref, out_ref, xbuf):
    halo = below_ref.shape[0] - 1
    block = image_ref.shape[0]
    xbuf[0:halo] = above_ref[0:halo]
    xbuf[halo : halo + block] = image_ref[...]
    xbuf[halo + block :] = below_ref[0:halo]
    rows1 = block + 2 * halo - 2
    first = gelu(conv_rows(xbuf[...], w1_ref, rows1))
    row = lax.broadcasted_iota(jnp.int32, first.shape, 0)
    inside = (row >= bounds_ref[0]) & (row < bounds_ref[1])
    first = jnp.where(inside, first, 0.0).astype(jnp.bfloat16)
    out_ref[...] = gelu(conv_rows(first, w2_ref, rows1 - 2)).astype(jnp.bfloat16)


def mix_kernel(coef_ref, fb_ref, rel_ref, own_ref, par_ref, fa_ref, above_ref, frame_ref,
               below_ref, w3_ref, out_ref, fbuf):
    halo = below_ref.shape[0] - 1
    block = frame_ref.shape[0]
    fbuf[0:1] = above_ref[halo : halo + 1]
    fbuf[1 : block + 1] = frame_ref[...]
    fbuf[block + 1 :] = below_ref[halo : halo + 1]
    f32 = jnp.float32
    summed = (
        coef_ref[0] * fb_ref[...].astype(f32)
        + coef_ref[1] * rel_ref[...].astype(f32)
        + coef_ref[2] * own_ref[...].astype(f32)
        + coef_ref[3] * par_ref[...].astype(f32)
        + coef_ref[4] * fa_ref[...].astype(f32)
    )
    mixed = (summed * fbuf[...].astype(f32)).astype(jnp.bfloat16)
    out_ref[...] = conv_rows(mixed, w3_ref, block).astype(jnp.bfloat16)


def vmem():
    return pl.BlockSpec(memory_space=pltpu.VMEM)


def smem():
    return pl.BlockSpec(memory_space=pltpu.SMEM)


def layers(bounds, above, image, below, w1, w2):
    block, cols, c = image.shape
    halo = below.shape[0] - 1
    rows = block + 2 * halo
    flops = 2 * 9 * c * c * cols * (2 * rows - 6)
    return pl.pallas_call(
        layers_kernel,
        out_shape=jax.ShapeDtypeStruct((rows - 4, cols, c), jnp.bfloat16),
        in_specs=[smem()] + [vmem()] * 5,
        out_specs=vmem(),
        scratch_shapes=[pltpu.VMEM((rows, cols, c), jnp.bfloat16)],
        cost_estimate=pl.CostEstimate(flops=flops, transcendentals=2 * rows * cols * c,
                                      bytes_accessed=4 * rows * cols * c + 4 * 9 * c * c),
    )(bounds, above, image, below, w1, w2)


def mix(coef, fb, rel, own, par, fa, above, frame, below, w3):
    block, cols, c = frame.shape
    flops = 2 * 9 * c * c * cols * block
    return pl.pallas_call(
        mix_kernel,
        out_shape=jax.ShapeDtypeStruct((block, cols, c), jnp.bfloat16),
        in_specs=[smem()] + [vmem()] * 9,
        out_specs=vmem(),
        scratch_shapes=[pltpu.VMEM((block + 2, cols, c), jnp.bfloat16)],
        cost_estimate=pl.CostEstimate(flops=flops, transcendentals=0,
                                      bytes_accessed=14 * (block + 2) * cols * c + 2 * 9 * c * c),
    )(coef, fb, rel, own, par, fa, above, frame, below, w3)


def shards(
    event_slices,
    frame_features,
    exposure_start,
    exposure_end,
    intersection_us,
    conv_first,
    conv_second,
    conv_frame,
):
    image = event_slices[0]
    frame = frame_features[0]
    block = image.shape[0]
    height = block * lax.axis_size("rows")
    row0 = lax.axis_index("rows") * block

    down = jnp.concatenate([image[block - 3 :], frame[block - 1 :]], axis=0)
    up = jnp.concatenate([image[:3], frame[:1]], axis=0)
    from_above = shifted(down, "rows", 1)
    from_below = shifted(up, "rows", -1)

    bounds = jnp.stack([2 - row0, height - row0 + 2]).astype(jnp.int32)
    second = layers(bounds, from_above, image, from_below, conv_first, conv_second)

    count = lax.axis_size("tm")
    t = lax.axis_index("tm")
    intersection = intersection_us[0].astype(jnp.float32)
    window = intersection.shape[0]
    radius = (window - 1) // 2
    slice_index = t + jnp.arange(window, dtype=jnp.int32) - radius
    valid = (slice_index >= exposure_start[0]) & (slice_index <= exposure_end[0])
    weights = jnp.where(valid, intersection, jnp.float32(0.0))
    weights = weights / jnp.sum(weights)

    swap = [(i, i ^ 1) for i in range(count)]
    partner = lax.ppermute(second, "tm", swap)
    from_behind = shifted(second, "tm", 2)
    from_ahead = shifted(second, "tm", -2)
    odd = t % 2
    forward = jnp.where(odd == 1, from_behind, from_ahead)
    relayed = lax.ppermute(forward, "tm", swap)
    is_odd = odd == 1
    coef = jnp.stack([
        weights[0],
        jnp.where(is_odd, weights[3], weights[1]),
        weights[2],
        jnp.where(is_odd, weights[1], weights[3]),
        weights[4],
    ])
    result = mix(coef, from_behind, relayed, second, partner, from_ahead,
                 from_above, frame, from_below, conv_frame)
    return result[None]


def solution(mesh):
    return jax.shard_map(
        shards,
        mesh=mesh,
        in_specs=(
            P("tm", "rows", None, None),
            P("tm", "rows", None, None),
            P("tm"),
            P("tm"),
            P("tm", None),
            P(),
            P(),
            P(),
        ),
        out_specs=P("tm", "rows", None, None),
        check_vma=False,
    )
```

time: 91.4 us -> 83.9 us (0.918)
  the two profiles are of different devices: /device:TPU:22 before, /device:TPU:1 now
where the time goes in v4:
time: 83.9 us; the launch traced here: 83.5 us
  waiting for transfers between devices  40 us (48%)
  starting transfers between devices  14.8 us (18%)
  Pallas kernels  14.8 us (18%)
  local copies, waits for them, and re-layouts  7.09 us (8%)
  between operations  3.92 us (5%)
  other arithmetic  2.91 us (3%)
    ppermute x4, waiting for transfers between devices, shifted(): return lax.ppermute(value, axis, pairs)  40 us
    ppermute x4, starting transfers between devices, shifted(): return lax.ppermute(value, axis, pairs)  9.79 us
    pallas_call x1, Pallas kernels, layers(): pl.pallas_call(layers_kernel, out_shape=jax.ShapeDtypeStruct((rows - 4, c...  8.9 us
    pallas_call x1, Pallas kernels, mix(): pl.pallas_call(mix_kernel, out_shape=jax.ShapeDtypeStruct((block, cols, c...  5.9 us
    ppermute x1, starting transfers between devices, shards(): relayed = lax.ppermute(forward, 'tm', swap)  2.78 us
    another operation x1, local copies, waits for them, and re-layouts, shards(): jnp.stack([weights[0], jnp.where(is_odd, weights[3], weights[1]), weights...  2.49 us
    ppermute x1, starting transfers between devices, shards(): partner = lax.ppermute(second, 'tm', swap)  2.21 us
    slice x2, local copies, waits for them, and re-layouts, shards(): up = jnp.concatenate([image[:3], frame[:1]], axis=0)  2.03 us
  transfers between devices with their start and end apart: 6, of which 4 were waited for; matrix products, arithmetic and copies ran while one was open for 7% of the time, Pallas kernels for 0%

profile of v4, /device:TPU:1, one launch (start us, length us, event | category | flops | bytes accessed | tf_op | source)
XLA Modules:
  0.0 83.5 jit_solution(9557447123130551530)
XLA Ops:
  0.0 1.1 %slice_bitcast_fusion = (bf16[3,160,256]{2,1,0:T(8,128)(2,1)S(1)}, bf16[3,160,256]{2,1,0:T(8,128)(2,1)S(1)}) fusion(bf16[1,8,160,256]{3,2,1,0:T(8,128)(2,1)} %param.8), kind=kLoop, calls=%fused_computation.3 | loop fusion | bytes 983040 | tf_op jit(solution)/shard_map/slice | solution.py:131
  1.1 0.9 %slice_bitcast_fusion.2 = (bf16[1,160,256]{2,1,0:T(8,128)(2,1)S(1)}, bf16[1,160,256]{2,1,0:T(8,128)(2,1)S(1)}) fusion(bf16[1,8,160,256]{3,2,1,0:T(8,128)(2,1)} %param.9), kind=kLoop, calls=%fused_computation.5 | loop fusion | bytes 327680 | tf_op jit(solution)/shard_map/slice | solution.py:131
  2.1 4.0 %collective-permute-start = (bf16[4,160,256]{2,1,0:T(8,128)(2,1)S(1)}, bf16[4,160,256]{2,1,0:T(8,128)(2,1)S(1)}, u32[]{:S(2)}, u32[]{:S(2)}) collective-permute-start(bf16[4,160,256]{2,1,0:T(8,128)(2,1)S(1)} %pad_maximum_fusion), channel_id=1, source_target_pairs={{0,1},{1,2},{2,3},{4,5},{5,6},{6,7},{8,9},{9,10},{10,11},{12,13},{... | collective-permute-start | bytes 983048 | tf_op jit(solution)/shard_map/ppermute | solution.py:16
  6.2 1.3 %collective-permute-start.1 = (bf16[4,160,256]{2,1,0:T(8,128)(2,1)S(1)}, bf16[4,160,256]{2,1,0:T(8,128)(2,1)S(1)}, u32[]{:S(2)}, u32[]{:S(2)}) collective-permute-start(bf16[4,160,256]{2,1,0:T(8,128)(2,1)S(1)} %pad_maximum_fusion.1), channel_id=1, source_target_pairs={{1,0},{2,1},{3,2},{5,4},{6,5},{7,6},{9,8},{10,9},{11,10},{13,12},{... | collective-permute-start | bytes 983048 | tf_op jit(solution)/shard_map/ppermute | solution.py:16
  7.5 0.6 pad_add_fusion.bounds_ref
  8.1 4.4 %collective-permute-done.above_ref = bf16[4,160,256]{2,1,0:T(8,128)(2,1)S(1)} collective-permute-done((bf16[4,160,256]{2,1,0:T(8,128)(2,1)S(1)}, bf16[4,160,256]{2,1,0:T(8,128)(2,1)S(1)}, u32[]{:S(2)}, u32[]{:S(2)}) %collective-permute-start) | collective-permute-done | bytes 327712 | tf_op jit(solution)/shard_map/ppermute | solution.py:16
  12.5 0.0 copy-start.4
  12.5 3.9 %collective-permute-done.1.below_ref = bf16[4,160,256]{2,1,0:T(8,128)(2,1)S(1)} collective-permute-done((bf16[4,160,256]{2,1,0:T(8,128)(2,1)S(1)}, bf16[4,160,256]{2,1,0:T(8,128)(2,1)S(1)}, u32[]{:S(2)}, u32[]{:S(2)}) %collective-permute-start.1) | collective-permute-done | bytes 327712 | tf_op jit(solution)/shard_map/ppermute | solution.py:16
  16.3 0.0 copy-start.5
  16.3 0.0 copy-done.4
  16.3 0.7 copy-done.5
  17.1 8.9 %shard_map.82.own_ref = bf16[10,160,256]{2,1,0:T(8,128)(2,1)} custom-call(s32[2]{0:T(128)} %pad_add_fusion.bounds_ref, bf16[4,160,256]{2,1,0:T(8,128)(2,1)} %copy-done.4, bf16[8,160,256]{2,1,0:T(8,128)(2,1)} %bitcast.25, bf16[4,160,256]{2,1,0:T(8,128)(2,1)} %copy-done.5, bf16[3,3,256,256]{3,2,1,0:T(8,128)(2,1)} %w1_ref.1, bf16[3,3,256,256]{3,2,1,0:T(8,128)(2,1)} %w2_ref.1), custom_call_target="tpu_custom_call" | custom-call | flops 4152360960 | bytes 4653056 | tf_op jit(solution)/shard_map/pallas_call | solution.py:89
  26.0 3.2 %collective-permute-start.2 = (bf16[10,160,256]{2,1,0:T(8,128)(2,1)}, bf16[10,160,256]{2,1,0:T(8,128)(2,1)S(1)}, u32[]{:S(2)}, u32[]{:S(2)}) collective-permute-start(bf16[10,160,256]{2,1,0:T(8,128)(2,1)} %shard_map.82.own_ref), channel_id=1, source_target_pairs={{0,8},{4,12},{8,16},{12,20},{16,24},{20,28},{1,9},{5,13},{9,17},{1... | collective-permute-start | bytes 2457608 | tf_op jit(solution)/shard_map/ppermute | solution.py:16
  29.1 1.3 %collective-permute-start.3 = (bf16[10,160,256]{2,1,0:T(8,128)(2,1)}, bf16[10,160,256]{2,1,0:T(8,128)(2,1)S(1)}, u32[]{:S(2)}, u32[]{:S(2)}) collective-permute-start(bf16[10,160,256]{2,1,0:T(8,128)(2,1)} %shard_map.82.own_ref), channel_id=1, source_target_pairs={{8,0},{12,4},{16,8},{20,12},{24,16},{28,20},{9,1},{13,5},{17,9},{2... | collective-permute-start | bytes 2457608 | tf_op jit(solution)/shard_map/ppermute | solution.py:16
  30.4 0.0 copy-start.6
  30.4 2.2 %collective-permute-start.5 = (bf16[10,160,256]{2,1,0:T(8,128)(2,1)}, bf16[10,160,256]{2,1,0:T(8,128)(2,1)S(1)}, u32[]{:S(2)}, u32[]{:S(2)}) collective-permute-start(bf16[10,160,256]{2,1,0:T(8,128)(2,1)} %shard_map.82.own_ref), channel_id=1, source_target_pairs={{0,4},{4,0},{8,12},{12,8},{16,20},{20,16},{24,28},{28,24},{1,5},{5... | collective-permute-start | bytes 2457608 | tf_op jit(solution)/shard_map/ppermute | solution.py:149
  32.7 12.4 %collective-permute-done.2.fb_ref = bf16[10,160,256]{2,1,0:T(8,128)(2,1)S(1)} collective-permute-done((bf16[10,160,256]{2,1,0:T(8,128)(2,1)}, bf16[10,160,256]{2,1,0:T(8,128)(2,1)S(1)}, u32[]{:S(2)}, u32[]{:S(2)}) %collective-permute-start.2) | collective-permute-done | bytes 819232 | tf_op jit(solution)/shard_map/ppermute | solution.py:16
  45.0 0.0 copy-start
  45.0 19.4 %collective-permute-done.3.fa_ref = bf16[10,160,256]{2,1,0:T(8,128)(2,1)S(1)} collective-permute-done((bf16[10,160,256]{2,1,0:T(8,128)(2,1)}, bf16[10,160,256]{2,1,0:T(8,128)(2,1)S(1)}, u32[]{:S(2)}, u32[]{:S(2)}) %collective-permute-start.3) | collective-permute-done | bytes 819232 | tf_op jit(solution)/shard_map/ppermute | solution.py:16
  64.4 0.0 copy-start.1
  64.4 1.1 %broadcast_select_fusion = bf16[10,160,256]{2,1,0:T(8,128)(2,1)} fusion(bf16[10,160,256]{2,1,0:T(8,128)(2,1)S(1)} %collective-permute-done.2.fb_ref, bf16[10,160,256]{2,1,0:T(8,128)(2,1)S(1)} %collective-permute-done.3.fa_ref, pred[]{:T(512)S(6)} %eq.6), kind=kLoop, calls=%fused_computation | loop fusion | flops 409600 | bytes 2457601 | tf_op jit(solution)/shard_map/jit(_where)/select_n | solution.py:153
  65.5 0.0 copy-done
  65.5 0.1 copy-done.1
  65.6 2.8 %collective-permute-start.4 = (bf16[10,160,256]{2,1,0:T(8,128)(2,1)}, bf16[10,160,256]{2,1,0:T(8,128)(2,1)S(1)}, u32[]{:S(2)}, u32[]{:S(2)}) collective-permute-start(bf16[10,160,256]{2,1,0:T(8,128)(2,1)} %broadcast_select_fusion), channel_id=1, source_target_pairs={{0,4},{4,0},{8,12},{12,8},{16,20},{20,16},{24,28},{28,24},{1,5},{5... | collective-permute-start | bytes 2457608 | tf_op jit(solution)/shard_map/ppermute | solution.py:154
  69.7 0.0 copy-done.6
  69.7 0.6 fusion
  70.3 0.6 broadcast_divide_fusion
  70.9 0.6 fusion.1
  74.0 2.5 %stack.20.coef_ref = f32[5]{0:T(128)} concatenate(f32[1]{0:T(128)} %get-tuple-element.15, f32[1]{0:T(128)} %bitcast.5, f32[1]{0:T(128)} %get-tuple-element.12, f32[1]{0:T(128)} %bitcast.6, f32[1]{0:T(128)} %get-tuple-element.11), dimensions={0} | concatenate | bytes 40 | tf_op jit(solution)/shard_map/stack | solution.py:156
  76.5 0.0 collective-permute-done.5.par_ref
  76.5 0.0 copy-start.2
  76.5 0.0 collective-permute-done.4.rel_ref
  76.5 0.0 copy-start.3
  76.5 0.9 %copy-done.2 = bf16[10,160,256]{2,1,0:T(8,128)(2,1)} copy-done((bf16[10,160,256]{2,1,0:T(8,128)(2,1)}, bf16[10,160,256]{2,1,0:T(8,128)(2,1)S(1)}, u32[]{:S(2)}) %copy-start.2) | copy-done | bytes 819224
  77.4 0.3 copy-done.3
  77.6 5.9 %shard_map.83 = bf16[8,160,256]{2,1,0:T(8,128)(2,1)} custom-call(f32[5]{0:T(128)} %stack.20.coef_ref, bf16[10,160,256]{2,1,0:T(8,128)(2,1)} %copy-done, bf16[10,160,256]{2,1,0:T(8,128)(2,1)} %copy-done.3, bf16[10,160,256]{2,1,0:T(8,128)(2,1)} %shard_map.82.own_ref, bf16[10,160,256]{2,1,0:T(8,128)(2,1)} %copy-done.2, bf16[10,160,256]{2,1,0:T(8,128)(2,1)} %copy-done.1, ...), custom_call_target="tpu_custom_call" | custom-call | flops 1509949440 | bytes 6914048 | tf_op jit(solution)/shard_map/pallas_call | solution.py:103
  (2 shorter events, 0.1 us)
Async XLA Ops:
  2.1 10.4 %collective-permute-start = (bf16[4,160,256]{2,1,0:T(8,128)(2,1)S(1)}, bf16[4,160,256]{2,1,0:T(8,128)(2,1)S(1)}, u32[]{:S(2)}, u32[]{:S(2)}) collective-permute-start(bf16[4,160,256]{2,1,0:T(8,128)(2,1)S(1)} %pad_maximum_fusion), channel_id=1, source_target_pairs={{0,1},{1,2},{2,3},{4,5},{5,6},{6,7},{8,9},{9,10},{10,11},{12,13},{... | collective-permute-start | bytes 983048 | tf_op jit(solution)/shard_map/ppermute | solution.py:16
  6.2 10.2 %collective-permute-start.1 = (bf16[4,160,256]{2,1,0:T(8,128)(2,1)S(1)}, bf16[4,160,256]{2,1,0:T(8,128)(2,1)S(1)}, u32[]{:S(2)}, u32[]{:S(2)}) collective-permute-start(bf16[4,160,256]{2,1,0:T(8,128)(2,1)S(1)} %pad_maximum_fusion.1), channel_id=1, source_target_pairs={{1,0},{2,1},{3,2},{5,4},{6,5},{7,6},{9,8},{10,9},{11,10},{13,12},{... | collective-permute-start | bytes 983048 | tf_op jit(solution)/shard_map/ppermute | solution.py:16
  12.5 3.9 %copy-start.4 = (bf16[4,160,256]{2,1,0:T(8,128)(2,1)}, bf16[4,160,256]{2,1,0:T(8,128)(2,1)S(1)}, u32[]{:S(2)}) copy-start(bf16[4,160,256]{2,1,0:T(8,128)(2,1)S(1)} %collective-permute-done.above_ref) | copy-start | bytes 983044
  16.3 0.7 copy-start.5
  26.0 19.1 %collective-permute-start.2 = (bf16[10,160,256]{2,1,0:T(8,128)(2,1)}, bf16[10,160,256]{2,1,0:T(8,128)(2,1)S(1)}, u32[]{:S(2)}, u32[]{:S(2)}) collective-permute-start(bf16[10,160,256]{2,1,0:T(8,128)(2,1)} %shard_map.82.own_ref), channel_id=1, source_target_pairs={{0,8},{4,12},{8,16},{12,20},{16,24},{20,28},{1,9},{5,13},{9,17},{1... | collective-permute-start | bytes 2457608 | tf_op jit(solution)/shard_map/ppermute | solution.py:16
  29.1 35.3 %collective-permute-start.3 = (bf16[10,160,256]{2,1,0:T(8,128)(2,1)}, bf16[10,160,256]{2,1,0:T(8,128)(2,1)S(1)}, u32[]{:S(2)}, u32[]{:S(2)}) collective-permute-start(bf16[10,160,256]{2,1,0:T(8,128)(2,1)} %shard_map.82.own_ref), channel_id=1, source_target_pairs={{8,0},{12,4},{16,8},{20,12},{24,16},{28,20},{9,1},{13,5},{17,9},{2... | collective-permute-start | bytes 2457608 | tf_op jit(solution)/shard_map/ppermute | solution.py:16
  30.4 39.3 %copy-start.6 = (s32[1,5]{1,0:T(1,128)S(1)}, s32[1,5]{1,0:T(1,128)}, u32[]{:S(2)}) copy-start(s32[1,5]{1,0:T(1,128)} %param.12) | copy-start | bytes 64
  30.4 46.0 %collective-permute-start.5 = (bf16[10,160,256]{2,1,0:T(8,128)(2,1)}, bf16[10,160,256]{2,1,0:T(8,128)(2,1)S(1)}, u32[]{:S(2)}, u32[]{:S(2)}) collective-permute-start(bf16[10,160,256]{2,1,0:T(8,128)(2,1)} %shard_map.82.own_ref), channel_id=1, source_target_pairs={{0,4},{4,0},{8,12},{12,8},{16,20},{20,16},{24,28},{28,24},{1,5},{5... | collective-permute-start | bytes 2457608 | tf_op jit(solution)/shard_map/ppermute | solution.py:149
  45.0 20.5 %copy-start = (bf16[10,160,256]{2,1,0:T(8,128)(2,1)}, bf16[10,160,256]{2,1,0:T(8,128)(2,1)S(1)}, u32[]{:S(2)}) copy-start(bf16[10,160,256]{2,1,0:T(8,128)(2,1)S(1)} %collective-permute-done.2.fb_ref) | copy-start | bytes 2457604
  64.4 1.2 %copy-start.1 = (bf16[10,160,256]{2,1,0:T(8,128)(2,1)}, bf16[10,160,256]{2,1,0:T(8,128)(2,1)S(1)}, u32[]{:S(2)}) copy-start(bf16[10,160,256]{2,1,0:T(8,128)(2,1)S(1)} %collective-permute-done.3.fa_ref) | copy-start | bytes 2457604
  65.6 10.9 %collective-permute-start.4 = (bf16[10,160,256]{2,1,0:T(8,128)(2,1)}, bf16[10,160,256]{2,1,0:T(8,128)(2,1)S(1)}, u32[]{:S(2)}, u32[]{:S(2)}) collective-permute-start(bf16[10,160,256]{2,1,0:T(8,128)(2,1)} %broadcast_select_fusion), channel_id=1, source_target_pairs={{0,4},{4,0},{8,12},{12,8},{16,20},{20,16},{24,28},{28,24},{1,5},{5... | collective-permute-start | bytes 2457608 | tf_op jit(solution)/shard_map/ppermute | solution.py:154
  76.5 0.9 %copy-start.2 = (bf16[10,160,256]{2,1,0:T(8,128)(2,1)}, bf16[10,160,256]{2,1,0:T(8,128)(2,1)S(1)}, u32[]{:S(2)}) copy-start(bf16[10,160,256]{2,1,0:T(8,128)(2,1)S(1)} %collective-permute-done.5.par_ref) | copy-start | bytes 2457604
  76.5 1.2 %copy-start.3 = (bf16[10,160,256]{2,1,0:T(8,128)(2,1)}, bf16[10,160,256]{2,1,0:T(8,128)(2,1)S(1)}, u32[]{:S(2)}) copy-start(bf16[10,160,256]{2,1,0:T(8,128)(2,1)S(1)} %collective-permute-done.4.rel_ref) | copy-start | bytes 2457604

commit v5 on v4

--- a/solution.py
+++ b/solution.py
@@ -54,7 +54,7 @@
     out_ref[...] = gelu(conv_rows(first, w2_ref, rows1 - 2)).astype(jnp.bfloat16)
 
 
-def mix_kernel(coef_ref, fb_ref, rel_ref, own_ref, par_ref, fa_ref, above_ref, frame_ref,
+def mix_kernel(coef_ref, fb_ref, rb_ref, own_ref, par_ref, ra_ref, fa_ref, above_ref, frame_ref,
                below_ref, w3_ref, out_ref, fbuf):
     halo = below_ref.shape[0] - 1
     block = frame_ref.shape[0]
@@ -64,10 +64,11 @@
     f32 = jnp.float32
     summed = (
         coef_ref[0] * fb_ref[...].astype(f32)
-        + coef_ref[1] * rel_ref[...].astype(f32)
+        + coef_ref[1] * rb_ref[...].astype(f32)
         + coef_ref[2] * own_ref[...].astype(f32)
         + coef_ref[3] * par_ref[...].astype(f32)
-        + coef_ref[4] * fa_ref[...].astype(f32)
+        + coef_ref[4] * ra_ref[...].astype(f32)
+        + coef_ref[5] * fa_ref[...].astype(f32)
     )
     mixed = (summed * fbuf[...].astype(f32)).astype(jnp.bfloat16)
     out_ref[...] = conv_rows(mixed, w3_ref, block).astype(jnp.bfloat16)
@@ -97,18 +98,18 @@
     )(bounds, above, image, below, w1, w2)
 
 
-def mix(coef, fb, rel, own, par, fa, above, frame, below, w3):
+def mix(coef, fb, rb, own, par, ra, fa, above, frame, below, w3):
     block, cols, c = frame.shape
     flops = 2 * 9 * c * c * cols * block
     return pl.pallas_call(
         mix_kernel,
         out_shape=jax.ShapeDtypeStruct((block, cols, c), jnp.bfloat16),
-        in_specs=[smem()] + [vmem()] * 9,
+        in_specs=[smem()] + [vmem()] * 10,
         out_specs=vmem(),
         scratch_shapes=[pltpu.VMEM((block + 2, cols, c), jnp.bfloat16)],
         cost_estimate=pl.CostEstimate(flops=flops, transcendentals=0,
-                                      bytes_accessed=14 * (block + 2) * cols * c + 2 * 9 * c * c),
-    )(coef, fb, rel, own, par, fa, above, frame, below, w3)
+                                      bytes_accessed=16 * (block + 2) * cols * c + 2 * 9 * c * c),
+    )(coef, fb, rb, own, par, ra, fa, above, frame, below, w3)
 
 
 def shards(
@@ -132,9 +133,6 @@
     from_above = shifted(down, "rows", 1)
     from_below = shifted(up, "rows", -1)
 
-    bounds = jnp.stack([2 - row0, height - row0 + 2]).astype(jnp.int32)
-    second = layers(bounds, from_above, image, from_below, conv_first, conv_second)
-
     count = lax.axis_size("tm")
     t = lax.axis_index("tm")
     intersection = intersection_us[0].astype(jnp.float32)
@@ -144,23 +142,20 @@
     valid = (slice_index >= exposure_start[0]) & (slice_index <= exposure_end[0])
     weights = jnp.where(valid, intersection, jnp.float32(0.0))
     weights = weights / jnp.sum(weights)
+    is_odd = (t % 2) == 1
+    partner_weight = jnp.where(is_odd, weights[1], weights[3])
+    coef = jnp.concatenate([weights[:3], partner_weight[None], weights[3:]])
+    bounds = jnp.stack([2 - row0, height - row0 + 2]).astype(jnp.int32)
+    coef, bounds, image = lax.optimization_barrier((coef, bounds, image))
 
-    swap = [(i, i ^ 1) for i in range(count)]
-    partner = lax.ppermute(second, "tm", swap)
+    second = layers(bounds, from_above, image, from_below, conv_first, conv_second)
+
+    partner = lax.ppermute(second, "tm", [(i, i ^ 1) for i in range(count)])
     from_behind = shifted(second, "tm", 2)
     from_ahead = shifted(second, "tm", -2)
-    odd = t % 2
-    forward = jnp.where(odd == 1, from_behind, from_ahead)
-    relayed = lax.ppermute(forward, "tm", swap)
-    is_odd = odd == 1
-    coef = jnp.stack([
-        weights[0],
-        jnp.where(is_odd, weights[3], weights[1]),
-        weights[2],
-        jnp.where(is_odd, weights[1], weights[3]),
-        weights[4],
-    ])
-    result = mix(coef, from_behind, relayed, second, partner, from_ahead,
+    relay_behind = lax.ppermute(from_behind, "tm", [(i + 1, i) for i in range(0, count, 2)])
+    relay_ahead = lax.ppermute(from_ahead, "tm", [(i, i + 1) for i in range(0, count, 2)])
+    result = mix(coef, from_behind, relay_behind, second, partner, relay_ahead, from_ahead,
                  from_above, frame, from_below, conv_frame)
     return result[None]
 

time: 83.9 us -> 76.8 us (0.915)
  the two profiles are of different devices: /device:TPU:1 before, /device:TPU:22 now
where the time goes in v5:
time: 76.8 us; the launch traced here: 76.1 us
  waiting for transfers between devices  38.7 us (50%)
  Pallas kernels  15.2 us (20%)
  starting transfers between devices  12.3 us (16%)
  local copies, waits for them, and re-layouts  4.44 us (6%)
  between operations  2.8 us (4%)
  other arithmetic  2.7 us (4%)
    ppermute x4, waiting for transfers between devices, shifted(): return lax.ppermute(value, axis, pairs)  35.8 us
    ppermute x4, starting transfers between devices, shifted(): return lax.ppermute(value, axis, pairs)  9.61 us
    pallas_call x1, Pallas kernels, layers(): pl.pallas_call(layers_kernel, out_shape=jax.ShapeDtypeStruct((rows - 4, c...  8.89 us
    pallas_call x1, Pallas kernels, mix(): pl.pallas_call(mix_kernel, out_shape=jax.ShapeDtypeStruct((block, cols, c...  6.3 us
    ppermute x1, waiting for transfers between devices, shards(): lax.ppermute(from_behind, 'tm', [(i + 1, i) for i in range(0, count, 2)])  2.89 us
    slice x2, local copies, waits for them, and re-layouts, shards(): up = jnp.concatenate([image[:3], frame[:1]], axis=0)  2.04 us
    unnamed x16, local copies, waits for them, and re-layouts  1.67 us
  transfers between devices with their start and end apart: 7, of which 4 were waited for; matrix products, arithmetic and copies ran while one was open for 4% of the time, Pallas kernels for 0%

profile of v5, /device:TPU:22, one launch (start us, length us, event | category | flops | bytes accessed | tf_op | source)
XLA Modules:
  0.0 76.1 jit_solution(7724940348080150066)
XLA Ops:
  0.0 0.9 %slice_bitcast_fusion.2 = (bf16[1,160,256]{2,1,0:T(8,128)(2,1)S(1)}, bf16[1,160,256]{2,1,0:T(8,128)(2,1)S(1)}) fusion(bf16[1,8,160,256]{3,2,1,0:T(8,128)(2,1)} %param.9), kind=kLoop, calls=%fused_computation.4 | loop fusion | bytes 327680 | tf_op jit(solution)/shard_map/slice | solution.py:132
  0.9 0.0 copy-start.7
  1.0 1.1 %slice_bitcast_fusion = (bf16[3,160,256]{2,1,0:T(8,128)(2,1)S(1)}, bf16[3,160,256]{2,1,0:T(8,128)(2,1)S(1)}) fusion(bf16[1,8,160,256]{3,2,1,0:T(8,128)(2,1)} %param.8), kind=kLoop, calls=%fused_computation.2 | loop fusion | bytes 983040 | tf_op jit(solution)/shard_map/slice | solution.py:132
  2.1 3.5 %collective-permute-start = (bf16[4,160,256]{2,1,0:T(8,128)(2,1)S(1)}, bf16[4,160,256]{2,1,0:T(8,128)(2,1)S(1)}, u32[]{:S(2)}, u32[]{:S(2)}) collective-permute-start(bf16[4,160,256]{2,1,0:T(8,128)(2,1)S(1)} %pad_maximum_fusion), channel_id=1, source_target_pairs={{0,1},{1,2},{2,3},{4,5},{5,6},{6,7},{8,9},{9,10},{10,11},{12,13},{... | collective-permute-start | bytes 983048 | tf_op jit(solution)/shard_map/ppermute | solution.py:16
  5.6 2.4 %collective-permute-start.1 = (bf16[4,160,256]{2,1,0:T(8,128)(2,1)S(1)}, bf16[4,160,256]{2,1,0:T(8,128)(2,1)S(1)}, u32[]{:S(2)}, u32[]{:S(2)}) collective-permute-start(bf16[4,160,256]{2,1,0:T(8,128)(2,1)S(1)} %pad_maximum_fusion.1), channel_id=1, source_target_pairs={{1,0},{2,1},{3,2},{5,4},{6,5},{7,6},{9,8},{10,9},{11,10},{13,12},{... | collective-permute-start | bytes 983048 | tf_op jit(solution)/shard_map/ppermute | solution.py:16
  9.3 0.0 copy-done.7
  9.3 0.7 fusion
  10.0 0.7 broadcast_divide_fusion
  10.7 0.1 slice.39
  10.8 0.7 fusion.1
  12.8 0.7 pad_add_fusion.bounds_ref
  13.4 0.6 pad_maximum_fusion.2.coef_ref
  14.0 0.0 collective-permute-done.above_ref
  14.0 0.0 copy-start.5
  14.0 2.7 %collective-permute-done.1.below_ref = bf16[4,160,256]{2,1,0:T(8,128)(2,1)S(1)} collective-permute-done((bf16[4,160,256]{2,1,0:T(8,128)(2,1)S(1)}, bf16[4,160,256]{2,1,0:T(8,128)(2,1)S(1)}, u32[]{:S(2)}, u32[]{:S(2)}) %collective-permute-start.1) | collective-permute-done | bytes 327712 | tf_op jit(solution)/shard_map/ppermute | solution.py:16
  16.7 0.0 copy-done.5
  16.7 0.0 copy-start.6
  16.7 0.7 copy-done.6
  17.4 8.9 %shard_map.82.own_ref = bf16[10,160,256]{2,1,0:T(8,128)(2,1)} custom-call(s32[2]{0:T(128)} %pad_add_fusion.bounds_ref, bf16[4,160,256]{2,1,0:T(8,128)(2,1)} %copy-done.5, bf16[8,160,256]{2,1,0:T(8,128)(2,1)} %bitcast.25, bf16[4,160,256]{2,1,0:T(8,128)(2,1)} %copy-done.6, bf16[3,3,256,256]{3,2,1,0:T(8,128)(2,1)} %w1_ref.1, bf16[3,3,256,256]{3,2,1,0:T(8,128)(2,1)} %w2_ref.1), custom_call_target="tpu_custom_call" | custom-call | flops 4152360960 | bytes 4653056 | tf_op jit(solution)/shard_map/pallas_call | solution.py:90
  26.3 2.5 %collective-permute-start.5 = (bf16[10,160,256]{2,1,0:T(8,128)(2,1)}, bf16[10,160,256]{2,1,0:T(8,128)(2,1)S(1)}, u32[]{:S(2)}, u32[]{:S(2)}) collective-permute-start(bf16[10,160,256]{2,1,0:T(8,128)(2,1)} %shard_map.82.own_ref), channel_id=1, source_target_pairs={{8,0},{12,4},{16,8},{20,12},{24,16},{28,20},{9,1},{13,5},{17,9},{2... | collective-permute-start | bytes 2457608 | tf_op jit(solution)/shard_map/ppermute | solution.py:16
  28.8 1.3 %collective-permute-start.2 = (bf16[10,160,256]{2,1,0:T(8,128)(2,1)}, bf16[10,160,256]{2,1,0:T(8,128)(2,1)S(1)}, u32[]{:S(2)}, u32[]{:S(2)}) collective-permute-start(bf16[10,160,256]{2,1,0:T(8,128)(2,1)} %shard_map.82.own_ref), channel_id=1, source_target_pairs={{0,8},{4,12},{8,16},{12,20},{16,24},{20,28},{1,9},{5,13},{9,17},{1... | collective-permute-start | bytes 2457608 | tf_op jit(solution)/shard_map/ppermute | solution.py:16
  30.1 0.1 collective-permute-start.4
  30.2 15.2 %collective-permute-done.5.fa_ref = bf16[10,160,256]{2,1,0:T(8,128)(2,1)S(1)} collective-permute-done((bf16[10,160,256]{2,1,0:T(8,128)(2,1)}, bf16[10,160,256]{2,1,0:T(8,128)(2,1)S(1)}, u32[]{:S(2)}, u32[]{:S(2)}) %collective-permute-start.5) | collective-permute-done | bytes 819232 | tf_op jit(solution)/shard_map/ppermute | solution.py:16
  45.4 0.0 copy-start
  45.4 1.3 %collective-permute-start.6 = (bf16[10,160,256]{2,1,0:T(8,128)(2,1)S(1)}, bf16[10,160,256]{2,1,0:T(8,128)(2,1)S(1)}, u32[]{:S(2)}, u32[]{:S(2)}) collective-permute-start(bf16[10,160,256]{2,1,0:T(8,128)(2,1)S(1)} %collective-permute-done.5.fa_ref), channel_id=1, source_target_pairs={{0,4},{8,12},{16,20},{24,28},{1,5},{9,13},{17,21},{25,29},{2,6},{1... | collective-permute-start | bytes 2457608 | tf_op jit(solution)/shard_map/ppermute | solution.py:157
  46.7 18.0 %collective-permute-done.2.fb_ref = bf16[10,160,256]{2,1,0:T(8,128)(2,1)S(1)} collective-permute-done((bf16[10,160,256]{2,1,0:T(8,128)(2,1)}, bf16[10,160,256]{2,1,0:T(8,128)(2,1)S(1)}, u32[]{:S(2)}, u32[]{:S(2)}) %collective-permute-start.2) | collective-permute-done | bytes 819232 | tf_op jit(solution)/shard_map/ppermute | solution.py:16
  64.7 0.0 copy-start.1
  64.7 1.3 %collective-permute-start.3 = (bf16[10,160,256]{2,1,0:T(8,128)(2,1)S(1)}, bf16[10,160,256]{2,1,0:T(8,128)(2,1)S(1)}, u32[]{:S(2)}, u32[]{:S(2)}) collective-permute-start(bf16[10,160,256]{2,1,0:T(8,128)(2,1)S(1)} %collective-permute-done.2.fb_ref), channel_id=1, source_target_pairs={{4,0},{12,8},{20,16},{28,24},{5,1},{13,9},{21,17},{29,25},{6,2},{1... | collective-permute-start | bytes 2457608 | tf_op jit(solution)/shard_map/ppermute | solution.py:156
  66.0 0.0 collective-permute-done.4.par_ref
  66.0 0.0 copy-start.2
  66.0 0.0 collective-permute-done.6.ra_ref
  66.0 0.0 copy-start.3
  66.0 2.9 %collective-permute-done.3.rb_ref = bf16[10,160,256]{2,1,0:T(8,128)(2,1)S(1)} collective-permute-done((bf16[10,160,256]{2,1,0:T(8,128)(2,1)S(1)}, bf16[10,160,256]{2,1,0:T(8,128)(2,1)S(1)}, u32[]{:S(2)}, u32[]{:S(2)}) %collective-permute-start.3) | collective-permute-done | bytes 819232 | tf_op jit(solution)/shard_map/ppermute | solution.py:156
  68.9 0.0 copy-start.4
  68.9 0.9 %copy-done.4 = bf16[10,160,256]{2,1,0:T(8,128)(2,1)} copy-done((bf16[10,160,256]{2,1,0:T(8,128)(2,1)}, bf16[10,160,256]{2,1,0:T(8,128)(2,1)S(1)}, u32[]{:S(2)}) %copy-start.4) | copy-done | bytes 819224
  69.8 0.0 copy-done
  69.8 0.0 copy-done.1
  69.8 0.0 copy-done.2
  69.8 0.0 copy-done.3
  69.8 6.3 %shard_map.83 = bf16[8,160,256]{2,1,0:T(8,128)(2,1)} custom-call(f32[6]{0:T(128)} %pad_maximum_fusion.2.coef_ref, bf16[10,160,256]{2,1,0:T(8,128)(2,1)} %copy-done.1, bf16[10,160,256]{2,1,0:T(8,128)(2,1)} %copy-done.4, bf16[10,160,256]{2,1,0:T(8,128)(2,1)} %shard_map.82.own_ref, bf16[10,160,256]{2,1,0:T(8,128)(2,1)} %copy-done.2, ...), custom_call_target="tpu_custom_call" | custom-call | flops 1509949440 | bytes 7733248 | tf_op jit(solution)/shard_map/pallas_call | solution.py:104
  (2 shorter events, 0.1 us)
Async XLA Ops:
  0.9 8.4 %copy-start.7 = (s32[1,5]{1,0:T(1,128)S(1)}, s32[1,5]{1,0:T(1,128)}, u32[]{:S(2)}) copy-start(s32[1,5]{1,0:T(1,128)} %param.12) | copy-start | bytes 64
  2.1 11.9 %collective-permute-start = (bf16[4,160,256]{2,1,0:T(8,128)(2,1)S(1)}, bf16[4,160,256]{2,1,0:T(8,128)(2,1)S(1)}, u32[]{:S(2)}, u32[]{:S(2)}) collective-permute-start(bf16[4,160,256]{2,1,0:T(8,128)(2,1)S(1)} %pad_maximum_fusion), channel_id=1, source_target_pairs={{0,1},{1,2},{2,3},{4,5},{5,6},{6,7},{8,9},{9,10},{10,11},{12,13},{... | collective-permute-start | bytes 983048 | tf_op jit(solution)/shard_map/ppermute | solution.py:16
  5.6 11.1 %collective-permute-start.1 = (bf16[4,160,256]{2,1,0:T(8,128)(2,1)S(1)}, bf16[4,160,256]{2,1,0:T(8,128)(2,1)S(1)}, u32[]{:S(2)}, u32[]{:S(2)}) collective-permute-start(bf16[4,160,256]{2,1,0:T(8,128)(2,1)S(1)} %pad_maximum_fusion.1), channel_id=1, source_target_pairs={{1,0},{2,1},{3,2},{5,4},{6,5},{7,6},{9,8},{10,9},{11,10},{13,12},{... | collective-permute-start | bytes 983048 | tf_op jit(solution)/shard_map/ppermute | solution.py:16
  14.0 2.7 %copy-start.5 = (bf16[4,160,256]{2,1,0:T(8,128)(2,1)}, bf16[4,160,256]{2,1,0:T(8,128)(2,1)S(1)}, u32[]{:S(2)}) copy-start(bf16[4,160,256]{2,1,0:T(8,128)(2,1)S(1)} %collective-permute-done.above_ref) | copy-start | bytes 983044
  16.7 0.7 copy-start.6
  26.3 19.0 %collective-permute-start.5 = (bf16[10,160,256]{2,1,0:T(8,128)(2,1)}, bf16[10,160,256]{2,1,0:T(8,128)(2,1)S(1)}, u32[]{:S(2)}, u32[]{:S(2)}) collective-permute-start(bf16[10,160,256]{2,1,0:T(8,128)(2,1)} %shard_map.82.own_ref), channel_id=1, source_target_pairs={{8,0},{12,4},{16,8},{20,12},{24,16},{28,20},{9,1},{13,5},{17,9},{2... | collective-permute-start | bytes 2457608 | tf_op jit(solution)/shard_map/ppermute | solution.py:16
  28.8 35.9 %collective-permute-start.2 = (bf16[10,160,256]{2,1,0:T(8,128)(2,1)}, bf16[10,160,256]{2,1,0:T(8,128)(2,1)S(1)}, u32[]{:S(2)}, u32[]{:S(2)}) collective-permute-start(bf16[10,160,256]{2,1,0:T(8,128)(2,1)} %shard_map.82.own_ref), channel_id=1, source_target_pairs={{0,8},{4,12},{8,16},{12,20},{16,24},{20,28},{1,9},{5,13},{9,17},{1... | collective-permute-start | bytes 2457608 | tf_op jit(solution)/shard_map/ppermute | solution.py:16
  30.1 35.9 %collective-permute-start.4 = (bf16[10,160,256]{2,1,0:T(8,128)(2,1)}, bf16[10,160,256]{2,1,0:T(8,128)(2,1)S(1)}, u32[]{:S(2)}, u32[]{:S(2)}) collective-permute-start(bf16[10,160,256]{2,1,0:T(8,128)(2,1)} %shard_map.82.own_ref), channel_id=1, source_target_pairs={{0,4},{4,0},{8,12},{12,8},{16,20},{20,16},{24,28},{28,24},{1,5},{5... | collective-permute-start | bytes 2457608 | tf_op jit(solution)/shard_map/ppermute | solution.py:153
  45.4 24.5 %copy-start = (bf16[10,160,256]{2,1,0:T(8,128)(2,1)}, bf16[10,160,256]{2,1,0:T(8,128)(2,1)S(1)}, u32[]{:S(2)}) copy-start(bf16[10,160,256]{2,1,0:T(8,128)(2,1)S(1)} %collective-permute-done.5.fa_ref) | copy-start | bytes 2457604
  45.4 20.6 %collective-permute-start.6 = (bf16[10,160,256]{2,1,0:T(8,128)(2,1)S(1)}, bf16[10,160,256]{2,1,0:T(8,128)(2,1)S(1)}, u32[]{:S(2)}, u32[]{:S(2)}) collective-permute-start(bf16[10,160,256]{2,1,0:T(8,128)(2,1)S(1)} %collective-permute-done.5.fa_ref), channel_id=1, source_target_pairs={{0,4},{8,12},{16,20},{24,28},{1,5},{9,13},{17,21},{25,29},{2,6},{1... | collective-permute-start | bytes 2457608 | tf_op jit(solution)/shard_map/ppermute | solution.py:157
  64.7 5.1 %copy-start.1 = (bf16[10,160,256]{2,1,0:T(8,128)(2,1)}, bf16[10,160,256]{2,1,0:T(8,128)(2,1)S(1)}, u32[]{:S(2)}) copy-start(bf16[10,160,256]{2,1,0:T(8,128)(2,1)S(1)} %collective-permute-done.2.fb_ref) | copy-start | bytes 2457604
  64.7 4.2 %collective-permute-start.3 = (bf16[10,160,256]{2,1,0:T(8,128)(2,1)S(1)}, bf16[10,160,256]{2,1,0:T(8,128)(2,1)S(1)}, u32[]{:S(2)}, u32[]{:S(2)}) collective-permute-start(bf16[10,160,256]{2,1,0:T(8,128)(2,1)S(1)} %collective-permute-done.2.fb_ref), channel_id=1, source_target_pairs={{4,0},{12,8},{20,16},{28,24},{5,1},{13,9},{21,17},{29,25},{6,2},{1... | collective-permute-start | bytes 2457608 | tf_op jit(solution)/shard_map/ppermute | solution.py:156
  66.0 3.8 %copy-start.2 = (bf16[10,160,256]{2,1,0:T(8,128)(2,1)}, bf16[10,160,256]{2,1,0:T(8,128)(2,1)S(1)}, u32[]{:S(2)}) copy-start(bf16[10,160,256]{2,1,0:T(8,128)(2,1)S(1)} %collective-permute-done.4.par_ref) | copy-start | bytes 2457604
  66.0 3.8 %copy-start.3 = (bf16[10,160,256]{2,1,0:T(8,128)(2,1)}, bf16[10,160,256]{2,1,0:T(8,128)(2,1)S(1)}, u32[]{:S(2)}) copy-start(bf16[10,160,256]{2,1,0:T(8,128)(2,1)S(1)} %collective-permute-done.6.ra_ref) | copy-start | bytes 2457604
  68.9 0.9 %copy-start.4 = (bf16[10,160,256]{2,1,0:T(8,128)(2,1)}, bf16[10,160,256]{2,1,0:T(8,128)(2,1)S(1)}, u32[]{:S(2)}) copy-start(bf16[10,160,256]{2,1,0:T(8,128)(2,1)S(1)} %collective-permute-done.3.rb_ref) | copy-start | bytes 2457604

commit v6 on v5

--- a/solution.py
+++ b/solution.py
@@ -21,18 +21,17 @@
     return v * (0.5 * (1.0 + jnp.tanh(c * (v + 0.044715 * (v * v * v)))))
 
 
-def conv_rows(x, w_ref, rows_out):
+def conv_rows(x, w_ref, stack, rows_out):
     cols, cin = x.shape[1], x.shape[2]
     cout = w_ref.shape[3]
     m = rows_out * cols
-    taps = []
-    for b in range(3):
-        acc = None
-        for a in range(3):
-            d = jnp.dot(x[a : a + rows_out].reshape(m, cin), w_ref[a, b],
-                        preferred_element_type=jnp.float32)
-            acc = d if acc is None else acc + d
-        taps.append(acc)
+    for a in range(3):
+        stack[0:rows_out, :, a * cin : (a + 1) * cin] = x[a : a + rows_out]
+    lhs = stack[0:rows_out].reshape(m, 3 * cin)
+    taps = [
+        jnp.dot(lhs, w_ref[:, b].reshape(3 * cin, cout), preferred_element_type=jnp.float32)
+        for b in range(3)
+    ]
     col = lax.broadcasted_iota(jnp.int32, (rows_out, cols, cout), 1).reshape(m, cout)
     left = pltpu.roll(taps[0], shift=1, axis=0)
     right = pltpu.roll(taps[2], shift=m - 1, axis=0)
@@ -40,22 +39,22 @@
     return out.reshape(rows_out, cols, cout)
 
 
-def layers_kernel(bounds_ref, above_ref, image_ref, below_ref, w1_ref, w2_ref, out_ref, xbuf):
+def layers_kernel(bounds_ref, above_ref, image_ref, below_ref, w1_ref, w2_ref, out_ref, xbuf, stack):
     halo = below_ref.shape[0] - 1
     block = image_ref.shape[0]
     xbuf[0:halo] = above_ref[0:halo]
     xbuf[halo : halo + block] = image_ref[...]
     xbuf[halo + block :] = below_ref[0:halo]
     rows1 = block + 2 * halo - 2
-    first = gelu(conv_rows(xbuf[...], w1_ref, rows1))
+    first = gelu(conv_rows(xbuf[...], w1_ref, stack, rows1))
     row = lax.broadcasted_iota(jnp.int32, first.shape, 0)
     inside = (row >= bounds_ref[0]) & (row < bounds_ref[1])
     first = jnp.where(inside, first, 0.0).astype(jnp.bfloat16)
-    out_ref[...] = gelu(conv_rows(first, w2_ref, rows1 - 2)).astype(jnp.bfloat16)
+    out_ref[...] = gelu(conv_rows(first, w2_ref, stack, rows1 - 2)).astype(jnp.bfloat16)
 
 
 def mix_kernel(coef_ref, fb_ref, rb_ref, own_ref, par_ref, ra_ref, fa_ref, above_ref, frame_ref,
-               below_ref, w3_ref, out_ref, fbuf):
+               below_ref, w3_ref, out_ref, fbuf, stack):
     halo = below_ref.shape[0] - 1
     block = frame_ref.shape[0]
     fbuf[0:1] = above_ref[halo : halo + 1]
@@ -71,7 +70,7 @@
         + coef_ref[5] * fa_ref[...].astype(f32)
     )
     mixed = (summed * fbuf[...].astype(f32)).astype(jnp.bfloat16)
-    out_ref[...] = conv_rows(mixed, w3_ref, block).astype(jnp.bfloat16)
+    out_ref[...] = conv_rows(mixed, w3_ref, stack, block).astype(jnp.bfloat16)
 
 
 def vmem():
@@ -92,7 +91,8 @@
         out_shape=jax.ShapeDtypeStruct((rows - 4, cols, c), jnp.bfloat16),
         in_specs=[smem()] + [vmem()] * 5,
         out_specs=vmem(),
-        scratch_shapes=[pltpu.VMEM((rows, cols, c), jnp.bfloat16)],
+        scratch_shapes=[pltpu.VMEM((rows, cols, c), jnp.bfloat16),
+                        pltpu.VMEM((rows - 2, cols, 3 * c), jnp.bfloat16)],
         cost_estimate=pl.CostEstimate(flops=flops, transcendentals=2 * rows * cols * c,
                                       bytes_accessed=4 * rows * cols * c + 4 * 9 * c * c),
     )(bounds, above, image, below, w1, w2)
@@ -106,7 +106,8 @@
         out_shape=jax.ShapeDtypeStruct((block, cols, c), jnp.bfloat16),
         in_specs=[smem()] + [vmem()] * 10,
         out_specs=vmem(),
-        scratch_shapes=[pltpu.VMEM((block + 2, cols, c), jnp.bfloat16)],
+        scratch_shapes=[pltpu.VMEM((block + 2, cols, c), jnp.bfloat16),
+                        pltpu.VMEM((block, cols, 3 * c), jnp.bfloat16)],
         cost_estimate=pl.CostEstimate(flops=flops, transcendentals=0,
                                       bytes_accessed=16 * (block + 2) * cols * c + 2 * 9 * c * c),
     )(coef, fb, rb, own, par, ra, fa, above, frame, below, w3)

time: 76.8 us -> 76.6 us (level)
  no operation moved by 1% of the time
where the time goes in v6:
time: 76.6 us; the launch traced here: 76 us
  waiting for transfers between devices  38.7 us (51%)
  Pallas kernels  15 us (20%)
  starting transfers between devices  12.3 us (16%)
  local copies, waits for them, and re-layouts  4.44 us (6%)
  between operations  2.8 us (4%)
  other arithmetic  2.7 us (4%)
    ppermute x4, waiting for transfers between devices, shifted(): return lax.ppermute(value, axis, pairs)  35.8 us
    ppermute x4, starting transfers between devices, shifted(): return lax.ppermute(value, axis, pairs)  9.61 us
    pallas_call x1, Pallas kernels, layers(): pl.pallas_call(layers_kernel, out_shape=jax.ShapeDtypeStruct((rows - 4, c...  8.73 us
    pallas_call x1, Pallas kernels, mix(): pl.pallas_call(mix_kernel, out_shape=jax.ShapeDtypeStruct((block, cols, c...  6.27 us
    ppermute x1, waiting for transfers between devices, shards(): lax.ppermute(from_behind, 'tm', [(i + 1, i) for i in range(0, count, 2)])  2.89 us
    slice x2, local copies, waits for them, and re-layouts, shards(): up = jnp.concatenate([image[:3], frame[:1]], axis=0)  2.04 us
    unnamed x16, local copies, waits for them, and re-layouts  1.67 us
  transfers between devices with their start and end apart: 7, of which 4 were waited for; matrix products, arithmetic and copies ran while one was open for 4% of the time, Pallas kernels for 0%

profile of v6, /device:TPU:22, one launch (start us, length us, event | category | flops | bytes accessed | tf_op | source)
XLA Modules:
  0.0 76.0 jit_solution(2062193699245558662)
XLA Ops:
  0.0 0.9 %slice_bitcast_fusion.2 = (bf16[1,160,256]{2,1,0:T(8,128)(2,1)S(1)}, bf16[1,160,256]{2,1,0:T(8,128)(2,1)S(1)}) fusion(bf16[1,8,160,256]{3,2,1,0:T(8,128)(2,1)} %param.9), kind=kLoop, calls=%fused_computation.4 | loop fusion | bytes 327680 | tf_op jit(solution)/shard_map/slice | solution.py:133
  0.9 0.0 copy-start.7
  1.0 1.1 %slice_bitcast_fusion = (bf16[3,160,256]{2,1,0:T(8,128)(2,1)S(1)}, bf16[3,160,256]{2,1,0:T(8,128)(2,1)S(1)}) fusion(bf16[1,8,160,256]{3,2,1,0:T(8,128)(2,1)} %param.8), kind=kLoop, calls=%fused_computation.2 | loop fusion | bytes 983040 | tf_op jit(solution)/shard_map/slice | solution.py:133
  2.1 3.5 %collective-permute-start = (bf16[4,160,256]{2,1,0:T(8,128)(2,1)S(1)}, bf16[4,160,256]{2,1,0:T(8,128)(2,1)S(1)}, u32[]{:S(2)}, u32[]{:S(2)}) collective-permute-start(bf16[4,160,256]{2,1,0:T(8,128)(2,1)S(1)} %pad_maximum_fusion), channel_id=1, source_target_pairs={{0,1},{1,2},{2,3},{4,5},{5,6},{6,7},{8,9},{9,10},{10,11},{12,13},{... | collective-permute-start | bytes 983048 | tf_op jit(solution)/shard_map/ppermute | solution.py:16
  5.6 2.4 %collective-permute-start.1 = (bf16[4,160,256]{2,1,0:T(8,128)(2,1)S(1)}, bf16[4,160,256]{2,1,0:T(8,128)(2,1)S(1)}, u32[]{:S(2)}, u32[]{:S(2)}) collective-permute-start(bf16[4,160,256]{2,1,0:T(8,128)(2,1)S(1)} %pad_maximum_fusion.1), channel_id=1, source_target_pairs={{1,0},{2,1},{3,2},{5,4},{6,5},{7,6},{9,8},{10,9},{11,10},{13,12},{... | collective-permute-start | bytes 983048 | tf_op jit(solution)/shard_map/ppermute | solution.py:16
  9.3 0.0 copy-done.7
  9.3 0.7 fusion
  10.0 0.7 broadcast_divide_fusion
  10.7 0.1 slice.39
  10.8 0.7 fusion.1
  12.8 0.7 pad_add_fusion.bounds_ref
  13.4 0.6 pad_maximum_fusion.2.coef_ref
  14.0 0.0 collective-permute-done.above_ref
  14.0 0.0 copy-start.5
  14.0 2.7 %collective-permute-done.1.below_ref = bf16[4,160,256]{2,1,0:T(8,128)(2,1)S(1)} collective-permute-done((bf16[4,160,256]{2,1,0:T(8,128)(2,1)S(1)}, bf16[4,160,256]{2,1,0:T(8,128)(2,1)S(1)}, u32[]{:S(2)}, u32[]{:S(2)}) %collective-permute-start.1) | collective-permute-done | bytes 327712 | tf_op jit(solution)/shard_map/ppermute | solution.py:16
  16.7 0.0 copy-done.5
  16.7 0.0 copy-start.6
  16.7 0.7 copy-done.6
  17.4 8.7 %shard_map.82.own_ref = bf16[10,160,256]{2,1,0:T(8,128)(2,1)} custom-call(s32[2]{0:T(128)} %pad_add_fusion.bounds_ref, bf16[4,160,256]{2,1,0:T(8,128)(2,1)} %copy-done.5, bf16[8,160,256]{2,1,0:T(8,128)(2,1)} %bitcast.25, bf16[4,160,256]{2,1,0:T(8,128)(2,1)} %copy-done.6, bf16[3,3,256,256]{3,2,1,0:T(8,128)(2,1)} %w1_ref.1, bf16[3,3,256,256]{3,2,1,0:T(8,128)(2,1)} %w2_ref.1), custom_call_target="tpu_custom_call" | custom-call | flops 4152360960 | bytes 4653056 | tf_op jit(solution)/shard_map/pallas_call | solution.py:89
  26.2 2.5 %collective-permute-start.5 = (bf16[10,160,256]{2,1,0:T(8,128)(2,1)}, bf16[10,160,256]{2,1,0:T(8,128)(2,1)S(1)}, u32[]{:S(2)}, u32[]{:S(2)}) collective-permute-start(bf16[10,160,256]{2,1,0:T(8,128)(2,1)} %shard_map.82.own_ref), channel_id=1, source_target_pairs={{8,0},{12,4},{16,8},{20,12},{24,16},{28,20},{9,1},{13,5},{17,9},{2... | collective-permute-start | bytes 2457608 | tf_op jit(solution)/shard_map/ppermute | solution.py:16
  28.7 1.3 %collective-permute-start.2 = (bf16[10,160,256]{2,1,0:T(8,128)(2,1)}, bf16[10,160,256]{2,1,0:T(8,128)(2,1)S(1)}, u32[]{:S(2)}, u32[]{:S(2)}) collective-permute-start(bf16[10,160,256]{2,1,0:T(8,128)(2,1)} %shard_map.82.own_ref), channel_id=1, source_target_pairs={{0,8},{4,12},{8,16},{12,20},{16,24},{20,28},{1,9},{5,13},{9,17},{1... | collective-permute-start | bytes 2457608 | tf_op jit(solution)/shard_map/ppermute | solution.py:16
  30.0 0.1 collective-permute-start.4
  30.0 15.2 %collective-permute-done.5.fa_ref = bf16[10,160,256]{2,1,0:T(8,128)(2,1)S(1)} collective-permute-done((bf16[10,160,256]{2,1,0:T(8,128)(2,1)}, bf16[10,160,256]{2,1,0:T(8,128)(2,1)S(1)}, u32[]{:S(2)}, u32[]{:S(2)}) %collective-permute-start.5) | collective-permute-done | bytes 819232 | tf_op jit(solution)/shard_map/ppermute | solution.py:16
  45.2 0.0 copy-start
  45.2 1.3 %collective-permute-start.6 = (bf16[10,160,256]{2,1,0:T(8,128)(2,1)S(1)}, bf16[10,160,256]{2,1,0:T(8,128)(2,1)S(1)}, u32[]{:S(2)}, u32[]{:S(2)}) collective-permute-start(bf16[10,160,256]{2,1,0:T(8,128)(2,1)S(1)} %collective-permute-done.5.fa_ref), channel_id=1, source_target_pairs={{0,4},{8,12},{16,20},{24,28},{1,5},{9,13},{17,21},{25,29},{2,6},{1... | collective-permute-start | bytes 2457608 | tf_op jit(solution)/shard_map/ppermute | solution.py:158
  46.6 18.0 %collective-permute-done.2.fb_ref = bf16[10,160,256]{2,1,0:T(8,128)(2,1)S(1)} collective-permute-done((bf16[10,160,256]{2,1,0:T(8,128)(2,1)}, bf16[10,160,256]{2,1,0:T(8,128)(2,1)S(1)}, u32[]{:S(2)}, u32[]{:S(2)}) %collective-permute-start.2) | collective-permute-done | bytes 819232 | tf_op jit(solution)/shard_map/ppermute | solution.py:16
  64.6 0.0 copy-start.1
  64.6 1.3 %collective-permute-start.3 = (bf16[10,160,256]{2,1,0:T(8,128)(2,1)S(1)}, bf16[10,160,256]{2,1,0:T(8,128)(2,1)S(1)}, u32[]{:S(2)}, u32[]{:S(2)}) collective-permute-start(bf16[10,160,256]{2,1,0:T(8,128)(2,1)S(1)} %collective-permute-done.2.fb_ref), channel_id=1, source_target_pairs={{4,0},{12,8},{20,16},{28,24},{5,1},{13,9},{21,17},{29,25},{6,2},{1... | collective-permute-start | bytes 2457608 | tf_op jit(solution)/shard_map/ppermute | solution.py:157
  65.8 0.0 collective-permute-done.4.par_ref
  65.9 0.0 copy-start.2
  65.9 0.0 collective-permute-done.6.ra_ref
  65.9 0.0 copy-start.3
  65.9 2.9 %collective-permute-done.3.rb_ref = bf16[10,160,256]{2,1,0:T(8,128)(2,1)S(1)} collective-permute-done((bf16[10,160,256]{2,1,0:T(8,128)(2,1)S(1)}, bf16[10,160,256]{2,1,0:T(8,128)(2,1)S(1)}, u32[]{:S(2)}, u32[]{:S(2)}) %collective-permute-start.3) | collective-permute-done | bytes 819232 | tf_op jit(solution)/shard_map/ppermute | solution.py:157
  68.8 0.0 copy-start.4
  68.8 0.9 %copy-done.4 = bf16[10,160,256]{2,1,0:T(8,128)(2,1)} copy-done((bf16[10,160,256]{2,1,0:T(8,128)(2,1)}, bf16[10,160,256]{2,1,0:T(8,128)(2,1)S(1)}, u32[]{:S(2)}) %copy-start.4) | copy-done | bytes 819224
  69.7 0.0 copy-done
  69.7 0.0 copy-done.1
  69.7 0.0 copy-done.2
  69.7 0.0 copy-done.3
  69.7 6.3 %shard_map.83 = bf16[8,160,256]{2,1,0:T(8,128)(2,1)} custom-call(f32[6]{0:T(128)} %pad_maximum_fusion.2.coef_ref, bf16[10,160,256]{2,1,0:T(8,128)(2,1)} %copy-done.1, bf16[10,160,256]{2,1,0:T(8,128)(2,1)} %copy-done.4, bf16[10,160,256]{2,1,0:T(8,128)(2,1)} %shard_map.82.own_ref, bf16[10,160,256]{2,1,0:T(8,128)(2,1)} %copy-done.2, ...), custom_call_target="tpu_custom_call" | custom-call | flops 1509949440 | bytes 7733248 | tf_op jit(solution)/shard_map/pallas_call | solution.py:104
  (2 shorter events, 0.1 us)
Async XLA Ops:
  0.9 8.4 %copy-start.7 = (s32[1,5]{1,0:T(1,128)S(1)}, s32[1,5]{1,0:T(1,128)}, u32[]{:S(2)}) copy-start(s32[1,5]{1,0:T(1,128)} %param.12) | copy-start | bytes 64
  2.1 11.9 %collective-permute-start = (bf16[4,160,256]{2,1,0:T(8,128)(2,1)S(1)}, bf16[4,160,256]{2,1,0:T(8,128)(2,1)S(1)}, u32[]{:S(2)}, u32[]{:S(2)}) collective-permute-start(bf16[4,160,256]{2,1,0:T(8,128)(2,1)S(1)} %pad_maximum_fusion), channel_id=1, source_target_pairs={{0,1},{1,2},{2,3},{4,5},{5,6},{6,7},{8,9},{9,10},{10,11},{12,13},{... | collective-permute-start | bytes 983048 | tf_op jit(solution)/shard_map/ppermute | solution.py:16
  5.6 11.1 %collective-permute-start.1 = (bf16[4,160,256]{2,1,0:T(8,128)(2,1)S(1)}, bf16[4,160,256]{2,1,0:T(8,128)(2,1)S(1)}, u32[]{:S(2)}, u32[]{:S(2)}) collective-permute-start(bf16[4,160,256]{2,1,0:T(8,128)(2,1)S(1)} %pad_maximum_fusion.1), channel_id=1, source_target_pairs={{1,0},{2,1},{3,2},{5,4},{6,5},{7,6},{9,8},{10,9},{11,10},{13,12},{... | collective-permute-start | bytes 983048 | tf_op jit(solution)/shard_map/ppermute | solution.py:16
  14.0 2.7 %copy-start.5 = (bf16[4,160,256]{2,1,0:T(8,128)(2,1)}, bf16[4,160,256]{2,1,0:T(8,128)(2,1)S(1)}, u32[]{:S(2)}) copy-start(bf16[4,160,256]{2,1,0:T(8,128)(2,1)S(1)} %collective-permute-done.above_ref) | copy-start | bytes 983044
  16.7 0.7 copy-start.6
  26.2 19.0 %collective-permute-start.5 = (bf16[10,160,256]{2,1,0:T(8,128)(2,1)}, bf16[10,160,256]{2,1,0:T(8,128)(2,1)S(1)}, u32[]{:S(2)}, u32[]{:S(2)}) collective-permute-start(bf16[10,160,256]{2,1,0:T(8,128)(2,1)} %shard_map.82.own_ref), channel_id=1, source_target_pairs={{8,0},{12,4},{16,8},{20,12},{24,16},{28,20},{9,1},{13,5},{17,9},{2... | collective-permute-start | bytes 2457608 | tf_op jit(solution)/shard_map/ppermute | solution.py:16
  28.7 35.9 %collective-permute-start.2 = (bf16[10,160,256]{2,1,0:T(8,128)(2,1)}, bf16[10,160,256]{2,1,0:T(8,128)(2,1)S(1)}, u32[]{:S(2)}, u32[]{:S(2)}) collective-permute-start(bf16[10,160,256]{2,1,0:T(8,128)(2,1)} %shard_map.82.own_ref), channel_id=1, source_target_pairs={{0,8},{4,12},{8,16},{12,20},{16,24},{20,28},{1,9},{5,13},{9,17},{1... | collective-permute-start | bytes 2457608 | tf_op jit(solution)/shard_map/ppermute | solution.py:16
  30.0 35.9 %collective-permute-start.4 = (bf16[10,160,256]{2,1,0:T(8,128)(2,1)}, bf16[10,160,256]{2,1,0:T(8,128)(2,1)S(1)}, u32[]{:S(2)}, u32[]{:S(2)}) collective-permute-start(bf16[10,160,256]{2,1,0:T(8,128)(2,1)} %shard_map.82.own_ref), channel_id=1, source_target_pairs={{0,4},{4,0},{8,12},{12,8},{16,20},{20,16},{24,28},{28,24},{1,5},{5... | collective-permute-start | bytes 2457608 | tf_op jit(solution)/shard_map/ppermute | solution.py:154
  45.2 24.5 %copy-start = (bf16[10,160,256]{2,1,0:T(8,128)(2,1)}, bf16[10,160,256]{2,1,0:T(8,128)(2,1)S(1)}, u32[]{:S(2)}) copy-start(bf16[10,160,256]{2,1,0:T(8,128)(2,1)S(1)} %collective-permute-done.5.fa_ref) | copy-start | bytes 2457604
  45.2 20.7 %collective-permute-start.6 = (bf16[10,160,256]{2,1,0:T(8,128)(2,1)S(1)}, bf16[10,160,256]{2,1,0:T(8,128)(2,1)S(1)}, u32[]{:S(2)}, u32[]{:S(2)}) collective-permute-start(bf16[10,160,256]{2,1,0:T(8,128)(2,1)S(1)} %collective-permute-done.5.fa_ref), channel_id=1, source_target_pairs={{0,4},{8,12},{16,20},{24,28},{1,5},{9,13},{17,21},{25,29},{2,6},{1... | collective-permute-start | bytes 2457608 | tf_op jit(solution)/shard_map/ppermute | solution.py:158
  64.6 5.1 %copy-start.1 = (bf16[10,160,256]{2,1,0:T(8,128)(2,1)}, bf16[10,160,256]{2,1,0:T(8,128)(2,1)S(1)}, u32[]{:S(2)}) copy-start(bf16[10,160,256]{2,1,0:T(8,128)(2,1)S(1)} %collective-permute-done.2.fb_ref) | copy-start | bytes 2457604
  64.6 4.2 %collective-permute-start.3 = (bf16[10,160,256]{2,1,0:T(8,128)(2,1)S(1)}, bf16[10,160,256]{2,1,0:T(8,128)(2,1)S(1)}, u32[]{:S(2)}, u32[]{:S(2)}) collective-permute-start(bf16[10,160,256]{2,1,0:T(8,128)(2,1)S(1)} %collective-permute-done.2.fb_ref), channel_id=1, source_target_pairs={{4,0},{12,8},{20,16},{28,24},{5,1},{13,9},{21,17},{29,25},{6,2},{1... | collective-permute-start | bytes 2457608 | tf_op jit(solution)/shard_map/ppermute | solution.py:157
  65.9 3.8 %copy-start.2 = (bf16[10,160,256]{2,1,0:T(8,128)(2,1)}, bf16[10,160,256]{2,1,0:T(8,128)(2,1)S(1)}, u32[]{:S(2)}) copy-start(bf16[10,160,256]{2,1,0:T(8,128)(2,1)S(1)} %collective-permute-done.4.par_ref) | copy-start | bytes 2457604
  65.9 3.8 %copy-start.3 = (bf16[10,160,256]{2,1,0:T(8,128)(2,1)}, bf16[10,160,256]{2,1,0:T(8,128)(2,1)S(1)}, u32[]{:S(2)}) copy-start(bf16[10,160,256]{2,1,0:T(8,128)(2,1)S(1)} %collective-permute-done.6.ra_ref) | copy-start | bytes 2457604
  68.8 0.9 %copy-start.4 = (bf16[10,160,256]{2,1,0:T(8,128)(2,1)}, bf16[10,160,256]{2,1,0:T(8,128)(2,1)S(1)}, u32[]{:S(2)}) copy-start(bf16[10,160,256]{2,1,0:T(8,128)(2,1)S(1)} %collective-permute-done.3.rb_ref) | copy-start | bytes 2457604

commit v7 on v6

--- a/solution.py
+++ b/solution.py
@@ -53,8 +53,8 @@
     out_ref[...] = gelu(conv_rows(first, w2_ref, stack, rows1 - 2)).astype(jnp.bfloat16)
 
 
-def mix_kernel(coef_ref, fb_ref, rb_ref, own_ref, par_ref, ra_ref, fa_ref, above_ref, frame_ref,
-               below_ref, w3_ref, out_ref, fbuf, stack):
+def mix_kernel(coef_ref, fb_ref, fb2_ref, rb_ref, own_ref, par_ref, ra_ref, fa2_ref, fa_ref,
+               above_ref, frame_ref, below_ref, w3_ref, out_ref, fbuf, stack):
     halo = below_ref.shape[0] - 1
     block = frame_ref.shape[0]
     fbuf[0:1] = above_ref[halo : halo + 1]
@@ -62,12 +62,12 @@
     fbuf[block + 1 :] = below_ref[halo : halo + 1]
     f32 = jnp.float32
     summed = (
-        coef_ref[0] * fb_ref[...].astype(f32)
+        coef_ref[0] * (fb_ref[...].astype(f32) + fb2_ref[...].astype(f32))
         + coef_ref[1] * rb_ref[...].astype(f32)
         + coef_ref[2] * own_ref[...].astype(f32)
         + coef_ref[3] * par_ref[...].astype(f32)
         + coef_ref[4] * ra_ref[...].astype(f32)
-        + coef_ref[5] * fa_ref[...].astype(f32)
+        + coef_ref[5] * (fa_ref[...].astype(f32) + fa2_ref[...].astype(f32))
     )
     mixed = (summed * fbuf[...].astype(f32)).astype(jnp.bfloat16)
     out_ref[...] = conv_rows(mixed, w3_ref, stack, block).astype(jnp.bfloat16)
@@ -98,19 +98,19 @@
     )(bounds, above, image, below, w1, w2)
 
 
-def mix(coef, fb, rb, own, par, ra, fa, above, frame, below, w3):
+def mix(coef, fb, fb2, rb, own, par, ra, fa2, fa, above, frame, below, w3):
     block, cols, c = frame.shape
     flops = 2 * 9 * c * c * cols * block
     return pl.pallas_call(
         mix_kernel,
         out_shape=jax.ShapeDtypeStruct((block, cols, c), jnp.bfloat16),
-        in_specs=[smem()] + [vmem()] * 10,
+        in_specs=[smem()] + [vmem()] * 12,
         out_specs=vmem(),
         scratch_shapes=[pltpu.VMEM((block + 2, cols, c), jnp.bfloat16),
                         pltpu.VMEM((block, cols, 3 * c), jnp.bfloat16)],
         cost_estimate=pl.CostEstimate(flops=flops, transcendentals=0,
-                                      bytes_accessed=16 * (block + 2) * cols * c + 2 * 9 * c * c),
-    )(coef, fb, rb, own, par, ra, fa, above, frame, below, w3)
+                                      bytes_accessed=20 * (block + 2) * cols * c + 2 * 9 * c * c),
+    )(coef, fb, fb2, rb, own, par, ra, fa2, fa, above, frame, below, w3)
 
 
 def shards(
@@ -152,12 +152,21 @@
     second = layers(bounds, from_above, image, from_below, conv_first, conv_second)
 
     partner = lax.ppermute(second, "tm", [(i, i ^ 1) for i in range(count)])
-    from_behind = shifted(second, "tm", 2)
-    from_ahead = shifted(second, "tm", -2)
+    if count == 8:
+        from_behind = lax.ppermute(second, "tm", [(0, 2), (1, 3), (3, 5), (4, 6), (5, 7)])
+        from_ahead = lax.ppermute(second, "tm", [(2, 0), (3, 1), (4, 2), (6, 4), (7, 5)])
+        hop = lax.ppermute(second, "tm", [(5, 1)])
+        behind_routed = lax.ppermute(from_ahead, "tm", [(0, 4)])
+        ahead_routed = lax.ppermute(hop, "tm", [(1, 3)])
+    else:
+        from_behind = shifted(second, "tm", 2)
+        from_ahead = shifted(second, "tm", -2)
+        behind_routed = jnp.zeros_like(second)
+        ahead_routed = jnp.zeros_like(second)
     relay_behind = lax.ppermute(from_behind, "tm", [(i + 1, i) for i in range(0, count, 2)])
     relay_ahead = lax.ppermute(from_ahead, "tm", [(i, i + 1) for i in range(0, count, 2)])
-    result = mix(coef, from_behind, relay_behind, second, partner, relay_ahead, from_ahead,
-                 from_above, frame, from_below, conv_frame)
+    result = mix(coef, from_behind, behind_routed, relay_behind, second, partner, relay_ahead,
+                 ahead_routed, from_ahead, from_above, frame, from_below, conv_frame)
     return result[None]
 
 

time: 76.6 us -> 75.5 us (0.986)
  the two profiles are of different devices: /device:TPU:22 before, /device:TPU:0 now
where the time goes in v7:
time: 75.5 us; the launch traced here: 75.1 us
  waiting for transfers between devices  29.9 us (40%)
  starting transfers between devices  18.8 us (25%)
  Pallas kernels  15.7 us (21%)
  local copies, waits for them, and re-layouts  5.32 us (7%)
  between operations  2.8 us (4%)
  other arithmetic  2.61 us (3%)
    ppermute x1, waiting for transfers between devices, shards(): lax.ppermute(second, 'tm', [(2, 0), (3, 1), (4, 2), (6, 4), (7, 5)])  16.6 us
    ppermute x1, waiting for transfers between devices, shards(): behind_routed = lax.ppermute(from_ahead, 'tm', [(0, 4)])  9.44 us
    pallas_call x1, Pallas kernels, layers(): pl.pallas_call(layers_kernel, out_shape=jax.ShapeDtypeStruct((rows - 4, c...  8.73 us
    pallas_call x1, Pallas kernels, mix(): pl.pallas_call(mix_kernel, out_shape=jax.ShapeDtypeStruct((block, cols, c...  6.96 us
    ppermute x2, starting transfers between devices, shifted(): return lax.ppermute(value, axis, pairs)  6.24 us
    ppermute x1, starting transfers between devices, shards(): lax.ppermute(second, 'tm', [(0, 2), (1, 3), (3, 5), (4, 6), (5, 7)])  4.6 us
    ppermute x2, waiting for transfers between devices, shifted(): return lax.ppermute(value, axis, pairs)  3.88 us
    unnamed x20, local copies, waits for them, and re-layouts  2.56 us
  transfers between devices with their start and end apart: 10, of which 3 were waited for; matrix products, arithmetic and copies ran while one was open for 4% of the time, Pallas kernels for 0%

profile of v7, /device:TPU:0, one launch (start us, length us, event | category | flops | bytes accessed | tf_op | source)
XLA Modules:
  0.0 75.1 jit_solution(2052813232911059286)
XLA Ops:
  0.0 0.9 %slice_bitcast_fusion.2 = (bf16[1,160,256]{2,1,0:T(8,128)(2,1)S(1)}, bf16[1,160,256]{2,1,0:T(8,128)(2,1)S(1)}) fusion(bf16[1,8,160,256]{3,2,1,0:T(8,128)(2,1)} %param.9), kind=kLoop, calls=%fused_computation.4 | loop fusion | bytes 327680 | tf_op jit(solution)/shard_map/slice | solution.py:133
  0.9 0.0 copy-start.9
  1.0 1.1 %slice_bitcast_fusion = (bf16[3,160,256]{2,1,0:T(8,128)(2,1)S(1)}, bf16[3,160,256]{2,1,0:T(8,128)(2,1)S(1)}) fusion(bf16[1,8,160,256]{3,2,1,0:T(8,128)(2,1)} %param.8), kind=kLoop, calls=%fused_computation.2 | loop fusion | bytes 983040 | tf_op jit(solution)/shard_map/slice | solution.py:133
  2.1 4.9 %collective-permute-start = (bf16[4,160,256]{2,1,0:T(8,128)(2,1)S(1)}, bf16[4,160,256]{2,1,0:T(8,128)(2,1)S(1)}, u32[]{:S(2)}, u32[]{:S(2)}) collective-permute-start(bf16[4,160,256]{2,1,0:T(8,128)(2,1)S(1)} %pad_maximum_fusion), channel_id=1, source_target_pairs={{0,1},{1,2},{2,3},{4,5},{5,6},{6,7},{8,9},{9,10},{10,11},{12,13},{... | collective-permute-start | bytes 983048 | tf_op jit(solution)/shard_map/ppermute | solution.py:16
  7.1 1.3 %collective-permute-start.1 = (bf16[4,160,256]{2,1,0:T(8,128)(2,1)S(1)}, bf16[4,160,256]{2,1,0:T(8,128)(2,1)S(1)}, u32[]{:S(2)}, u32[]{:S(2)}) collective-permute-start(bf16[4,160,256]{2,1,0:T(8,128)(2,1)S(1)} %pad_maximum_fusion.1), channel_id=1, source_target_pairs={{1,0},{2,1},{3,2},{5,4},{6,5},{7,6},{9,8},{10,9},{11,10},{13,12},{... | collective-permute-start | bytes 983048 | tf_op jit(solution)/shard_map/ppermute | solution.py:16
  9.7 0.0 copy-done.9
  9.7 0.6 fusion
  10.3 0.6 broadcast_divide_fusion
  11.0 0.1 slice.39
  11.0 0.7 fusion.1
  13.0 0.6 pad_add_fusion.bounds_ref
  13.6 0.7 pad_maximum_fusion.2.coef_ref
  14.3 0.0 collective-permute-done.above_ref
  14.3 0.0 copy-start.7
  14.3 3.9 %collective-permute-done.1.below_ref = bf16[4,160,256]{2,1,0:T(8,128)(2,1)S(1)} collective-permute-done((bf16[4,160,256]{2,1,0:T(8,128)(2,1)S(1)}, bf16[4,160,256]{2,1,0:T(8,128)(2,1)S(1)}, u32[]{:S(2)}, u32[]{:S(2)}) %collective-permute-start.1) | collective-permute-done | bytes 327712 | tf_op jit(solution)/shard_map/ppermute | solution.py:16
  18.2 0.0 copy-done.7
  18.2 0.0 copy-start.8
  18.2 0.7 copy-done.8
  18.9 8.7 %shard_map.82.own_ref = bf16[10,160,256]{2,1,0:T(8,128)(2,1)} custom-call(s32[2]{0:T(128)} %pad_add_fusion.bounds_ref, bf16[4,160,256]{2,1,0:T(8,128)(2,1)} %copy-done.7, bf16[8,160,256]{2,1,0:T(8,128)(2,1)} %bitcast.25, bf16[4,160,256]{2,1,0:T(8,128)(2,1)} %copy-done.8, bf16[3,3,256,256]{3,2,1,0:T(8,128)(2,1)} %w1_ref.1, bf16[3,3,256,256]{3,2,1,0:T(8,128)(2,1)} %w2_ref.1), custom_call_target="tpu_custom_call" | custom-call | flops 4152360960 | bytes 4653056 | tf_op jit(solution)/shard_map/pallas_call | solution.py:89
  27.6 0.7 collective-permute-start.8
  28.3 1.3 %collective-permute-start.3 = (bf16[10,160,256]{2,1,0:T(8,128)(2,1)}, bf16[10,160,256]{2,1,0:T(8,128)(2,1)S(1)}, u32[]{:S(2)}, u32[]{:S(2)}) collective-permute-start(bf16[10,160,256]{2,1,0:T(8,128)(2,1)} %shard_map.82.own_ref), channel_id=1, source_target_pairs={{8,0},{12,4},{16,8},{24,16},{28,20},{9,1},{13,5},{17,9},{25,17},{2... | collective-permute-start | bytes 2457608 | tf_op jit(solution)/shard_map/ppermute | solution.py:157
  29.6 4.6 %collective-permute-start.2 = (bf16[10,160,256]{2,1,0:T(8,128)(2,1)}, bf16[10,160,256]{2,1,0:T(8,128)(2,1)S(1)}, u32[]{:S(2)}, u32[]{:S(2)}) collective-permute-start(bf16[10,160,256]{2,1,0:T(8,128)(2,1)} %shard_map.82.own_ref), channel_id=1, source_target_pairs={{0,8},{4,12},{12,20},{16,24},{20,28},{1,9},{5,13},{13,21},{17,25},... | collective-permute-start | bytes 2457608 | tf_op jit(solution)/shard_map/ppermute | solution.py:156
  34.2 0.1 collective-permute-start.6
  34.3 0.0 collective-permute-done.8
  34.3 0.7 collective-permute-start.9
  35.0 16.6 %collective-permute-done.3.fa_ref = bf16[10,160,256]{2,1,0:T(8,128)(2,1)S(1)} collective-permute-done((bf16[10,160,256]{2,1,0:T(8,128)(2,1)}, bf16[10,160,256]{2,1,0:T(8,128)(2,1)S(1)}, u32[]{:S(2)}, u32[]{:S(2)}) %collective-permute-start.3) | collective-permute-done | bytes 819232 | tf_op jit(solution)/shard_map/ppermute | solution.py:157
  51.6 0.0 copy-start
  51.6 1.3 %collective-permute-start.7 = (bf16[10,160,256]{2,1,0:T(8,128)(2,1)S(1)}, bf16[10,160,256]{2,1,0:T(8,128)(2,1)S(1)}, u32[]{:S(2)}, u32[]{:S(2)}) collective-permute-start(bf16[10,160,256]{2,1,0:T(8,128)(2,1)S(1)} %collective-permute-done.3.fa_ref), channel_id=1, source_target_pairs={{0,4},{8,12},{16,20},{24,28},{1,5},{9,13},{17,21},{25,29},{2,6},{1... | collective-permute-start | bytes 2457608 | tf_op jit(solution)/shard_map/ppermute | solution.py:167
  52.9 2.5 %collective-permute-start.4 = (bf16[10,160,256]{2,1,0:T(8,128)(2,1)S(1)}, bf16[10,160,256]{2,1,0:T(8,128)(2,1)S(1)}, u32[]{:S(2)}, u32[]{:S(2)}) collective-permute-start(bf16[10,160,256]{2,1,0:T(8,128)(2,1)S(1)} %collective-permute-done.3.fa_ref), channel_id=1, source_target_pairs={{0,16},{1,17},{2,18},{3,19}} | collective-permute-start | bytes 2457608 | tf_op jit(solution)/shard_map/ppermute | solution.py:159
  55.5 0.0 collective-permute-done.2.fb_ref
  55.5 0.0 copy-start.1
  55.5 1.3 %collective-permute-start.5 = (bf16[10,160,256]{2,1,0:T(8,128)(2,1)S(1)}, bf16[10,160,256]{2,1,0:T(8,128)(2,1)S(1)}, u32[]{:S(2)}, u32[]{:S(2)}) collective-permute-start(bf16[10,160,256]{2,1,0:T(8,128)(2,1)S(1)} %collective-permute-done.2.fb_ref), channel_id=1, source_target_pairs={{4,0},{12,8},{20,16},{28,24},{5,1},{13,9},{21,17},{29,25},{6,2},{1... | collective-permute-start | bytes 2457608 | tf_op jit(solution)/shard_map/ppermute | solution.py:166
  56.8 0.0 collective-permute-done.6.par_ref
  56.8 0.0 copy-start.2
  56.8 0.0 collective-permute-done.9.fa2_ref
  56.9 0.0 copy-start.3
  56.9 0.0 collective-permute-done.7.ra_ref
  56.9 0.0 copy-start.4
  56.9 9.4 %collective-permute-done.4.fb2_ref = bf16[10,160,256]{2,1,0:T(8,128)(2,1)S(1)} collective-permute-done((bf16[10,160,256]{2,1,0:T(8,128)(2,1)S(1)}, bf16[10,160,256]{2,1,0:T(8,128)(2,1)S(1)}, u32[]{:S(2)}, u32[]{:S(2)}) %collective-permute-start.4) | collective-permute-done | bytes 819232 | tf_op jit(solution)/shard_map/ppermute | solution.py:159
  66.3 0.0 collective-permute-done.5.rb_ref
  66.3 0.0 copy-done.4
  66.3 0.9 %copy-done.5 = bf16[10,160,256]{2,1,0:T(8,128)(2,1)} copy-done((bf16[10,160,256]{2,1,0:T(8,128)(2,1)}, bf16[10,160,256]{2,1,0:T(8,128)(2,1)S(1)}, u32[]{:S(2)}) %copy-start.5) | copy-done | bytes 819224
  67.2 0.9 %copy-done.6 = bf16[10,160,256]{2,1,0:T(8,128)(2,1)} copy-done((bf16[10,160,256]{2,1,0:T(8,128)(2,1)}, bf16[10,160,256]{2,1,0:T(8,128)(2,1)S(1)}, u32[]{:S(2)}) %copy-start.6) | copy-done | bytes 819224
  68.1 0.0 copy-done
  68.1 0.0 copy-done.1
  68.1 0.0 copy-done.2
  68.1 0.0 copy-done.3
  68.2 7.0 %shard_map.83 = bf16[8,160,256]{2,1,0:T(8,128)(2,1)} custom-call(f32[6]{0:T(128)} %pad_maximum_fusion.2.coef_ref, bf16[10,160,256]{2,1,0:T(8,128)(2,1)} %copy-done.1, bf16[10,160,256]{2,1,0:T(8,128)(2,1)} %copy-done.5, bf16[10,160,256]{2,1,0:T(8,128)(2,1)} %copy-done.6, bf16[10,160,256]{2,1,0:T(8,128)(2,1)} %shard_map.82.own_ref, ...), custom_call_target="tpu_custom_call" | custom-call | flops 1509949440 | bytes 9371648 | tf_op jit(solution)/shard_map/pallas_call | solution.py:104
  (4 shorter events, 0.1 us)
Async XLA Ops:
  0.9 8.8 %copy-start.9 = (s32[1,5]{1,0:T(1,128)S(1)}, s32[1,5]{1,0:T(1,128)}, u32[]{:S(2)}) copy-start(s32[1,5]{1,0:T(1,128)} %param.12) | copy-start | bytes 64
  2.1 12.2 %collective-permute-start = (bf16[4,160,256]{2,1,0:T(8,128)(2,1)S(1)}, bf16[4,160,256]{2,1,0:T(8,128)(2,1)S(1)}, u32[]{:S(2)}, u32[]{:S(2)}) collective-permute-start(bf16[4,160,256]{2,1,0:T(8,128)(2,1)S(1)} %pad_maximum_fusion), channel_id=1, source_target_pairs={{0,1},{1,2},{2,3},{4,5},{5,6},{6,7},{8,9},{9,10},{10,11},{12,13},{... | collective-permute-start | bytes 983048 | tf_op jit(solution)/shard_map/ppermute | solution.py:16
  7.1 11.1 %collective-permute-start.1 = (bf16[4,160,256]{2,1,0:T(8,128)(2,1)S(1)}, bf16[4,160,256]{2,1,0:T(8,128)(2,1)S(1)}, u32[]{:S(2)}, u32[]{:S(2)}) collective-permute-start(bf16[4,160,256]{2,1,0:T(8,128)(2,1)S(1)} %pad_maximum_fusion.1), channel_id=1, source_target_pairs={{1,0},{2,1},{3,2},{5,4},{6,5},{7,6},{9,8},{10,9},{11,10},{13,12},{... | collective-permute-start | bytes 983048 | tf_op jit(solution)/shard_map/ppermute | solution.py:16
  14.3 3.9 %copy-start.7 = (bf16[4,160,256]{2,1,0:T(8,128)(2,1)}, bf16[4,160,256]{2,1,0:T(8,128)(2,1)S(1)}, u32[]{:S(2)}) copy-start(bf16[4,160,256]{2,1,0:T(8,128)(2,1)S(1)} %collective-permute-done.above_ref) | copy-start | bytes 983044
  18.2 0.7 copy-start.8
  27.6 6.7 %collective-permute-start.8 = (bf16[10,160,256]{2,1,0:T(8,128)(2,1)}, bf16[10,160,256]{2,1,0:T(8,128)(2,1)S(1)}, u32[]{:S(2)}, u32[]{:S(2)}) collective-permute-start(bf16[10,160,256]{2,1,0:T(8,128)(2,1)} %shard_map.82.own_ref), channel_id=1, source_target_pairs={{20,4},{21,5},{22,6},{23,7}} | collective-permute-start | bytes 2457608 | tf_op jit(solution)/shard_map/ppermute | solution.py:158
  28.3 23.3 %collective-permute-start.3 = (bf16[10,160,256]{2,1,0:T(8,128)(2,1)}, bf16[10,160,256]{2,1,0:T(8,128)(2,1)S(1)}, u32[]{:S(2)}, u32[]{:S(2)}) collective-permute-start(bf16[10,160,256]{2,1,0:T(8,128)(2,1)} %shard_map.82.own_ref), channel_id=1, source_target_pairs={{8,0},{12,4},{16,8},{24,16},{28,20},{9,1},{13,5},{17,9},{25,17},{2... | collective-permute-start | bytes 2457608 | tf_op jit(solution)/shard_map/ppermute | solution.py:157
  29.6 25.9 %collective-permute-start.2 = (bf16[10,160,256]{2,1,0:T(8,128)(2,1)}, bf16[10,160,256]{2,1,0:T(8,128)(2,1)S(1)}, u32[]{:S(2)}, u32[]{:S(2)}) collective-permute-start(bf16[10,160,256]{2,1,0:T(8,128)(2,1)} %shard_map.82.own_ref), channel_id=1, source_target_pairs={{0,8},{4,12},{12,20},{16,24},{20,28},{1,9},{5,13},{13,21},{17,25},... | collective-permute-start | bytes 2457608 | tf_op jit(solution)/shard_map/ppermute | solution.py:156
  34.2 22.6 %collective-permute-start.6 = (bf16[10,160,256]{2,1,0:T(8,128)(2,1)}, bf16[10,160,256]{2,1,0:T(8,128)(2,1)S(1)}, u32[]{:S(2)}, u32[]{:S(2)}) collective-permute-start(bf16[10,160,256]{2,1,0:T(8,128)(2,1)} %shard_map.82.own_ref), channel_id=1, source_target_pairs={{0,4},{4,0},{8,12},{12,8},{16,20},{20,16},{24,28},{28,24},{1,5},{5... | collective-permute-start | bytes 2457608 | tf_op jit(solution)/shard_map/ppermute | solution.py:154
  34.3 22.5 %collective-permute-start.9 = (bf16[10,160,256]{2,1,0:T(8,128)(2,1)S(1)}, bf16[10,160,256]{2,1,0:T(8,128)(2,1)S(1)}, u32[]{:S(2)}, u32[]{:S(2)}) collective-permute-start(bf16[10,160,256]{2,1,0:T(8,128)(2,1)S(1)} %collective-permute-done.8), channel_id=1, source_target_pairs={{4,12},{5,13},{6,14},{7,15}} | collective-permute-start | bytes 2457608 | tf_op jit(solution)/shard_map/ppermute | solution.py:160
  51.6 16.5 %copy-start = (bf16[10,160,256]{2,1,0:T(8,128)(2,1)}, bf16[10,160,256]{2,1,0:T(8,128)(2,1)S(1)}, u32[]{:S(2)}) copy-start(bf16[10,160,256]{2,1,0:T(8,128)(2,1)S(1)} %collective-permute-done.3.fa_ref) | copy-start | bytes 2457604
  51.6 5.3 %collective-permute-start.7 = (bf16[10,160,256]{2,1,0:T(8,128)(2,1)S(1)}, bf16[10,160,256]{2,1,0:T(8,128)(2,1)S(1)}, u32[]{:S(2)}, u32[]{:S(2)}) collective-permute-start(bf16[10,160,256]{2,1,0:T(8,128)(2,1)S(1)} %collective-permute-done.3.fa_ref), channel_id=1, source_target_pairs={{0,4},{8,12},{16,20},{24,28},{1,5},{9,13},{17,21},{25,29},{2,6},{1... | collective-permute-start | bytes 2457608 | tf_op jit(solution)/shard_map/ppermute | solution.py:167
  52.9 13.4 %collective-permute-start.4 = (bf16[10,160,256]{2,1,0:T(8,128)(2,1)S(1)}, bf16[10,160,256]{2,1,0:T(8,128)(2,1)S(1)}, u32[]{:S(2)}, u32[]{:S(2)}) collective-permute-start(bf16[10,160,256]{2,1,0:T(8,128)(2,1)S(1)} %collective-permute-done.3.fa_ref), channel_id=1, source_target_pairs={{0,16},{1,17},{2,18},{3,19}} | collective-permute-start | bytes 2457608 | tf_op jit(solution)/shard_map/ppermute | solution.py:159
  55.5 12.6 %copy-start.1 = (bf16[10,160,256]{2,1,0:T(8,128)(2,1)}, bf16[10,160,256]{2,1,0:T(8,128)(2,1)S(1)}, u32[]{:S(2)}) copy-start(bf16[10,160,256]{2,1,0:T(8,128)(2,1)S(1)} %collective-permute-done.2.fb_ref) | copy-start | bytes 2457604
  55.5 10.8 %collective-permute-start.5 = (bf16[10,160,256]{2,1,0:T(8,128)(2,1)S(1)}, bf16[10,160,256]{2,1,0:T(8,128)(2,1)S(1)}, u32[]{:S(2)}, u32[]{:S(2)}) collective-permute-start(bf16[10,160,256]{2,1,0:T(8,128)(2,1)S(1)} %collective-permute-done.2.fb_ref), channel_id=1, source_target_pairs={{4,0},{12,8},{20,16},{28,24},{5,1},{13,9},{21,17},{29,25},{6,2},{1... | collective-permute-start | bytes 2457608 | tf_op jit(solution)/shard_map/ppermute | solution.py:166
  56.8 11.3 %copy-start.2 = (bf16[10,160,256]{2,1,0:T(8,128)(2,1)}, bf16[10,160,256]{2,1,0:T(8,128)(2,1)S(1)}, u32[]{:S(2)}) copy-start(bf16[10,160,256]{2,1,0:T(8,128)(2,1)S(1)} %collective-permute-done.6.par_ref) | copy-start | bytes 2457604
  56.9 11.3 %copy-start.3 = (bf16[10,160,256]{2,1,0:T(8,128)(2,1)}, bf16[10,160,256]{2,1,0:T(8,128)(2,1)S(1)}, u32[]{:S(2)}) copy-start(bf16[10,160,256]{2,1,0:T(8,128)(2,1)S(1)} %collective-permute-done.9.fa2_ref) | copy-start | bytes 2457604
  56.9 9.5 %copy-start.4 = (bf16[10,160,256]{2,1,0:T(8,128)(2,1)}, bf16[10,160,256]{2,1,0:T(8,128)(2,1)S(1)}, u32[]{:S(2)}) copy-start(bf16[10,160,256]{2,1,0:T(8,128)(2,1)S(1)} %collective-permute-done.7.ra_ref) | copy-start | bytes 2457604
  66.3 0.9 %copy-start.5 = (bf16[10,160,256]{2,1,0:T(8,128)(2,1)}, bf16[10,160,256]{2,1,0:T(8,128)(2,1)S(1)}, u32[]{:S(2)}) copy-start(bf16[10,160,256]{2,1,0:T(8,128)(2,1)S(1)} %collective-permute-done.4.fb2_ref) | copy-start | bytes 2457604
  67.2 0.9 %copy-start.6 = (bf16[10,160,256]{2,1,0:T(8,128)(2,1)}, bf16[10,160,256]{2,1,0:T(8,128)(2,1)S(1)}, u32[]{:S(2)}) copy-start(bf16[10,160,256]{2,1,0:T(8,128)(2,1)S(1)} %collective-permute-done.5.rb_ref) | copy-start | bytes 2457604

commit v8 on v6

--- a/solution.py
+++ b/solution.py
@@ -53,8 +53,8 @@
     out_ref[...] = gelu(conv_rows(first, w2_ref, stack, rows1 - 2)).astype(jnp.bfloat16)
 
 
-def mix_kernel(coef_ref, fb_ref, rb_ref, own_ref, par_ref, ra_ref, fa_ref, above_ref, frame_ref,
-               below_ref, w3_ref, out_ref, fbuf, stack):
+def mix_kernel(coef_ref, fb_ref, rb_ref, own_ref, par_ref, ra_ref, fa_ref, routed_ref,
+               above_ref, frame_ref, below_ref, w3_ref, out_ref, fbuf, stack):
     halo = below_ref.shape[0] - 1
     block = frame_ref.shape[0]
     fbuf[0:1] = above_ref[halo : halo + 1]
@@ -68,6 +68,7 @@
         + coef_ref[3] * par_ref[...].astype(f32)
         + coef_ref[4] * ra_ref[...].astype(f32)
         + coef_ref[5] * fa_ref[...].astype(f32)
+        + coef_ref[6] * routed_ref[...].astype(f32)
     )
     mixed = (summed * fbuf[...].astype(f32)).astype(jnp.bfloat16)
     out_ref[...] = conv_rows(mixed, w3_ref, stack, block).astype(jnp.bfloat16)
@@ -98,19 +99,19 @@
     )(bounds, above, image, below, w1, w2)
 
 
-def mix(coef, fb, rb, own, par, ra, fa, above, frame, below, w3):
+def mix(coef, fb, rb, own, par, ra, fa, routed, above, frame, below, w3):
     block, cols, c = frame.shape
     flops = 2 * 9 * c * c * cols * block
     return pl.pallas_call(
         mix_kernel,
         out_shape=jax.ShapeDtypeStruct((block, cols, c), jnp.bfloat16),
-        in_specs=[smem()] + [vmem()] * 10,
+        in_specs=[smem()] + [vmem()] * 11,
         out_specs=vmem(),
         scratch_shapes=[pltpu.VMEM((block + 2, cols, c), jnp.bfloat16),
                         pltpu.VMEM((block, cols, 3 * c), jnp.bfloat16)],
         cost_estimate=pl.CostEstimate(flops=flops, transcendentals=0,
-                                      bytes_accessed=16 * (block + 2) * cols * c + 2 * 9 * c * c),
-    )(coef, fb, rb, own, par, ra, fa, above, frame, below, w3)
+                                      bytes_accessed=18 * (block + 2) * cols * c + 2 * 9 * c * c),
+    )(coef, fb, rb, own, par, ra, fa, routed, above, frame, below, w3)
 
 
 def shards(
@@ -145,18 +146,26 @@
     weights = weights / jnp.sum(weights)
     is_odd = (t % 2) == 1
     partner_weight = jnp.where(is_odd, weights[1], weights[3])
-    coef = jnp.concatenate([weights[:3], partner_weight[None], weights[3:]])
+    routed_weight = jnp.where(is_odd, weights[4], weights[0])
+    coef = jnp.concatenate([weights[:3], partner_weight[None], weights[3:], routed_weight[None]])
     bounds = jnp.stack([2 - row0, height - row0 + 2]).astype(jnp.int32)
     coef, bounds, image = lax.optimization_barrier((coef, bounds, image))
 
     second = layers(bounds, from_above, image, from_below, conv_first, conv_second)
 
     partner = lax.ppermute(second, "tm", [(i, i ^ 1) for i in range(count)])
-    from_behind = shifted(second, "tm", 2)
-    from_ahead = shifted(second, "tm", -2)
+    if count == 8:
+        from_behind = lax.ppermute(second, "tm", [(0, 2), (1, 3), (3, 5), (4, 6), (5, 7)])
+        from_ahead = lax.ppermute(second, "tm", [(2, 0), (3, 1), (4, 2), (6, 4), (7, 5)])
+        hop = lax.ppermute(second, "tm", [(2, 6), (5, 1)])
+        routed = lax.ppermute(hop, "tm", [(6, 4), (1, 3)])
+    else:
+        from_behind = shifted(second, "tm", 2)
+        from_ahead = shifted(second, "tm", -2)
+        routed = jnp.zeros_like(second)
     relay_behind = lax.ppermute(from_behind, "tm", [(i + 1, i) for i in range(0, count, 2)])
     relay_ahead = lax.ppermute(from_ahead, "tm", [(i, i + 1) for i in range(0, count, 2)])
-    result = mix(coef, from_behind, relay_behind, second, partner, relay_ahead, from_ahead,
+    result = mix(coef, from_behind, relay_behind, second, partner, relay_ahead, from_ahead, routed,
                  from_above, frame, from_below, conv_frame)
     return result[None]
 

time: 76.6 us -> 72.7 us (0.949)
  waiting for transfers between devices: 38.7 us -> 31.2 us
  starting transfers between devices: 12.3 us -> 14.3 us
  between operations: 2.8 us -> 4.02 us
    ppermute x4 -> x2, waiting for transfers between devices: 35.8 us -> 1.56 us  [shifted(): return lax.ppermute(value, axis, pairs)]
    ppermute x0 -> x4, waiting for transfers between devices: none -> 26.8 us  [the longest x1 11.5 us: shards(): lax.ppermute(second, 'tm', [(0, 2), (1, 3), (3, 5), (4, 6), (5, 7)])]
    ppermute x0 -> x4, starting transfers between devices: none -> 5.81 us  [the longest x1 1.91 us: shards(): lax.ppermute(second, 'tm', [(2, 0), (3, 1), (4, 2), (6, 4), (7, 5)])]
    ppermute x4 -> x2, starting transfers between devices: 9.61 us -> 5.84 us  [shifted(): return lax.ppermute(value, axis, pairs)]
    unnamed x16 -> x18, local copies, waits for them, and re-layouts: 1.67 us -> 1.65 us
  transfers between devices with their start and end apart: 7 -> 9, of which waited for: 4 -> 5; matrix products, arithmetic and copies ran while one was open for 4% -> 5% of each run, Pallas kernels for 0% -> 0%
where the time goes in v8:
time: 72.7 us; the launch traced here: 72 us
  waiting for transfers between devices  31.2 us (43%)
  Pallas kernels  15.4 us (21%)
  starting transfers between devices  14.3 us (20%)
  local copies, waits for them, and re-layouts  4.42 us (6%)
  between operations  4.02 us (6%)
  other arithmetic  2.62 us (4%)
    ppermute x1, waiting for transfers between devices, shards(): lax.ppermute(second, 'tm', [(0, 2), (1, 3), (3, 5), (4, 6), (5, 7)])  11.5 us
    ppermute x1, waiting for transfers between devices, shards(): hop = lax.ppermute(second, 'tm', [(2, 6), (5, 1)])  9.85 us
    pallas_call x1, Pallas kernels, layers(): pl.pallas_call(layers_kernel, out_shape=jax.ShapeDtypeStruct((rows - 4, c...  8.72 us
    pallas_call x1, Pallas kernels, mix(): pl.pallas_call(mix_kernel, out_shape=jax.ShapeDtypeStruct((block, cols, c...  6.67 us
    ppermute x2, starting transfers between devices, shifted(): return lax.ppermute(value, axis, pairs)  5.84 us
    ppermute x1, waiting for transfers between devices, shards(): lax.ppermute(second, 'tm', [(2, 0), (3, 1), (4, 2), (6, 4), (7, 5)])  5.46 us
    ppermute x1, waiting for transfers between devices, shards(): lax.ppermute(from_behind, 'tm', [(i + 1, i) for i in range(0, count, 2)])  2.86 us
    slice x2, local copies, waits for them, and re-layouts, shards(): up = jnp.concatenate([image[:3], frame[:1]], axis=0)  2.04 us
  transfers between devices with their start and end apart: 9, of which 5 were waited for; matrix products, arithmetic and copies ran while one was open for 5% of the time, Pallas kernels for 0%

profile of v8, /device:TPU:22, one launch (start us, length us, event | category | flops | bytes accessed | tf_op | source)
XLA Modules:
  0.0 72.0 jit_solution(3556546852267479441)
XLA Ops:
  0.0 0.9 %slice_bitcast_fusion.2 = (bf16[1,160,256]{2,1,0:T(8,128)(2,1)S(1)}, bf16[1,160,256]{2,1,0:T(8,128)(2,1)S(1)}) fusion(bf16[1,8,160,256]{3,2,1,0:T(8,128)(2,1)} %param.9), kind=kLoop, calls=%fused_computation.4 | loop fusion | bytes 327680 | tf_op jit(solution)/shard_map/slice | solution.py:134
  0.9 0.0 copy-start.8
  1.0 1.1 %slice_bitcast_fusion = (bf16[3,160,256]{2,1,0:T(8,128)(2,1)S(1)}, bf16[3,160,256]{2,1,0:T(8,128)(2,1)S(1)}) fusion(bf16[1,8,160,256]{3,2,1,0:T(8,128)(2,1)} %param.8), kind=kLoop, calls=%fused_computation.2 | loop fusion | bytes 983040 | tf_op jit(solution)/shard_map/slice | solution.py:134
  2.1 3.5 %collective-permute-start = (bf16[4,160,256]{2,1,0:T(8,128)(2,1)S(1)}, bf16[4,160,256]{2,1,0:T(8,128)(2,1)S(1)}, u32[]{:S(2)}, u32[]{:S(2)}) collective-permute-start(bf16[4,160,256]{2,1,0:T(8,128)(2,1)S(1)} %pad_maximum_fusion), channel_id=1, source_target_pairs={{0,1},{1,2},{2,3},{4,5},{5,6},{6,7},{8,9},{9,10},{10,11},{12,13},{... | collective-permute-start | bytes 983048 | tf_op jit(solution)/shard_map/ppermute | solution.py:16
  5.6 2.4 %collective-permute-start.1 = (bf16[4,160,256]{2,1,0:T(8,128)(2,1)S(1)}, bf16[4,160,256]{2,1,0:T(8,128)(2,1)S(1)}, u32[]{:S(2)}, u32[]{:S(2)}) collective-permute-start(bf16[4,160,256]{2,1,0:T(8,128)(2,1)S(1)} %pad_maximum_fusion.1), channel_id=1, source_target_pairs={{1,0},{2,1},{3,2},{5,4},{6,5},{7,6},{9,8},{10,9},{11,10},{13,12},{... | collective-permute-start | bytes 983048 | tf_op jit(solution)/shard_map/ppermute | solution.py:16
  9.3 0.0 copy-done.8
  9.3 0.6 fusion
  10.0 0.6 broadcast_divide_fusion
  10.6 0.1 slice.45
  10.7 0.7 fusion.1
  13.8 0.6 pad_add_fusion.bounds_ref
  14.5 0.6 pad_maximum_fusion.2.coef_ref
  15.1 0.0 collective-permute-done.above_ref
  15.1 0.0 copy-start.6
  15.1 1.6 %collective-permute-done.1.below_ref = bf16[4,160,256]{2,1,0:T(8,128)(2,1)S(1)} collective-permute-done((bf16[4,160,256]{2,1,0:T(8,128)(2,1)S(1)}, bf16[4,160,256]{2,1,0:T(8,128)(2,1)S(1)}, u32[]{:S(2)}, u32[]{:S(2)}) %collective-permute-start.1) | collective-permute-done | bytes 327712 | tf_op jit(solution)/shard_map/ppermute | solution.py:16
  16.7 0.0 copy-done.6
  16.7 0.0 copy-start.7
  16.7 0.7 %copy-done.7 = bf16[4,160,256]{2,1,0:T(8,128)(2,1)} copy-done((bf16[4,160,256]{2,1,0:T(8,128)(2,1)}, bf16[4,160,256]{2,1,0:T(8,128)(2,1)S(1)}, u32[]{:S(2)}) %copy-start.7) | copy-done | bytes 327704
  17.4 8.7 %shard_map.82.own_ref = bf16[10,160,256]{2,1,0:T(8,128)(2,1)} custom-call(s32[2]{0:T(128)} %pad_add_fusion.bounds_ref, bf16[4,160,256]{2,1,0:T(8,128)(2,1)} %copy-done.6, bf16[8,160,256]{2,1,0:T(8,128)(2,1)} %bitcast.28, bf16[4,160,256]{2,1,0:T(8,128)(2,1)} %copy-done.7, bf16[3,3,256,256]{3,2,1,0:T(8,128)(2,1)} %w1_ref.1, bf16[3,3,256,256]{3,2,1,0:T(8,128)(2,1)} %w2_ref.1), custom_call_target="tpu_custom_call" | custom-call | flops 4152360960 | bytes 4653056 | tf_op jit(solution)/shard_map/pallas_call | solution.py:90
  26.1 1.3 %collective-permute-start.7 = (bf16[10,160,256]{2,1,0:T(8,128)(2,1)}, bf16[10,160,256]{2,1,0:T(8,128)(2,1)S(1)}, u32[]{:S(2)}, u32[]{:S(2)}) collective-permute-start(bf16[10,160,256]{2,1,0:T(8,128)(2,1)} %shard_map.82.own_ref), channel_id=1, source_target_pairs={{8,24},{20,4},{9,25},{21,5},{10,26},{22,6},{11,27},{23,7}} | collective-permute-start | bytes 2457608 | tf_op jit(solution)/shard_map/ppermute | solution.py:160
  27.4 1.9 %collective-permute-start.5 = (bf16[10,160,256]{2,1,0:T(8,128)(2,1)}, bf16[10,160,256]{2,1,0:T(8,128)(2,1)S(1)}, u32[]{:S(2)}, u32[]{:S(2)}) collective-permute-start(bf16[10,160,256]{2,1,0:T(8,128)(2,1)} %shard_map.82.own_ref), channel_id=1, source_target_pairs={{8,0},{12,4},{16,8},{24,16},{28,20},{9,1},{13,5},{17,9},{25,17},{2... | collective-permute-start | bytes 2457608 | tf_op jit(solution)/shard_map/ppermute | solution.py:159
  29.3 1.3 %collective-permute-start.2 = (bf16[10,160,256]{2,1,0:T(8,128)(2,1)}, bf16[10,160,256]{2,1,0:T(8,128)(2,1)S(1)}, u32[]{:S(2)}, u32[]{:S(2)}) collective-permute-start(bf16[10,160,256]{2,1,0:T(8,128)(2,1)} %shard_map.82.own_ref), channel_id=1, source_target_pairs={{0,8},{4,12},{12,20},{16,24},{20,28},{1,9},{5,13},{13,21},{17,25},... | collective-permute-start | bytes 2457608 | tf_op jit(solution)/shard_map/ppermute | solution.py:158
  30.6 0.1 collective-permute-start.4
  30.7 9.8 %collective-permute-done.7 = bf16[10,160,256]{2,1,0:T(8,128)(2,1)S(1)} collective-permute-done((bf16[10,160,256]{2,1,0:T(8,128)(2,1)}, bf16[10,160,256]{2,1,0:T(8,128)(2,1)S(1)}, u32[]{:S(2)}, u32[]{:S(2)}) %collective-permute-start.7) | collective-permute-done | bytes 819232 | tf_op jit(solution)/shard_map/ppermute | solution.py:160
  40.6 1.3 %collective-permute-start.8 = (bf16[10,160,256]{2,1,0:T(8,128)(2,1)S(1)}, bf16[10,160,256]{2,1,0:T(8,128)(2,1)S(1)}, u32[]{:S(2)}, u32[]{:S(2)}) collective-permute-start(bf16[10,160,256]{2,1,0:T(8,128)(2,1)S(1)} %collective-permute-done.7), channel_id=1, source_target_pairs={{24,16},{4,12},{25,17},{5,13},{26,18},{6,14},{27,19},{7,15}} | collective-permute-start | bytes 2457608 | tf_op jit(solution)/shard_map/ppermute | solution.py:161
  41.9 5.5 %collective-permute-done.5.fa_ref = bf16[10,160,256]{2,1,0:T(8,128)(2,1)S(1)} collective-permute-done((bf16[10,160,256]{2,1,0:T(8,128)(2,1)}, bf16[10,160,256]{2,1,0:T(8,128)(2,1)S(1)}, u32[]{:S(2)}, u32[]{:S(2)}) %collective-permute-start.5) | collective-permute-done | bytes 819232 | tf_op jit(solution)/shard_map/ppermute | solution.py:159
  47.4 0.0 copy-start
  47.4 1.3 %collective-permute-start.6 = (bf16[10,160,256]{2,1,0:T(8,128)(2,1)S(1)}, bf16[10,160,256]{2,1,0:T(8,128)(2,1)S(1)}, u32[]{:S(2)}, u32[]{:S(2)}) collective-permute-start(bf16[10,160,256]{2,1,0:T(8,128)(2,1)S(1)} %collective-permute-done.5.fa_ref), channel_id=1, source_target_pairs={{0,4},{8,12},{16,20},{24,28},{1,5},{9,13},{17,21},{25,29},{2,6},{1... | collective-permute-start | bytes 2457608 | tf_op jit(solution)/shard_map/ppermute | solution.py:167
  48.7 11.5 %collective-permute-done.2.fb_ref = bf16[10,160,256]{2,1,0:T(8,128)(2,1)S(1)} collective-permute-done((bf16[10,160,256]{2,1,0:T(8,128)(2,1)}, bf16[10,160,256]{2,1,0:T(8,128)(2,1)S(1)}, u32[]{:S(2)}, u32[]{:S(2)}) %collective-permute-start.2) | collective-permute-done | bytes 819232 | tf_op jit(solution)/shard_map/ppermute | solution.py:158
  60.2 0.0 copy-start.1
  60.2 1.3 %collective-permute-start.3 = (bf16[10,160,256]{2,1,0:T(8,128)(2,1)S(1)}, bf16[10,160,256]{2,1,0:T(8,128)(2,1)S(1)}, u32[]{:S(2)}, u32[]{:S(2)}) collective-permute-start(bf16[10,160,256]{2,1,0:T(8,128)(2,1)S(1)} %collective-permute-done.2.fb_ref), channel_id=1, source_target_pairs={{4,0},{12,8},{20,16},{28,24},{5,1},{13,9},{21,17},{29,25},{6,2},{1... | collective-permute-start | bytes 2457608 | tf_op jit(solution)/shard_map/ppermute | solution.py:166
  61.5 0.0 collective-permute-done.4.par_ref
  61.5 0.0 copy-start.2
  61.5 0.0 collective-permute-done.8.routed_ref
  61.5 0.0 copy-start.3
  61.5 0.0 collective-permute-done.6.ra_ref
  61.6 0.0 copy-start.4
  61.6 2.9 %collective-permute-done.3.rb_ref = bf16[10,160,256]{2,1,0:T(8,128)(2,1)S(1)} collective-permute-done((bf16[10,160,256]{2,1,0:T(8,128)(2,1)S(1)}, bf16[10,160,256]{2,1,0:T(8,128)(2,1)S(1)}, u32[]{:S(2)}, u32[]{:S(2)}) %collective-permute-start.3) | collective-permute-done | bytes 819232 | tf_op jit(solution)/shard_map/ppermute | solution.py:166
  64.4 0.0 copy-done.4
  64.4 0.0 copy-start.5
  64.4 0.9 %copy-done.5 = bf16[10,160,256]{2,1,0:T(8,128)(2,1)} copy-done((bf16[10,160,256]{2,1,0:T(8,128)(2,1)}, bf16[10,160,256]{2,1,0:T(8,128)(2,1)S(1)}, u32[]{:S(2)}) %copy-start.5) | copy-done | bytes 819224
  65.3 0.0 copy-done
  65.3 0.0 copy-done.1
  65.3 0.0 copy-done.2
  65.3 0.0 copy-done.3
  65.3 6.7 %shard_map.83 = bf16[8,160,256]{2,1,0:T(8,128)(2,1)} custom-call(f32[7]{0:T(128)} %pad_maximum_fusion.2.coef_ref, bf16[10,160,256]{2,1,0:T(8,128)(2,1)} %copy-done.1, bf16[10,160,256]{2,1,0:T(8,128)(2,1)} %copy-done.5, bf16[10,160,256]{2,1,0:T(8,128)(2,1)} %shard_map.82.own_ref, bf16[10,160,256]{2,1,0:T(8,128)(2,1)} %copy-done.2, ...), custom_call_target="tpu_custom_call" | custom-call | flops 1509949440 | bytes 8552448 | tf_op jit(solution)/shard_map/pallas_call | solution.py:105
  (2 shorter events, 0.1 us)
Async XLA Ops:
  0.9 8.4 %copy-start.8 = (s32[1,5]{1,0:T(1,128)S(1)}, s32[1,5]{1,0:T(1,128)}, u32[]{:S(2)}) copy-start(s32[1,5]{1,0:T(1,128)} %param.12) | copy-start | bytes 64
  2.1 13.0 %collective-permute-start = (bf16[4,160,256]{2,1,0:T(8,128)(2,1)S(1)}, bf16[4,160,256]{2,1,0:T(8,128)(2,1)S(1)}, u32[]{:S(2)}, u32[]{:S(2)}) collective-permute-start(bf16[4,160,256]{2,1,0:T(8,128)(2,1)S(1)} %pad_maximum_fusion), channel_id=1, source_target_pairs={{0,1},{1,2},{2,3},{4,5},{5,6},{6,7},{8,9},{9,10},{10,11},{12,13},{... | collective-permute-start | bytes 983048 | tf_op jit(solution)/shard_map/ppermute | solution.py:16
  5.6 11.1 %collective-permute-start.1 = (bf16[4,160,256]{2,1,0:T(8,128)(2,1)S(1)}, bf16[4,160,256]{2,1,0:T(8,128)(2,1)S(1)}, u32[]{:S(2)}, u32[]{:S(2)}) collective-permute-start(bf16[4,160,256]{2,1,0:T(8,128)(2,1)S(1)} %pad_maximum_fusion.1), channel_id=1, source_target_pairs={{1,0},{2,1},{3,2},{5,4},{6,5},{7,6},{9,8},{10,9},{11,10},{13,12},{... | collective-permute-start | bytes 983048 | tf_op jit(solution)/shard_map/ppermute | solution.py:16
  15.1 1.6 %copy-start.6 = (bf16[4,160,256]{2,1,0:T(8,128)(2,1)}, bf16[4,160,256]{2,1,0:T(8,128)(2,1)S(1)}, u32[]{:S(2)}) copy-start(bf16[4,160,256]{2,1,0:T(8,128)(2,1)S(1)} %collective-permute-done.above_ref) | copy-start | bytes 983044
  16.7 0.7 %copy-start.7 = (bf16[4,160,256]{2,1,0:T(8,128)(2,1)}, bf16[4,160,256]{2,1,0:T(8,128)(2,1)S(1)}, u32[]{:S(2)}) copy-start(bf16[4,160,256]{2,1,0:T(8,128)(2,1)S(1)} %collective-permute-done.1.below_ref) | copy-start | bytes 983044
  26.1 14.4 %collective-permute-start.7 = (bf16[10,160,256]{2,1,0:T(8,128)(2,1)}, bf16[10,160,256]{2,1,0:T(8,128)(2,1)S(1)}, u32[]{:S(2)}, u32[]{:S(2)}) collective-permute-start(bf16[10,160,256]{2,1,0:T(8,128)(2,1)} %shard_map.82.own_ref), channel_id=1, source_target_pairs={{8,24},{20,4},{9,25},{21,5},{10,26},{22,6},{11,27},{23,7}} | collective-permute-start | bytes 2457608 | tf_op jit(solution)/shard_map/ppermute | solution.py:160
  27.4 19.9 %collective-permute-start.5 = (bf16[10,160,256]{2,1,0:T(8,128)(2,1)}, bf16[10,160,256]{2,1,0:T(8,128)(2,1)S(1)}, u32[]{:S(2)}, u32[]{:S(2)}) collective-permute-start(bf16[10,160,256]{2,1,0:T(8,128)(2,1)} %shard_map.82.own_ref), channel_id=1, source_target_pairs={{8,0},{12,4},{16,8},{24,16},{28,20},{9,1},{13,5},{17,9},{25,17},{2... | collective-permute-start | bytes 2457608 | tf_op jit(solution)/shard_map/ppermute | solution.py:159
  29.3 30.9 %collective-permute-start.2 = (bf16[10,160,256]{2,1,0:T(8,128)(2,1)}, bf16[10,160,256]{2,1,0:T(8,128)(2,1)S(1)}, u32[]{:S(2)}, u32[]{:S(2)}) collective-permute-start(bf16[10,160,256]{2,1,0:T(8,128)(2,1)} %shard_map.82.own_ref), channel_id=1, source_target_pairs={{0,8},{4,12},{12,20},{16,24},{20,28},{1,9},{5,13},{13,21},{17,25},... | collective-permute-start | bytes 2457608 | tf_op jit(solution)/shard_map/ppermute | solution.py:158
  30.6 30.9 %collective-permute-start.4 = (bf16[10,160,256]{2,1,0:T(8,128)(2,1)}, bf16[10,160,256]{2,1,0:T(8,128)(2,1)S(1)}, u32[]{:S(2)}, u32[]{:S(2)}) collective-permute-start(bf16[10,160,256]{2,1,0:T(8,128)(2,1)} %shard_map.82.own_ref), channel_id=1, source_target_pairs={{0,4},{4,0},{8,12},{12,8},{16,20},{20,16},{24,28},{28,24},{1,5},{5... | collective-permute-start | bytes 2457608 | tf_op jit(solution)/shard_map/ppermute | solution.py:156
  40.6 21.0 %collective-permute-start.8 = (bf16[10,160,256]{2,1,0:T(8,128)(2,1)S(1)}, bf16[10,160,256]{2,1,0:T(8,128)(2,1)S(1)}, u32[]{:S(2)}, u32[]{:S(2)}) collective-permute-start(bf16[10,160,256]{2,1,0:T(8,128)(2,1)S(1)} %collective-permute-done.7), channel_id=1, source_target_pairs={{24,16},{4,12},{25,17},{5,13},{26,18},{6,14},{27,19},{7,15}} | collective-permute-start | bytes 2457608 | tf_op jit(solution)/shard_map/ppermute | solution.py:161
  47.4 18.0 %copy-start = (bf16[10,160,256]{2,1,0:T(8,128)(2,1)}, bf16[10,160,256]{2,1,0:T(8,128)(2,1)S(1)}, u32[]{:S(2)}) copy-start(bf16[10,160,256]{2,1,0:T(8,128)(2,1)S(1)} %collective-permute-done.5.fa_ref) | copy-start | bytes 2457604
  47.4 14.2 %collective-permute-start.6 = (bf16[10,160,256]{2,1,0:T(8,128)(2,1)S(1)}, bf16[10,160,256]{2,1,0:T(8,128)(2,1)S(1)}, u32[]{:S(2)}, u32[]{:S(2)}) collective-permute-start(bf16[10,160,256]{2,1,0:T(8,128)(2,1)S(1)} %collective-permute-done.5.fa_ref), channel_id=1, source_target_pairs={{0,4},{8,12},{16,20},{24,28},{1,5},{9,13},{17,21},{25,29},{2,6},{1... | collective-permute-start | bytes 2457608 | tf_op jit(solution)/shard_map/ppermute | solution.py:167
  60.2 5.1 %copy-start.1 = (bf16[10,160,256]{2,1,0:T(8,128)(2,1)}, bf16[10,160,256]{2,1,0:T(8,128)(2,1)S(1)}, u32[]{:S(2)}) copy-start(bf16[10,160,256]{2,1,0:T(8,128)(2,1)S(1)} %collective-permute-done.2.fb_ref) | copy-start | bytes 2457604
  60.2 4.2 %collective-permute-start.3 = (bf16[10,160,256]{2,1,0:T(8,128)(2,1)S(1)}, bf16[10,160,256]{2,1,0:T(8,128)(2,1)S(1)}, u32[]{:S(2)}, u32[]{:S(2)}) collective-permute-start(bf16[10,160,256]{2,1,0:T(8,128)(2,1)S(1)} %collective-permute-done.2.fb_ref), channel_id=1, source_target_pairs={{4,0},{12,8},{20,16},{28,24},{5,1},{13,9},{21,17},{29,25},{6,2},{1... | collective-permute-start | bytes 2457608 | tf_op jit(solution)/shard_map/ppermute | solution.py:166
  61.5 3.8 %copy-start.2 = (bf16[10,160,256]{2,1,0:T(8,128)(2,1)}, bf16[10,160,256]{2,1,0:T(8,128)(2,1)S(1)}, u32[]{:S(2)}) copy-start(bf16[10,160,256]{2,1,0:T(8,128)(2,1)S(1)} %collective-permute-done.4.par_ref) | copy-start | bytes 2457604
  61.5 3.8 %copy-start.3 = (bf16[10,160,256]{2,1,0:T(8,128)(2,1)}, bf16[10,160,256]{2,1,0:T(8,128)(2,1)S(1)}, u32[]{:S(2)}) copy-start(bf16[10,160,256]{2,1,0:T(8,128)(2,1)S(1)} %collective-permute-done.8.routed_ref) | copy-start | bytes 2457604
  61.6 2.9 %copy-start.4 = (bf16[10,160,256]{2,1,0:T(8,128)(2,1)}, bf16[10,160,256]{2,1,0:T(8,128)(2,1)S(1)}, u32[]{:S(2)}) copy-start(bf16[10,160,256]{2,1,0:T(8,128)(2,1)S(1)} %collective-permute-done.6.ra_ref) | copy-start | bytes 2457604
  64.4 0.9 %copy-start.5 = (bf16[10,160,256]{2,1,0:T(8,128)(2,1)}, bf16[10,160,256]{2,1,0:T(8,128)(2,1)S(1)}, u32[]{:S(2)}) copy-start(bf16[10,160,256]{2,1,0:T(8,128)(2,1)S(1)} %collective-permute-done.3.rb_ref) | copy-start | bytes 2457604

commit v9 on v8

--- a/solution.py
+++ b/solution.py
@@ -39,18 +39,38 @@
     return out.reshape(rows_out, cols, cout)
 
 
-def layers_kernel(bounds_ref, above_ref, image_ref, below_ref, w1_ref, w2_ref, out_ref, xbuf, stack):
+def interior_kernel(image_ref, w1_ref, w2_ref, first_ref, second_ref, stack):
+    block = image_ref.shape[0]
+    first = gelu(conv_rows(image_ref[...], w1_ref, stack, block - 2)).astype(jnp.bfloat16)
+    first_ref[...] = first
+    second_ref[...] = gelu(conv_rows(first, w2_ref, stack, block - 4)).astype(jnp.bfloat16)
+
+
+def edges_kernel(bounds_ref, above_ref, image_ref, below_ref, first_in_ref, second_in_ref, w1_ref,
+                 w2_ref, out_ref, xbuf, first_buf, stack):
     halo = below_ref.shape[0] - 1
     block = image_ref.shape[0]
+    rows1 = block + 2 * halo - 2
+    edge = halo + 2
+    row = lax.broadcasted_iota(jnp.int32, (halo, image_ref.shape[1], image_ref.shape[2]), 0)
     xbuf[0:halo] = above_ref[0:halo]
-    xbuf[halo : halo + block] = image_ref[...]
-    xbuf[halo + block :] = below_ref[0:halo]
-    rows1 = block + 2 * halo - 2
-    first = gelu(conv_rows(xbuf[...], w1_ref, stack, rows1))
-    row = lax.broadcasted_iota(jnp.int32, first.shape, 0)
-    inside = (row >= bounds_ref[0]) & (row < bounds_ref[1])
-    first = jnp.where(inside, first, 0.0).astype(jnp.bfloat16)
-    out_ref[...] = gelu(conv_rows(first, w2_ref, stack, rows1 - 2)).astype(jnp.bfloat16)
+    xbuf[halo:edge] = image_ref[0:2]
+    top = gelu(conv_rows(xbuf[...], w1_ref, stack, halo))
+    top = jnp.where((row >= bounds_ref[0]) & (row < bounds_ref[1]), top, 0.0)
+    first_buf[0:halo] = top.astype(jnp.bfloat16)
+    xbuf[0:2] = image_ref[block - 2 :]
+    xbuf[2:edge] = below_ref[0:halo]
+    bottom = gelu(conv_rows(xbuf[...], w1_ref, stack, halo))
+    low = rows1 - halo
+    bottom = jnp.where((row + low >= bounds_ref[0]) & (row + low < bounds_ref[1]), bottom, 0.0)
+    first_buf[low:] = bottom.astype(jnp.bfloat16)
+    first_buf[halo:low] = first_in_ref[...]
+    top2 = gelu(conv_rows(first_buf[0 : halo + 2], w2_ref, stack, halo))
+    bottom2 = gelu(conv_rows(first_buf[low - 2 :], w2_ref, stack, halo))
+    rows2 = rows1 - 2
+    out_ref[0:halo] = top2.astype(jnp.bfloat16)
+    out_ref[halo : rows2 - halo] = second_in_ref[...]
+    out_ref[rows2 - halo :] = bottom2.astype(jnp.bfloat16)
 
 
 def mix_kernel(coef_ref, fb_ref, rb_ref, own_ref, par_ref, ra_ref, fa_ref, routed_ref,
@@ -86,17 +106,29 @@
     block, cols, c = image.shape
     halo = below.shape[0] - 1
     rows = block + 2 * halo
-    flops = 2 * 9 * c * c * cols * (2 * rows - 6)
+    inner_flops = 2 * 9 * c * c * cols * (2 * block - 6)
+    first_in, second_in = pl.pallas_call(
+        interior_kernel,
+        out_shape=(jax.ShapeDtypeStruct((block - 2, cols, c), jnp.bfloat16),
+                   jax.ShapeDtypeStruct((block - 4, cols, c), jnp.bfloat16)),
+        in_specs=[vmem()] * 3,
+        out_specs=(vmem(), vmem()),
+        scratch_shapes=[pltpu.VMEM((block - 2, cols, 3 * c), jnp.bfloat16)],
+        cost_estimate=pl.CostEstimate(flops=inner_flops, transcendentals=2 * block * cols * c,
+                                      bytes_accessed=4 * block * cols * c + 4 * 9 * c * c),
+    )(image, w1, w2)
+    edge_flops = 2 * 9 * c * c * cols * 4 * halo
     return pl.pallas_call(
-        layers_kernel,
+        edges_kernel,
         out_shape=jax.ShapeDtypeStruct((rows - 4, cols, c), jnp.bfloat16),
-        in_specs=[smem()] + [vmem()] * 5,
+        in_specs=[smem()] + [vmem()] * 7,
         out_specs=vmem(),
-        scratch_shapes=[pltpu.VMEM((rows, cols, c), jnp.bfloat16),
-                        pltpu.VMEM((rows - 2, cols, 3 * c), jnp.bfloat16)],
-        cost_estimate=pl.CostEstimate(flops=flops, transcendentals=2 * rows * cols * c,
-                                      bytes_accessed=4 * rows * cols * c + 4 * 9 * c * c),
-    )(bounds, above, image, below, w1, w2)
+        scratch_shapes=[pltpu.VMEM((halo + 2, cols, c), jnp.bfloat16),
+                        pltpu.VMEM((rows - 2, cols, c), jnp.bfloat16),
+                        pltpu.VMEM((halo, cols, 3 * c), jnp.bfloat16)],
+        cost_estimate=pl.CostEstimate(flops=edge_flops, transcendentals=4 * halo * cols * c,
+                                      bytes_accessed=6 * rows * cols * c + 4 * 9 * c * c),
+    )(bounds, above, image, below, first_in, second_in, w1, w2)
 
 
 def mix(coef, fb, rb, own, par, ra, fa, routed, above, frame, below, w3):

time: 72.7 us -> 74.3 us (1.022)
  Pallas kernels: 15.4 us -> 17.7 us
  waiting for transfers between devices: 31.2 us -> 29.4 us
  starting transfers between devices: 14.3 us -> 15.3 us
    pallas_call x1 -> x2, Pallas kernels: 8.72 us -> 11.1 us  [the longest x1 5.83 us: layers(): pl.pallas_call(edges_kernel, out_shape=jax.ShapeDtypeStruct((rows - 4, co...]
    ppermute x2, waiting for transfers between devices: 1.56 us -> 0.01 us  [shifted(): return lax.ppermute(value, axis, pairs)]
  transfers between devices with their start and end apart: 9 -> 9, of which waited for: 5 -> 4; matrix products, arithmetic and copies ran while one was open for 5% -> 5% of each run, Pallas kernels for 0% -> 7%
where the time goes in v9:
time: 74.3 us; the launch traced here: 73.6 us
  waiting for transfers between devices  29.4 us (40%)
  Pallas kernels  17.7 us (24%)
  starting transfers between devices  15.3 us (21%)
  local copies, waits for them, and re-layouts  4.52 us (6%)
  between operations  4.01 us (5%)
  other arithmetic  2.67 us (4%)
    ppermute x1, waiting for transfers between devices, shards(): lax.ppermute(second, 'tm', [(0, 2), (1, 3), (3, 5), (4, 6), (5, 7)])  11 us
    ppermute x1, waiting for transfers between devices, shards(): hop = lax.ppermute(second, 'tm', [(2, 6), (5, 1)])  9.4 us
    pallas_call x1, Pallas kernels, mix(): pl.pallas_call(mix_kernel, out_shape=jax.ShapeDtypeStruct((block, cols, c...  6.67 us
    ppermute x1, waiting for transfers between devices, shards(): lax.ppermute(second, 'tm', [(2, 0), (3, 1), (4, 2), (6, 4), (7, 5)])  6.09 us
    ppermute x2, starting transfers between devices, shifted(): return lax.ppermute(value, axis, pairs)  5.84 us
    pallas_call x1, Pallas kernels, layers(): pl.pallas_call(edges_kernel, out_shape=jax.ShapeDtypeStruct((rows - 4, co...  5.83 us
    pallas_call x1, Pallas kernels, layers(): pl.pallas_call(interior_kernel, out_shape=(jax.ShapeDtypeStruct((block -...  5.23 us
    ppermute x1, waiting for transfers between devices, shards(): lax.ppermute(from_behind, 'tm', [(i + 1, i) for i in range(0, count, 2)])  2.86 us
  transfers between devices with their start and end apart: 9, of which 4 were waited for; matrix products, arithmetic and copies ran while one was open for 5% of the time, Pallas kernels for 7%

profile of v9, /device:TPU:22, one launch (start us, length us, event | category | flops | bytes accessed | tf_op | source)
XLA Modules:
  0.0 73.6 jit_solution(9683804881225321077)
XLA Ops:
  0.0 0.9 %slice_bitcast_fusion.2 = (bf16[1,160,256]{2,1,0:T(8,128)(2,1)S(1)}, bf16[1,160,256]{2,1,0:T(8,128)(2,1)S(1)}) fusion(bf16[1,8,160,256]{3,2,1,0:T(8,128)(2,1)} %param.9), kind=kLoop, calls=%fused_computation.4 | loop fusion | bytes 327680 | tf_op jit(solution)/shard_map/slice | solution.py:166
  0.9 0.0 copy-start.8
  1.0 1.1 %slice_bitcast_fusion = (bf16[3,160,256]{2,1,0:T(8,128)(2,1)S(1)}, bf16[3,160,256]{2,1,0:T(8,128)(2,1)S(1)}) fusion(bf16[1,8,160,256]{3,2,1,0:T(8,128)(2,1)} %param.8), kind=kLoop, calls=%fused_computation.2 | loop fusion | bytes 983040 | tf_op jit(solution)/shard_map/slice | solution.py:166
  2.1 3.5 %collective-permute-start = (bf16[4,160,256]{2,1,0:T(8,128)(2,1)S(1)}, bf16[4,160,256]{2,1,0:T(8,128)(2,1)S(1)}, u32[]{:S(2)}, u32[]{:S(2)}) collective-permute-start(bf16[4,160,256]{2,1,0:T(8,128)(2,1)S(1)} %pad_maximum_fusion), channel_id=1, source_target_pairs={{0,1},{1,2},{2,3},{4,5},{5,6},{6,7},{8,9},{9,10},{10,11},{12,13},{... | collective-permute-start | bytes 983048 | tf_op jit(solution)/shard_map/ppermute | solution.py:16
  5.6 2.4 %collective-permute-start.1 = (bf16[4,160,256]{2,1,0:T(8,128)(2,1)S(1)}, bf16[4,160,256]{2,1,0:T(8,128)(2,1)S(1)}, u32[]{:S(2)}, u32[]{:S(2)}) collective-permute-start(bf16[4,160,256]{2,1,0:T(8,128)(2,1)S(1)} %pad_maximum_fusion.1), channel_id=1, source_target_pairs={{1,0},{2,1},{3,2},{5,4},{6,5},{7,6},{9,8},{10,9},{11,10},{13,12},{... | collective-permute-start | bytes 983048 | tf_op jit(solution)/shard_map/ppermute | solution.py:16
  9.3 0.0 copy-done.8
  9.3 0.7 fusion
  10.0 0.6 broadcast_divide_fusion
  10.6 0.7 fusion.1
  11.3 0.6 pad_add_fusion.bounds_ref
  11.9 0.1 slice.45
  14.5 0.7 pad_maximum_fusion.2.coef_ref
  15.2 5.2 %shard_map.82 = (bf16[6,160,256]{2,1,0:T(8,128)(2,1)}, bf16[4,160,256]{2,1,0:T(8,128)(2,1)}) custom-call(bf16[8,160,256]{2,1,0:T(8,128)(2,1)} %bitcast.28, bf16[3,3,256,256]{3,2,1,0:T(8,128)(2,1)} %w1_ref.3, bf16[3,3,256,256]{3,2,1,0:T(8,128)(2,1)} %w2_ref.3), custom_call_target="tpu_custom_call" | custom-call | flops 1887436800 | bytes 3670016 | tf_op jit(solution)/shard_map/pallas_call | solution.py:110
  20.4 0.0 collective-permute-done.above_ref
  20.4 0.0 copy-start.6
  20.4 0.0 collective-permute-done.1.below_ref
  20.4 0.0 copy-start.7
  20.4 0.7 copy-done.6
  21.1 0.1 copy-done.7
  21.3 5.8 %shard_map.83.own_ref = bf16[10,160,256]{2,1,0:T(8,128)(2,1)} custom-call(s32[2]{0:T(128)} %pad_add_fusion.bounds_ref, bf16[4,160,256]{2,1,0:T(8,128)(2,1)} %copy-done.6, bf16[8,160,256]{2,1,0:T(8,128)(2,1)} %bitcast.29, bf16[4,160,256]{2,1,0:T(8,128)(2,1)} %copy-done.7, bf16[6,160,256]{2,1,0:T(8,128)(2,1)} %get-tuple-element.13.first_in_ref, ...), custom_call_target="tpu_custom_call" | custom-call | flops 2264924160 | bytes 5799936 | tf_op jit(solution)/shard_map/pallas_call | solution.py:121
  27.1 1.3 %collective-permute-start.7 = (bf16[10,160,256]{2,1,0:T(8,128)(2,1)}, bf16[10,160,256]{2,1,0:T(8,128)(2,1)S(1)}, u32[]{:S(2)}, u32[]{:S(2)}) collective-permute-start(bf16[10,160,256]{2,1,0:T(8,128)(2,1)} %shard_map.83.own_ref), channel_id=1, source_target_pairs={{8,24},{20,4},{9,25},{21,5},{10,26},{22,6},{11,27},{23,7}} | collective-permute-start | bytes 2457608 | tf_op jit(solution)/shard_map/ppermute | solution.py:192
  28.4 1.9 %collective-permute-start.5 = (bf16[10,160,256]{2,1,0:T(8,128)(2,1)}, bf16[10,160,256]{2,1,0:T(8,128)(2,1)S(1)}, u32[]{:S(2)}, u32[]{:S(2)}) collective-permute-start(bf16[10,160,256]{2,1,0:T(8,128)(2,1)} %shard_map.83.own_ref), channel_id=1, source_target_pairs={{8,0},{12,4},{16,8},{24,16},{28,20},{9,1},{13,5},{17,9},{25,17},{2... | collective-permute-start | bytes 2457608 | tf_op jit(solution)/shard_map/ppermute | solution.py:191
  30.3 1.3 %collective-permute-start.2 = (bf16[10,160,256]{2,1,0:T(8,128)(2,1)}, bf16[10,160,256]{2,1,0:T(8,128)(2,1)S(1)}, u32[]{:S(2)}, u32[]{:S(2)}) collective-permute-start(bf16[10,160,256]{2,1,0:T(8,128)(2,1)} %shard_map.83.own_ref), channel_id=1, source_target_pairs={{0,8},{4,12},{12,20},{16,24},{20,28},{1,9},{5,13},{13,21},{17,25},... | collective-permute-start | bytes 2457608 | tf_op jit(solution)/shard_map/ppermute | solution.py:190
  31.6 0.5 collective-permute-start.4
  32.1 9.4 %collective-permute-done.7 = bf16[10,160,256]{2,1,0:T(8,128)(2,1)S(1)} collective-permute-done((bf16[10,160,256]{2,1,0:T(8,128)(2,1)}, bf16[10,160,256]{2,1,0:T(8,128)(2,1)S(1)}, u32[]{:S(2)}, u32[]{:S(2)}) %collective-permute-start.7) | collective-permute-done | bytes 819232 | tf_op jit(solution)/shard_map/ppermute | solution.py:192
  41.5 1.3 %collective-permute-start.8 = (bf16[10,160,256]{2,1,0:T(8,128)(2,1)S(1)}, bf16[10,160,256]{2,1,0:T(8,128)(2,1)S(1)}, u32[]{:S(2)}, u32[]{:S(2)}) collective-permute-start(bf16[10,160,256]{2,1,0:T(8,128)(2,1)S(1)} %collective-permute-done.7), channel_id=1, source_target_pairs={{24,16},{4,12},{25,17},{5,13},{26,18},{6,14},{27,19},{7,15}} | collective-permute-start | bytes 2457608 | tf_op jit(solution)/shard_map/ppermute | solution.py:193
  42.9 6.1 %collective-permute-done.5.fa_ref = bf16[10,160,256]{2,1,0:T(8,128)(2,1)S(1)} collective-permute-done((bf16[10,160,256]{2,1,0:T(8,128)(2,1)}, bf16[10,160,256]{2,1,0:T(8,128)(2,1)S(1)}, u32[]{:S(2)}, u32[]{:S(2)}) %collective-permute-start.5) | collective-permute-done | bytes 819232 | tf_op jit(solution)/shard_map/ppermute | solution.py:191
  49.0 0.0 copy-start
  49.0 1.8 %collective-permute-start.6 = (bf16[10,160,256]{2,1,0:T(8,128)(2,1)S(1)}, bf16[10,160,256]{2,1,0:T(8,128)(2,1)S(1)}, u32[]{:S(2)}, u32[]{:S(2)}) collective-permute-start(bf16[10,160,256]{2,1,0:T(8,128)(2,1)S(1)} %collective-permute-done.5.fa_ref), channel_id=1, source_target_pairs={{0,4},{8,12},{16,20},{24,28},{1,5},{9,13},{17,21},{25,29},{2,6},{1... | collective-permute-start | bytes 2457608 | tf_op jit(solution)/shard_map/ppermute | solution.py:199
  50.8 11.0 %collective-permute-done.2.fb_ref = bf16[10,160,256]{2,1,0:T(8,128)(2,1)S(1)} collective-permute-done((bf16[10,160,256]{2,1,0:T(8,128)(2,1)}, bf16[10,160,256]{2,1,0:T(8,128)(2,1)S(1)}, u32[]{:S(2)}, u32[]{:S(2)}) %collective-permute-start.2) | collective-permute-done | bytes 819232 | tf_op jit(solution)/shard_map/ppermute | solution.py:190
  61.8 0.0 copy-start.1
  61.8 1.3 %collective-permute-start.3 = (bf16[10,160,256]{2,1,0:T(8,128)(2,1)S(1)}, bf16[10,160,256]{2,1,0:T(8,128)(2,1)S(1)}, u32[]{:S(2)}, u32[]{:S(2)}) collective-permute-start(bf16[10,160,256]{2,1,0:T(8,128)(2,1)S(1)} %collective-permute-done.2.fb_ref), channel_id=1, source_target_pairs={{4,0},{12,8},{20,16},{28,24},{5,1},{13,9},{21,17},{29,25},{6,2},{1... | collective-permute-start | bytes 2457608 | tf_op jit(solution)/shard_map/ppermute | solution.py:198
  63.1 0.0 collective-permute-done.4.par_ref
  63.1 0.0 copy-start.2
  63.1 0.0 collective-permute-done.8.routed_ref
  63.1 0.0 copy-start.3
  63.1 0.0 collective-permute-done.6.ra_ref
  63.1 0.0 copy-start.4
  63.1 2.9 %collective-permute-done.3.rb_ref = bf16[10,160,256]{2,1,0:T(8,128)(2,1)S(1)} collective-permute-done((bf16[10,160,256]{2,1,0:T(8,128)(2,1)S(1)}, bf16[10,160,256]{2,1,0:T(8,128)(2,1)S(1)}, u32[]{:S(2)}, u32[]{:S(2)}) %collective-permute-start.3) | collective-permute-done | bytes 819232 | tf_op jit(solution)/shard_map/ppermute | solution.py:198
  66.0 0.0 copy-done.4
  66.0 0.0 copy-start.5
  66.0 0.9 %copy-done.5 = bf16[10,160,256]{2,1,0:T(8,128)(2,1)} copy-done((bf16[10,160,256]{2,1,0:T(8,128)(2,1)}, bf16[10,160,256]{2,1,0:T(8,128)(2,1)S(1)}, u32[]{:S(2)}) %copy-start.5) | copy-done | bytes 819224
  66.9 0.0 copy-done
  66.9 0.0 copy-done.1
  66.9 0.0 copy-done.2
  66.9 0.0 copy-done.3
  66.9 6.7 %shard_map.84 = bf16[8,160,256]{2,1,0:T(8,128)(2,1)} custom-call(f32[7]{0:T(128)} %pad_maximum_fusion.2.coef_ref, bf16[10,160,256]{2,1,0:T(8,128)(2,1)} %copy-done.1, bf16[10,160,256]{2,1,0:T(8,128)(2,1)} %copy-done.5, bf16[10,160,256]{2,1,0:T(8,128)(2,1)} %shard_map.83.own_ref, bf16[10,160,256]{2,1,0:T(8,128)(2,1)} %copy-done.2, ...), custom_call_target="tpu_custom_call" | custom-call | flops 1509949440 | bytes 8552448 | tf_op jit(solution)/shard_map/pallas_call | solution.py:137
  (2 shorter events, 0.1 us)
Async XLA Ops:
  0.9 8.4 %copy-start.8 = (s32[1,5]{1,0:T(1,128)S(1)}, s32[1,5]{1,0:T(1,128)}, u32[]{:S(2)}) copy-start(s32[1,5]{1,0:T(1,128)} %param.12) | copy-start | bytes 64
  2.1 18.3 %collective-permute-start = (bf16[4,160,256]{2,1,0:T(8,128)(2,1)S(1)}, bf16[4,160,256]{2,1,0:T(8,128)(2,1)S(1)}, u32[]{:S(2)}, u32[]{:S(2)}) collective-permute-start(bf16[4,160,256]{2,1,0:T(8,128)(2,1)S(1)} %pad_maximum_fusion), channel_id=1, source_target_pairs={{0,1},{1,2},{2,3},{4,5},{5,6},{6,7},{8,9},{9,10},{10,11},{12,13},{... | collective-permute-start | bytes 983048 | tf_op jit(solution)/shard_map/ppermute | solution.py:16
  5.6 14.8 %collective-permute-start.1 = (bf16[4,160,256]{2,1,0:T(8,128)(2,1)S(1)}, bf16[4,160,256]{2,1,0:T(8,128)(2,1)S(1)}, u32[]{:S(2)}, u32[]{:S(2)}) collective-permute-start(bf16[4,160,256]{2,1,0:T(8,128)(2,1)S(1)} %pad_maximum_fusion.1), channel_id=1, source_target_pairs={{1,0},{2,1},{3,2},{5,4},{6,5},{7,6},{9,8},{10,9},{11,10},{13,12},{... | collective-permute-start | bytes 983048 | tf_op jit(solution)/shard_map/ppermute | solution.py:16
  20.4 0.7 copy-start.6
  20.4 0.8 %copy-start.7 = (bf16[4,160,256]{2,1,0:T(8,128)(2,1)}, bf16[4,160,256]{2,1,0:T(8,128)(2,1)S(1)}, u32[]{:S(2)}) copy-start(bf16[4,160,256]{2,1,0:T(8,128)(2,1)S(1)} %collective-permute-done.1.below_ref) | copy-start | bytes 983044
  27.1 14.4 %collective-permute-start.7 = (bf16[10,160,256]{2,1,0:T(8,128)(2,1)}, bf16[10,160,256]{2,1,0:T(8,128)(2,1)S(1)}, u32[]{:S(2)}, u32[]{:S(2)}) collective-permute-start(bf16[10,160,256]{2,1,0:T(8,128)(2,1)} %shard_map.83.own_ref), channel_id=1, source_target_pairs={{8,24},{20,4},{9,25},{21,5},{10,26},{22,6},{11,27},{23,7}} | collective-permute-start | bytes 2457608 | tf_op jit(solution)/shard_map/ppermute | solution.py:192
  28.4 20.6 %collective-permute-start.5 = (bf16[10,160,256]{2,1,0:T(8,128)(2,1)}, bf16[10,160,256]{2,1,0:T(8,128)(2,1)S(1)}, u32[]{:S(2)}, u32[]{:S(2)}) collective-permute-start(bf16[10,160,256]{2,1,0:T(8,128)(2,1)} %shard_map.83.own_ref), channel_id=1, source_target_pairs={{8,0},{12,4},{16,8},{24,16},{28,20},{9,1},{13,5},{17,9},{25,17},{2... | collective-permute-start | bytes 2457608 | tf_op jit(solution)/shard_map/ppermute | solution.py:191
  30.3 31.5 %collective-permute-start.2 = (bf16[10,160,256]{2,1,0:T(8,128)(2,1)}, bf16[10,160,256]{2,1,0:T(8,128)(2,1)S(1)}, u32[]{:S(2)}, u32[]{:S(2)}) collective-permute-start(bf16[10,160,256]{2,1,0:T(8,128)(2,1)} %shard_map.83.own_ref), channel_id=1, source_target_pairs={{0,8},{4,12},{12,20},{16,24},{20,28},{1,9},{5,13},{13,21},{17,25},... | collective-permute-start | bytes 2457608 | tf_op jit(solution)/shard_map/ppermute | solution.py:190
  31.6 31.5 %collective-permute-start.4 = (bf16[10,160,256]{2,1,0:T(8,128)(2,1)}, bf16[10,160,256]{2,1,0:T(8,128)(2,1)S(1)}, u32[]{:S(2)}, u32[]{:S(2)}) collective-permute-start(bf16[10,160,256]{2,1,0:T(8,128)(2,1)} %shard_map.83.own_ref), channel_id=1, source_target_pairs={{0,4},{4,0},{8,12},{12,8},{16,20},{20,16},{24,28},{28,24},{1,5},{5... | collective-permute-start | bytes 2457608 | tf_op jit(solution)/shard_map/ppermute | solution.py:188
  41.5 21.6 %collective-permute-start.8 = (bf16[10,160,256]{2,1,0:T(8,128)(2,1)S(1)}, bf16[10,160,256]{2,1,0:T(8,128)(2,1)S(1)}, u32[]{:S(2)}, u32[]{:S(2)}) collective-permute-start(bf16[10,160,256]{2,1,0:T(8,128)(2,1)S(1)} %collective-permute-done.7), channel_id=1, source_target_pairs={{24,16},{4,12},{25,17},{5,13},{26,18},{6,14},{27,19},{7,15}} | collective-permute-start | bytes 2457608 | tf_op jit(solution)/shard_map/ppermute | solution.py:193
  49.0 18.0 %copy-start = (bf16[10,160,256]{2,1,0:T(8,128)(2,1)}, bf16[10,160,256]{2,1,0:T(8,128)(2,1)S(1)}, u32[]{:S(2)}) copy-start(bf16[10,160,256]{2,1,0:T(8,128)(2,1)S(1)} %collective-permute-done.5.fa_ref) | copy-start | bytes 2457604
  49.0 14.2 %collective-permute-start.6 = (bf16[10,160,256]{2,1,0:T(8,128)(2,1)S(1)}, bf16[10,160,256]{2,1,0:T(8,128)(2,1)S(1)}, u32[]{:S(2)}, u32[]{:S(2)}) collective-permute-start(bf16[10,160,256]{2,1,0:T(8,128)(2,1)S(1)} %collective-permute-done.5.fa_ref), channel_id=1, source_target_pairs={{0,4},{8,12},{16,20},{24,28},{1,5},{9,13},{17,21},{25,29},{2,6},{1... | collective-permute-start | bytes 2457608 | tf_op jit(solution)/shard_map/ppermute | solution.py:199
  61.8 5.1 %copy-start.1 = (bf16[10,160,256]{2,1,0:T(8,128)(2,1)}, bf16[10,160,256]{2,1,0:T(8,128)(2,1)S(1)}, u32[]{:S(2)}) copy-start(bf16[10,160,256]{2,1,0:T(8,128)(2,1)S(1)} %collective-permute-done.2.fb_ref) | copy-start | bytes 2457604
  61.8 4.2 %collective-permute-start.3 = (bf16[10,160,256]{2,1,0:T(8,128)(2,1)S(1)}, bf16[10,160,256]{2,1,0:T(8,128)(2,1)S(1)}, u32[]{:S(2)}, u32[]{:S(2)}) collective-permute-start(bf16[10,160,256]{2,1,0:T(8,128)(2,1)S(1)} %collective-permute-done.2.fb_ref), channel_id=1, source_target_pairs={{4,0},{12,8},{20,16},{28,24},{5,1},{13,9},{21,17},{29,25},{6,2},{1... | collective-permute-start | bytes 2457608 | tf_op jit(solution)/shard_map/ppermute | solution.py:198
  63.1 3.8 %copy-start.2 = (bf16[10,160,256]{2,1,0:T(8,128)(2,1)}, bf16[10,160,256]{2,1,0:T(8,128)(2,1)S(1)}, u32[]{:S(2)}) copy-start(bf16[10,160,256]{2,1,0:T(8,128)(2,1)S(1)} %collective-permute-done.4.par_ref) | copy-start | bytes 2457604
  63.1 3.8 %copy-start.3 = (bf16[10,160,256]{2,1,0:T(8,128)(2,1)}, bf16[10,160,256]{2,1,0:T(8,128)(2,1)S(1)}, u32[]{:S(2)}) copy-start(bf16[10,160,256]{2,1,0:T(8,128)(2,1)S(1)} %collective-permute-done.8.routed_ref) | copy-start | bytes 2457604
  63.1 2.9 %copy-start.4 = (bf16[10,160,256]{2,1,0:T(8,128)(2,1)}, bf16[10,160,256]{2,1,0:T(8,128)(2,1)S(1)}, u32[]{:S(2)}) copy-start(bf16[10,160,256]{2,1,0:T(8,128)(2,1)S(1)} %collective-permute-done.6.ra_ref) | copy-start | bytes 2457604
  66.0 0.9 %copy-start.5 = (bf16[10,160,256]{2,1,0:T(8,128)(2,1)}, bf16[10,160,256]{2,1,0:T(8,128)(2,1)S(1)}, u32[]{:S(2)}) copy-start(bf16[10,160,256]{2,1,0:T(8,128)(2,1)S(1)} %collective-permute-done.3.rb_ref) | copy-start | bytes 2457604

commit v10 on v8

--- a/solution.py
+++ b/solution.py
@@ -53,13 +53,8 @@
     out_ref[...] = gelu(conv_rows(first, w2_ref, stack, rows1 - 2)).astype(jnp.bfloat16)
 
 
-def mix_kernel(coef_ref, fb_ref, rb_ref, own_ref, par_ref, ra_ref, fa_ref, routed_ref,
-               above_ref, frame_ref, below_ref, w3_ref, out_ref, fbuf, stack):
-    halo = below_ref.shape[0] - 1
-    block = frame_ref.shape[0]
-    fbuf[0:1] = above_ref[halo : halo + 1]
-    fbuf[1 : block + 1] = frame_ref[...]
-    fbuf[block + 1 :] = below_ref[halo : halo + 1]
+def mix_kernel(coef_ref, fb_ref, rb_ref, own_ref, par_ref, ra_ref, fa_ref, routed_ref, frame_ref,
+               w3_ref, out_ref, stack):
     f32 = jnp.float32
     summed = (
         coef_ref[0] * fb_ref[...].astype(f32)
@@ -70,8 +65,8 @@
         + coef_ref[5] * fa_ref[...].astype(f32)
         + coef_ref[6] * routed_ref[...].astype(f32)
     )
-    mixed = (summed * fbuf[...].astype(f32)).astype(jnp.bfloat16)
-    out_ref[...] = conv_rows(mixed, w3_ref, stack, block).astype(jnp.bfloat16)
+    mixed = (summed * frame_ref[...].astype(f32)).astype(jnp.bfloat16)
+    out_ref[...] = conv_rows(mixed, w3_ref, stack, out_ref.shape[0]).astype(jnp.bfloat16)
 
 
 def vmem():
@@ -99,19 +94,23 @@
     )(bounds, above, image, below, w1, w2)
 
 
-def mix(coef, fb, rb, own, par, ra, fa, routed, above, frame, below, w3):
-    block, cols, c = frame.shape
+def mix(coef, fb, rb, own, par, ra, fa, routed, frame_ext, w3):
+    rows, cols, c = frame_ext.shape
+    block = rows - 2
+    half = block // 2
+    window = pl.BlockSpec((pl.Element(half + 2), pl.Element(cols), pl.Element(c)),
+                          lambda i: (i * half, 0, 0))
     flops = 2 * 9 * c * c * cols * block
     return pl.pallas_call(
         mix_kernel,
+        grid=(2,),
         out_shape=jax.ShapeDtypeStruct((block, cols, c), jnp.bfloat16),
-        in_specs=[smem()] + [vmem()] * 11,
-        out_specs=vmem(),
-        scratch_shapes=[pltpu.VMEM((block + 2, cols, c), jnp.bfloat16),
-                        pltpu.VMEM((block, cols, 3 * c), jnp.bfloat16)],
+        in_specs=[smem()] + [window] * 8 + [pl.BlockSpec(w3.shape, lambda i: (0, 0, 0, 0))],
+        out_specs=pl.BlockSpec((half, cols, c), lambda i: (i, 0, 0)),
+        scratch_shapes=[pltpu.VMEM((half, cols, 3 * c), jnp.bfloat16)],
         cost_estimate=pl.CostEstimate(flops=flops, transcendentals=0,
-                                      bytes_accessed=18 * (block + 2) * cols * c + 2 * 9 * c * c),
-    )(coef, fb, rb, own, par, ra, fa, routed, above, frame, below, w3)
+                                      bytes_accessed=18 * rows * cols * c + 2 * 9 * c * c),
+    )(coef, fb, rb, own, par, ra, fa, routed, frame_ext, w3)
 
 
 def shards(
@@ -163,10 +162,11 @@
         from_behind = shifted(second, "tm", 2)
         from_ahead = shifted(second, "tm", -2)
         routed = jnp.zeros_like(second)
-    relay_behind = lax.ppermute(from_behind, "tm", [(i + 1, i) for i in range(0, count, 2)])
-    relay_ahead = lax.ppermute(from_ahead, "tm", [(i, i + 1) for i in range(0, count, 2)])
+    relay_behind = lax.ppermute(from_behind, "tm", [(i + 1, i) for i in range(2, count, 2)])
+    relay_ahead = lax.ppermute(from_ahead, "tm", [(i, i + 1) for i in range(0, count - 2, 2)])
+    frame_ext = jnp.concatenate([from_above[3:], frame, from_below[3:]], axis=0)
     result = mix(coef, from_behind, relay_behind, second, partner, relay_ahead, from_ahead, routed,
-                 from_above, frame, from_below, conv_frame)
+                 frame_ext, conv_frame)
     return result[None]
 
 

time: 72.7 us -> 75.5 us (1.039)
  the two profiles are of different devices: /device:TPU:22 before, /device:TPU:7 now
where the time goes in v10:
time: 75.5 us; the launch traced here: 75.1 us
  starting transfers between devices  26 us (34%)
  waiting for transfers between devices  19 us (25%)
  Pallas kernels  15.4 us (20%)
  local copies, waits for them, and re-layouts  7.13 us (9%)
  between operations  3.98 us (5%)
  other arithmetic  3.57 us (5%)
    ppermute x1, waiting for transfers between devices, shards(): lax.ppermute(second, 'tm', [(2, 0), (3, 1), (4, 2), (6, 4), (7, 5)])  14.7 us
    ppermute x1, starting transfers between devices, shards(): lax.ppermute(from_behind, 'tm', [(i + 1, i) for i in range(2, count, 2)])  13.7 us
    pallas_call x1, Pallas kernels, layers(): pl.pallas_call(layers_kernel, out_shape=jax.ShapeDtypeStruct((rows - 4, c...  8.72 us
    pallas_call x1, Pallas kernels, mix(): pl.pallas_call(mix_kernel, grid=(2,), out_shape=jax.ShapeDtypeStruct((blo...  6.69 us
    ppermute x2, starting transfers between devices, shifted(): return lax.ppermute(value, axis, pairs)  4.51 us
    ppermute x1, starting transfers between devices, shards(): lax.ppermute(second, 'tm', [(2, 0), (3, 1), (4, 2), (6, 4), (7, 5)])  3.68 us
    unnamed x18, local copies, waits for them, and re-layouts  2.58 us
    ppermute x1, waiting for transfers between devices, shards(): lax.ppermute(second, 'tm', [(0, 2), (1, 3), (3, 5), (4, 6), (5, 7)])  2.5 us
  transfers between devices with their start and end apart: 9, of which 3 were waited for; matrix products, arithmetic and copies ran while one was open for 8% of the time, Pallas kernels for 0%

profile of v10, /device:TPU:7, one launch (start us, length us, event | category | flops | bytes accessed | tf_op | source)
XLA Modules:
  0.0 75.1 jit_solution(7414988349979342125)
XLA Ops:
  0.0 0.9 %slice_bitcast_fusion.2 = (bf16[1,160,256]{2,1,0:T(8,128)(2,1)S(1)}, bf16[1,160,256]{2,1,0:T(8,128)(2,1)S(1)}) fusion(bf16[1,8,160,256]{3,2,1,0:T(8,128)(2,1)} %param.9), kind=kLoop, calls=%fused_computation.5 | loop fusion | bytes 327680 | tf_op jit(solution)/shard_map/slice | solution.py:133
  0.9 0.0 copy-start.8
  1.0 1.1 %slice_bitcast_fusion = (bf16[3,160,256]{2,1,0:T(8,128)(2,1)S(1)}, bf16[3,160,256]{2,1,0:T(8,128)(2,1)S(1)}) fusion(bf16[1,8,160,256]{3,2,1,0:T(8,128)(2,1)} %param.8), kind=kLoop, calls=%fused_computation.3 | loop fusion | bytes 983040 | tf_op jit(solution)/shard_map/slice | solution.py:133
  2.1 3.2 %collective-permute-start = (bf16[4,160,256]{2,1,0:T(8,128)(2,1)S(1)}, bf16[4,160,256]{2,1,0:T(8,128)(2,1)S(1)}, u32[]{:S(2)}, u32[]{:S(2)}) collective-permute-start(bf16[4,160,256]{2,1,0:T(8,128)(2,1)S(1)} %pad_maximum_fusion.1), channel_id=1, source_target_pairs={{0,1},{1,2},{2,3},{4,5},{5,6},{6,7},{8,9},{9,10},{10,11},{12,13},{... | collective-permute-start | bytes 983048 | tf_op jit(solution)/shard_map/ppermute | solution.py:16
  5.4 1.3 %collective-permute-start.1 = (bf16[4,160,256]{2,1,0:T(8,128)(2,1)S(1)}, bf16[4,160,256]{2,1,0:T(8,128)(2,1)S(1)}, u32[]{:S(2)}, u32[]{:S(2)}) collective-permute-start(bf16[4,160,256]{2,1,0:T(8,128)(2,1)S(1)} %pad_maximum_fusion.2), channel_id=1, source_target_pairs={{1,0},{2,1},{3,2},{5,4},{6,5},{7,6},{9,8},{10,9},{11,10},{13,12},{... | collective-permute-start | bytes 983048 | tf_op jit(solution)/shard_map/ppermute | solution.py:16
  8.0 0.0 copy-done.8
  8.0 0.6 fusion
  8.6 0.6 broadcast_divide_fusion
  9.3 0.1 slice.51
  9.3 0.7 fusion.1
  12.5 0.6 pad_add_fusion.bounds_ref
  13.2 0.6 pad_maximum_fusion.3.coef_ref
  13.7 0.0 collective-permute-done.above_ref
  13.7 0.0 copy-start.6
  13.8 1.8 %collective-permute-done.1.below_ref = bf16[4,160,256]{2,1,0:T(8,128)(2,1)S(1)} collective-permute-done((bf16[4,160,256]{2,1,0:T(8,128)(2,1)S(1)}, bf16[4,160,256]{2,1,0:T(8,128)(2,1)S(1)}, u32[]{:S(2)}, u32[]{:S(2)}) %collective-permute-start.1) | collective-permute-done | bytes 327712 | tf_op jit(solution)/shard_map/ppermute | solution.py:16
  15.5 0.0 copy-done.6
  15.5 0.0 copy-start.7
  15.5 0.7 copy-done.7
  16.2 8.7 %shard_map.82.own_ref = bf16[10,160,256]{2,1,0:T(8,128)(2,1)} custom-call(s32[2]{0:T(128)} %pad_add_fusion.bounds_ref, bf16[4,160,256]{2,1,0:T(8,128)(2,1)} %copy-done.6, bf16[8,160,256]{2,1,0:T(8,128)(2,1)} %bitcast.28, bf16[4,160,256]{2,1,0:T(8,128)(2,1)} %copy-done.7, bf16[3,3,256,256]{3,2,1,0:T(8,128)(2,1)} %w1_ref.1, bf16[3,3,256,256]{3,2,1,0:T(8,128)(2,1)} %w2_ref.1), custom_call_target="tpu_custom_call" | custom-call | flops 4152360960 | bytes 4653056 | tf_op jit(solution)/shard_map/pallas_call | solution.py:85
  25.0 0.7 collective-permute-start.7
  25.7 3.7 %collective-permute-start.5 = (bf16[10,160,256]{2,1,0:T(8,128)(2,1)}, bf16[10,160,256]{2,1,0:T(8,128)(2,1)S(1)}, u32[]{:S(2)}, u32[]{:S(2)}) collective-permute-start(bf16[10,160,256]{2,1,0:T(8,128)(2,1)} %shard_map.82.own_ref), channel_id=1, source_target_pairs={{8,0},{12,4},{16,8},{24,16},{28,20},{9,1},{13,5},{17,9},{25,17},{2... | collective-permute-start | bytes 2457608 | tf_op jit(solution)/shard_map/ppermute | solution.py:158
  29.4 1.3 %collective-permute-start.2 = (bf16[10,160,256]{2,1,0:T(8,128)(2,1)}, bf16[10,160,256]{2,1,0:T(8,128)(2,1)S(1)}, u32[]{:S(2)}, u32[]{:S(2)}) collective-permute-start(bf16[10,160,256]{2,1,0:T(8,128)(2,1)} %shard_map.82.own_ref), channel_id=1, source_target_pairs={{0,8},{4,12},{12,20},{16,24},{20,28},{1,9},{5,13},{13,21},{17,25},... | collective-permute-start | bytes 2457608 | tf_op jit(solution)/shard_map/ppermute | solution.py:157
  30.7 0.7 collective-permute-start.4
  31.4 0.0 collective-permute-done.7
  31.4 0.7 collective-permute-start.8
  32.1 14.7 %collective-permute-done.5.fa_ref = bf16[10,160,256]{2,1,0:T(8,128)(2,1)S(1)} collective-permute-done((bf16[10,160,256]{2,1,0:T(8,128)(2,1)}, bf16[10,160,256]{2,1,0:T(8,128)(2,1)S(1)}, u32[]{:S(2)}, u32[]{:S(2)}) %collective-permute-start.5) | collective-permute-done | bytes 819232 | tf_op jit(solution)/shard_map/ppermute | solution.py:158
  46.8 0.0 copy-start.1
  46.8 0.7 collective-permute-start.6
  47.5 2.5 %collective-permute-done.2.fb_ref = bf16[10,160,256]{2,1,0:T(8,128)(2,1)S(1)} collective-permute-done((bf16[10,160,256]{2,1,0:T(8,128)(2,1)}, bf16[10,160,256]{2,1,0:T(8,128)(2,1)S(1)}, u32[]{:S(2)}, u32[]{:S(2)}) %collective-permute-start.2) | collective-permute-done | bytes 819232 | tf_op jit(solution)/shard_map/ppermute | solution.py:157
  50.0 0.0 copy-start.2
  50.0 13.7 %collective-permute-start.3 = (bf16[10,160,256]{2,1,0:T(8,128)(2,1)S(1)}, bf16[10,160,256]{2,1,0:T(8,128)(2,1)}, u32[]{:S(2)}, u32[]{:S(2)}) collective-permute-start(bf16[10,160,256]{2,1,0:T(8,128)(2,1)S(1)} %collective-permute-done.2.fb_ref), channel_id=1, source_target_pairs={{12,8},{20,16},{28,24},{13,9},{21,17},{29,25},{14,10},{22,18},{30,... | collective-permute-start | bytes 2457608 | tf_op jit(solution)/shard_map/ppermute | solution.py:165
  63.7 0.9 %slice.64 = bf16[1,160,256]{2,1,0:T(8,128)(2,1)S(1)} slice(bf16[4,160,256]{2,1,0:T(8,128)(2,1)} %copy-done.6), slice={[3:4], [0:160], [0:256]} | slice | bytes 163840 | tf_op jit(solution)/shard_map/slice | solution.py:167
  64.6 0.9 %slice.65 = bf16[1,160,256]{2,1,0:T(8,128)(2,1)S(1)} slice(bf16[4,160,256]{2,1,0:T(8,128)(2,1)} %copy-done.7), slice={[3:4], [0:160], [0:256]} | slice | bytes 163840 | tf_op jit(solution)/shard_map/slice | solution.py:167
  65.5 0.0 copy-done
  65.5 1.0 %pad_maximum_fusion.frame_ref = bf16[10,160,256]{2,1,0:T(8,128)(2,1)} fusion(bf16[1,160,256]{2,1,0:T(8,128)(2,1)S(1)} %slice.65, bf16[8,160,256]{2,1,0:T(8,128)(2,1)S(1)} %bitcast.27, bf16[1,160,256]{2,1,0:T(8,128)(2,1)S(1)} %slice.64), kind=kLoop, calls=%fused_computation | loop fusion | flops 819200 | bytes 1638400 | tf_op jit(solution)/shard_map/concatenate | solution.py:167
  66.5 0.0 collective-permute-done.4.par_ref
  66.5 0.0 copy-start.3
  66.5 0.0 collective-permute-done.8.routed_ref
  66.5 0.0 copy-start.4
  66.5 0.0 collective-permute-done.6.ra_ref
  66.5 0.9 %copy-done.4 = bf16[10,160,256]{2,1,0:T(8,128)(2,1)} copy-done((bf16[10,160,256]{2,1,0:T(8,128)(2,1)}, bf16[10,160,256]{2,1,0:T(8,128)(2,1)S(1)}, u32[]{:S(2)}) %copy-start.4) | copy-done | bytes 819224
  67.5 0.0 copy-start.5
  67.5 0.9 %copy-done.5 = bf16[10,160,256]{2,1,0:T(8,128)(2,1)} copy-done((bf16[10,160,256]{2,1,0:T(8,128)(2,1)}, bf16[10,160,256]{2,1,0:T(8,128)(2,1)S(1)}, u32[]{:S(2)}) %copy-start.5) | copy-done | bytes 819224
  68.4 0.0 collective-permute-done.3.rb_ref
  68.4 0.0 copy-done.1
  68.4 0.0 copy-done.2
  68.4 0.0 copy-done.3
  68.4 6.7 %shard_map.83 = bf16[8,160,256]{2,1,0:T(8,128)(2,1)} custom-call(f32[7]{0:T(128)} %pad_maximum_fusion.3.coef_ref, bf16[10,160,256]{2,1,0:T(8,128)(2,1)} %copy-done.2, bf16[10,160,256]{2,1,0:T(8,128)(2,1)} %collective-permute-done.3.rb_ref, bf16[10,160,256]{2,1,0:T(8,128)(2,1)} %shard_map.82.own_ref, bf16[10,160,256]{2,1,0:T(8,128)(2,1)} %copy-done.3, ...), custom_call_target="tpu_custom_call" | custom-call | flops 1509949440 | bytes 8552448 | tf_op jit(solution)/shard_map/pallas_call | solution.py:104
  (3 shorter events, 0.1 us)
Async XLA Ops:
  0.9 7.0 %copy-start.8 = (s32[1,5]{1,0:T(1,128)S(1)}, s32[1,5]{1,0:T(1,128)}, u32[]{:S(2)}) copy-start(s32[1,5]{1,0:T(1,128)} %param.12) | copy-start | bytes 64
  2.1 11.7 %collective-permute-start = (bf16[4,160,256]{2,1,0:T(8,128)(2,1)S(1)}, bf16[4,160,256]{2,1,0:T(8,128)(2,1)S(1)}, u32[]{:S(2)}, u32[]{:S(2)}) collective-permute-start(bf16[4,160,256]{2,1,0:T(8,128)(2,1)S(1)} %pad_maximum_fusion.1), channel_id=1, source_target_pairs={{0,1},{1,2},{2,3},{4,5},{5,6},{6,7},{8,9},{9,10},{10,11},{12,13},{... | collective-permute-start | bytes 983048 | tf_op jit(solution)/shard_map/ppermute | solution.py:16
  5.4 10.2 %collective-permute-start.1 = (bf16[4,160,256]{2,1,0:T(8,128)(2,1)S(1)}, bf16[4,160,256]{2,1,0:T(8,128)(2,1)S(1)}, u32[]{:S(2)}, u32[]{:S(2)}) collective-permute-start(bf16[4,160,256]{2,1,0:T(8,128)(2,1)S(1)} %pad_maximum_fusion.2), channel_id=1, source_target_pairs={{1,0},{2,1},{3,2},{5,4},{6,5},{7,6},{9,8},{10,9},{11,10},{13,12},{... | collective-permute-start | bytes 983048 | tf_op jit(solution)/shard_map/ppermute | solution.py:16
  13.7 51.7 %copy-start = (bf16[1,8,160,256]{3,2,1,0:T(8,128)(2,1)S(1)}, bf16[1,8,160,256]{3,2,1,0:T(8,128)(2,1)}, u32[]{:S(2)}) copy-start(bf16[1,8,160,256]{3,2,1,0:T(8,128)(2,1)} %param.9) | copy-start | bytes 1966084
  13.7 1.8 %copy-start.6 = (bf16[4,160,256]{2,1,0:T(8,128)(2,1)}, bf16[4,160,256]{2,1,0:T(8,128)(2,1)S(1)}, u32[]{:S(2)}) copy-start(bf16[4,160,256]{2,1,0:T(8,128)(2,1)S(1)} %collective-permute-done.above_ref) | copy-start | bytes 983044
  15.5 0.7 copy-start.7
  25.0 6.4 %collective-permute-start.7 = (bf16[10,160,256]{2,1,0:T(8,128)(2,1)}, bf16[10,160,256]{2,1,0:T(8,128)(2,1)S(1)}, u32[]{:S(2)}, u32[]{:S(2)}) collective-permute-start(bf16[10,160,256]{2,1,0:T(8,128)(2,1)} %shard_map.82.own_ref), channel_id=1, source_target_pairs={{8,24},{20,4},{9,25},{21,5},{10,26},{22,6},{11,27},{23,7}} | collective-permute-start | bytes 2457608 | tf_op jit(solution)/shard_map/ppermute | solution.py:159
  25.7 21.2 %collective-permute-start.5 = (bf16[10,160,256]{2,1,0:T(8,128)(2,1)}, bf16[10,160,256]{2,1,0:T(8,128)(2,1)S(1)}, u32[]{:S(2)}, u32[]{:S(2)}) collective-permute-start(bf16[10,160,256]{2,1,0:T(8,128)(2,1)} %shard_map.82.own_ref), channel_id=1, source_target_pairs={{8,0},{12,4},{16,8},{24,16},{28,20},{9,1},{13,5},{17,9},{25,17},{2... | collective-permute-start | bytes 2457608 | tf_op jit(solution)/shard_map/ppermute | solution.py:158
  29.4 20.7 %collective-permute-start.2 = (bf16[10,160,256]{2,1,0:T(8,128)(2,1)}, bf16[10,160,256]{2,1,0:T(8,128)(2,1)S(1)}, u32[]{:S(2)}, u32[]{:S(2)}) collective-permute-start(bf16[10,160,256]{2,1,0:T(8,128)(2,1)} %shard_map.82.own_ref), channel_id=1, source_target_pairs={{0,8},{4,12},{12,20},{16,24},{20,28},{1,9},{5,13},{13,21},{17,25},... | collective-permute-start | bytes 2457608 | tf_op jit(solution)/shard_map/ppermute | solution.py:157
  30.7 35.8 %collective-permute-start.4 = (bf16[10,160,256]{2,1,0:T(8,128)(2,1)}, bf16[10,160,256]{2,1,0:T(8,128)(2,1)S(1)}, u32[]{:S(2)}, u32[]{:S(2)}) collective-permute-start(bf16[10,160,256]{2,1,0:T(8,128)(2,1)} %shard_map.82.own_ref), channel_id=1, source_target_pairs={{0,4},{4,0},{8,12},{12,8},{16,20},{20,16},{24,28},{28,24},{1,5},{5... | collective-permute-start | bytes 2457608 | tf_op jit(solution)/shard_map/ppermute | solution.py:155
  31.4 35.1 %collective-permute-start.8 = (bf16[10,160,256]{2,1,0:T(8,128)(2,1)S(1)}, bf16[10,160,256]{2,1,0:T(8,128)(2,1)S(1)}, u32[]{:S(2)}, u32[]{:S(2)}) collective-permute-start(bf16[10,160,256]{2,1,0:T(8,128)(2,1)S(1)} %collective-permute-done.7), channel_id=1, source_target_pairs={{24,16},{4,12},{25,17},{5,13},{26,18},{6,14},{27,19},{7,15}} | collective-permute-start | bytes 2457608 | tf_op jit(solution)/shard_map/ppermute | solution.py:160
  46.8 21.5 %copy-start.1 = (bf16[10,160,256]{2,1,0:T(8,128)(2,1)}, bf16[10,160,256]{2,1,0:T(8,128)(2,1)S(1)}, u32[]{:S(2)}) copy-start(bf16[10,160,256]{2,1,0:T(8,128)(2,1)S(1)} %collective-permute-done.5.fa_ref) | copy-start | bytes 2457604
  46.8 19.7 %collective-permute-start.6 = (bf16[10,160,256]{2,1,0:T(8,128)(2,1)S(1)}, bf16[10,160,256]{2,1,0:T(8,128)(2,1)S(1)}, u32[]{:S(2)}, u32[]{:S(2)}) collective-permute-start(bf16[10,160,256]{2,1,0:T(8,128)(2,1)S(1)} %collective-permute-done.5.fa_ref), channel_id=1, source_target_pairs={{0,4},{8,12},{16,20},{1,5},{9,13},{17,21},{2,6},{10,14},{18,22},{3... | collective-permute-start | bytes 2457608 | tf_op jit(solution)/shard_map/ppermute | solution.py:166
  50.0 18.3 %copy-start.2 = (bf16[10,160,256]{2,1,0:T(8,128)(2,1)}, bf16[10,160,256]{2,1,0:T(8,128)(2,1)S(1)}, u32[]{:S(2)}) copy-start(bf16[10,160,256]{2,1,0:T(8,128)(2,1)S(1)} %collective-permute-done.2.fb_ref) | copy-start | bytes 2457604
  50.0 18.3 %collective-permute-start.3 = (bf16[10,160,256]{2,1,0:T(8,128)(2,1)S(1)}, bf16[10,160,256]{2,1,0:T(8,128)(2,1)}, u32[]{:S(2)}, u32[]{:S(2)}) collective-permute-start(bf16[10,160,256]{2,1,0:T(8,128)(2,1)S(1)} %collective-permute-done.2.fb_ref), channel_id=1, source_target_pairs={{12,8},{20,16},{28,24},{13,9},{21,17},{29,25},{14,10},{22,18},{30,... | collective-permute-start | bytes 2457608 | tf_op jit(solution)/shard_map/ppermute | solution.py:165
  66.5 1.9 %copy-start.3 = (bf16[10,160,256]{2,1,0:T(8,128)(2,1)}, bf16[10,160,256]{2,1,0:T(8,128)(2,1)S(1)}, u32[]{:S(2)}) copy-start(bf16[10,160,256]{2,1,0:T(8,128)(2,1)S(1)} %collective-permute-done.4.par_ref) | copy-start | bytes 2457604
  66.5 1.0 %copy-start.4 = (bf16[10,160,256]{2,1,0:T(8,128)(2,1)}, bf16[10,160,256]{2,1,0:T(8,128)(2,1)S(1)}, u32[]{:S(2)}) copy-start(bf16[10,160,256]{2,1,0:T(8,128)(2,1)S(1)} %collective-permute-done.8.routed_ref) | copy-start | bytes 2457604
  67.5 0.9 %copy-start.5 = (bf16[10,160,256]{2,1,0:T(8,128)(2,1)}, bf16[10,160,256]{2,1,0:T(8,128)(2,1)S(1)}, u32[]{:S(2)}) copy-start(bf16[10,160,256]{2,1,0:T(8,128)(2,1)S(1)} %collective-permute-done.6.ra_ref) | copy-start | bytes 2457604

commit v11 on v8

--- a/solution.py
+++ b/solution.py
@@ -21,57 +21,77 @@
     return v * (0.5 * (1.0 + jnp.tanh(c * (v + 0.044715 * (v * v * v)))))
 
 
-def conv_rows(x, w_ref, stack, rows_out):
-    cols, cin = x.shape[1], x.shape[2]
+def conv_rows(src_ref, w_ref, stack, rows_out, emit):
+    chunk = stack.shape[0]
+    cols, cin = src_ref.shape[1], src_ref.shape[2]
     cout = w_ref.shape[3]
-    m = rows_out * cols
-    for a in range(3):
-        stack[0:rows_out, :, a * cin : (a + 1) * cin] = x[a : a + rows_out]
-    lhs = stack[0:rows_out].reshape(m, 3 * cin)
-    taps = [
-        jnp.dot(lhs, w_ref[:, b].reshape(3 * cin, cout), preferred_element_type=jnp.float32)
-        for b in range(3)
-    ]
-    col = lax.broadcasted_iota(jnp.int32, (rows_out, cols, cout), 1).reshape(m, cout)
-    left = pltpu.roll(taps[0], shift=1, axis=0)
-    right = pltpu.roll(taps[2], shift=m - 1, axis=0)
-    out = taps[1] + jnp.where(col == 0, 0.0, left) + jnp.where(col == cols - 1, 0.0, right)
-    return out.reshape(rows_out, cols, cout)
-
-
-def layers_kernel(bounds_ref, above_ref, image_ref, below_ref, w1_ref, w2_ref, out_ref, xbuf, stack):
+    r0 = 0
+    while r0 < rows_out:
+        n = min(chunk, rows_out - r0)
+        m = n * cols
+        for a in range(3):
+            stack[0:n, :, a * cin : (a + 1) * cin] = src_ref[r0 + a : r0 + a + n]
+        lhs = stack[0:n].reshape(m, 3 * cin)
+        taps = [
+            jnp.dot(lhs, w_ref[:, b].reshape(3 * cin, cout), preferred_element_type=jnp.float32)
+            for b in range(3)
+        ]
+        col = lax.broadcasted_iota(jnp.int32, (n, cols, cout), 1).reshape(m, cout)
+        left = pltpu.roll(taps[0], shift=1, axis=0)
+        right = pltpu.roll(taps[2], shift=m - 1, axis=0)
+        out = taps[1] + jnp.where(col == 0, 0.0, left) + jnp.where(col == cols - 1, 0.0, right)
+        emit(r0, n, out.reshape(n, cols, cout))
+        r0 += n
+
+
+def layers_kernel(bounds_ref, above_ref, image_ref, below_ref, w1_ref, w2_ref, out_ref, xbuf,
+                  first_buf, stack):
     halo = below_ref.shape[0] - 1
     block = image_ref.shape[0]
     xbuf[0:halo] = above_ref[0:halo]
     xbuf[halo : halo + block] = image_ref[...]
     xbuf[halo + block :] = below_ref[0:halo]
     rows1 = block + 2 * halo - 2
-    first = gelu(conv_rows(xbuf[...], w1_ref, stack, rows1))
-    row = lax.broadcasted_iota(jnp.int32, first.shape, 0)
-    inside = (row >= bounds_ref[0]) & (row < bounds_ref[1])
-    first = jnp.where(inside, first, 0.0).astype(jnp.bfloat16)
-    out_ref[...] = gelu(conv_rows(first, w2_ref, stack, rows1 - 2)).astype(jnp.bfloat16)
+
+    def emit_first(r0, n, value):
+        value = gelu(value)
+        row = lax.broadcasted_iota(jnp.int32, value.shape, 0) + r0
+        inside = (row >= bounds_ref[0]) & (row < bounds_ref[1])
+        first_buf[r0 : r0 + n] = jnp.where(inside, value, 0.0).astype(jnp.bfloat16)
+
+    def emit_second(r0, n, value):
+        out_ref[r0 : r0 + n] = gelu(value).astype(jnp.bfloat16)
+
+    conv_rows(xbuf, w1_ref, stack, rows1, emit_first)
+    conv_rows(first_buf, w2_ref, stack, rows1 - 2, emit_second)
 
 
 def mix_kernel(coef_ref, fb_ref, rb_ref, own_ref, par_ref, ra_ref, fa_ref, routed_ref,
-               above_ref, frame_ref, below_ref, w3_ref, out_ref, fbuf, stack):
+               above_ref, frame_ref, below_ref, w3_ref, out_ref, fbuf, mixed_buf, stack):
     halo = below_ref.shape[0] - 1
     block = frame_ref.shape[0]
     fbuf[0:1] = above_ref[halo : halo + 1]
     fbuf[1 : block + 1] = frame_ref[...]
     fbuf[block + 1 :] = below_ref[halo : halo + 1]
     f32 = jnp.float32
-    summed = (
-        coef_ref[0] * fb_ref[...].astype(f32)
-        + coef_ref[1] * rb_ref[...].astype(f32)
-        + coef_ref[2] * own_ref[...].astype(f32)
-        + coef_ref[3] * par_ref[...].astype(f32)
-        + coef_ref[4] * ra_ref[...].astype(f32)
-        + coef_ref[5] * fa_ref[...].astype(f32)
-        + coef_ref[6] * routed_ref[...].astype(f32)
-    )
-    mixed = (summed * fbuf[...].astype(f32)).astype(jnp.bfloat16)
-    out_ref[...] = conv_rows(mixed, w3_ref, stack, block).astype(jnp.bfloat16)
+    step = stack.shape[0]
+    for r0 in range(0, block + 2, step):
+        rows = pl.ds(r0, min(step, block + 2 - r0))
+        summed = (
+            coef_ref[0] * fb_ref[rows].astype(f32)
+            + coef_ref[1] * rb_ref[rows].astype(f32)
+            + coef_ref[2] * own_ref[rows].astype(f32)
+            + coef_ref[3] * par_ref[rows].astype(f32)
+            + coef_ref[4] * ra_ref[rows].astype(f32)
+            + coef_ref[5] * fa_ref[rows].astype(f32)
+            + coef_ref[6] * routed_ref[rows].astype(f32)
+        )
+        mixed_buf[rows] = (summed * fbuf[rows].astype(f32)).astype(jnp.bfloat16)
+
+    def emit(r0, n, value):
+        out_ref[r0 : r0 + n] = value.astype(jnp.bfloat16)
+
+    conv_rows(mixed_buf, w3_ref, stack, block, emit)
 
 
 def vmem():
@@ -80,6 +100,9 @@
 
 def smem():
     return pl.BlockSpec(memory_space=pltpu.SMEM)
+
+
+CHUNK = 2
 
 
 def layers(bounds, above, image, below, w1, w2):
@@ -93,7 +116,8 @@
         in_specs=[smem()] + [vmem()] * 5,
         out_specs=vmem(),
         scratch_shapes=[pltpu.VMEM((rows, cols, c), jnp.bfloat16),
-                        pltpu.VMEM((rows - 2, cols, 3 * c), jnp.bfloat16)],
+                        pltpu.VMEM((rows - 2, cols, c), jnp.bfloat16),
+                        pltpu.VMEM((CHUNK, cols, 3 * c), jnp.bfloat16)],
         cost_estimate=pl.CostEstimate(flops=flops, transcendentals=2 * rows * cols * c,
                                       bytes_accessed=4 * rows * cols * c + 4 * 9 * c * c),
     )(bounds, above, image, below, w1, w2)
@@ -108,7 +132,8 @@
         in_specs=[smem()] + [vmem()] * 11,
         out_specs=vmem(),
         scratch_shapes=[pltpu.VMEM((block + 2, cols, c), jnp.bfloat16),
-                        pltpu.VMEM((block, cols, 3 * c), jnp.bfloat16)],
+                        pltpu.VMEM((block + 2, cols, c), jnp.bfloat16),
+                        pltpu.VMEM((CHUNK, cols, 3 * c), jnp.bfloat16)],
         cost_estimate=pl.CostEstimate(flops=flops, transcendentals=0,
                                       bytes_accessed=18 * (block + 2) * cols * c + 2 * 9 * c * c),
     )(coef, fb, rb, own, par, ra, fa, routed, above, frame, below, w3)
@@ -163,8 +188,8 @@
         from_behind = shifted(second, "tm", 2)
         from_ahead = shifted(second, "tm", -2)
         routed = jnp.zeros_like(second)
-    relay_behind = lax.ppermute(from_behind, "tm", [(i + 1, i) for i in range(0, count, 2)])
-    relay_ahead = lax.ppermute(from_ahead, "tm", [(i, i + 1) for i in range(0, count, 2)])
+    relay_behind = lax.ppermute(from_behind, "tm", [(i + 1, i) for i in range(2, count, 2)])
+    relay_ahead = lax.ppermute(from_ahead, "tm", [(i, i + 1) for i in range(0, count - 2, 2)])
     result = mix(coef, from_behind, relay_behind, second, partner, relay_ahead, from_ahead, routed,
                  from_above, frame, from_below, conv_frame)
     return result[None]

time: 72.7 us -> 71.4 us (0.982)
  Pallas kernels: 15.4 us -> 14.1 us
    pallas_call x1, Pallas kernels: 8.72 us -> 7.64 us  [layers(): pl.pallas_call(layers_kernel, out_shape=jax.ShapeDtypeStruct((rows - 4, c...]
where the time goes in v11:
time: 71.4 us; the launch traced here: 70.7 us
  waiting for transfers between devices  31.9 us (45%)
  Pallas kernels  14.1 us (20%)
  starting transfers between devices  13.7 us (19%)
  local copies, waits for them, and re-layouts  4.42 us (6%)
  between operations  4.02 us (6%)
  other arithmetic  2.62 us (4%)
    ppermute x1, waiting for transfers between devices, shards(): lax.ppermute(second, 'tm', [(0, 2), (1, 3), (3, 5), (4, 6), (5, 7)])  12.1 us
    ppermute x1, waiting for transfers between devices, shards(): hop = lax.ppermute(second, 'tm', [(2, 6), (5, 1)])  9.85 us
    pallas_call x1, Pallas kernels, layers(): pl.pallas_call(layers_kernel, out_shape=jax.ShapeDtypeStruct((rows - 4, c...  7.64 us
    pallas_call x1, Pallas kernels, mix(): pl.pallas_call(mix_kernel, out_shape=jax.ShapeDtypeStruct((block, cols, c...  6.46 us
    ppermute x2, starting transfers between devices, shifted(): return lax.ppermute(value, axis, pairs)  5.84 us
    ppermute x1, waiting for transfers between devices, shards(): lax.ppermute(second, 'tm', [(2, 0), (3, 1), (4, 2), (6, 4), (7, 5)])  5.46 us
    ppermute x1, waiting for transfers between devices, shards(): lax.ppermute(from_behind, 'tm', [(i + 1, i) for i in range(2, count, 2)])  2.86 us
    slice x2, local copies, waits for them, and re-layouts, shards(): up = jnp.concatenate([image[:3], frame[:1]], axis=0)  2.04 us
  transfers between devices with their start and end apart: 9, of which 5 were waited for; matrix products, arithmetic and copies ran while one was open for 5% of the time, Pallas kernels for 0%

profile of v11, /device:TPU:22, one launch (start us, length us, event | category | flops | bytes accessed | tf_op | source)
XLA Modules:
  0.0 70.7 jit_solution(16434557358598752595)
XLA Ops:
  0.0 0.9 %slice_bitcast_fusion.2 = (bf16[1,160,256]{2,1,0:T(8,128)(2,1)S(1)}, bf16[1,160,256]{2,1,0:T(8,128)(2,1)S(1)}) fusion(bf16[1,8,160,256]{3,2,1,0:T(8,128)(2,1)} %param.9), kind=kLoop, calls=%fused_computation.4 | loop fusion | bytes 327680 | tf_op jit(solution)/shard_map/slice | solution.py:159
  0.9 0.0 copy-start.8
  1.0 1.1 %slice_bitcast_fusion = (bf16[3,160,256]{2,1,0:T(8,128)(2,1)S(1)}, bf16[3,160,256]{2,1,0:T(8,128)(2,1)S(1)}) fusion(bf16[1,8,160,256]{3,2,1,0:T(8,128)(2,1)} %param.8), kind=kLoop, calls=%fused_computation.2 | loop fusion | bytes 983040 | tf_op jit(solution)/shard_map/slice | solution.py:159
  2.1 3.5 %collective-permute-start = (bf16[4,160,256]{2,1,0:T(8,128)(2,1)S(1)}, bf16[4,160,256]{2,1,0:T(8,128)(2,1)S(1)}, u32[]{:S(2)}, u32[]{:S(2)}) collective-permute-start(bf16[4,160,256]{2,1,0:T(8,128)(2,1)S(1)} %pad_maximum_fusion), channel_id=1, source_target_pairs={{0,1},{1,2},{2,3},{4,5},{5,6},{6,7},{8,9},{9,10},{10,11},{12,13},{... | collective-permute-start | bytes 983048 | tf_op jit(solution)/shard_map/ppermute | solution.py:16
  5.6 2.4 %collective-permute-start.1 = (bf16[4,160,256]{2,1,0:T(8,128)(2,1)S(1)}, bf16[4,160,256]{2,1,0:T(8,128)(2,1)S(1)}, u32[]{:S(2)}, u32[]{:S(2)}) collective-permute-start(bf16[4,160,256]{2,1,0:T(8,128)(2,1)S(1)} %pad_maximum_fusion.1), channel_id=1, source_target_pairs={{1,0},{2,1},{3,2},{5,4},{6,5},{7,6},{9,8},{10,9},{11,10},{13,12},{... | collective-permute-start | bytes 983048 | tf_op jit(solution)/shard_map/ppermute | solution.py:16
  9.3 0.0 copy-done.8
  9.3 0.6 fusion
  10.0 0.6 broadcast_divide_fusion
  10.6 0.1 slice.45
  10.7 0.7 fusion.1
  13.8 0.6 pad_add_fusion.bounds_ref
  14.5 0.6 pad_maximum_fusion.2.coef_ref
  15.1 0.0 collective-permute-done.above_ref
  15.1 0.0 copy-start.6
  15.1 1.6 %collective-permute-done.1.below_ref = bf16[4,160,256]{2,1,0:T(8,128)(2,1)S(1)} collective-permute-done((bf16[4,160,256]{2,1,0:T(8,128)(2,1)S(1)}, bf16[4,160,256]{2,1,0:T(8,128)(2,1)S(1)}, u32[]{:S(2)}, u32[]{:S(2)}) %collective-permute-start.1) | collective-permute-done | bytes 327712 | tf_op jit(solution)/shard_map/ppermute | solution.py:16
  16.7 0.0 copy-done.6
  16.7 0.0 copy-start.7
  16.7 0.7 %copy-done.7 = bf16[4,160,256]{2,1,0:T(8,128)(2,1)} copy-done((bf16[4,160,256]{2,1,0:T(8,128)(2,1)}, bf16[4,160,256]{2,1,0:T(8,128)(2,1)S(1)}, u32[]{:S(2)}) %copy-start.7) | copy-done | bytes 327704
  17.4 7.6 %shard_map.82.own_ref = bf16[10,160,256]{2,1,0:T(8,128)(2,1)} custom-call(s32[2]{0:T(128)} %pad_add_fusion.bounds_ref, bf16[4,160,256]{2,1,0:T(8,128)(2,1)} %copy-done.6, bf16[8,160,256]{2,1,0:T(8,128)(2,1)} %bitcast.28, bf16[4,160,256]{2,1,0:T(8,128)(2,1)} %copy-done.7, bf16[3,3,256,256]{3,2,1,0:T(8,128)(2,1)} %w1_ref.1, bf16[3,3,256,256]{3,2,1,0:T(8,128)(2,1)} %w2_ref.1), custom_call_target="tpu_custom_call" | custom-call | flops 4152360960 | bytes 4653056 | tf_op jit(solution)/shard_map/pallas_call | solution.py:113
  25.1 1.3 %collective-permute-start.7 = (bf16[10,160,256]{2,1,0:T(8,128)(2,1)}, bf16[10,160,256]{2,1,0:T(8,128)(2,1)S(1)}, u32[]{:S(2)}, u32[]{:S(2)}) collective-permute-start(bf16[10,160,256]{2,1,0:T(8,128)(2,1)} %shard_map.82.own_ref), channel_id=1, source_target_pairs={{8,24},{20,4},{9,25},{21,5},{10,26},{22,6},{11,27},{23,7}} | collective-permute-start | bytes 2457608 | tf_op jit(solution)/shard_map/ppermute | solution.py:185
  26.4 1.9 %collective-permute-start.5 = (bf16[10,160,256]{2,1,0:T(8,128)(2,1)}, bf16[10,160,256]{2,1,0:T(8,128)(2,1)S(1)}, u32[]{:S(2)}, u32[]{:S(2)}) collective-permute-start(bf16[10,160,256]{2,1,0:T(8,128)(2,1)} %shard_map.82.own_ref), channel_id=1, source_target_pairs={{8,0},{12,4},{16,8},{24,16},{28,20},{9,1},{13,5},{17,9},{25,17},{2... | collective-permute-start | bytes 2457608 | tf_op jit(solution)/shard_map/ppermute | solution.py:184
  28.3 1.3 %collective-permute-start.2 = (bf16[10,160,256]{2,1,0:T(8,128)(2,1)}, bf16[10,160,256]{2,1,0:T(8,128)(2,1)S(1)}, u32[]{:S(2)}, u32[]{:S(2)}) collective-permute-start(bf16[10,160,256]{2,1,0:T(8,128)(2,1)} %shard_map.82.own_ref), channel_id=1, source_target_pairs={{0,8},{4,12},{12,20},{16,24},{20,28},{1,9},{5,13},{13,21},{17,25},... | collective-permute-start | bytes 2457608 | tf_op jit(solution)/shard_map/ppermute | solution.py:183
  29.6 0.1 collective-permute-start.4
  29.7 9.8 %collective-permute-done.7 = bf16[10,160,256]{2,1,0:T(8,128)(2,1)S(1)} collective-permute-done((bf16[10,160,256]{2,1,0:T(8,128)(2,1)}, bf16[10,160,256]{2,1,0:T(8,128)(2,1)S(1)}, u32[]{:S(2)}, u32[]{:S(2)}) %collective-permute-start.7) | collective-permute-done | bytes 819232 | tf_op jit(solution)/shard_map/ppermute | solution.py:185
  39.5 1.3 %collective-permute-start.8 = (bf16[10,160,256]{2,1,0:T(8,128)(2,1)S(1)}, bf16[10,160,256]{2,1,0:T(8,128)(2,1)S(1)}, u32[]{:S(2)}, u32[]{:S(2)}) collective-permute-start(bf16[10,160,256]{2,1,0:T(8,128)(2,1)S(1)} %collective-permute-done.7), channel_id=1, source_target_pairs={{24,16},{4,12},{25,17},{5,13},{26,18},{6,14},{27,19},{7,15}} | collective-permute-start | bytes 2457608 | tf_op jit(solution)/shard_map/ppermute | solution.py:186
  40.8 5.5 %collective-permute-done.5.fa_ref = bf16[10,160,256]{2,1,0:T(8,128)(2,1)S(1)} collective-permute-done((bf16[10,160,256]{2,1,0:T(8,128)(2,1)}, bf16[10,160,256]{2,1,0:T(8,128)(2,1)S(1)}, u32[]{:S(2)}, u32[]{:S(2)}) %collective-permute-start.5) | collective-permute-done | bytes 819232 | tf_op jit(solution)/shard_map/ppermute | solution.py:184
  46.3 0.0 copy-start
  46.3 0.7 collective-permute-start.6
  47.0 12.1 %collective-permute-done.2.fb_ref = bf16[10,160,256]{2,1,0:T(8,128)(2,1)S(1)} collective-permute-done((bf16[10,160,256]{2,1,0:T(8,128)(2,1)}, bf16[10,160,256]{2,1,0:T(8,128)(2,1)S(1)}, u32[]{:S(2)}, u32[]{:S(2)}) %collective-permute-start.2) | collective-permute-done | bytes 819232 | tf_op jit(solution)/shard_map/ppermute | solution.py:183
  59.1 0.0 copy-start.1
  59.1 1.3 %collective-permute-start.3 = (bf16[10,160,256]{2,1,0:T(8,128)(2,1)S(1)}, bf16[10,160,256]{2,1,0:T(8,128)(2,1)S(1)}, u32[]{:S(2)}, u32[]{:S(2)}) collective-permute-start(bf16[10,160,256]{2,1,0:T(8,128)(2,1)S(1)} %collective-permute-done.2.fb_ref), channel_id=1, source_target_pairs={{12,8},{20,16},{28,24},{13,9},{21,17},{29,25},{14,10},{22,18},{30,... | collective-permute-start | bytes 2457608 | tf_op jit(solution)/shard_map/ppermute | solution.py:191
  60.4 0.0 collective-permute-done.4.par_ref
  60.4 0.0 copy-start.2
  60.4 0.0 collective-permute-done.8.routed_ref
  60.5 0.0 copy-start.3
  60.5 0.0 collective-permute-done.6.ra_ref
  60.5 0.0 copy-start.4
  60.5 2.9 %collective-permute-done.3.rb_ref = bf16[10,160,256]{2,1,0:T(8,128)(2,1)S(1)} collective-permute-done((bf16[10,160,256]{2,1,0:T(8,128)(2,1)S(1)}, bf16[10,160,256]{2,1,0:T(8,128)(2,1)S(1)}, u32[]{:S(2)}, u32[]{:S(2)}) %collective-permute-start.3) | collective-permute-done | bytes 819232 | tf_op jit(solution)/shard_map/ppermute | solution.py:191
  63.4 0.0 copy-done.4
  63.4 0.0 copy-start.5
  63.4 0.9 %copy-done.5 = bf16[10,160,256]{2,1,0:T(8,128)(2,1)} copy-done((bf16[10,160,256]{2,1,0:T(8,128)(2,1)}, bf16[10,160,256]{2,1,0:T(8,128)(2,1)S(1)}, u32[]{:S(2)}) %copy-start.5) | copy-done | bytes 819224
  64.3 0.0 copy-done
  64.3 0.0 copy-done.1
  64.3 0.0 copy-done.2
  64.3 0.0 copy-done.3
  64.3 6.5 %shard_map.83 = bf16[8,160,256]{2,1,0:T(8,128)(2,1)} custom-call(f32[7]{0:T(128)} %pad_maximum_fusion.2.coef_ref, bf16[10,160,256]{2,1,0:T(8,128)(2,1)} %copy-done.1, bf16[10,160,256]{2,1,0:T(8,128)(2,1)} %copy-done.5, bf16[10,160,256]{2,1,0:T(8,128)(2,1)} %shard_map.82.own_ref, bf16[10,160,256]{2,1,0:T(8,128)(2,1)} %copy-done.2, ...), custom_call_target="tpu_custom_call" | custom-call | flops 1509949440 | bytes 8552448 | tf_op jit(solution)/shard_map/pallas_call | solution.py:129
  (2 shorter events, 0.1 us)
Async XLA Ops:
  0.9 8.4 %copy-start.8 = (s32[1,5]{1,0:T(1,128)S(1)}, s32[1,5]{1,0:T(1,128)}, u32[]{:S(2)}) copy-start(s32[1,5]{1,0:T(1,128)} %param.12) | copy-start | bytes 64
  2.1 13.0 %collective-permute-start = (bf16[4,160,256]{2,1,0:T(8,128)(2,1)S(1)}, bf16[4,160,256]{2,1,0:T(8,128)(2,1)S(1)}, u32[]{:S(2)}, u32[]{:S(2)}) collective-permute-start(bf16[4,160,256]{2,1,0:T(8,128)(2,1)S(1)} %pad_maximum_fusion), channel_id=1, source_target_pairs={{0,1},{1,2},{2,3},{4,5},{5,6},{6,7},{8,9},{9,10},{10,11},{12,13},{... | collective-permute-start | bytes 983048 | tf_op jit(solution)/shard_map/ppermute | solution.py:16
  5.6 11.1 %collective-permute-start.1 = (bf16[4,160,256]{2,1,0:T(8,128)(2,1)S(1)}, bf16[4,160,256]{2,1,0:T(8,128)(2,1)S(1)}, u32[]{:S(2)}, u32[]{:S(2)}) collective-permute-start(bf16[4,160,256]{2,1,0:T(8,128)(2,1)S(1)} %pad_maximum_fusion.1), channel_id=1, source_target_pairs={{1,0},{2,1},{3,2},{5,4},{6,5},{7,6},{9,8},{10,9},{11,10},{13,12},{... | collective-permute-start | bytes 983048 | tf_op jit(solution)/shard_map/ppermute | solution.py:16
  15.1 1.6 %copy-start.6 = (bf16[4,160,256]{2,1,0:T(8,128)(2,1)}, bf16[4,160,256]{2,1,0:T(8,128)(2,1)S(1)}, u32[]{:S(2)}) copy-start(bf16[4,160,256]{2,1,0:T(8,128)(2,1)S(1)} %collective-permute-done.above_ref) | copy-start | bytes 983044
  16.7 0.7 %copy-start.7 = (bf16[4,160,256]{2,1,0:T(8,128)(2,1)}, bf16[4,160,256]{2,1,0:T(8,128)(2,1)S(1)}, u32[]{:S(2)}) copy-start(bf16[4,160,256]{2,1,0:T(8,128)(2,1)S(1)} %collective-permute-done.1.below_ref) | copy-start | bytes 983044
  25.1 14.4 %collective-permute-start.7 = (bf16[10,160,256]{2,1,0:T(8,128)(2,1)}, bf16[10,160,256]{2,1,0:T(8,128)(2,1)S(1)}, u32[]{:S(2)}, u32[]{:S(2)}) collective-permute-start(bf16[10,160,256]{2,1,0:T(8,128)(2,1)} %shard_map.82.own_ref), channel_id=1, source_target_pairs={{8,24},{20,4},{9,25},{21,5},{10,26},{22,6},{11,27},{23,7}} | collective-permute-start | bytes 2457608 | tf_op jit(solution)/shard_map/ppermute | solution.py:185
  26.4 19.9 %collective-permute-start.5 = (bf16[10,160,256]{2,1,0:T(8,128)(2,1)}, bf16[10,160,256]{2,1,0:T(8,128)(2,1)S(1)}, u32[]{:S(2)}, u32[]{:S(2)}) collective-permute-start(bf16[10,160,256]{2,1,0:T(8,128)(2,1)} %shard_map.82.own_ref), channel_id=1, source_target_pairs={{8,0},{12,4},{16,8},{24,16},{28,20},{9,1},{13,5},{17,9},{25,17},{2... | collective-permute-start | bytes 2457608 | tf_op jit(solution)/shard_map/ppermute | solution.py:184
  28.3 30.9 %collective-permute-start.2 = (bf16[10,160,256]{2,1,0:T(8,128)(2,1)}, bf16[10,160,256]{2,1,0:T(8,128)(2,1)S(1)}, u32[]{:S(2)}, u32[]{:S(2)}) collective-permute-start(bf16[10,160,256]{2,1,0:T(8,128)(2,1)} %shard_map.82.own_ref), channel_id=1, source_target_pairs={{0,8},{4,12},{12,20},{16,24},{20,28},{1,9},{5,13},{13,21},{17,25},... | collective-permute-start | bytes 2457608 | tf_op jit(solution)/shard_map/ppermute | solution.py:183
  29.6 30.9 %collective-permute-start.4 = (bf16[10,160,256]{2,1,0:T(8,128)(2,1)}, bf16[10,160,256]{2,1,0:T(8,128)(2,1)S(1)}, u32[]{:S(2)}, u32[]{:S(2)}) collective-permute-start(bf16[10,160,256]{2,1,0:T(8,128)(2,1)} %shard_map.82.own_ref), channel_id=1, source_target_pairs={{0,4},{4,0},{8,12},{12,8},{16,20},{20,16},{24,28},{28,24},{1,5},{5... | collective-permute-start | bytes 2457608 | tf_op jit(solution)/shard_map/ppermute | solution.py:181
  39.5 20.9 %collective-permute-start.8 = (bf16[10,160,256]{2,1,0:T(8,128)(2,1)S(1)}, bf16[10,160,256]{2,1,0:T(8,128)(2,1)S(1)}, u32[]{:S(2)}, u32[]{:S(2)}) collective-permute-start(bf16[10,160,256]{2,1,0:T(8,128)(2,1)S(1)} %collective-permute-done.7), channel_id=1, source_target_pairs={{24,16},{4,12},{25,17},{5,13},{26,18},{6,14},{27,19},{7,15}} | collective-permute-start | bytes 2457608 | tf_op jit(solution)/shard_map/ppermute | solution.py:186
  46.3 18.0 %copy-start = (bf16[10,160,256]{2,1,0:T(8,128)(2,1)}, bf16[10,160,256]{2,1,0:T(8,128)(2,1)S(1)}, u32[]{:S(2)}) copy-start(bf16[10,160,256]{2,1,0:T(8,128)(2,1)S(1)} %collective-permute-done.5.fa_ref) | copy-start | bytes 2457604
  46.3 14.2 %collective-permute-start.6 = (bf16[10,160,256]{2,1,0:T(8,128)(2,1)S(1)}, bf16[10,160,256]{2,1,0:T(8,128)(2,1)S(1)}, u32[]{:S(2)}, u32[]{:S(2)}) collective-permute-start(bf16[10,160,256]{2,1,0:T(8,128)(2,1)S(1)} %collective-permute-done.5.fa_ref), channel_id=1, source_target_pairs={{0,4},{8,12},{16,20},{1,5},{9,13},{17,21},{2,6},{10,14},{18,22},{3... | collective-permute-start | bytes 2457608 | tf_op jit(solution)/shard_map/ppermute | solution.py:192
  59.1 5.1 %copy-start.1 = (bf16[10,160,256]{2,1,0:T(8,128)(2,1)}, bf16[10,160,256]{2,1,0:T(8,128)(2,1)S(1)}, u32[]{:S(2)}) copy-start(bf16[10,160,256]{2,1,0:T(8,128)(2,1)S(1)} %collective-permute-done.2.fb_ref) | copy-start | bytes 2457604
  59.1 4.2 %collective-permute-start.3 = (bf16[10,160,256]{2,1,0:T(8,128)(2,1)S(1)}, bf16[10,160,256]{2,1,0:T(8,128)(2,1)S(1)}, u32[]{:S(2)}, u32[]{:S(2)}) collective-permute-start(bf16[10,160,256]{2,1,0:T(8,128)(2,1)S(1)} %collective-permute-done.2.fb_ref), channel_id=1, source_target_pairs={{12,8},{20,16},{28,24},{13,9},{21,17},{29,25},{14,10},{22,18},{30,... | collective-permute-start | bytes 2457608 | tf_op jit(solution)/shard_map/ppermute | solution.py:191
  60.4 3.8 %copy-start.2 = (bf16[10,160,256]{2,1,0:T(8,128)(2,1)}, bf16[10,160,256]{2,1,0:T(8,128)(2,1)S(1)}, u32[]{:S(2)}) copy-start(bf16[10,160,256]{2,1,0:T(8,128)(2,1)S(1)} %collective-permute-done.4.par_ref) | copy-start | bytes 2457604
  60.5 3.8 %copy-start.3 = (bf16[10,160,256]{2,1,0:T(8,128)(2,1)}, bf16[10,160,256]{2,1,0:T(8,128)(2,1)S(1)}, u32[]{:S(2)}) copy-start(bf16[10,160,256]{2,1,0:T(8,128)(2,1)S(1)} %collective-permute-done.8.routed_ref) | copy-start | bytes 2457604
  60.5 2.9 %copy-start.4 = (bf16[10,160,256]{2,1,0:T(8,128)(2,1)}, bf16[10,160,256]{2,1,0:T(8,128)(2,1)S(1)}, u32[]{:S(2)}) copy-start(bf16[10,160,256]{2,1,0:T(8,128)(2,1)S(1)} %collective-permute-done.6.ra_ref) | copy-start | bytes 2457604
  63.4 0.9 %copy-start.5 = (bf16[10,160,256]{2,1,0:T(8,128)(2,1)}, bf16[10,160,256]{2,1,0:T(8,128)(2,1)S(1)}, u32[]{:S(2)}) copy-start(bf16[10,160,256]{2,1,0:T(8,128)(2,1)S(1)} %collective-permute-done.3.rb_ref) | copy-start | bytes 2457604

commit v12 on v11

--- a/solution.py
+++ b/solution.py
@@ -66,8 +66,8 @@
     conv_rows(first_buf, w2_ref, stack, rows1 - 2, emit_second)
 
 
-def mix_kernel(coef_ref, fb_ref, rb_ref, own_ref, par_ref, ra_ref, fa_ref, routed_ref,
-               above_ref, frame_ref, below_ref, w3_ref, out_ref, fbuf, mixed_buf, stack):
+def mix_kernel(coef_ref, fbe_ref, fbo_ref, rb_ref, own_ref, par_ref, ra_ref, fae_ref, fao_ref,
+               routed_ref, above_ref, frame_ref, below_ref, w3_ref, out_ref, fbuf, mixed_buf, stack):
     halo = below_ref.shape[0] - 1
     block = frame_ref.shape[0]
     fbuf[0:1] = above_ref[halo : halo + 1]
@@ -75,15 +75,27 @@
     fbuf[block + 1 :] = below_ref[halo : halo + 1]
     f32 = jnp.float32
     step = stack.shape[0]
+    odd = coef_ref[7] > 0.5
     for r0 in range(0, block + 2, step):
         rows = pl.ds(r0, min(step, block + 2 - r0))
-        summed = (
-            coef_ref[0] * fb_ref[rows].astype(f32)
-            + coef_ref[1] * rb_ref[rows].astype(f32)
-            + coef_ref[2] * own_ref[rows].astype(f32)
+
+        def even_terms():
+            return (
+                coef_ref[0] * fbe_ref[rows].astype(f32)
+                + coef_ref[1] * rb_ref[rows].astype(f32)
+                + coef_ref[5] * fae_ref[rows].astype(f32)
+            )
+
+        def odd_terms():
+            return (
+                coef_ref[0] * fbo_ref[rows].astype(f32)
+                + coef_ref[4] * ra_ref[rows].astype(f32)
+                + coef_ref[5] * fao_ref[rows].astype(f32)
+            )
+
+        summed = lax.cond(odd, odd_terms, even_terms) + (
+            coef_ref[2] * own_ref[rows].astype(f32)
             + coef_ref[3] * par_ref[rows].astype(f32)
-            + coef_ref[4] * ra_ref[rows].astype(f32)
-            + coef_ref[5] * fa_ref[rows].astype(f32)
             + coef_ref[6] * routed_ref[rows].astype(f32)
         )
         mixed_buf[rows] = (summed * fbuf[rows].astype(f32)).astype(jnp.bfloat16)
@@ -123,20 +135,20 @@
     )(bounds, above, image, below, w1, w2)
 
 
-def mix(coef, fb, rb, own, par, ra, fa, routed, above, frame, below, w3):
+def mix(coef, fbe, fbo, rb, own, par, ra, fae, fao, routed, above, frame, below, w3):
     block, cols, c = frame.shape
     flops = 2 * 9 * c * c * cols * block
     return pl.pallas_call(
         mix_kernel,
         out_shape=jax.ShapeDtypeStruct((block, cols, c), jnp.bfloat16),
-        in_specs=[smem()] + [vmem()] * 11,
+        in_specs=[smem()] + [vmem()] * 13,
         out_specs=vmem(),
         scratch_shapes=[pltpu.VMEM((block + 2, cols, c), jnp.bfloat16),
                         pltpu.VMEM((block + 2, cols, c), jnp.bfloat16),
                         pltpu.VMEM((CHUNK, cols, 3 * c), jnp.bfloat16)],
         cost_estimate=pl.CostEstimate(flops=flops, transcendentals=0,
                                       bytes_accessed=18 * (block + 2) * cols * c + 2 * 9 * c * c),
-    )(coef, fb, rb, own, par, ra, fa, routed, above, frame, below, w3)
+    )(coef, fbe, fbo, rb, own, par, ra, fae, fao, routed, above, frame, below, w3)
 
 
 def shards(
@@ -172,7 +184,8 @@
     is_odd = (t % 2) == 1
     partner_weight = jnp.where(is_odd, weights[1], weights[3])
     routed_weight = jnp.where(is_odd, weights[4], weights[0])
-    coef = jnp.concatenate([weights[:3], partner_weight[None], weights[3:], routed_weight[None]])
+    coef = jnp.concatenate([weights[:3], partner_weight[None], weights[3:], routed_weight[None],
+                            is_odd.astype(jnp.float32)[None]])
     bounds = jnp.stack([2 - row0, height - row0 + 2]).astype(jnp.int32)
     coef, bounds, image = lax.optimization_barrier((coef, bounds, image))
 
@@ -180,18 +193,26 @@
 
     partner = lax.ppermute(second, "tm", [(i, i ^ 1) for i in range(count)])
     if count == 8:
-        from_behind = lax.ppermute(second, "tm", [(0, 2), (1, 3), (3, 5), (4, 6), (5, 7)])
-        from_ahead = lax.ppermute(second, "tm", [(2, 0), (3, 1), (4, 2), (6, 4), (7, 5)])
+        behind_pairs = [(0, 2), (1, 3), (3, 5), (4, 6), (5, 7)]
+        ahead_pairs = [(2, 0), (3, 1), (4, 2), (6, 4), (7, 5)]
         hop = lax.ppermute(second, "tm", [(2, 6), (5, 1)])
         routed = lax.ppermute(hop, "tm", [(6, 4), (1, 3)])
     else:
-        from_behind = shifted(second, "tm", 2)
-        from_ahead = shifted(second, "tm", -2)
+        behind_pairs = [(i, i + 2) for i in range(count - 2)]
+        ahead_pairs = [(i + 2, i) for i in range(count - 2)]
         routed = jnp.zeros_like(second)
-    relay_behind = lax.ppermute(from_behind, "tm", [(i + 1, i) for i in range(2, count, 2)])
-    relay_ahead = lax.ppermute(from_ahead, "tm", [(i, i + 1) for i in range(0, count - 2, 2)])
-    result = mix(coef, from_behind, relay_behind, second, partner, relay_ahead, from_ahead, routed,
-                 from_above, frame, from_below, conv_frame)
+    def by_parity(pairs, parity):
+        chosen = [(a, b) for a, b in pairs if b % 2 == parity]
+        return lax.ppermute(second, "tm", chosen) if chosen else jnp.zeros_like(second)
+
+    behind_even = by_parity(behind_pairs, 0)
+    behind_odd = by_parity(behind_pairs, 1)
+    ahead_even = by_parity(ahead_pairs, 0)
+    ahead_odd = by_parity(ahead_pairs, 1)
+    relay_behind = lax.ppermute(behind_odd, "tm", [(i + 1, i) for i in range(2, count, 2)])
+    relay_ahead = lax.ppermute(ahead_even, "tm", [(i, i + 1) for i in range(0, count - 2, 2)])
+    result = mix(coef, behind_even, behind_odd, relay_behind, second, partner, relay_ahead,
+                 ahead_even, ahead_odd, routed, from_above, frame, from_below, conv_frame)
     return result[None]
 
 

time: 71.4 us -> 72.2 us (1.011)
  the two profiles are of different devices: /device:TPU:22 before, /device:TPU:1 now
where the time goes in v12:
time: 72.2 us; the launch traced here: 71.8 us
  waiting for transfers between devices  27.3 us (38%)
  starting transfers between devices  16.8 us (23%)
  Pallas kernels  15.4 us (21%)
  local copies, waits for them, and re-layouts  6.21 us (9%)
  between operations  4.19 us (6%)
  other arithmetic  1.89 us (3%)
    ppermute x1, waiting for transfers between devices, shards(): routed = lax.ppermute(hop, 'tm', [(6, 4), (1, 3)])  14.9 us
    pallas_call x1, Pallas kernels, mix(): pl.pallas_call(mix_kernel, out_shape=jax.ShapeDtypeStruct((block, cols, c...  7.75 us
    pallas_call x1, Pallas kernels, layers(): pl.pallas_call(layers_kernel, out_shape=jax.ShapeDtypeStruct((rows - 4, c...  7.65 us
    ppermute x4, starting transfers between devices, by_parity(): lax.ppermute(second, 'tm', chosen)  6.79 us
    ppermute x1, waiting for transfers between devices, shards(): hop = lax.ppermute(second, 'tm', [(2, 6), (5, 1)])  6.1 us
    ppermute x2, starting transfers between devices, shifted(): return lax.ppermute(value, axis, pairs)  5.34 us
    ppermute x4, waiting for transfers between devices, by_parity(): lax.ppermute(second, 'tm', chosen)  4.61 us
    unnamed x22, local copies, waits for them, and re-layouts  2.82 us
  transfers between devices with their start and end apart: 11, of which 4 were waited for; matrix products, arithmetic and copies ran while one was open for 4% of the time, Pallas kernels for 0%

profile of v12, /device:TPU:1, one launch (start us, length us, event | category | flops | bytes accessed | tf_op | source)
XLA Modules:
  0.0 71.8 jit_solution(4977625211793097998)
XLA Ops:
  0.0 0.9 %slice_bitcast_fusion.2 = (bf16[1,160,256]{2,1,0:T(8,128)(2,1)S(1)}, bf16[1,160,256]{2,1,0:T(8,128)(2,1)S(1)}) fusion(bf16[1,8,160,256]{3,2,1,0:T(8,128)(2,1)} %param.9), kind=kLoop, calls=%fused_computation.4 | loop fusion | bytes 327680 | tf_op jit(solution)/shard_map/slice | solution.py:171
  0.9 0.0 copy-start.10
  1.0 1.1 %slice_bitcast_fusion = (bf16[3,160,256]{2,1,0:T(8,128)(2,1)S(1)}, bf16[3,160,256]{2,1,0:T(8,128)(2,1)S(1)}) fusion(bf16[1,8,160,256]{3,2,1,0:T(8,128)(2,1)} %param.8), kind=kLoop, calls=%fused_computation.2 | loop fusion | bytes 983040 | tf_op jit(solution)/shard_map/slice | solution.py:171
  2.1 4.0 %collective-permute-start = (bf16[4,160,256]{2,1,0:T(8,128)(2,1)S(1)}, bf16[4,160,256]{2,1,0:T(8,128)(2,1)S(1)}, u32[]{:S(2)}, u32[]{:S(2)}) collective-permute-start(bf16[4,160,256]{2,1,0:T(8,128)(2,1)S(1)} %pad_maximum_fusion), channel_id=1, source_target_pairs={{0,1},{1,2},{2,3},{4,5},{5,6},{6,7},{8,9},{9,10},{10,11},{12,13},{... | collective-permute-start | bytes 983048 | tf_op jit(solution)/shard_map/ppermute | solution.py:16
  6.2 1.3 %collective-permute-start.1 = (bf16[4,160,256]{2,1,0:T(8,128)(2,1)S(1)}, bf16[4,160,256]{2,1,0:T(8,128)(2,1)S(1)}, u32[]{:S(2)}, u32[]{:S(2)}) collective-permute-start(bf16[4,160,256]{2,1,0:T(8,128)(2,1)S(1)} %pad_maximum_fusion.1), channel_id=1, source_target_pairs={{1,0},{2,1},{3,2},{5,4},{6,5},{7,6},{9,8},{10,9},{11,10},{13,12},{... | collective-permute-start | bytes 983048 | tf_op jit(solution)/shard_map/ppermute | solution.py:16
  8.8 0.0 copy-done.10
  8.8 0.6 fusion
  9.4 0.6 broadcast_divide_fusion
  10.1 0.1 slice.45
  10.1 0.7 fusion.1
  13.5 0.6 concatenate.9.coef_ref
  14.1 0.6 pad_add_fusion.bounds_ref
  14.7 0.0 collective-permute-done.above_ref
  14.7 1.7 %collective-permute-done.1.below_ref = bf16[4,160,256]{2,1,0:T(8,128)(2,1)S(1)} collective-permute-done((bf16[4,160,256]{2,1,0:T(8,128)(2,1)S(1)}, bf16[4,160,256]{2,1,0:T(8,128)(2,1)S(1)}, u32[]{:S(2)}, u32[]{:S(2)}) %collective-permute-start.1) | collective-permute-done | bytes 327712 | tf_op jit(solution)/shard_map/ppermute | solution.py:16
  16.3 0.0 copy-done.8
  16.4 0.7 %copy-done.9 = bf16[4,160,256]{2,1,0:T(8,128)(2,1)} copy-done((bf16[4,160,256]{2,1,0:T(8,128)(2,1)}, bf16[4,160,256]{2,1,0:T(8,128)(2,1)S(1)}, u32[]{:S(2)}) %copy-start.9) | copy-done | bytes 327704
  17.1 7.6 %shard_map.82.own_ref = bf16[10,160,256]{2,1,0:T(8,128)(2,1)} custom-call(s32[2]{0:T(128)} %pad_add_fusion.bounds_ref, bf16[4,160,256]{2,1,0:T(8,128)(2,1)} %copy-done.8, bf16[8,160,256]{2,1,0:T(8,128)(2,1)} %bitcast.29, bf16[4,160,256]{2,1,0:T(8,128)(2,1)} %copy-done.9, bf16[3,3,256,256]{3,2,1,0:T(8,128)(2,1)} %w1_ref.1, bf16[3,3,256,256]{3,2,1,0:T(8,128)(2,1)} %w2_ref.1), custom_call_target="tpu_custom_call" | custom-call | flops 4152360960 | bytes 4653056 | tf_op jit(solution)/shard_map/pallas_call | solution.py:125
  24.7 1.3 %collective-permute-start.9 = (bf16[10,160,256]{2,1,0:T(8,128)(2,1)}, bf16[10,160,256]{2,1,0:T(8,128)(2,1)S(1)}, u32[]{:S(2)}, u32[]{:S(2)}) collective-permute-start(bf16[10,160,256]{2,1,0:T(8,128)(2,1)} %shard_map.82.own_ref), channel_id=1, source_target_pairs={{8,24},{20,4},{9,25},{21,5},{10,26},{22,6},{11,27},{23,7}} | collective-permute-start | bytes 2457608 | tf_op jit(solution)/shard_map/ppermute | solution.py:198
  26.0 1.3 %collective-permute-start.8 = (bf16[10,160,256]{2,1,0:T(8,128)(2,1)}, bf16[10,160,256]{2,1,0:T(8,128)(2,1)S(1)}, u32[]{:S(2)}, u32[]{:S(2)}) collective-permute-start(bf16[10,160,256]{2,1,0:T(8,128)(2,1)} %shard_map.82.own_ref), channel_id=1, source_target_pairs={{12,4},{28,20},{13,5},{29,21},{14,6},{30,22},{15,7},{31,23}} | collective-permute-start | bytes 2457608 | tf_op jit(solution)/shard_map/ppermute | solution.py:206
  27.3 0.7 collective-permute-start.6
  28.1 4.1 %collective-permute-start.3 = (bf16[10,160,256]{2,1,0:T(8,128)(2,1)}, bf16[10,160,256]{2,1,0:T(8,128)(2,1)S(1)}, u32[]{:S(2)}, u32[]{:S(2)}) collective-permute-start(bf16[10,160,256]{2,1,0:T(8,128)(2,1)} %shard_map.82.own_ref), channel_id=1, source_target_pairs={{4,12},{12,20},{20,28},{5,13},{13,21},{21,29},{6,14},{14,22},{22,3... | collective-permute-start | bytes 2457608 | tf_op jit(solution)/shard_map/ppermute | solution.py:206
  32.1 0.1 collective-permute-start.5
  32.2 6.1 %collective-permute-done.9 = bf16[10,160,256]{2,1,0:T(8,128)(2,1)S(1)} collective-permute-done((bf16[10,160,256]{2,1,0:T(8,128)(2,1)}, bf16[10,160,256]{2,1,0:T(8,128)(2,1)S(1)}, u32[]{:S(2)}, u32[]{:S(2)}) %collective-permute-start.9) | collective-permute-done | bytes 819232 | tf_op jit(solution)/shard_map/ppermute | solution.py:198
  38.3 0.7 collective-permute-start.2
  39.0 4.6 %collective-permute-done.8.fao_ref = bf16[10,160,256]{2,1,0:T(8,128)(2,1)S(1)} collective-permute-done((bf16[10,160,256]{2,1,0:T(8,128)(2,1)}, bf16[10,160,256]{2,1,0:T(8,128)(2,1)S(1)}, u32[]{:S(2)}, u32[]{:S(2)}) %collective-permute-start.8) | collective-permute-done | bytes 819232 | tf_op jit(solution)/shard_map/ppermute | solution.py:206
  43.6 1.3 %collective-permute-start.10 = (bf16[10,160,256]{2,1,0:T(8,128)(2,1)S(1)}, bf16[10,160,256]{2,1,0:T(8,128)(2,1)S(1)}, u32[]{:S(2)}, u32[]{:S(2)}) collective-permute-start(bf16[10,160,256]{2,1,0:T(8,128)(2,1)S(1)} %collective-permute-done.9), channel_id=1, source_target_pairs={{24,16},{4,12},{25,17},{5,13},{26,18},{6,14},{27,19},{7,15}} | collective-permute-start | bytes 2457608 | tf_op jit(solution)/shard_map/ppermute | solution.py:199
  45.0 0.0 collective-permute-done.6.fae_ref
  45.0 0.0 copy-start.1
  45.0 1.3 %collective-permute-start.7 = (bf16[10,160,256]{2,1,0:T(8,128)(2,1)S(1)}, bf16[10,160,256]{2,1,0:T(8,128)(2,1)S(1)}, u32[]{:S(2)}, u32[]{:S(2)}) collective-permute-start(bf16[10,160,256]{2,1,0:T(8,128)(2,1)S(1)} %collective-permute-done.6.fae_ref), channel_id=1, source_target_pairs={{0,4},{8,12},{16,20},{1,5},{9,13},{17,21},{2,6},{10,14},{18,22},{3... | collective-permute-start | bytes 2457608 | tf_op jit(solution)/shard_map/ppermute | solution.py:213
  46.3 0.0 collective-permute-done.3.fbo_ref
  46.3 0.0 copy-start.2
  46.3 0.7 collective-permute-start.4
  47.0 0.0 collective-permute-done.5.par_ref
  47.0 0.0 copy-start.3
  47.1 0.0 collective-permute-done.2.fbe_ref
  47.1 0.0 copy-start.4
  47.1 14.9 %collective-permute-done.10.routed_ref = bf16[10,160,256]{2,1,0:T(8,128)(2,1)S(1)} collective-permute-done((bf16[10,160,256]{2,1,0:T(8,128)(2,1)S(1)}, bf16[10,160,256]{2,1,0:T(8,128)(2,1)S(1)}, u32[]{:S(2)}, u32[]{:S(2)}) %collective-permute-start.10) | collective-permute-done | bytes 819232 | tf_op jit(solution)/shard_map/ppermute | solution.py:199
  62.0 0.0 collective-permute-done.7.ra_ref
  62.0 0.0 collective-permute-done.4.rb_ref
  62.0 0.0 copy-done.4
  62.0 0.9 %copy-done.5 = bf16[10,160,256]{2,1,0:T(8,128)(2,1)} copy-done((bf16[10,160,256]{2,1,0:T(8,128)(2,1)}, bf16[10,160,256]{2,1,0:T(8,128)(2,1)S(1)}, u32[]{:S(2)}) %copy-start.5) | copy-done | bytes 819224
  62.9 0.3 copy-done.6
  63.2 0.9 %copy-done.7 = bf16[10,160,256]{2,1,0:T(8,128)(2,1)} copy-done((bf16[10,160,256]{2,1,0:T(8,128)(2,1)}, bf16[10,160,256]{2,1,0:T(8,128)(2,1)S(1)}, u32[]{:S(2)}) %copy-start.7) | copy-done | bytes 819224
  64.1 0.0 copy-done
  64.1 0.0 copy-done.1
  64.1 0.0 copy-done.2
  64.1 0.0 copy-done.3
  64.1 7.8 %shard_map.83 = bf16[8,160,256]{2,1,0:T(8,128)(2,1)} custom-call(f32[8]{0:T(128)} %concatenate.9.coef_ref, bf16[10,160,256]{2,1,0:T(8,128)(2,1)} %copy-done.4, bf16[10,160,256]{2,1,0:T(8,128)(2,1)} %copy-done.2, bf16[10,160,256]{2,1,0:T(8,128)(2,1)} %copy-done.7, bf16[10,160,256]{2,1,0:T(8,128)(2,1)} %shard_map.82.own_ref, bf16[10,160,256]{2,1,0:T(8,128)(2,1)} %copy-done.3, ...), custom_call_target="tpu_custom_call" | custom-call | flops 1509949440 | bytes 8552448 | tf_op jit(solution)/shard_map/pallas_call | solution.py:141
  (8 shorter events, 0.1 us)
Async XLA Ops:
  0.9 7.9 %copy-start.10 = (s32[1,5]{1,0:T(1,128)S(1)}, s32[1,5]{1,0:T(1,128)}, u32[]{:S(2)}) copy-start(s32[1,5]{1,0:T(1,128)} %param.12) | copy-start | bytes 64
  2.1 12.6 %collective-permute-start = (bf16[4,160,256]{2,1,0:T(8,128)(2,1)S(1)}, bf16[4,160,256]{2,1,0:T(8,128)(2,1)S(1)}, u32[]{:S(2)}, u32[]{:S(2)}) collective-permute-start(bf16[4,160,256]{2,1,0:T(8,128)(2,1)S(1)} %pad_maximum_fusion), channel_id=1, source_target_pairs={{0,1},{1,2},{2,3},{4,5},{5,6},{6,7},{8,9},{9,10},{10,11},{12,13},{... | collective-permute-start | bytes 983048 | tf_op jit(solution)/shard_map/ppermute | solution.py:16
  6.2 10.2 %collective-permute-start.1 = (bf16[4,160,256]{2,1,0:T(8,128)(2,1)S(1)}, bf16[4,160,256]{2,1,0:T(8,128)(2,1)S(1)}, u32[]{:S(2)}, u32[]{:S(2)}) collective-permute-start(bf16[4,160,256]{2,1,0:T(8,128)(2,1)S(1)} %pad_maximum_fusion.1), channel_id=1, source_target_pairs={{1,0},{2,1},{3,2},{5,4},{6,5},{7,6},{9,8},{10,9},{11,10},{13,12},{... | collective-permute-start | bytes 983048 | tf_op jit(solution)/shard_map/ppermute | solution.py:16
  14.7 1.7 %copy-start.8 = (bf16[4,160,256]{2,1,0:T(8,128)(2,1)}, bf16[4,160,256]{2,1,0:T(8,128)(2,1)S(1)}, u32[]{:S(2)}) copy-start(bf16[4,160,256]{2,1,0:T(8,128)(2,1)S(1)} %collective-permute-done.above_ref) | copy-start | bytes 983044
  16.4 0.7 %copy-start.9 = (bf16[4,160,256]{2,1,0:T(8,128)(2,1)}, bf16[4,160,256]{2,1,0:T(8,128)(2,1)S(1)}, u32[]{:S(2)}) copy-start(bf16[4,160,256]{2,1,0:T(8,128)(2,1)S(1)} %collective-permute-done.1.below_ref) | copy-start | bytes 983044
  24.7 13.6 %collective-permute-start.9 = (bf16[10,160,256]{2,1,0:T(8,128)(2,1)}, bf16[10,160,256]{2,1,0:T(8,128)(2,1)S(1)}, u32[]{:S(2)}, u32[]{:S(2)}) collective-permute-start(bf16[10,160,256]{2,1,0:T(8,128)(2,1)} %shard_map.82.own_ref), channel_id=1, source_target_pairs={{8,24},{20,4},{9,25},{21,5},{10,26},{22,6},{11,27},{23,7}} | collective-permute-start | bytes 2457608 | tf_op jit(solution)/shard_map/ppermute | solution.py:198
  26.0 17.6 %collective-permute-start.8 = (bf16[10,160,256]{2,1,0:T(8,128)(2,1)}, bf16[10,160,256]{2,1,0:T(8,128)(2,1)S(1)}, u32[]{:S(2)}, u32[]{:S(2)}) collective-permute-start(bf16[10,160,256]{2,1,0:T(8,128)(2,1)} %shard_map.82.own_ref), channel_id=1, source_target_pairs={{12,4},{28,20},{13,5},{29,21},{14,6},{30,22},{15,7},{31,23}} | collective-permute-start | bytes 2457608 | tf_op jit(solution)/shard_map/ppermute | solution.py:206
  27.3 17.6 %collective-permute-start.6 = (bf16[10,160,256]{2,1,0:T(8,128)(2,1)}, bf16[10,160,256]{2,1,0:T(8,128)(2,1)S(1)}, u32[]{:S(2)}, u32[]{:S(2)}) collective-permute-start(bf16[10,160,256]{2,1,0:T(8,128)(2,1)} %shard_map.82.own_ref), channel_id=1, source_target_pairs={{8,0},{16,8},{24,16},{9,1},{17,9},{25,17},{10,2},{18,10},{26,18},{... | collective-permute-start | bytes 2457608 | tf_op jit(solution)/shard_map/ppermute | solution.py:206
  28.1 18.2 %collective-permute-start.3 = (bf16[10,160,256]{2,1,0:T(8,128)(2,1)}, bf16[10,160,256]{2,1,0:T(8,128)(2,1)S(1)}, u32[]{:S(2)}, u32[]{:S(2)}) collective-permute-start(bf16[10,160,256]{2,1,0:T(8,128)(2,1)} %shard_map.82.own_ref), channel_id=1, source_target_pairs={{4,12},{12,20},{20,28},{5,13},{13,21},{21,29},{6,14},{14,22},{22,3... | collective-permute-start | bytes 2457608 | tf_op jit(solution)/shard_map/ppermute | solution.py:206
  32.1 14.9 %collective-permute-start.5 = (bf16[10,160,256]{2,1,0:T(8,128)(2,1)}, bf16[10,160,256]{2,1,0:T(8,128)(2,1)S(1)}, u32[]{:S(2)}, u32[]{:S(2)}) collective-permute-start(bf16[10,160,256]{2,1,0:T(8,128)(2,1)} %shard_map.82.own_ref), channel_id=1, source_target_pairs={{0,4},{4,0},{8,12},{12,8},{16,20},{20,16},{24,28},{28,24},{1,5},{5... | collective-permute-start | bytes 2457608 | tf_op jit(solution)/shard_map/ppermute | solution.py:194
  38.3 8.7 %collective-permute-start.2 = (bf16[10,160,256]{2,1,0:T(8,128)(2,1)}, bf16[10,160,256]{2,1,0:T(8,128)(2,1)S(1)}, u32[]{:S(2)}, u32[]{:S(2)}) collective-permute-start(bf16[10,160,256]{2,1,0:T(8,128)(2,1)} %shard_map.82.own_ref), channel_id=1, source_target_pairs={{0,8},{16,24},{1,9},{17,25},{2,10},{18,26},{3,11},{19,27}} | collective-permute-start | bytes 2457608 | tf_op jit(solution)/shard_map/ppermute | solution.py:206
  43.6 20.4 %copy-start = (bf16[10,160,256]{2,1,0:T(8,128)(2,1)}, bf16[10,160,256]{2,1,0:T(8,128)(2,1)S(1)}, u32[]{:S(2)}) copy-start(bf16[10,160,256]{2,1,0:T(8,128)(2,1)S(1)} %collective-permute-done.8.fao_ref) | copy-start | bytes 2457604
  43.6 18.4 %collective-permute-start.10 = (bf16[10,160,256]{2,1,0:T(8,128)(2,1)S(1)}, bf16[10,160,256]{2,1,0:T(8,128)(2,1)S(1)}, u32[]{:S(2)}, u32[]{:S(2)}) collective-permute-start(bf16[10,160,256]{2,1,0:T(8,128)(2,1)S(1)} %collective-permute-done.9), channel_id=1, source_target_pairs={{24,16},{4,12},{25,17},{5,13},{26,18},{6,14},{27,19},{7,15}} | collective-permute-start | bytes 2457608 | tf_op jit(solution)/shard_map/ppermute | solution.py:199
  45.0 19.1 %copy-start.1 = (bf16[10,160,256]{2,1,0:T(8,128)(2,1)}, bf16[10,160,256]{2,1,0:T(8,128)(2,1)S(1)}, u32[]{:S(2)}) copy-start(bf16[10,160,256]{2,1,0:T(8,128)(2,1)S(1)} %collective-permute-done.6.fae_ref) | copy-start | bytes 2457604
  45.0 17.0 %collective-permute-start.7 = (bf16[10,160,256]{2,1,0:T(8,128)(2,1)S(1)}, bf16[10,160,256]{2,1,0:T(8,128)(2,1)S(1)}, u32[]{:S(2)}, u32[]{:S(2)}) collective-permute-start(bf16[10,160,256]{2,1,0:T(8,128)(2,1)S(1)} %collective-permute-done.6.fae_ref), channel_id=1, source_target_pairs={{0,4},{8,12},{16,20},{1,5},{9,13},{17,21},{2,6},{10,14},{18,22},{3... | collective-permute-start | bytes 2457608 | tf_op jit(solution)/shard_map/ppermute | solution.py:213
  46.3 17.8 %copy-start.2 = (bf16[10,160,256]{2,1,0:T(8,128)(2,1)}, bf16[10,160,256]{2,1,0:T(8,128)(2,1)S(1)}, u32[]{:S(2)}) copy-start(bf16[10,160,256]{2,1,0:T(8,128)(2,1)S(1)} %collective-permute-done.3.fbo_ref) | copy-start | bytes 2457604
  46.3 15.7 %collective-permute-start.4 = (bf16[10,160,256]{2,1,0:T(8,128)(2,1)S(1)}, bf16[10,160,256]{2,1,0:T(8,128)(2,1)S(1)}, u32[]{:S(2)}, u32[]{:S(2)}) collective-permute-start(bf16[10,160,256]{2,1,0:T(8,128)(2,1)S(1)} %collective-permute-done.3.fbo_ref), channel_id=1, source_target_pairs={{12,8},{20,16},{28,24},{13,9},{21,17},{29,25},{14,10},{22,18},{30,... | collective-permute-start | bytes 2457608 | tf_op jit(solution)/shard_map/ppermute | solution.py:212
  47.0 17.0 %copy-start.3 = (bf16[10,160,256]{2,1,0:T(8,128)(2,1)}, bf16[10,160,256]{2,1,0:T(8,128)(2,1)S(1)}, u32[]{:S(2)}) copy-start(bf16[10,160,256]{2,1,0:T(8,128)(2,1)S(1)} %collective-permute-done.5.par_ref) | copy-start | bytes 2457604
  47.1 15.0 %copy-start.4 = (bf16[10,160,256]{2,1,0:T(8,128)(2,1)}, bf16[10,160,256]{2,1,0:T(8,128)(2,1)S(1)}, u32[]{:S(2)}) copy-start(bf16[10,160,256]{2,1,0:T(8,128)(2,1)S(1)} %collective-permute-done.2.fbe_ref) | copy-start | bytes 2457604
  62.0 0.9 %copy-start.5 = (bf16[10,160,256]{2,1,0:T(8,128)(2,1)}, bf16[10,160,256]{2,1,0:T(8,128)(2,1)S(1)}, u32[]{:S(2)}) copy-start(bf16[10,160,256]{2,1,0:T(8,128)(2,1)S(1)} %collective-permute-done.10.routed_ref) | copy-start | bytes 2457604
  62.0 1.2 %copy-start.6 = (bf16[10,160,256]{2,1,0:T(8,128)(2,1)}, bf16[10,160,256]{2,1,0:T(8,128)(2,1)S(1)}, u32[]{:S(2)}) copy-start(bf16[10,160,256]{2,1,0:T(8,128)(2,1)S(1)} %collective-permute-done.7.ra_ref) | copy-start | bytes 2457604
  63.2 0.9 %copy-start.7 = (bf16[10,160,256]{2,1,0:T(8,128)(2,1)}, bf16[10,160,256]{2,1,0:T(8,128)(2,1)S(1)}, u32[]{:S(2)}) copy-start(bf16[10,160,256]{2,1,0:T(8,128)(2,1)S(1)} %collective-permute-done.4.rb_ref) | copy-start | bytes 2457604

commit v13 on v11

--- a/solution.py
+++ b/solution.py
@@ -46,7 +46,7 @@
 
 def layers_kernel(bounds_ref, above_ref, image_ref, below_ref, w1_ref, w2_ref, out_ref, xbuf,
                   first_buf, stack):
-    halo = below_ref.shape[0] - 1
+    halo = below_ref.shape[0]
     block = image_ref.shape[0]
     xbuf[0:halo] = above_ref[0:halo]
     xbuf[halo : halo + block] = image_ref[...]
@@ -68,11 +68,10 @@
 
 def mix_kernel(coef_ref, fb_ref, rb_ref, own_ref, par_ref, ra_ref, fa_ref, routed_ref,
                above_ref, frame_ref, below_ref, w3_ref, out_ref, fbuf, mixed_buf, stack):
-    halo = below_ref.shape[0] - 1
     block = frame_ref.shape[0]
-    fbuf[0:1] = above_ref[halo : halo + 1]
+    fbuf[0:1] = above_ref[...]
     fbuf[1 : block + 1] = frame_ref[...]
-    fbuf[block + 1 :] = below_ref[halo : halo + 1]
+    fbuf[block + 1 :] = below_ref[...]
     f32 = jnp.float32
     step = stack.shape[0]
     for r0 in range(0, block + 2, step):
@@ -107,7 +106,7 @@
 
 def layers(bounds, above, image, below, w1, w2):
     block, cols, c = image.shape
-    halo = below.shape[0] - 1
+    halo = below.shape[0]
     rows = block + 2 * halo
     flops = 2 * 9 * c * c * cols * (2 * rows - 6)
     return pl.pallas_call(
@@ -155,10 +154,10 @@
     height = block * lax.axis_size("rows")
     row0 = lax.axis_index("rows") * block
 
-    down = jnp.concatenate([image[block - 3 :], frame[block - 1 :]], axis=0)
-    up = jnp.concatenate([image[:3], frame[:1]], axis=0)
-    from_above = shifted(down, "rows", 1)
-    from_below = shifted(up, "rows", -1)
+    image_above = shifted(image[block - 3 :], "rows", 1)
+    image_below = shifted(image[:3], "rows", -1)
+    frame_above = shifted(frame[block - 1 :], "rows", 1)
+    frame_below = shifted(frame[:1], "rows", -1)
 
     count = lax.axis_size("tm")
     t = lax.axis_index("tm")
@@ -176,7 +175,7 @@
     bounds = jnp.stack([2 - row0, height - row0 + 2]).astype(jnp.int32)
     coef, bounds, image = lax.optimization_barrier((coef, bounds, image))
 
-    second = layers(bounds, from_above, image, from_below, conv_first, conv_second)
+    second = layers(bounds, image_above, image, image_below, conv_first, conv_second)
 
     partner = lax.ppermute(second, "tm", [(i, i ^ 1) for i in range(count)])
     if count == 8:
@@ -191,7 +190,7 @@
     relay_behind = lax.ppermute(from_behind, "tm", [(i + 1, i) for i in range(2, count, 2)])
     relay_ahead = lax.ppermute(from_ahead, "tm", [(i, i + 1) for i in range(0, count - 2, 2)])
     result = mix(coef, from_behind, relay_behind, second, partner, relay_ahead, from_ahead, routed,
-                 from_above, frame, from_below, conv_frame)
+                 frame_above, frame, frame_below, conv_frame)
     return result[None]
 
 

time: 71.4 us -> 82.8 us (1.16)
  waiting for transfers between devices: 31.9 us -> 36.7 us
  starting transfers between devices: 13.7 us -> 18.4 us
  local copies, waits for them, and re-layouts: 4.42 us -> 6.03 us
    ppermute x2 -> x4, waiting for transfers between devices: 1.56 us -> 9.08 us  [shifted(): return lax.ppermute(value, axis, pairs)]
    ppermute x2 -> x4, starting transfers between devices: 5.84 us -> 10.1 us  [shifted(): return lax.ppermute(value, axis, pairs)]
    ppermute x1, waiting for transfers between devices: 2.86 us -> 0.01 us  [shards(): lax.ppermute(from_behind, 'tm', [(i + 1, i) for i in range(2, count, 2)])]
    unnamed x18 -> x20, local copies, waits for them, and re-layouts: 1.65 us -> 3.27 us
  transfers between devices with their start and end apart: 9 -> 11, of which waited for: 5 -> 5; matrix products, arithmetic and copies ran while one was open for 5% -> 6% of each run, Pallas kernels for 0% -> 0%
where the time goes in v13:
time: 82.8 us; the launch traced here: 82.3 us
  waiting for transfers between devices  36.7 us (44%)
  starting transfers between devices  18.4 us (22%)
  Pallas kernels  13.9 us (17%)
  local copies, waits for them, and re-layouts  6.03 us (7%)
  between operations  4.05 us (5%)
  other arithmetic  3.21 us (4%)
    ppermute x1, waiting for transfers between devices, shards(): lax.ppermute(second, 'tm', [(0, 2), (1, 3), (3, 5), (4, 6), (5, 7)])  12.1 us
    ppermute x4, starting transfers between devices, shifted(): return lax.ppermute(value, axis, pairs)  10.1 us
    ppermute x1, waiting for transfers between devices, shards(): hop = lax.ppermute(second, 'tm', [(2, 6), (5, 1)])  9.4 us
    ppermute x4, waiting for transfers between devices, shifted(): return lax.ppermute(value, axis, pairs)  9.08 us
    pallas_call x1, Pallas kernels, layers(): pl.pallas_call(layers_kernel, out_shape=jax.ShapeDtypeStruct((rows - 4, c...  7.6 us
    pallas_call x1, Pallas kernels, mix(): pl.pallas_call(mix_kernel, out_shape=jax.ShapeDtypeStruct((block, cols, c...  6.32 us
    ppermute x1, waiting for transfers between devices, shards(): lax.ppermute(second, 'tm', [(2, 0), (3, 1), (4, 2), (6, 4), (7, 5)])  6.09 us
    unnamed x20, local copies, waits for them, and re-layouts  3.27 us
  transfers between devices with their start and end apart: 11, of which 5 were waited for; matrix products, arithmetic and copies ran while one was open for 6% of the time, Pallas kernels for 0%

profile of v13, /device:TPU:22, one launch (start us, length us, event | category | flops | bytes accessed | tf_op | source)
XLA Modules:
  0.0 82.3 jit_solution(9514192755721568215)
XLA Ops:
  0.0 1.1 %slice_bitcast_fusion = (bf16[3,160,256]{2,1,0:T(8,128)(2,1)S(1)}, bf16[3,160,256]{2,1,0:T(8,128)(2,1)S(1)}) fusion(bf16[1,8,160,256]{3,2,1,0:T(8,128)(2,1)} %param.8), kind=kLoop, calls=%fused_computation | loop fusion | bytes 983040 | tf_op jit(solution)/shard_map/slice | solution.py:158
  1.1 2.4 %collective-permute-start.1 = (bf16[3,160,256]{2,1,0:T(8,128)(2,1)S(1)}, bf16[3,160,256]{2,1,0:T(8,128)(2,1)S(1)}, u32[]{:S(2)}, u32[]{:S(2)}) collective-permute-start(bf16[3,160,256]{2,1,0:T(8,128)(2,1)S(1)} %get-tuple-element.15), channel_id=1, source_target_pairs={{1,0},{2,1},{3,2},{5,4},{6,5},{7,6},{9,8},{10,9},{11,10},{13,12},{... | collective-permute-start | bytes 737288 | tf_op jit(solution)/shard_map/ppermute | solution.py:16
  3.5 3.5 %collective-permute-start = (bf16[3,160,256]{2,1,0:T(8,128)(2,1)S(1)}, bf16[3,160,256]{2,1,0:T(8,128)(2,1)S(1)}, u32[]{:S(2)}, u32[]{:S(2)}) collective-permute-start(bf16[3,160,256]{2,1,0:T(8,128)(2,1)S(1)} %get-tuple-element.16), channel_id=1, source_target_pairs={{0,1},{1,2},{2,3},{4,5},{5,6},{6,7},{8,9},{9,10},{10,11},{12,13},{... | collective-permute-start | bytes 737288 | tf_op jit(solution)/shard_map/ppermute | solution.py:16
  8.3 1.3 %fusion = (f32[]{:T(128)}, f32[5]{0:T(128)S(1)}) fusion(s32[1,5]{1,0:T(1,128)} %param.12, s32[]{:T(128)} %bitcast.26, s32[]{:T(128)} %bitcast.25, s32[]{:T(128)S(6)} %axis_index.23), kind=kLoop, calls=%fused_computation.8 | loop fusion | flops 39 | bytes 56 | tf_op jit(solution)/shard_map/reduce_sum | solution.py:170
  9.6 0.6 broadcast_divide_fusion
  10.2 0.7 fusion.1
  10.9 0.1 slice.45
  13.5 0.6 pad_add_fusion.bounds_ref
  14.1 0.6 pad_maximum_fusion.coef_ref
  14.8 0.0 collective-permute-done.1.below_ref
  14.8 0.0 copy-start.8
  14.8 0.0 collective-permute-done.above_ref
  14.8 0.7 copy-done.8
  15.5 0.0 copy-start.9
  15.5 0.7 copy-done.9
  16.2 7.6 %shard_map.82.own_ref = bf16[10,160,256]{2,1,0:T(8,128)(2,1)} custom-call(s32[2]{0:T(128)} %pad_add_fusion.bounds_ref, bf16[3,160,256]{2,1,0:T(8,128)(2,1)} %copy-done.9, bf16[8,160,256]{2,1,0:T(8,128)(2,1)} %bitcast.28, bf16[3,160,256]{2,1,0:T(8,128)(2,1)} %copy-done.8, bf16[3,3,256,256]{3,2,1,0:T(8,128)(2,1)} %w1_ref.1, bf16[3,3,256,256]{3,2,1,0:T(8,128)(2,1)} %w2_ref.1), custom_call_target="tpu_custom_call" | custom-call | flops 4152360960 | bytes 4653056 | tf_op jit(solution)/shard_map/pallas_call | solution.py:112
  23.8 1.3 %collective-permute-start.7 = (bf16[10,160,256]{2,1,0:T(8,128)(2,1)}, bf16[10,160,256]{2,1,0:T(8,128)(2,1)S(1)}, u32[]{:S(2)}, u32[]{:S(2)}) collective-permute-start(bf16[10,160,256]{2,1,0:T(8,128)(2,1)} %shard_map.82.own_ref), channel_id=1, source_target_pairs={{8,24},{20,4},{9,25},{21,5},{10,26},{22,6},{11,27},{23,7}} | collective-permute-start | bytes 2457608 | tf_op jit(solution)/shard_map/ppermute | solution.py:184
  25.1 1.9 %collective-permute-start.5 = (bf16[10,160,256]{2,1,0:T(8,128)(2,1)}, bf16[10,160,256]{2,1,0:T(8,128)(2,1)S(1)}, u32[]{:S(2)}, u32[]{:S(2)}) collective-permute-start(bf16[10,160,256]{2,1,0:T(8,128)(2,1)} %shard_map.82.own_ref), channel_id=1, source_target_pairs={{8,0},{12,4},{16,8},{24,16},{28,20},{9,1},{13,5},{17,9},{25,17},{2... | collective-permute-start | bytes 2457608 | tf_op jit(solution)/shard_map/ppermute | solution.py:183
  27.0 1.3 %collective-permute-start.2 = (bf16[10,160,256]{2,1,0:T(8,128)(2,1)}, bf16[10,160,256]{2,1,0:T(8,128)(2,1)S(1)}, u32[]{:S(2)}, u32[]{:S(2)}) collective-permute-start(bf16[10,160,256]{2,1,0:T(8,128)(2,1)} %shard_map.82.own_ref), channel_id=1, source_target_pairs={{0,8},{4,12},{12,20},{16,24},{20,28},{1,9},{5,13},{13,21},{17,25},... | collective-permute-start | bytes 2457608 | tf_op jit(solution)/shard_map/ppermute | solution.py:182
  28.3 0.5 collective-permute-start.4
  28.8 9.4 %collective-permute-done.7 = bf16[10,160,256]{2,1,0:T(8,128)(2,1)S(1)} collective-permute-done((bf16[10,160,256]{2,1,0:T(8,128)(2,1)}, bf16[10,160,256]{2,1,0:T(8,128)(2,1)S(1)}, u32[]{:S(2)}, u32[]{:S(2)}) %collective-permute-start.7) | collective-permute-done | bytes 819232 | tf_op jit(solution)/shard_map/ppermute | solution.py:184
  38.2 1.3 %collective-permute-start.8 = (bf16[10,160,256]{2,1,0:T(8,128)(2,1)S(1)}, bf16[10,160,256]{2,1,0:T(8,128)(2,1)S(1)}, u32[]{:S(2)}, u32[]{:S(2)}) collective-permute-start(bf16[10,160,256]{2,1,0:T(8,128)(2,1)S(1)} %collective-permute-done.7), channel_id=1, source_target_pairs={{24,16},{4,12},{25,17},{5,13},{26,18},{6,14},{27,19},{7,15}} | collective-permute-start | bytes 2457608 | tf_op jit(solution)/shard_map/ppermute | solution.py:185
  39.6 6.1 %collective-permute-done.5.fa_ref = bf16[10,160,256]{2,1,0:T(8,128)(2,1)S(1)} collective-permute-done((bf16[10,160,256]{2,1,0:T(8,128)(2,1)}, bf16[10,160,256]{2,1,0:T(8,128)(2,1)S(1)}, u32[]{:S(2)}, u32[]{:S(2)}) %collective-permute-start.5) | collective-permute-done | bytes 819232 | tf_op jit(solution)/shard_map/ppermute | solution.py:183
  45.6 0.0 copy-start
  45.6 0.7 collective-permute-start.6
  46.4 12.1 %collective-permute-done.2.fb_ref = bf16[10,160,256]{2,1,0:T(8,128)(2,1)S(1)} collective-permute-done((bf16[10,160,256]{2,1,0:T(8,128)(2,1)}, bf16[10,160,256]{2,1,0:T(8,128)(2,1)S(1)}, u32[]{:S(2)}, u32[]{:S(2)}) %collective-permute-start.2) | collective-permute-done | bytes 819232 | tf_op jit(solution)/shard_map/ppermute | solution.py:182
  58.5 0.0 copy-start.1
  58.5 1.3 %collective-permute-start.3 = (bf16[10,160,256]{2,1,0:T(8,128)(2,1)S(1)}, bf16[10,160,256]{2,1,0:T(8,128)(2,1)S(1)}, u32[]{:S(2)}, u32[]{:S(2)}) collective-permute-start(bf16[10,160,256]{2,1,0:T(8,128)(2,1)S(1)} %collective-permute-done.2.fb_ref), channel_id=1, source_target_pairs={{12,8},{20,16},{28,24},{13,9},{21,17},{29,25},{14,10},{22,18},{30,... | collective-permute-start | bytes 2457608 | tf_op jit(solution)/shard_map/ppermute | solution.py:190
  59.8 0.9 %slice_bitcast_fusion.2 = (bf16[1,160,256]{2,1,0:T(8,128)(2,1)S(1)}, bf16[1,160,256]{2,1,0:T(8,128)(2,1)S(1)}) fusion(bf16[1,8,160,256]{3,2,1,0:T(8,128)(2,1)} %param.9), kind=kLoop, calls=%fused_computation.2 | loop fusion | bytes 327680 | tf_op jit(solution)/shard_map/slice | solution.py:160
  60.7 2.3 %collective-permute-start.10 = (bf16[1,160,256]{2,1,0:T(8,128)(2,1)S(1)}, bf16[1,160,256]{2,1,0:T(8,128)(2,1)S(1)}, u32[]{:S(2)}, u32[]{:S(2)}) collective-permute-start(bf16[1,160,256]{2,1,0:T(8,128)(2,1)S(1)} %get-tuple-element.13), channel_id=1, source_target_pairs={{1,0},{2,1},{3,2},{5,4},{6,5},{7,6},{9,8},{10,9},{11,10},{13,12},{... | collective-permute-start | bytes 245768 | tf_op jit(solution)/shard_map/ppermute | solution.py:16
  63.1 4.6 %collective-permute-done.10.below_ref = bf16[1,160,256]{2,1,0:T(8,128)(2,1)S(1)} collective-permute-done((bf16[1,160,256]{2,1,0:T(8,128)(2,1)S(1)}, bf16[1,160,256]{2,1,0:T(8,128)(2,1)S(1)}, u32[]{:S(2)}, u32[]{:S(2)}) %collective-permute-start.10) | collective-permute-done | bytes 81952 | tf_op jit(solution)/shard_map/ppermute | solution.py:16
  67.7 1.9 %collective-permute-start.9 = (bf16[1,160,256]{2,1,0:T(8,128)(2,1)S(1)}, bf16[1,160,256]{2,1,0:T(8,128)(2,1)S(1)}, u32[]{:S(2)}, u32[]{:S(2)}) collective-permute-start(bf16[1,160,256]{2,1,0:T(8,128)(2,1)S(1)} %get-tuple-element.14), channel_id=1, source_target_pairs={{0,1},{1,2},{2,3},{4,5},{5,6},{6,7},{8,9},{9,10},{10,11},{12,13},{... | collective-permute-start | bytes 245768 | tf_op jit(solution)/shard_map/ppermute | solution.py:16
  69.6 4.4 %collective-permute-done.9.above_ref = bf16[1,160,256]{2,1,0:T(8,128)(2,1)S(1)} collective-permute-done((bf16[1,160,256]{2,1,0:T(8,128)(2,1)S(1)}, bf16[1,160,256]{2,1,0:T(8,128)(2,1)S(1)}, u32[]{:S(2)}, u32[]{:S(2)}) %collective-permute-start.9) | collective-permute-done | bytes 81952 | tf_op jit(solution)/shard_map/ppermute | solution.py:16
  74.1 0.0 collective-permute-done.4.par_ref
  74.1 0.0 collective-permute-done.8.routed_ref
  74.1 0.0 copy-start.3
  74.1 0.0 collective-permute-done.6.ra_ref
  74.1 0.0 copy-start.4
  74.1 0.0 collective-permute-done.3.rb_ref
  74.1 1.0 %copy-done.4 = bf16[10,160,256]{2,1,0:T(8,128)(2,1)} copy-done((bf16[10,160,256]{2,1,0:T(8,128)(2,1)}, bf16[10,160,256]{2,1,0:T(8,128)(2,1)S(1)}, u32[]{:S(2)}) %copy-start.4) | copy-done | bytes 819224
  75.1 0.9 %copy-done.5 = bf16[10,160,256]{2,1,0:T(8,128)(2,1)} copy-done((bf16[10,160,256]{2,1,0:T(8,128)(2,1)}, bf16[10,160,256]{2,1,0:T(8,128)(2,1)S(1)}, u32[]{:S(2)}) %copy-start.5) | copy-done | bytes 819224
  76.0 0.0 copy-done
  76.0 0.0 copy-done.1
  76.0 0.0 copy-done.6
  76.0 0.0 copy-done.7
  76.0 0.0 copy-done.2
  76.0 0.0 copy-done.3
  76.0 6.3 %shard_map.83 = bf16[8,160,256]{2,1,0:T(8,128)(2,1)} custom-call(f32[7]{0:T(128)} %pad_maximum_fusion.coef_ref, bf16[10,160,256]{2,1,0:T(8,128)(2,1)} %copy-done.1, bf16[10,160,256]{2,1,0:T(8,128)(2,1)} %copy-done.5, bf16[10,160,256]{2,1,0:T(8,128)(2,1)} %shard_map.82.own_ref, bf16[10,160,256]{2,1,0:T(8,128)(2,1)} %copy-done.2, ...), custom_call_target="tpu_custom_call" | custom-call | flops 1509949440 | bytes 8552448 | tf_op jit(solution)/shard_map/pallas_call | solution.py:128
  (4 shorter events, 0.0 us)
Async XLA Ops:
  1.1 13.7 %collective-permute-start.1 = (bf16[3,160,256]{2,1,0:T(8,128)(2,1)S(1)}, bf16[3,160,256]{2,1,0:T(8,128)(2,1)S(1)}, u32[]{:S(2)}, u32[]{:S(2)}) collective-permute-start(bf16[3,160,256]{2,1,0:T(8,128)(2,1)S(1)} %get-tuple-element.15), channel_id=1, source_target_pairs={{1,0},{2,1},{3,2},{5,4},{6,5},{7,6},{9,8},{10,9},{11,10},{13,12},{... | collective-permute-start | bytes 737288 | tf_op jit(solution)/shard_map/ppermute | solution.py:16
  3.5 11.3 %collective-permute-start = (bf16[3,160,256]{2,1,0:T(8,128)(2,1)S(1)}, bf16[3,160,256]{2,1,0:T(8,128)(2,1)S(1)}, u32[]{:S(2)}, u32[]{:S(2)}) collective-permute-start(bf16[3,160,256]{2,1,0:T(8,128)(2,1)S(1)} %get-tuple-element.16), channel_id=1, source_target_pairs={{0,1},{1,2},{2,3},{4,5},{5,6},{6,7},{8,9},{9,10},{10,11},{12,13},{... | collective-permute-start | bytes 737288 | tf_op jit(solution)/shard_map/ppermute | solution.py:16
  14.8 0.7 copy-start.8
  15.5 0.7 copy-start.9
  23.8 14.4 %collective-permute-start.7 = (bf16[10,160,256]{2,1,0:T(8,128)(2,1)}, bf16[10,160,256]{2,1,0:T(8,128)(2,1)S(1)}, u32[]{:S(2)}, u32[]{:S(2)}) collective-permute-start(bf16[10,160,256]{2,1,0:T(8,128)(2,1)} %shard_map.82.own_ref), channel_id=1, source_target_pairs={{8,24},{20,4},{9,25},{21,5},{10,26},{22,6},{11,27},{23,7}} | collective-permute-start | bytes 2457608 | tf_op jit(solution)/shard_map/ppermute | solution.py:184
  25.1 20.6 %collective-permute-start.5 = (bf16[10,160,256]{2,1,0:T(8,128)(2,1)}, bf16[10,160,256]{2,1,0:T(8,128)(2,1)S(1)}, u32[]{:S(2)}, u32[]{:S(2)}) collective-permute-start(bf16[10,160,256]{2,1,0:T(8,128)(2,1)} %shard_map.82.own_ref), channel_id=1, source_target_pairs={{8,0},{12,4},{16,8},{24,16},{28,20},{9,1},{13,5},{17,9},{25,17},{2... | collective-permute-start | bytes 2457608 | tf_op jit(solution)/shard_map/ppermute | solution.py:183
  27.0 31.5 %collective-permute-start.2 = (bf16[10,160,256]{2,1,0:T(8,128)(2,1)}, bf16[10,160,256]{2,1,0:T(8,128)(2,1)S(1)}, u32[]{:S(2)}, u32[]{:S(2)}) collective-permute-start(bf16[10,160,256]{2,1,0:T(8,128)(2,1)} %shard_map.82.own_ref), channel_id=1, source_target_pairs={{0,8},{4,12},{12,20},{16,24},{20,28},{1,9},{5,13},{13,21},{17,25},... | collective-permute-start | bytes 2457608 | tf_op jit(solution)/shard_map/ppermute | solution.py:182
  28.3 45.8 %collective-permute-start.4 = (bf16[10,160,256]{2,1,0:T(8,128)(2,1)}, bf16[10,160,256]{2,1,0:T(8,128)(2,1)S(1)}, u32[]{:S(2)}, u32[]{:S(2)}) collective-permute-start(bf16[10,160,256]{2,1,0:T(8,128)(2,1)} %shard_map.82.own_ref), channel_id=1, source_target_pairs={{0,4},{4,0},{8,12},{12,8},{16,20},{20,16},{24,28},{28,24},{1,5},{5... | collective-permute-start | bytes 2457608 | tf_op jit(solution)/shard_map/ppermute | solution.py:180
  38.2 35.9 %collective-permute-start.8 = (bf16[10,160,256]{2,1,0:T(8,128)(2,1)S(1)}, bf16[10,160,256]{2,1,0:T(8,128)(2,1)S(1)}, u32[]{:S(2)}, u32[]{:S(2)}) collective-permute-start(bf16[10,160,256]{2,1,0:T(8,128)(2,1)S(1)} %collective-permute-done.7), channel_id=1, source_target_pairs={{24,16},{4,12},{25,17},{5,13},{26,18},{6,14},{27,19},{7,15}} | collective-permute-start | bytes 2457608 | tf_op jit(solution)/shard_map/ppermute | solution.py:185
  45.6 30.4 %copy-start = (bf16[10,160,256]{2,1,0:T(8,128)(2,1)}, bf16[10,160,256]{2,1,0:T(8,128)(2,1)S(1)}, u32[]{:S(2)}) copy-start(bf16[10,160,256]{2,1,0:T(8,128)(2,1)S(1)} %collective-permute-done.5.fa_ref) | copy-start | bytes 2457604
  45.6 28.4 %collective-permute-start.6 = (bf16[10,160,256]{2,1,0:T(8,128)(2,1)S(1)}, bf16[10,160,256]{2,1,0:T(8,128)(2,1)S(1)}, u32[]{:S(2)}, u32[]{:S(2)}) collective-permute-start(bf16[10,160,256]{2,1,0:T(8,128)(2,1)S(1)} %collective-permute-done.5.fa_ref), channel_id=1, source_target_pairs={{0,4},{8,12},{16,20},{1,5},{9,13},{17,21},{2,6},{10,14},{18,22},{3... | collective-permute-start | bytes 2457608 | tf_op jit(solution)/shard_map/ppermute | solution.py:191
  58.5 17.5 %copy-start.1 = (bf16[10,160,256]{2,1,0:T(8,128)(2,1)}, bf16[10,160,256]{2,1,0:T(8,128)(2,1)S(1)}, u32[]{:S(2)}) copy-start(bf16[10,160,256]{2,1,0:T(8,128)(2,1)S(1)} %collective-permute-done.2.fb_ref) | copy-start | bytes 2457604
  58.5 15.6 %collective-permute-start.3 = (bf16[10,160,256]{2,1,0:T(8,128)(2,1)S(1)}, bf16[10,160,256]{2,1,0:T(8,128)(2,1)S(1)}, u32[]{:S(2)}, u32[]{:S(2)}) collective-permute-start(bf16[10,160,256]{2,1,0:T(8,128)(2,1)S(1)} %collective-permute-done.2.fb_ref), channel_id=1, source_target_pairs={{12,8},{20,16},{28,24},{13,9},{21,17},{29,25},{14,10},{22,18},{30,... | collective-permute-start | bytes 2457608 | tf_op jit(solution)/shard_map/ppermute | solution.py:190
  60.7 7.0 %collective-permute-start.10 = (bf16[1,160,256]{2,1,0:T(8,128)(2,1)S(1)}, bf16[1,160,256]{2,1,0:T(8,128)(2,1)S(1)}, u32[]{:S(2)}, u32[]{:S(2)}) collective-permute-start(bf16[1,160,256]{2,1,0:T(8,128)(2,1)S(1)} %get-tuple-element.13), channel_id=1, source_target_pairs={{1,0},{2,1},{3,2},{5,4},{6,5},{7,6},{9,8},{10,9},{11,10},{13,12},{... | collective-permute-start | bytes 245768 | tf_op jit(solution)/shard_map/ppermute | solution.py:16
  67.7 8.3 %copy-start.6 = (bf16[1,160,256]{2,1,0:T(8,128)(2,1)}, bf16[1,160,256]{2,1,0:T(8,128)(2,1)S(1)}, u32[]{:S(2)}) copy-start(bf16[1,160,256]{2,1,0:T(8,128)(2,1)S(1)} %collective-permute-done.10.below_ref) | copy-start | bytes 245764
  67.7 6.3 %collective-permute-start.9 = (bf16[1,160,256]{2,1,0:T(8,128)(2,1)S(1)}, bf16[1,160,256]{2,1,0:T(8,128)(2,1)S(1)}, u32[]{:S(2)}, u32[]{:S(2)}) collective-permute-start(bf16[1,160,256]{2,1,0:T(8,128)(2,1)S(1)} %get-tuple-element.14), channel_id=1, source_target_pairs={{0,1},{1,2},{2,3},{4,5},{5,6},{6,7},{8,9},{9,10},{10,11},{12,13},{... | collective-permute-start | bytes 245768 | tf_op jit(solution)/shard_map/ppermute | solution.py:16
  74.1 1.9 %copy-start.7 = (bf16[1,160,256]{2,1,0:T(8,128)(2,1)}, bf16[1,160,256]{2,1,0:T(8,128)(2,1)S(1)}, u32[]{:S(2)}) copy-start(bf16[1,160,256]{2,1,0:T(8,128)(2,1)S(1)} %collective-permute-done.9.above_ref) | copy-start | bytes 245764
  74.1 1.9 %copy-start.2 = (bf16[10,160,256]{2,1,0:T(8,128)(2,1)}, bf16[10,160,256]{2,1,0:T(8,128)(2,1)S(1)}, u32[]{:S(2)}) copy-start(bf16[10,160,256]{2,1,0:T(8,128)(2,1)S(1)} %collective-permute-done.4.par_ref) | copy-start | bytes 2457604
  74.1 1.9 %copy-start.3 = (bf16[10,160,256]{2,1,0:T(8,128)(2,1)}, bf16[10,160,256]{2,1,0:T(8,128)(2,1)S(1)}, u32[]{:S(2)}) copy-start(bf16[10,160,256]{2,1,0:T(8,128)(2,1)S(1)} %collective-permute-done.8.routed_ref) | copy-start | bytes 2457604
  74.1 1.0 %copy-start.4 = (bf16[10,160,256]{2,1,0:T(8,128)(2,1)}, bf16[10,160,256]{2,1,0:T(8,128)(2,1)S(1)}, u32[]{:S(2)}) copy-start(bf16[10,160,256]{2,1,0:T(8,128)(2,1)S(1)} %collective-permute-done.6.ra_ref) | copy-start | bytes 2457604
  75.1 0.9 %copy-start.5 = (bf16[10,160,256]{2,1,0:T(8,128)(2,1)}, bf16[10,160,256]{2,1,0:T(8,128)(2,1)S(1)}, u32[]{:S(2)}) copy-start(bf16[10,160,256]{2,1,0:T(8,128)(2,1)S(1)} %collective-permute-done.3.rb_ref) | copy-start | bytes 2457604

commit v14 on v11

--- a/solution.py
+++ b/solution.py
@@ -21,27 +21,28 @@
     return v * (0.5 * (1.0 + jnp.tanh(c * (v + 0.044715 * (v * v * v)))))
 
 
+def conv_chunk(src_ref, w_ref, stack, r0, n, emit):
+    cols, cin = src_ref.shape[1], src_ref.shape[2]
+    cout = w_ref.shape[3]
+    m = n * cols
+    for a in range(3):
+        stack[0:n, :, a * cin : (a + 1) * cin] = src_ref[r0 + a : r0 + a + n]
+    lhs = stack[0:n].reshape(m, 3 * cin)
+    taps = [
+        jnp.dot(lhs, w_ref[:, b].reshape(3 * cin, cout), preferred_element_type=jnp.float32)
+        for b in range(3)
+    ]
+    col = lax.broadcasted_iota(jnp.int32, (n, cols, cout), 1).reshape(m, cout)
+    left = pltpu.roll(taps[0], shift=1, axis=0)
+    right = pltpu.roll(taps[2], shift=m - 1, axis=0)
+    out = taps[1] + jnp.where(col == 0, 0.0, left) + jnp.where(col == cols - 1, 0.0, right)
+    emit(r0, n, out.reshape(n, cols, cout))
+
+
 def conv_rows(src_ref, w_ref, stack, rows_out, emit):
     chunk = stack.shape[0]
-    cols, cin = src_ref.shape[1], src_ref.shape[2]
-    cout = w_ref.shape[3]
-    r0 = 0
-    while r0 < rows_out:
-        n = min(chunk, rows_out - r0)
-        m = n * cols
-        for a in range(3):
-            stack[0:n, :, a * cin : (a + 1) * cin] = src_ref[r0 + a : r0 + a + n]
-        lhs = stack[0:n].reshape(m, 3 * cin)
-        taps = [
-            jnp.dot(lhs, w_ref[:, b].reshape(3 * cin, cout), preferred_element_type=jnp.float32)
-            for b in range(3)
-        ]
-        col = lax.broadcasted_iota(jnp.int32, (n, cols, cout), 1).reshape(m, cout)
-        left = pltpu.roll(taps[0], shift=1, axis=0)
-        right = pltpu.roll(taps[2], shift=m - 1, axis=0)
-        out = taps[1] + jnp.where(col == 0, 0.0, left) + jnp.where(col == cols - 1, 0.0, right)
-        emit(r0, n, out.reshape(n, cols, cout))
-        r0 += n
+    for r0 in range(0, rows_out, chunk):
+        conv_chunk(src_ref, w_ref, stack, r0, min(chunk, rows_out - r0), emit)
 
 
 def layers_kernel(bounds_ref, above_ref, image_ref, below_ref, w1_ref, w2_ref, out_ref, xbuf,
@@ -75,8 +76,9 @@
     fbuf[block + 1 :] = below_ref[halo : halo + 1]
     f32 = jnp.float32
     step = stack.shape[0]
-    for r0 in range(0, block + 2, step):
-        rows = pl.ds(r0, min(step, block + 2 - r0))
+
+    def join(r0, n):
+        rows = pl.ds(r0, n)
         summed = (
             coef_ref[0] * fb_ref[rows].astype(f32)
             + coef_ref[1] * rb_ref[rows].astype(f32)
@@ -91,7 +93,17 @@
     def emit(r0, n, value):
         out_ref[r0 : r0 + n] = value.astype(jnp.bfloat16)
 
-    conv_rows(mixed_buf, w3_ref, stack, block, emit)
+    join(0, 2)
+    done = 2
+    r0 = 0
+    while r0 < block:
+        n = min(step, block - r0)
+        need = r0 + n + 2
+        if need > done:
+            join(done, need - done)
+            done = need
+        conv_chunk(mixed_buf, w3_ref, stack, r0, n, emit)
+        r0 += n
 
 
 def vmem():

time: 71.4 us -> 71.4 us (level)
  no operation moved by 1% of the time
where the time goes in v14:
time: 71.4 us; the launch traced here: 70.7 us
  waiting for transfers between devices  31.9 us (45%)
  Pallas kernels  14.1 us (20%)
  starting transfers between devices  13.7 us (19%)
  local copies, waits for them, and re-layouts  4.42 us (6%)
  between operations  4.02 us (6%)
  other arithmetic  2.62 us (4%)
    ppermute x1, waiting for transfers between devices, shards(): lax.ppermute(second, 'tm', [(0, 2), (1, 3), (3, 5), (4, 6), (5, 7)])  12.1 us
    ppermute x1, waiting for transfers between devices, shards(): hop = lax.ppermute(second, 'tm', [(2, 6), (5, 1)])  9.85 us
    pallas_call x1, Pallas kernels, layers(): pl.pallas_call(layers_kernel, out_shape=jax.ShapeDtypeStruct((rows - 4, c...  7.64 us
    pallas_call x1, Pallas kernels, mix(): pl.pallas_call(mix_kernel, out_shape=jax.ShapeDtypeStruct((block, cols, c...  6.46 us
    ppermute x2, starting transfers between devices, shifted(): return lax.ppermute(value, axis, pairs)  5.84 us
    ppermute x1, waiting for transfers between devices, shards(): lax.ppermute(second, 'tm', [(2, 0), (3, 1), (4, 2), (6, 4), (7, 5)])  5.46 us
    ppermute x1, waiting for transfers between devices, shards(): lax.ppermute(from_behind, 'tm', [(i + 1, i) for i in range(2, count, 2)])  2.86 us
    slice x2, local copies, waits for them, and re-layouts, shards(): up = jnp.concatenate([image[:3], frame[:1]], axis=0)  2.04 us
  transfers between devices with their start and end apart: 9, of which 5 were waited for; matrix products, arithmetic and copies ran while one was open for 5% of the time, Pallas kernels for 0%

profile of v14, /device:TPU:22, one launch (start us, length us, event | category | flops | bytes accessed | tf_op | source)
XLA Modules:
  0.0 70.7 jit_solution(16434557358598752595)
XLA Ops:
  0.0 0.9 %slice_bitcast_fusion.2 = (bf16[1,160,256]{2,1,0:T(8,128)(2,1)S(1)}, bf16[1,160,256]{2,1,0:T(8,128)(2,1)S(1)}) fusion(bf16[1,8,160,256]{3,2,1,0:T(8,128)(2,1)} %param.9), kind=kLoop, calls=%fused_computation.4 | loop fusion | bytes 327680 | tf_op jit(solution)/shard_map/slice | solution.py:171
  0.9 0.0 copy-start.8
  1.0 1.1 %slice_bitcast_fusion = (bf16[3,160,256]{2,1,0:T(8,128)(2,1)S(1)}, bf16[3,160,256]{2,1,0:T(8,128)(2,1)S(1)}) fusion(bf16[1,8,160,256]{3,2,1,0:T(8,128)(2,1)} %param.8), kind=kLoop, calls=%fused_computation.2 | loop fusion | bytes 983040 | tf_op jit(solution)/shard_map/slice | solution.py:171
  2.1 3.5 %collective-permute-start = (bf16[4,160,256]{2,1,0:T(8,128)(2,1)S(1)}, bf16[4,160,256]{2,1,0:T(8,128)(2,1)S(1)}, u32[]{:S(2)}, u32[]{:S(2)}) collective-permute-start(bf16[4,160,256]{2,1,0:T(8,128)(2,1)S(1)} %pad_maximum_fusion), channel_id=1, source_target_pairs={{0,1},{1,2},{2,3},{4,5},{5,6},{6,7},{8,9},{9,10},{10,11},{12,13},{... | collective-permute-start | bytes 983048 | tf_op jit(solution)/shard_map/ppermute | solution.py:16
  5.6 2.4 %collective-permute-start.1 = (bf16[4,160,256]{2,1,0:T(8,128)(2,1)S(1)}, bf16[4,160,256]{2,1,0:T(8,128)(2,1)S(1)}, u32[]{:S(2)}, u32[]{:S(2)}) collective-permute-start(bf16[4,160,256]{2,1,0:T(8,128)(2,1)S(1)} %pad_maximum_fusion.1), channel_id=1, source_target_pairs={{1,0},{2,1},{3,2},{5,4},{6,5},{7,6},{9,8},{10,9},{11,10},{13,12},{... | collective-permute-start | bytes 983048 | tf_op jit(solution)/shard_map/ppermute | solution.py:16
  9.3 0.0 copy-done.8
  9.3 0.6 fusion
  10.0 0.6 broadcast_divide_fusion
  10.6 0.1 slice.45
  10.7 0.7 fusion.1
  13.8 0.6 pad_add_fusion.bounds_ref
  14.5 0.6 pad_maximum_fusion.2.coef_ref
  15.1 0.0 collective-permute-done.above_ref
  15.1 0.0 copy-start.6
  15.1 1.6 %collective-permute-done.1.below_ref = bf16[4,160,256]{2,1,0:T(8,128)(2,1)S(1)} collective-permute-done((bf16[4,160,256]{2,1,0:T(8,128)(2,1)S(1)}, bf16[4,160,256]{2,1,0:T(8,128)(2,1)S(1)}, u32[]{:S(2)}, u32[]{:S(2)}) %collective-permute-start.1) | collective-permute-done | bytes 327712 | tf_op jit(solution)/shard_map/ppermute | solution.py:16
  16.7 0.0 copy-done.6
  16.7 0.0 copy-start.7
  16.7 0.7 %copy-done.7 = bf16[4,160,256]{2,1,0:T(8,128)(2,1)} copy-done((bf16[4,160,256]{2,1,0:T(8,128)(2,1)}, bf16[4,160,256]{2,1,0:T(8,128)(2,1)S(1)}, u32[]{:S(2)}) %copy-start.7) | copy-done | bytes 327704
  17.4 7.6 %shard_map.82.own_ref = bf16[10,160,256]{2,1,0:T(8,128)(2,1)} custom-call(s32[2]{0:T(128)} %pad_add_fusion.bounds_ref, bf16[4,160,256]{2,1,0:T(8,128)(2,1)} %copy-done.6, bf16[8,160,256]{2,1,0:T(8,128)(2,1)} %bitcast.28, bf16[4,160,256]{2,1,0:T(8,128)(2,1)} %copy-done.7, bf16[3,3,256,256]{3,2,1,0:T(8,128)(2,1)} %w1_ref.1, bf16[3,3,256,256]{3,2,1,0:T(8,128)(2,1)} %w2_ref.1), custom_call_target="tpu_custom_call" | custom-call | flops 4152360960 | bytes 4653056 | tf_op jit(solution)/shard_map/pallas_call | solution.py:125
  25.1 1.3 %collective-permute-start.7 = (bf16[10,160,256]{2,1,0:T(8,128)(2,1)}, bf16[10,160,256]{2,1,0:T(8,128)(2,1)S(1)}, u32[]{:S(2)}, u32[]{:S(2)}) collective-permute-start(bf16[10,160,256]{2,1,0:T(8,128)(2,1)} %shard_map.82.own_ref), channel_id=1, source_target_pairs={{8,24},{20,4},{9,25},{21,5},{10,26},{22,6},{11,27},{23,7}} | collective-permute-start | bytes 2457608 | tf_op jit(solution)/shard_map/ppermute | solution.py:197
  26.4 1.9 %collective-permute-start.5 = (bf16[10,160,256]{2,1,0:T(8,128)(2,1)}, bf16[10,160,256]{2,1,0:T(8,128)(2,1)S(1)}, u32[]{:S(2)}, u32[]{:S(2)}) collective-permute-start(bf16[10,160,256]{2,1,0:T(8,128)(2,1)} %shard_map.82.own_ref), channel_id=1, source_target_pairs={{8,0},{12,4},{16,8},{24,16},{28,20},{9,1},{13,5},{17,9},{25,17},{2... | collective-permute-start | bytes 2457608 | tf_op jit(solution)/shard_map/ppermute | solution.py:196
  28.3 1.3 %collective-permute-start.2 = (bf16[10,160,256]{2,1,0:T(8,128)(2,1)}, bf16[10,160,256]{2,1,0:T(8,128)(2,1)S(1)}, u32[]{:S(2)}, u32[]{:S(2)}) collective-permute-start(bf16[10,160,256]{2,1,0:T(8,128)(2,1)} %shard_map.82.own_ref), channel_id=1, source_target_pairs={{0,8},{4,12},{12,20},{16,24},{20,28},{1,9},{5,13},{13,21},{17,25},... | collective-permute-start | bytes 2457608 | tf_op jit(solution)/shard_map/ppermute | solution.py:195
  29.6 0.1 collective-permute-start.4
  29.7 9.8 %collective-permute-done.7 = bf16[10,160,256]{2,1,0:T(8,128)(2,1)S(1)} collective-permute-done((bf16[10,160,256]{2,1,0:T(8,128)(2,1)}, bf16[10,160,256]{2,1,0:T(8,128)(2,1)S(1)}, u32[]{:S(2)}, u32[]{:S(2)}) %collective-permute-start.7) | collective-permute-done | bytes 819232 | tf_op jit(solution)/shard_map/ppermute | solution.py:197
  39.5 1.3 %collective-permute-start.8 = (bf16[10,160,256]{2,1,0:T(8,128)(2,1)S(1)}, bf16[10,160,256]{2,1,0:T(8,128)(2,1)S(1)}, u32[]{:S(2)}, u32[]{:S(2)}) collective-permute-start(bf16[10,160,256]{2,1,0:T(8,128)(2,1)S(1)} %collective-permute-done.7), channel_id=1, source_target_pairs={{24,16},{4,12},{25,17},{5,13},{26,18},{6,14},{27,19},{7,15}} | collective-permute-start | bytes 2457608 | tf_op jit(solution)/shard_map/ppermute | solution.py:198
  40.8 5.5 %collective-permute-done.5.fa_ref = bf16[10,160,256]{2,1,0:T(8,128)(2,1)S(1)} collective-permute-done((bf16[10,160,256]{2,1,0:T(8,128)(2,1)}, bf16[10,160,256]{2,1,0:T(8,128)(2,1)S(1)}, u32[]{:S(2)}, u32[]{:S(2)}) %collective-permute-start.5) | collective-permute-done | bytes 819232 | tf_op jit(solution)/shard_map/ppermute | solution.py:196
  46.3 0.0 copy-start
  46.3 0.7 collective-permute-start.6
  47.0 12.1 %collective-permute-done.2.fb_ref = bf16[10,160,256]{2,1,0:T(8,128)(2,1)S(1)} collective-permute-done((bf16[10,160,256]{2,1,0:T(8,128)(2,1)}, bf16[10,160,256]{2,1,0:T(8,128)(2,1)S(1)}, u32[]{:S(2)}, u32[]{:S(2)}) %collective-permute-start.2) | collective-permute-done | bytes 819232 | tf_op jit(solution)/shard_map/ppermute | solution.py:195
  59.1 0.0 copy-start.1
  59.1 1.3 %collective-permute-start.3 = (bf16[10,160,256]{2,1,0:T(8,128)(2,1)S(1)}, bf16[10,160,256]{2,1,0:T(8,128)(2,1)S(1)}, u32[]{:S(2)}, u32[]{:S(2)}) collective-permute-start(bf16[10,160,256]{2,1,0:T(8,128)(2,1)S(1)} %collective-permute-done.2.fb_ref), channel_id=1, source_target_pairs={{12,8},{20,16},{28,24},{13,9},{21,17},{29,25},{14,10},{22,18},{30,... | collective-permute-start | bytes 2457608 | tf_op jit(solution)/shard_map/ppermute | solution.py:203
  60.4 0.0 collective-permute-done.4.par_ref
  60.4 0.0 copy-start.2
  60.4 0.0 collective-permute-done.8.routed_ref
  60.5 0.0 copy-start.3
  60.5 0.0 collective-permute-done.6.ra_ref
  60.5 0.0 copy-start.4
  60.5 2.9 %collective-permute-done.3.rb_ref = bf16[10,160,256]{2,1,0:T(8,128)(2,1)S(1)} collective-permute-done((bf16[10,160,256]{2,1,0:T(8,128)(2,1)S(1)}, bf16[10,160,256]{2,1,0:T(8,128)(2,1)S(1)}, u32[]{:S(2)}, u32[]{:S(2)}) %collective-permute-start.3) | collective-permute-done | bytes 819232 | tf_op jit(solution)/shard_map/ppermute | solution.py:203
  63.4 0.0 copy-done.4
  63.4 0.0 copy-start.5
  63.4 0.9 %copy-done.5 = bf16[10,160,256]{2,1,0:T(8,128)(2,1)} copy-done((bf16[10,160,256]{2,1,0:T(8,128)(2,1)}, bf16[10,160,256]{2,1,0:T(8,128)(2,1)S(1)}, u32[]{:S(2)}) %copy-start.5) | copy-done | bytes 819224
  64.3 0.0 copy-done
  64.3 0.0 copy-done.1
  64.3 0.0 copy-done.2
  64.3 0.0 copy-done.3
  64.3 6.5 %shard_map.83 = bf16[8,160,256]{2,1,0:T(8,128)(2,1)} custom-call(f32[7]{0:T(128)} %pad_maximum_fusion.2.coef_ref, bf16[10,160,256]{2,1,0:T(8,128)(2,1)} %copy-done.1, bf16[10,160,256]{2,1,0:T(8,128)(2,1)} %copy-done.5, bf16[10,160,256]{2,1,0:T(8,128)(2,1)} %shard_map.82.own_ref, bf16[10,160,256]{2,1,0:T(8,128)(2,1)} %copy-done.2, ...), custom_call_target="tpu_custom_call" | custom-call | flops 1509949440 | bytes 8552448 | tf_op jit(solution)/shard_map/pallas_call | solution.py:141
  (2 shorter events, 0.1 us)
Async XLA Ops:
  0.9 8.4 %copy-start.8 = (s32[1,5]{1,0:T(1,128)S(1)}, s32[1,5]{1,0:T(1,128)}, u32[]{:S(2)}) copy-start(s32[1,5]{1,0:T(1,128)} %param.12) | copy-start | bytes 64
  2.1 13.0 %collective-permute-start = (bf16[4,160,256]{2,1,0:T(8,128)(2,1)S(1)}, bf16[4,160,256]{2,1,0:T(8,128)(2,1)S(1)}, u32[]{:S(2)}, u32[]{:S(2)}) collective-permute-start(bf16[4,160,256]{2,1,0:T(8,128)(2,1)S(1)} %pad_maximum_fusion), channel_id=1, source_target_pairs={{0,1},{1,2},{2,3},{4,5},{5,6},{6,7},{8,9},{9,10},{10,11},{12,13},{... | collective-permute-start | bytes 983048 | tf_op jit(solution)/shard_map/ppermute | solution.py:16
  5.6 11.1 %collective-permute-start.1 = (bf16[4,160,256]{2,1,0:T(8,128)(2,1)S(1)}, bf16[4,160,256]{2,1,0:T(8,128)(2,1)S(1)}, u32[]{:S(2)}, u32[]{:S(2)}) collective-permute-start(bf16[4,160,256]{2,1,0:T(8,128)(2,1)S(1)} %pad_maximum_fusion.1), channel_id=1, source_target_pairs={{1,0},{2,1},{3,2},{5,4},{6,5},{7,6},{9,8},{10,9},{11,10},{13,12},{... | collective-permute-start | bytes 983048 | tf_op jit(solution)/shard_map/ppermute | solution.py:16
  15.1 1.6 %copy-start.6 = (bf16[4,160,256]{2,1,0:T(8,128)(2,1)}, bf16[4,160,256]{2,1,0:T(8,128)(2,1)S(1)}, u32[]{:S(2)}) copy-start(bf16[4,160,256]{2,1,0:T(8,128)(2,1)S(1)} %collective-permute-done.above_ref) | copy-start | bytes 983044
  16.7 0.7 %copy-start.7 = (bf16[4,160,256]{2,1,0:T(8,128)(2,1)}, bf16[4,160,256]{2,1,0:T(8,128)(2,1)S(1)}, u32[]{:S(2)}) copy-start(bf16[4,160,256]{2,1,0:T(8,128)(2,1)S(1)} %collective-permute-done.1.below_ref) | copy-start | bytes 983044
  25.1 14.4 %collective-permute-start.7 = (bf16[10,160,256]{2,1,0:T(8,128)(2,1)}, bf16[10,160,256]{2,1,0:T(8,128)(2,1)S(1)}, u32[]{:S(2)}, u32[]{:S(2)}) collective-permute-start(bf16[10,160,256]{2,1,0:T(8,128)(2,1)} %shard_map.82.own_ref), channel_id=1, source_target_pairs={{8,24},{20,4},{9,25},{21,5},{10,26},{22,6},{11,27},{23,7}} | collective-permute-start | bytes 2457608 | tf_op jit(solution)/shard_map/ppermute | solution.py:197
  26.4 19.9 %collective-permute-start.5 = (bf16[10,160,256]{2,1,0:T(8,128)(2,1)}, bf16[10,160,256]{2,1,0:T(8,128)(2,1)S(1)}, u32[]{:S(2)}, u32[]{:S(2)}) collective-permute-start(bf16[10,160,256]{2,1,0:T(8,128)(2,1)} %shard_map.82.own_ref), channel_id=1, source_target_pairs={{8,0},{12,4},{16,8},{24,16},{28,20},{9,1},{13,5},{17,9},{25,17},{2... | collective-permute-start | bytes 2457608 | tf_op jit(solution)/shard_map/ppermute | solution.py:196
  28.3 30.9 %collective-permute-start.2 = (bf16[10,160,256]{2,1,0:T(8,128)(2,1)}, bf16[10,160,256]{2,1,0:T(8,128)(2,1)S(1)}, u32[]{:S(2)}, u32[]{:S(2)}) collective-permute-start(bf16[10,160,256]{2,1,0:T(8,128)(2,1)} %shard_map.82.own_ref), channel_id=1, source_target_pairs={{0,8},{4,12},{12,20},{16,24},{20,28},{1,9},{5,13},{13,21},{17,25},... | collective-permute-start | bytes 2457608 | tf_op jit(solution)/shard_map/ppermute | solution.py:195
  29.6 30.9 %collective-permute-start.4 = (bf16[10,160,256]{2,1,0:T(8,128)(2,1)}, bf16[10,160,256]{2,1,0:T(8,128)(2,1)S(1)}, u32[]{:S(2)}, u32[]{:S(2)}) collective-permute-start(bf16[10,160,256]{2,1,0:T(8,128)(2,1)} %shard_map.82.own_ref), channel_id=1, source_target_pairs={{0,4},{4,0},{8,12},{12,8},{16,20},{20,16},{24,28},{28,24},{1,5},{5... | collective-permute-start | bytes 2457608 | tf_op jit(solution)/shard_map/ppermute | solution.py:193
  39.5 20.9 %collective-permute-start.8 = (bf16[10,160,256]{2,1,0:T(8,128)(2,1)S(1)}, bf16[10,160,256]{2,1,0:T(8,128)(2,1)S(1)}, u32[]{:S(2)}, u32[]{:S(2)}) collective-permute-start(bf16[10,160,256]{2,1,0:T(8,128)(2,1)S(1)} %collective-permute-done.7), channel_id=1, source_target_pairs={{24,16},{4,12},{25,17},{5,13},{26,18},{6,14},{27,19},{7,15}} | collective-permute-start | bytes 2457608 | tf_op jit(solution)/shard_map/ppermute | solution.py:198
  46.3 18.0 %copy-start = (bf16[10,160,256]{2,1,0:T(8,128)(2,1)}, bf16[10,160,256]{2,1,0:T(8,128)(2,1)S(1)}, u32[]{:S(2)}) copy-start(bf16[10,160,256]{2,1,0:T(8,128)(2,1)S(1)} %collective-permute-done.5.fa_ref) | copy-start | bytes 2457604
  46.3 14.2 %collective-permute-start.6 = (bf16[10,160,256]{2,1,0:T(8,128)(2,1)S(1)}, bf16[10,160,256]{2,1,0:T(8,128)(2,1)S(1)}, u32[]{:S(2)}, u32[]{:S(2)}) collective-permute-start(bf16[10,160,256]{2,1,0:T(8,128)(2,1)S(1)} %collective-permute-done.5.fa_ref), channel_id=1, source_target_pairs={{0,4},{8,12},{16,20},{1,5},{9,13},{17,21},{2,6},{10,14},{18,22},{3... | collective-permute-start | bytes 2457608 | tf_op jit(solution)/shard_map/ppermute | solution.py:204
  59.1 5.1 %copy-start.1 = (bf16[10,160,256]{2,1,0:T(8,128)(2,1)}, bf16[10,160,256]{2,1,0:T(8,128)(2,1)S(1)}, u32[]{:S(2)}) copy-start(bf16[10,160,256]{2,1,0:T(8,128)(2,1)S(1)} %collective-permute-done.2.fb_ref) | copy-start | bytes 2457604
  59.1 4.2 %collective-permute-start.3 = (bf16[10,160,256]{2,1,0:T(8,128)(2,1)S(1)}, bf16[10,160,256]{2,1,0:T(8,128)(2,1)S(1)}, u32[]{:S(2)}, u32[]{:S(2)}) collective-permute-start(bf16[10,160,256]{2,1,0:T(8,128)(2,1)S(1)} %collective-permute-done.2.fb_ref), channel_id=1, source_target_pairs={{12,8},{20,16},{28,24},{13,9},{21,17},{29,25},{14,10},{22,18},{30,... | collective-permute-start | bytes 2457608 | tf_op jit(solution)/shard_map/ppermute | solution.py:203
  60.4 3.8 %copy-start.2 = (bf16[10,160,256]{2,1,0:T(8,128)(2,1)}, bf16[10,160,256]{2,1,0:T(8,128)(2,1)S(1)}, u32[]{:S(2)}) copy-start(bf16[10,160,256]{2,1,0:T(8,128)(2,1)S(1)} %collective-permute-done.4.par_ref) | copy-start | bytes 2457604
  60.5 3.8 %copy-start.3 = (bf16[10,160,256]{2,1,0:T(8,128)(2,1)}, bf16[10,160,256]{2,1,0:T(8,128)(2,1)S(1)}, u32[]{:S(2)}) copy-start(bf16[10,160,256]{2,1,0:T(8,128)(2,1)S(1)} %collective-permute-done.8.routed_ref) | copy-start | bytes 2457604
  60.5 2.9 %copy-start.4 = (bf16[10,160,256]{2,1,0:T(8,128)(2,1)}, bf16[10,160,256]{2,1,0:T(8,128)(2,1)S(1)}, u32[]{:S(2)}) copy-start(bf16[10,160,256]{2,1,0:T(8,128)(2,1)S(1)} %collective-permute-done.6.ra_ref) | copy-start | bytes 2457604
  63.4 0.9 %copy-start.5 = (bf16[10,160,256]{2,1,0:T(8,128)(2,1)}, bf16[10,160,256]{2,1,0:T(8,128)(2,1)S(1)}, u32[]{:S(2)}) copy-start(bf16[10,160,256]{2,1,0:T(8,128)(2,1)S(1)} %collective-permute-done.3.rb_ref) | copy-start | bytes 2457604

commit v15 on v14

--- a/solution.py
+++ b/solution.py
@@ -79,16 +79,17 @@
 
     def join(r0, n):
         rows = pl.ds(r0, n)
+        bf = jnp.bfloat16
         summed = (
-            coef_ref[0] * fb_ref[rows].astype(f32)
-            + coef_ref[1] * rb_ref[rows].astype(f32)
-            + coef_ref[2] * own_ref[rows].astype(f32)
-            + coef_ref[3] * par_ref[rows].astype(f32)
-            + coef_ref[4] * ra_ref[rows].astype(f32)
-            + coef_ref[5] * fa_ref[rows].astype(f32)
-            + coef_ref[6] * routed_ref[rows].astype(f32)
+            coef_ref[0].astype(bf) * fb_ref[rows]
+            + coef_ref[1].astype(bf) * rb_ref[rows]
+            + coef_ref[2].astype(bf) * own_ref[rows]
+            + coef_ref[3].astype(bf) * par_ref[rows]
+            + coef_ref[4].astype(bf) * ra_ref[rows]
+            + coef_ref[5].astype(bf) * fa_ref[rows]
+            + coef_ref[6].astype(bf) * routed_ref[rows]
         )
-        mixed_buf[rows] = (summed * fbuf[rows].astype(f32)).astype(jnp.bfloat16)
+        mixed_buf[rows] = summed * fbuf[rows]
 
     def emit(r0, n, value):
         out_ref[r0 : r0 + n] = value.astype(jnp.bfloat16)

time: 71.4 us -> 71 us (level)
  no operation moved by 1% of the time
where the time goes in v15:
time: 71 us; the launch traced here: 70.3 us
  waiting for transfers between devices  31.9 us (45%)
  starting transfers between devices  13.7 us (19%)
  Pallas kernels  13.6 us (19%)
  local copies, waits for them, and re-layouts  4.42 us (6%)
  between operations  4.02 us (6%)
  other arithmetic  2.62 us (4%)
    ppermute x1, waiting for transfers between devices, shards(): lax.ppermute(second, 'tm', [(0, 2), (1, 3), (3, 5), (4, 6), (5, 7)])  12.1 us
    ppermute x1, waiting for transfers between devices, shards(): hop = lax.ppermute(second, 'tm', [(2, 6), (5, 1)])  9.85 us
    pallas_call x1, Pallas kernels, layers(): pl.pallas_call(layers_kernel, out_shape=jax.ShapeDtypeStruct((rows - 4, c...  7.64 us
    pallas_call x1, Pallas kernels, mix(): pl.pallas_call(mix_kernel, out_shape=jax.ShapeDtypeStruct((block, cols, c...  6.01 us
    ppermute x2, starting transfers between devices, shifted(): return lax.ppermute(value, axis, pairs)  5.84 us
    ppermute x1, waiting for transfers between devices, shards(): lax.ppermute(second, 'tm', [(2, 0), (3, 1), (4, 2), (6, 4), (7, 5)])  5.46 us
    ppermute x1, waiting for transfers between devices, shards(): lax.ppermute(from_behind, 'tm', [(i + 1, i) for i in range(2, count, 2)])  2.86 us
    slice x2, local copies, waits for them, and re-layouts, shards(): up = jnp.concatenate([image[:3], frame[:1]], axis=0)  2.04 us
  transfers between devices with their start and end apart: 9, of which 5 were waited for; matrix products, arithmetic and copies ran while one was open for 5% of the time, Pallas kernels for 0%

profile of v15, /device:TPU:22, one launch (start us, length us, event | category | flops | bytes accessed | tf_op | source)
XLA Modules:
  0.0 70.3 jit_solution(6843421368883232932)
XLA Ops:
  0.0 0.9 %slice_bitcast_fusion.2 = (bf16[1,160,256]{2,1,0:T(8,128)(2,1)S(1)}, bf16[1,160,256]{2,1,0:T(8,128)(2,1)S(1)}) fusion(bf16[1,8,160,256]{3,2,1,0:T(8,128)(2,1)} %param.9), kind=kLoop, calls=%fused_computation.4 | loop fusion | bytes 327680 | tf_op jit(solution)/shard_map/slice | solution.py:172
  0.9 0.0 copy-start.8
  1.0 1.1 %slice_bitcast_fusion = (bf16[3,160,256]{2,1,0:T(8,128)(2,1)S(1)}, bf16[3,160,256]{2,1,0:T(8,128)(2,1)S(1)}) fusion(bf16[1,8,160,256]{3,2,1,0:T(8,128)(2,1)} %param.8), kind=kLoop, calls=%fused_computation.2 | loop fusion | bytes 983040 | tf_op jit(solution)/shard_map/slice | solution.py:172
  2.1 3.5 %collective-permute-start = (bf16[4,160,256]{2,1,0:T(8,128)(2,1)S(1)}, bf16[4,160,256]{2,1,0:T(8,128)(2,1)S(1)}, u32[]{:S(2)}, u32[]{:S(2)}) collective-permute-start(bf16[4,160,256]{2,1,0:T(8,128)(2,1)S(1)} %pad_maximum_fusion), channel_id=1, source_target_pairs={{0,1},{1,2},{2,3},{4,5},{5,6},{6,7},{8,9},{9,10},{10,11},{12,13},{... | collective-permute-start | bytes 983048 | tf_op jit(solution)/shard_map/ppermute | solution.py:16
  5.6 2.4 %collective-permute-start.1 = (bf16[4,160,256]{2,1,0:T(8,128)(2,1)S(1)}, bf16[4,160,256]{2,1,0:T(8,128)(2,1)S(1)}, u32[]{:S(2)}, u32[]{:S(2)}) collective-permute-start(bf16[4,160,256]{2,1,0:T(8,128)(2,1)S(1)} %pad_maximum_fusion.1), channel_id=1, source_target_pairs={{1,0},{2,1},{3,2},{5,4},{6,5},{7,6},{9,8},{10,9},{11,10},{13,12},{... | collective-permute-start | bytes 983048 | tf_op jit(solution)/shard_map/ppermute | solution.py:16
  9.3 0.0 copy-done.8
  9.3 0.6 fusion
  10.0 0.6 broadcast_divide_fusion
  10.6 0.1 slice.45
  10.7 0.7 fusion.1
  13.8 0.6 pad_add_fusion.bounds_ref
  14.5 0.6 pad_maximum_fusion.2.coef_ref
  15.1 0.0 collective-permute-done.above_ref
  15.1 0.0 copy-start.6
  15.1 1.6 %collective-permute-done.1.below_ref = bf16[4,160,256]{2,1,0:T(8,128)(2,1)S(1)} collective-permute-done((bf16[4,160,256]{2,1,0:T(8,128)(2,1)S(1)}, bf16[4,160,256]{2,1,0:T(8,128)(2,1)S(1)}, u32[]{:S(2)}, u32[]{:S(2)}) %collective-permute-start.1) | collective-permute-done | bytes 327712 | tf_op jit(solution)/shard_map/ppermute | solution.py:16
  16.7 0.0 copy-done.6
  16.7 0.0 copy-start.7
  16.7 0.7 %copy-done.7 = bf16[4,160,256]{2,1,0:T(8,128)(2,1)} copy-done((bf16[4,160,256]{2,1,0:T(8,128)(2,1)}, bf16[4,160,256]{2,1,0:T(8,128)(2,1)S(1)}, u32[]{:S(2)}) %copy-start.7) | copy-done | bytes 327704
  17.4 7.6 %shard_map.82.own_ref = bf16[10,160,256]{2,1,0:T(8,128)(2,1)} custom-call(s32[2]{0:T(128)} %pad_add_fusion.bounds_ref, bf16[4,160,256]{2,1,0:T(8,128)(2,1)} %copy-done.6, bf16[8,160,256]{2,1,0:T(8,128)(2,1)} %bitcast.28, bf16[4,160,256]{2,1,0:T(8,128)(2,1)} %copy-done.7, bf16[3,3,256,256]{3,2,1,0:T(8,128)(2,1)} %w1_ref.1, bf16[3,3,256,256]{3,2,1,0:T(8,128)(2,1)} %w2_ref.1), custom_call_target="tpu_custom_call" | custom-call | flops 4152360960 | bytes 4653056 | tf_op jit(solution)/shard_map/pallas_call | solution.py:126
  25.1 1.3 %collective-permute-start.7 = (bf16[10,160,256]{2,1,0:T(8,128)(2,1)}, bf16[10,160,256]{2,1,0:T(8,128)(2,1)S(1)}, u32[]{:S(2)}, u32[]{:S(2)}) collective-permute-start(bf16[10,160,256]{2,1,0:T(8,128)(2,1)} %shard_map.82.own_ref), channel_id=1, source_target_pairs={{8,24},{20,4},{9,25},{21,5},{10,26},{22,6},{11,27},{23,7}} | collective-permute-start | bytes 2457608 | tf_op jit(solution)/shard_map/ppermute | solution.py:198
  26.4 1.9 %collective-permute-start.5 = (bf16[10,160,256]{2,1,0:T(8,128)(2,1)}, bf16[10,160,256]{2,1,0:T(8,128)(2,1)S(1)}, u32[]{:S(2)}, u32[]{:S(2)}) collective-permute-start(bf16[10,160,256]{2,1,0:T(8,128)(2,1)} %shard_map.82.own_ref), channel_id=1, source_target_pairs={{8,0},{12,4},{16,8},{24,16},{28,20},{9,1},{13,5},{17,9},{25,17},{2... | collective-permute-start | bytes 2457608 | tf_op jit(solution)/shard_map/ppermute | solution.py:197
  28.3 1.3 %collective-permute-start.2 = (bf16[10,160,256]{2,1,0:T(8,128)(2,1)}, bf16[10,160,256]{2,1,0:T(8,128)(2,1)S(1)}, u32[]{:S(2)}, u32[]{:S(2)}) collective-permute-start(bf16[10,160,256]{2,1,0:T(8,128)(2,1)} %shard_map.82.own_ref), channel_id=1, source_target_pairs={{0,8},{4,12},{12,20},{16,24},{20,28},{1,9},{5,13},{13,21},{17,25},... | collective-permute-start | bytes 2457608 | tf_op jit(solution)/shard_map/ppermute | solution.py:196
  29.6 0.1 collective-permute-start.4
  29.7 9.8 %collective-permute-done.7 = bf16[10,160,256]{2,1,0:T(8,128)(2,1)S(1)} collective-permute-done((bf16[10,160,256]{2,1,0:T(8,128)(2,1)}, bf16[10,160,256]{2,1,0:T(8,128)(2,1)S(1)}, u32[]{:S(2)}, u32[]{:S(2)}) %collective-permute-start.7) | collective-permute-done | bytes 819232 | tf_op jit(solution)/shard_map/ppermute | solution.py:198
  39.5 1.3 %collective-permute-start.8 = (bf16[10,160,256]{2,1,0:T(8,128)(2,1)S(1)}, bf16[10,160,256]{2,1,0:T(8,128)(2,1)S(1)}, u32[]{:S(2)}, u32[]{:S(2)}) collective-permute-start(bf16[10,160,256]{2,1,0:T(8,128)(2,1)S(1)} %collective-permute-done.7), channel_id=1, source_target_pairs={{24,16},{4,12},{25,17},{5,13},{26,18},{6,14},{27,19},{7,15}} | collective-permute-start | bytes 2457608 | tf_op jit(solution)/shard_map/ppermute | solution.py:199
  40.8 5.5 %collective-permute-done.5.fa_ref = bf16[10,160,256]{2,1,0:T(8,128)(2,1)S(1)} collective-permute-done((bf16[10,160,256]{2,1,0:T(8,128)(2,1)}, bf16[10,160,256]{2,1,0:T(8,128)(2,1)S(1)}, u32[]{:S(2)}, u32[]{:S(2)}) %collective-permute-start.5) | collective-permute-done | bytes 819232 | tf_op jit(solution)/shard_map/ppermute | solution.py:197
  46.3 0.0 copy-start
  46.3 0.7 collective-permute-start.6
  47.0 12.1 %collective-permute-done.2.fb_ref = bf16[10,160,256]{2,1,0:T(8,128)(2,1)S(1)} collective-permute-done((bf16[10,160,256]{2,1,0:T(8,128)(2,1)}, bf16[10,160,256]{2,1,0:T(8,128)(2,1)S(1)}, u32[]{:S(2)}, u32[]{:S(2)}) %collective-permute-start.2) | collective-permute-done | bytes 819232 | tf_op jit(solution)/shard_map/ppermute | solution.py:196
  59.1 0.0 copy-start.1
  59.1 1.3 %collective-permute-start.3 = (bf16[10,160,256]{2,1,0:T(8,128)(2,1)S(1)}, bf16[10,160,256]{2,1,0:T(8,128)(2,1)S(1)}, u32[]{:S(2)}, u32[]{:S(2)}) collective-permute-start(bf16[10,160,256]{2,1,0:T(8,128)(2,1)S(1)} %collective-permute-done.2.fb_ref), channel_id=1, source_target_pairs={{12,8},{20,16},{28,24},{13,9},{21,17},{29,25},{14,10},{22,18},{30,... | collective-permute-start | bytes 2457608 | tf_op jit(solution)/shard_map/ppermute | solution.py:204
  60.4 0.0 collective-permute-done.4.par_ref
  60.4 0.0 copy-start.2
  60.4 0.0 collective-permute-done.8.routed_ref
  60.5 0.0 copy-start.3
  60.5 0.0 collective-permute-done.6.ra_ref
  60.5 0.0 copy-start.4
  60.5 2.9 %collective-permute-done.3.rb_ref = bf16[10,160,256]{2,1,0:T(8,128)(2,1)S(1)} collective-permute-done((bf16[10,160,256]{2,1,0:T(8,128)(2,1)S(1)}, bf16[10,160,256]{2,1,0:T(8,128)(2,1)S(1)}, u32[]{:S(2)}, u32[]{:S(2)}) %collective-permute-start.3) | collective-permute-done | bytes 819232 | tf_op jit(solution)/shard_map/ppermute | solution.py:204
  63.4 0.0 copy-done.4
  63.4 0.0 copy-start.5
  63.4 0.9 %copy-done.5 = bf16[10,160,256]{2,1,0:T(8,128)(2,1)} copy-done((bf16[10,160,256]{2,1,0:T(8,128)(2,1)}, bf16[10,160,256]{2,1,0:T(8,128)(2,1)S(1)}, u32[]{:S(2)}) %copy-start.5) | copy-done | bytes 819224
  64.3 0.0 copy-done
  64.3 0.0 copy-done.1
  64.3 0.0 copy-done.2
  64.3 0.0 copy-done.3
  64.3 6.0 %shard_map.83 = bf16[8,160,256]{2,1,0:T(8,128)(2,1)} custom-call(f32[7]{0:T(128)} %pad_maximum_fusion.2.coef_ref, bf16[10,160,256]{2,1,0:T(8,128)(2,1)} %copy-done.1, bf16[10,160,256]{2,1,0:T(8,128)(2,1)} %copy-done.5, bf16[10,160,256]{2,1,0:T(8,128)(2,1)} %shard_map.82.own_ref, bf16[10,160,256]{2,1,0:T(8,128)(2,1)} %copy-done.2, ...), custom_call_target="tpu_custom_call" | custom-call | flops 1509949440 | bytes 8552448 | tf_op jit(solution)/shard_map/pallas_call | solution.py:142
  (2 shorter events, 0.1 us)
Async XLA Ops:
  0.9 8.4 %copy-start.8 = (s32[1,5]{1,0:T(1,128)S(1)}, s32[1,5]{1,0:T(1,128)}, u32[]{:S(2)}) copy-start(s32[1,5]{1,0:T(1,128)} %param.12) | copy-start | bytes 64
  2.1 13.0 %collective-permute-start = (bf16[4,160,256]{2,1,0:T(8,128)(2,1)S(1)}, bf16[4,160,256]{2,1,0:T(8,128)(2,1)S(1)}, u32[]{:S(2)}, u32[]{:S(2)}) collective-permute-start(bf16[4,160,256]{2,1,0:T(8,128)(2,1)S(1)} %pad_maximum_fusion), channel_id=1, source_target_pairs={{0,1},{1,2},{2,3},{4,5},{5,6},{6,7},{8,9},{9,10},{10,11},{12,13},{... | collective-permute-start | bytes 983048 | tf_op jit(solution)/shard_map/ppermute | solution.py:16
  5.6 11.1 %collective-permute-start.1 = (bf16[4,160,256]{2,1,0:T(8,128)(2,1)S(1)}, bf16[4,160,256]{2,1,0:T(8,128)(2,1)S(1)}, u32[]{:S(2)}, u32[]{:S(2)}) collective-permute-start(bf16[4,160,256]{2,1,0:T(8,128)(2,1)S(1)} %pad_maximum_fusion.1), channel_id=1, source_target_pairs={{1,0},{2,1},{3,2},{5,4},{6,5},{7,6},{9,8},{10,9},{11,10},{13,12},{... | collective-permute-start | bytes 983048 | tf_op jit(solution)/shard_map/ppermute | solution.py:16
  15.1 1.6 %copy-start.6 = (bf16[4,160,256]{2,1,0:T(8,128)(2,1)}, bf16[4,160,256]{2,1,0:T(8,128)(2,1)S(1)}, u32[]{:S(2)}) copy-start(bf16[4,160,256]{2,1,0:T(8,128)(2,1)S(1)} %collective-permute-done.above_ref) | copy-start | bytes 983044
  16.7 0.7 %copy-start.7 = (bf16[4,160,256]{2,1,0:T(8,128)(2,1)}, bf16[4,160,256]{2,1,0:T(8,128)(2,1)S(1)}, u32[]{:S(2)}) copy-start(bf16[4,160,256]{2,1,0:T(8,128)(2,1)S(1)} %collective-permute-done.1.below_ref) | copy-start | bytes 983044
  25.1 14.4 %collective-permute-start.7 = (bf16[10,160,256]{2,1,0:T(8,128)(2,1)}, bf16[10,160,256]{2,1,0:T(8,128)(2,1)S(1)}, u32[]{:S(2)}, u32[]{:S(2)}) collective-permute-start(bf16[10,160,256]{2,1,0:T(8,128)(2,1)} %shard_map.82.own_ref), channel_id=1, source_target_pairs={{8,24},{20,4},{9,25},{21,5},{10,26},{22,6},{11,27},{23,7}} | collective-permute-start | bytes 2457608 | tf_op jit(solution)/shard_map/ppermute | solution.py:198
  26.4 19.9 %collective-permute-start.5 = (bf16[10,160,256]{2,1,0:T(8,128)(2,1)}, bf16[10,160,256]{2,1,0:T(8,128)(2,1)S(1)}, u32[]{:S(2)}, u32[]{:S(2)}) collective-permute-start(bf16[10,160,256]{2,1,0:T(8,128)(2,1)} %shard_map.82.own_ref), channel_id=1, source_target_pairs={{8,0},{12,4},{16,8},{24,16},{28,20},{9,1},{13,5},{17,9},{25,17},{2... | collective-permute-start | bytes 2457608 | tf_op jit(solution)/shard_map/ppermute | solution.py:197
  28.3 30.9 %collective-permute-start.2 = (bf16[10,160,256]{2,1,0:T(8,128)(2,1)}, bf16[10,160,256]{2,1,0:T(8,128)(2,1)S(1)}, u32[]{:S(2)}, u32[]{:S(2)}) collective-permute-start(bf16[10,160,256]{2,1,0:T(8,128)(2,1)} %shard_map.82.own_ref), channel_id=1, source_target_pairs={{0,8},{4,12},{12,20},{16,24},{20,28},{1,9},{5,13},{13,21},{17,25},... | collective-permute-start | bytes 2457608 | tf_op jit(solution)/shard_map/ppermute | solution.py:196
  29.6 30.9 %collective-permute-start.4 = (bf16[10,160,256]{2,1,0:T(8,128)(2,1)}, bf16[10,160,256]{2,1,0:T(8,128)(2,1)S(1)}, u32[]{:S(2)}, u32[]{:S(2)}) collective-permute-start(bf16[10,160,256]{2,1,0:T(8,128)(2,1)} %shard_map.82.own_ref), channel_id=1, source_target_pairs={{0,4},{4,0},{8,12},{12,8},{16,20},{20,16},{24,28},{28,24},{1,5},{5... | collective-permute-start | bytes 2457608 | tf_op jit(solution)/shard_map/ppermute | solution.py:194
  39.5 20.9 %collective-permute-start.8 = (bf16[10,160,256]{2,1,0:T(8,128)(2,1)S(1)}, bf16[10,160,256]{2,1,0:T(8,128)(2,1)S(1)}, u32[]{:S(2)}, u32[]{:S(2)}) collective-permute-start(bf16[10,160,256]{2,1,0:T(8,128)(2,1)S(1)} %collective-permute-done.7), channel_id=1, source_target_pairs={{24,16},{4,12},{25,17},{5,13},{26,18},{6,14},{27,19},{7,15}} | collective-permute-start | bytes 2457608 | tf_op jit(solution)/shard_map/ppermute | solution.py:199
  46.3 18.0 %copy-start = (bf16[10,160,256]{2,1,0:T(8,128)(2,1)}, bf16[10,160,256]{2,1,0:T(8,128)(2,1)S(1)}, u32[]{:S(2)}) copy-start(bf16[10,160,256]{2,1,0:T(8,128)(2,1)S(1)} %collective-permute-done.5.fa_ref) | copy-start | bytes 2457604
  46.3 14.2 %collective-permute-start.6 = (bf16[10,160,256]{2,1,0:T(8,128)(2,1)S(1)}, bf16[10,160,256]{2,1,0:T(8,128)(2,1)S(1)}, u32[]{:S(2)}, u32[]{:S(2)}) collective-permute-start(bf16[10,160,256]{2,1,0:T(8,128)(2,1)S(1)} %collective-permute-done.5.fa_ref), channel_id=1, source_target_pairs={{0,4},{8,12},{16,20},{1,5},{9,13},{17,21},{2,6},{10,14},{18,22},{3... | collective-permute-start | bytes 2457608 | tf_op jit(solution)/shard_map/ppermute | solution.py:205
  59.1 5.1 %copy-start.1 = (bf16[10,160,256]{2,1,0:T(8,128)(2,1)}, bf16[10,160,256]{2,1,0:T(8,128)(2,1)S(1)}, u32[]{:S(2)}) copy-start(bf16[10,160,256]{2,1,0:T(8,128)(2,1)S(1)} %collective-permute-done.2.fb_ref) | copy-start | bytes 2457604
  59.1 4.2 %collective-permute-start.3 = (bf16[10,160,256]{2,1,0:T(8,128)(2,1)S(1)}, bf16[10,160,256]{2,1,0:T(8,128)(2,1)S(1)}, u32[]{:S(2)}, u32[]{:S(2)}) collective-permute-start(bf16[10,160,256]{2,1,0:T(8,128)(2,1)S(1)} %collective-permute-done.2.fb_ref), channel_id=1, source_target_pairs={{12,8},{20,16},{28,24},{13,9},{21,17},{29,25},{14,10},{22,18},{30,... | collective-permute-start | bytes 2457608 | tf_op jit(solution)/shard_map/ppermute | solution.py:204
  60.4 3.8 %copy-start.2 = (bf16[10,160,256]{2,1,0:T(8,128)(2,1)}, bf16[10,160,256]{2,1,0:T(8,128)(2,1)S(1)}, u32[]{:S(2)}) copy-start(bf16[10,160,256]{2,1,0:T(8,128)(2,1)S(1)} %collective-permute-done.4.par_ref) | copy-start | bytes 2457604
  60.5 3.8 %copy-start.3 = (bf16[10,160,256]{2,1,0:T(8,128)(2,1)}, bf16[10,160,256]{2,1,0:T(8,128)(2,1)S(1)}, u32[]{:S(2)}) copy-start(bf16[10,160,256]{2,1,0:T(8,128)(2,1)S(1)} %collective-permute-done.8.routed_ref) | copy-start | bytes 2457604
  60.5 2.9 %copy-start.4 = (bf16[10,160,256]{2,1,0:T(8,128)(2,1)}, bf16[10,160,256]{2,1,0:T(8,128)(2,1)S(1)}, u32[]{:S(2)}) copy-start(bf16[10,160,256]{2,1,0:T(8,128)(2,1)S(1)} %collective-permute-done.6.ra_ref) | copy-start | bytes 2457604
  63.4 0.9 %copy-start.5 = (bf16[10,160,256]{2,1,0:T(8,128)(2,1)}, bf16[10,160,256]{2,1,0:T(8,128)(2,1)S(1)}, u32[]{:S(2)}) copy-start(bf16[10,160,256]{2,1,0:T(8,128)(2,1)S(1)} %collective-permute-done.3.rb_ref) | copy-start | bytes 2457604

commit v16 on v14

--- a/solution.py
+++ b/solution.py
@@ -67,41 +67,59 @@
     conv_rows(first_buf, w2_ref, stack, rows1 - 2, emit_second)
 
 
-def mix_kernel(coef_ref, fb_ref, rb_ref, own_ref, par_ref, ra_ref, fa_ref, routed_ref,
-               above_ref, frame_ref, below_ref, w3_ref, out_ref, fbuf, mixed_buf, stack):
-    halo = below_ref.shape[0] - 1
-    block = frame_ref.shape[0]
-    fbuf[0:1] = above_ref[halo : halo + 1]
-    fbuf[1 : block + 1] = frame_ref[...]
-    fbuf[block + 1 :] = below_ref[halo : halo + 1]
+def mix_kernel(coef_ref, *refs):
+    (fb_hbm, rb_hbm, own_hbm, par_hbm, ra_hbm, fa_hbm, routed_hbm, above_hbm, frame_hbm, below_hbm,
+     w3_hbm, out_ref, fb_ref, rb_ref, own_ref, par_ref, ra_ref, fa_ref, routed_ref, fbuf, w3_ref,
+     mixed_buf, stack, sems) = refs
+    block = frame_hbm.shape[0]
+    rows = block + 2
+    split = rows // 2 + 1
+    slices = [(fb_hbm, fb_ref), (rb_hbm, rb_ref), (own_hbm, own_ref), (par_hbm, par_ref),
+              (ra_hbm, ra_ref), (fa_hbm, fa_ref), (routed_hbm, routed_ref)]
+    first = [pltpu.make_async_copy(w3_hbm, w3_ref, sems.at[0])]
+    for i, (src, dst) in enumerate(slices):
+        first.append(pltpu.make_async_copy(src.at[0:split], dst.at[0:split], sems.at[1 + i]))
+    halo = below_hbm.shape[0] - 1
+    first.append(pltpu.make_async_copy(above_hbm.at[halo : halo + 1], fbuf.at[0:1], sems.at[8]))
+    first.append(pltpu.make_async_copy(frame_hbm, fbuf.at[1 : block + 1], sems.at[9]))
+    first.append(pltpu.make_async_copy(below_hbm.at[halo : halo + 1], fbuf.at[block + 1 :], sems.at[10]))
+    second = [
+        pltpu.make_async_copy(src.at[split:rows], dst.at[split:rows], sems.at[11 + i])
+        for i, (src, dst) in enumerate(slices)
+    ]
+    for c in first + second:
+        c.start()
     f32 = jnp.float32
     step = stack.shape[0]
 
     def join(r0, n):
-        rows = pl.ds(r0, n)
+        part = pl.ds(r0, n)
         summed = (
-            coef_ref[0] * fb_ref[rows].astype(f32)
-            + coef_ref[1] * rb_ref[rows].astype(f32)
-            + coef_ref[2] * own_ref[rows].astype(f32)
-            + coef_ref[3] * par_ref[rows].astype(f32)
-            + coef_ref[4] * ra_ref[rows].astype(f32)
-            + coef_ref[5] * fa_ref[rows].astype(f32)
-            + coef_ref[6] * routed_ref[rows].astype(f32)
+            coef_ref[0] * fb_ref[part].astype(f32)
+            + coef_ref[1] * rb_ref[part].astype(f32)
+            + coef_ref[2] * own_ref[part].astype(f32)
+            + coef_ref[3] * par_ref[part].astype(f32)
+            + coef_ref[4] * ra_ref[part].astype(f32)
+            + coef_ref[5] * fa_ref[part].astype(f32)
+            + coef_ref[6] * routed_ref[part].astype(f32)
         )
-        mixed_buf[rows] = (summed * fbuf[rows].astype(f32)).astype(jnp.bfloat16)
+        mixed_buf[part] = (summed * fbuf[part].astype(f32)).astype(jnp.bfloat16)
 
     def emit(r0, n, value):
         out_ref[r0 : r0 + n] = value.astype(jnp.bfloat16)
 
-    join(0, 2)
-    done = 2
+    for c in first:
+        c.wait()
+    join(0, split)
     r0 = 0
+    while r0 + step + 2 <= split:
+        conv_chunk(mixed_buf, w3_ref, stack, r0, step, emit)
+        r0 += step
+    for c in second:
+        c.wait()
+    join(split, rows - split)
     while r0 < block:
         n = min(step, block - r0)
-        need = r0 + n + 2
-        if need > done:
-            join(done, need - done)
-            done = need
         conv_chunk(mixed_buf, w3_ref, stack, r0, n, emit)
         r0 += n
 
@@ -138,14 +156,20 @@
 def mix(coef, fb, rb, own, par, ra, fa, routed, above, frame, below, w3):
     block, cols, c = frame.shape
     flops = 2 * 9 * c * c * cols * block
+    hbm = pl.BlockSpec(memory_space=pl.ANY)
+    slab = pltpu.VMEM((block + 2, cols, c), jnp.bfloat16)
     return pl.pallas_call(
         mix_kernel,
         out_shape=jax.ShapeDtypeStruct((block, cols, c), jnp.bfloat16),
-        in_specs=[smem()] + [vmem()] * 11,
+        in_specs=[smem()] + [hbm] * 11,
         out_specs=vmem(),
-        scratch_shapes=[pltpu.VMEM((block + 2, cols, c), jnp.bfloat16),
-                        pltpu.VMEM((block + 2, cols, c), jnp.bfloat16),
-                        pltpu.VMEM((CHUNK, cols, 3 * c), jnp.bfloat16)],
+        scratch_shapes=[slab] * 7 + [
+            slab,
+            pltpu.VMEM(w3.shape, w3.dtype),
+            slab,
+            pltpu.VMEM((CHUNK, cols, 3 * c), jnp.bfloat16),
+            pltpu.SemaphoreType.DMA((18,)),
+        ],
         cost_estimate=pl.CostEstimate(flops=flops, transcendentals=0,
                                       bytes_accessed=18 * (block + 2) * cols * c + 2 * 9 * c * c),
     )(coef, fb, rb, own, par, ra, fa, routed, above, frame, below, w3)

time: 71.4 us -> 71.5 us (level)
  no operation moved by 1% of the time
where the time goes in v16:
time: 71.5 us; the launch traced here: 70.8 us
  waiting for transfers between devices  31.9 us (45%)
  Pallas kernels  14.2 us (20%)
  starting transfers between devices  13.7 us (19%)
  local copies, waits for them, and re-layouts  4.42 us (6%)
  between operations  4.02 us (6%)
  other arithmetic  2.62 us (4%)
    ppermute x1, waiting for transfers between devices, shards(): lax.ppermute(second, 'tm', [(0, 2), (1, 3), (3, 5), (4, 6), (5, 7)])  12.1 us
    ppermute x1, waiting for transfers between devices, shards(): hop = lax.ppermute(second, 'tm', [(2, 6), (5, 1)])  9.85 us
    pallas_call x1, Pallas kernels, layers(): pl.pallas_call(layers_kernel, out_shape=jax.ShapeDtypeStruct((rows - 4, c...  7.64 us
    pallas_call x1, Pallas kernels, mix(): pl.pallas_call(mix_kernel, out_shape=jax.ShapeDtypeStruct((block, cols, c...  6.56 us
    ppermute x2, starting transfers between devices, shifted(): return lax.ppermute(value, axis, pairs)  5.84 us
    ppermute x1, waiting for transfers between devices, shards(): lax.ppermute(second, 'tm', [(2, 0), (3, 1), (4, 2), (6, 4), (7, 5)])  5.46 us
    ppermute x1, waiting for transfers between devices, shards(): lax.ppermute(from_behind, 'tm', [(i + 1, i) for i in range(2, count, 2)])  2.86 us
    slice x2, local copies, waits for them, and re-layouts, shards(): up = jnp.concatenate([image[:3], frame[:1]], axis=0)  2.04 us
  transfers between devices with their start and end apart: 9, of which 5 were waited for; matrix products, arithmetic and copies ran while one was open for 5% of the time, Pallas kernels for 0%

profile of v16, /device:TPU:22, one launch (start us, length us, event | category | flops | bytes accessed | tf_op | source)
XLA Modules:
  0.0 70.8 jit_solution(6387894636250832062)
XLA Ops:
  0.0 0.9 %slice_bitcast_fusion.2 = (bf16[1,160,256]{2,1,0:T(8,128)(2,1)S(1)}, bf16[1,160,256]{2,1,0:T(8,128)(2,1)S(1)}) fusion(bf16[1,8,160,256]{3,2,1,0:T(8,128)(2,1)} %param.9), kind=kLoop, calls=%fused_computation.4 | loop fusion | bytes 327680 | tf_op jit(solution)/shard_map/slice | solution.py:195
  0.9 0.0 copy-start.8
  1.0 1.1 %slice_bitcast_fusion = (bf16[3,160,256]{2,1,0:T(8,128)(2,1)S(1)}, bf16[3,160,256]{2,1,0:T(8,128)(2,1)S(1)}) fusion(bf16[1,8,160,256]{3,2,1,0:T(8,128)(2,1)} %param.8), kind=kLoop, calls=%fused_computation.2 | loop fusion | bytes 983040 | tf_op jit(solution)/shard_map/slice | solution.py:195
  2.1 3.5 %collective-permute-start = (bf16[4,160,256]{2,1,0:T(8,128)(2,1)S(1)}, bf16[4,160,256]{2,1,0:T(8,128)(2,1)S(1)}, u32[]{:S(2)}, u32[]{:S(2)}) collective-permute-start(bf16[4,160,256]{2,1,0:T(8,128)(2,1)S(1)} %pad_maximum_fusion), channel_id=1, source_target_pairs={{0,1},{1,2},{2,3},{4,5},{5,6},{6,7},{8,9},{9,10},{10,11},{12,13},{... | collective-permute-start | bytes 983048 | tf_op jit(solution)/shard_map/ppermute | solution.py:16
  5.6 2.4 %collective-permute-start.1 = (bf16[4,160,256]{2,1,0:T(8,128)(2,1)S(1)}, bf16[4,160,256]{2,1,0:T(8,128)(2,1)S(1)}, u32[]{:S(2)}, u32[]{:S(2)}) collective-permute-start(bf16[4,160,256]{2,1,0:T(8,128)(2,1)S(1)} %pad_maximum_fusion.1), channel_id=1, source_target_pairs={{1,0},{2,1},{3,2},{5,4},{6,5},{7,6},{9,8},{10,9},{11,10},{13,12},{... | collective-permute-start | bytes 983048 | tf_op jit(solution)/shard_map/ppermute | solution.py:16
  9.3 0.0 copy-done.8
  9.3 0.6 fusion
  10.0 0.6 broadcast_divide_fusion
  10.6 0.1 slice.45
  10.7 0.7 fusion.1
  13.8 0.6 pad_add_fusion.bounds_ref
  14.5 0.6 pad_maximum_fusion.2.coef_ref
  15.1 0.0 collective-permute-done.above_ref.refs_7_
  15.1 0.0 copy-start.6
  15.1 1.6 %collective-permute-done.1.below_ref.refs_9_ = bf16[4,160,256]{2,1,0:T(8,128)(2,1)S(1)} collective-permute-done((bf16[4,160,256]{2,1,0:T(8,128)(2,1)S(1)}, bf16[4,160,256]{2,1,0:T(8,128)(2,1)S(1)}, u32[]{:S(2)}, u32[]{:S(2)}) %collective-permute-start.1) | collective-permute-done | bytes 327712 | tf_op jit(solution)/shard_map/ppermute | solution.py:16
  16.7 0.0 copy-done.6
  16.7 0.0 copy-start.7
  16.7 0.7 %copy-done.7 = bf16[4,160,256]{2,1,0:T(8,128)(2,1)} copy-done((bf16[4,160,256]{2,1,0:T(8,128)(2,1)}, bf16[4,160,256]{2,1,0:T(8,128)(2,1)S(1)}, u32[]{:S(2)}) %copy-start.7) | copy-done | bytes 327704
  17.4 7.6 %shard_map.82.refs_2_ = bf16[10,160,256]{2,1,0:T(8,128)(2,1)} custom-call(s32[2]{0:T(128)} %pad_add_fusion.bounds_ref, bf16[4,160,256]{2,1,0:T(8,128)(2,1)} %copy-done.6, bf16[8,160,256]{2,1,0:T(8,128)(2,1)} %bitcast.28, bf16[4,160,256]{2,1,0:T(8,128)(2,1)} %copy-done.7, bf16[3,3,256,256]{3,2,1,0:T(8,128)(2,1)} %w1_ref.1, bf16[3,3,256,256]{3,2,1,0:T(8,128)(2,1)} %w2_ref.1), custom_call_target="tpu_custom_call" | custom-call | flops 4152360960 | bytes 4653056 | tf_op jit(solution)/shard_map/pallas_call | solution.py:143
  25.1 1.3 %collective-permute-start.7 = (bf16[10,160,256]{2,1,0:T(8,128)(2,1)}, bf16[10,160,256]{2,1,0:T(8,128)(2,1)S(1)}, u32[]{:S(2)}, u32[]{:S(2)}) collective-permute-start(bf16[10,160,256]{2,1,0:T(8,128)(2,1)} %shard_map.82.refs_2_), channel_id=1, source_target_pairs={{8,24},{20,4},{9,25},{21,5},{10,26},{22,6},{11,27},{23,7}} | collective-permute-start | bytes 2457608 | tf_op jit(solution)/shard_map/ppermute | solution.py:221
  26.4 1.9 %collective-permute-start.5 = (bf16[10,160,256]{2,1,0:T(8,128)(2,1)}, bf16[10,160,256]{2,1,0:T(8,128)(2,1)S(1)}, u32[]{:S(2)}, u32[]{:S(2)}) collective-permute-start(bf16[10,160,256]{2,1,0:T(8,128)(2,1)} %shard_map.82.refs_2_), channel_id=1, source_target_pairs={{8,0},{12,4},{16,8},{24,16},{28,20},{9,1},{13,5},{17,9},{25,17},{2... | collective-permute-start | bytes 2457608 | tf_op jit(solution)/shard_map/ppermute | solution.py:220
  28.3 1.3 %collective-permute-start.2 = (bf16[10,160,256]{2,1,0:T(8,128)(2,1)}, bf16[10,160,256]{2,1,0:T(8,128)(2,1)S(1)}, u32[]{:S(2)}, u32[]{:S(2)}) collective-permute-start(bf16[10,160,256]{2,1,0:T(8,128)(2,1)} %shard_map.82.refs_2_), channel_id=1, source_target_pairs={{0,8},{4,12},{12,20},{16,24},{20,28},{1,9},{5,13},{13,21},{17,25},... | collective-permute-start | bytes 2457608 | tf_op jit(solution)/shard_map/ppermute | solution.py:219
  29.6 0.1 collective-permute-start.4
  29.7 9.8 %collective-permute-done.7 = bf16[10,160,256]{2,1,0:T(8,128)(2,1)S(1)} collective-permute-done((bf16[10,160,256]{2,1,0:T(8,128)(2,1)}, bf16[10,160,256]{2,1,0:T(8,128)(2,1)S(1)}, u32[]{:S(2)}, u32[]{:S(2)}) %collective-permute-start.7) | collective-permute-done | bytes 819232 | tf_op jit(solution)/shard_map/ppermute | solution.py:221
  39.5 1.3 %collective-permute-start.8 = (bf16[10,160,256]{2,1,0:T(8,128)(2,1)S(1)}, bf16[10,160,256]{2,1,0:T(8,128)(2,1)S(1)}, u32[]{:S(2)}, u32[]{:S(2)}) collective-permute-start(bf16[10,160,256]{2,1,0:T(8,128)(2,1)S(1)} %collective-permute-done.7), channel_id=1, source_target_pairs={{24,16},{4,12},{25,17},{5,13},{26,18},{6,14},{27,19},{7,15}} | collective-permute-start | bytes 2457608 | tf_op jit(solution)/shard_map/ppermute | solution.py:222
  40.8 5.5 %collective-permute-done.5.refs_5_ = bf16[10,160,256]{2,1,0:T(8,128)(2,1)S(1)} collective-permute-done((bf16[10,160,256]{2,1,0:T(8,128)(2,1)}, bf16[10,160,256]{2,1,0:T(8,128)(2,1)S(1)}, u32[]{:S(2)}, u32[]{:S(2)}) %collective-permute-start.5) | collective-permute-done | bytes 819232 | tf_op jit(solution)/shard_map/ppermute | solution.py:220
  46.3 0.0 copy-start
  46.3 0.7 collective-permute-start.6
  47.0 12.1 %collective-permute-done.2.refs_0_ = bf16[10,160,256]{2,1,0:T(8,128)(2,1)S(1)} collective-permute-done((bf16[10,160,256]{2,1,0:T(8,128)(2,1)}, bf16[10,160,256]{2,1,0:T(8,128)(2,1)S(1)}, u32[]{:S(2)}, u32[]{:S(2)}) %collective-permute-start.2) | collective-permute-done | bytes 819232 | tf_op jit(solution)/shard_map/ppermute | solution.py:219
  59.1 0.0 copy-start.1
  59.1 1.3 %collective-permute-start.3 = (bf16[10,160,256]{2,1,0:T(8,128)(2,1)S(1)}, bf16[10,160,256]{2,1,0:T(8,128)(2,1)S(1)}, u32[]{:S(2)}, u32[]{:S(2)}) collective-permute-start(bf16[10,160,256]{2,1,0:T(8,128)(2,1)S(1)} %collective-permute-done.2.refs_0_), channel_id=1, source_target_pairs={{12,8},{20,16},{28,24},{13,9},{21,17},{29,25},{14,10},{22,18},{30,... | collective-permute-start | bytes 2457608 | tf_op jit(solution)/shard_map/ppermute | solution.py:227
  60.4 0.0 collective-permute-done.4.refs_3_
  60.4 0.0 copy-start.2
  60.4 0.0 collective-permute-done.8.refs_6_
  60.5 0.0 copy-start.3
  60.5 0.0 collective-permute-done.6.refs_4_
  60.5 0.0 copy-start.4
  60.5 2.9 %collective-permute-done.3.refs_1_ = bf16[10,160,256]{2,1,0:T(8,128)(2,1)S(1)} collective-permute-done((bf16[10,160,256]{2,1,0:T(8,128)(2,1)S(1)}, bf16[10,160,256]{2,1,0:T(8,128)(2,1)S(1)}, u32[]{:S(2)}, u32[]{:S(2)}) %collective-permute-start.3) | collective-permute-done | bytes 819232 | tf_op jit(solution)/shard_map/ppermute | solution.py:227
  63.4 0.0 copy-done.4
  63.4 0.0 copy-start.5
  63.4 0.9 %copy-done.5 = bf16[10,160,256]{2,1,0:T(8,128)(2,1)} copy-done((bf16[10,160,256]{2,1,0:T(8,128)(2,1)}, bf16[10,160,256]{2,1,0:T(8,128)(2,1)S(1)}, u32[]{:S(2)}) %copy-start.5) | copy-done | bytes 819224
  64.3 0.0 copy-done
  64.3 0.0 copy-done.1
  64.3 0.0 copy-done.2
  64.3 0.0 copy-done.3
  64.3 6.6 %shard_map.83 = bf16[8,160,256]{2,1,0:T(8,128)(2,1)} custom-call(f32[7]{0:T(128)} %pad_maximum_fusion.2.coef_ref, bf16[10,160,256]{2,1,0:T(8,128)(2,1)} %copy-done.1, bf16[10,160,256]{2,1,0:T(8,128)(2,1)} %copy-done.5, bf16[10,160,256]{2,1,0:T(8,128)(2,1)} %shard_map.82.refs_2_, bf16[10,160,256]{2,1,0:T(8,128)(2,1)} %copy-done.2, ...), custom_call_target="tpu_custom_call" | custom-call | flops 1509949440 | bytes 8552448 | tf_op jit(solution)/shard_map/pallas_call | solution.py:161
  (2 shorter events, 0.1 us)
Async XLA Ops:
  0.9 8.4 %copy-start.8 = (s32[1,5]{1,0:T(1,128)S(1)}, s32[1,5]{1,0:T(1,128)}, u32[]{:S(2)}) copy-start(s32[1,5]{1,0:T(1,128)} %param.12) | copy-start | bytes 64
  2.1 13.0 %collective-permute-start = (bf16[4,160,256]{2,1,0:T(8,128)(2,1)S(1)}, bf16[4,160,256]{2,1,0:T(8,128)(2,1)S(1)}, u32[]{:S(2)}, u32[]{:S(2)}) collective-permute-start(bf16[4,160,256]{2,1,0:T(8,128)(2,1)S(1)} %pad_maximum_fusion), channel_id=1, source_target_pairs={{0,1},{1,2},{2,3},{4,5},{5,6},{6,7},{8,9},{9,10},{10,11},{12,13},{... | collective-permute-start | bytes 983048 | tf_op jit(solution)/shard_map/ppermute | solution.py:16
  5.6 11.1 %collective-permute-start.1 = (bf16[4,160,256]{2,1,0:T(8,128)(2,1)S(1)}, bf16[4,160,256]{2,1,0:T(8,128)(2,1)S(1)}, u32[]{:S(2)}, u32[]{:S(2)}) collective-permute-start(bf16[4,160,256]{2,1,0:T(8,128)(2,1)S(1)} %pad_maximum_fusion.1), channel_id=1, source_target_pairs={{1,0},{2,1},{3,2},{5,4},{6,5},{7,6},{9,8},{10,9},{11,10},{13,12},{... | collective-permute-start | bytes 983048 | tf_op jit(solution)/shard_map/ppermute | solution.py:16
  15.1 1.6 %copy-start.6 = (bf16[4,160,256]{2,1,0:T(8,128)(2,1)}, bf16[4,160,256]{2,1,0:T(8,128)(2,1)S(1)}, u32[]{:S(2)}) copy-start(bf16[4,160,256]{2,1,0:T(8,128)(2,1)S(1)} %collective-permute-done.above_ref.refs_7_) | copy-start | bytes 983044
  16.7 0.7 %copy-start.7 = (bf16[4,160,256]{2,1,0:T(8,128)(2,1)}, bf16[4,160,256]{2,1,0:T(8,128)(2,1)S(1)}, u32[]{:S(2)}) copy-start(bf16[4,160,256]{2,1,0:T(8,128)(2,1)S(1)} %collective-permute-done.1.below_ref.refs_9_) | copy-start | bytes 983044
  25.1 14.4 %collective-permute-start.7 = (bf16[10,160,256]{2,1,0:T(8,128)(2,1)}, bf16[10,160,256]{2,1,0:T(8,128)(2,1)S(1)}, u32[]{:S(2)}, u32[]{:S(2)}) collective-permute-start(bf16[10,160,256]{2,1,0:T(8,128)(2,1)} %shard_map.82.refs_2_), channel_id=1, source_target_pairs={{8,24},{20,4},{9,25},{21,5},{10,26},{22,6},{11,27},{23,7}} | collective-permute-start | bytes 2457608 | tf_op jit(solution)/shard_map/ppermute | solution.py:221
  26.4 19.9 %collective-permute-start.5 = (bf16[10,160,256]{2,1,0:T(8,128)(2,1)}, bf16[10,160,256]{2,1,0:T(8,128)(2,1)S(1)}, u32[]{:S(2)}, u32[]{:S(2)}) collective-permute-start(bf16[10,160,256]{2,1,0:T(8,128)(2,1)} %shard_map.82.refs_2_), channel_id=1, source_target_pairs={{8,0},{12,4},{16,8},{24,16},{28,20},{9,1},{13,5},{17,9},{25,17},{2... | collective-permute-start | bytes 2457608 | tf_op jit(solution)/shard_map/ppermute | solution.py:220
  28.3 30.9 %collective-permute-start.2 = (bf16[10,160,256]{2,1,0:T(8,128)(2,1)}, bf16[10,160,256]{2,1,0:T(8,128)(2,1)S(1)}, u32[]{:S(2)}, u32[]{:S(2)}) collective-permute-start(bf16[10,160,256]{2,1,0:T(8,128)(2,1)} %shard_map.82.refs_2_), channel_id=1, source_target_pairs={{0,8},{4,12},{12,20},{16,24},{20,28},{1,9},{5,13},{13,21},{17,25},... | collective-permute-start | bytes 2457608 | tf_op jit(solution)/shard_map/ppermute | solution.py:219
  29.6 30.9 %collective-permute-start.4 = (bf16[10,160,256]{2,1,0:T(8,128)(2,1)}, bf16[10,160,256]{2,1,0:T(8,128)(2,1)S(1)}, u32[]{:S(2)}, u32[]{:S(2)}) collective-permute-start(bf16[10,160,256]{2,1,0:T(8,128)(2,1)} %shard_map.82.refs_2_), channel_id=1, source_target_pairs={{0,4},{4,0},{8,12},{12,8},{16,20},{20,16},{24,28},{28,24},{1,5},{5... | collective-permute-start | bytes 2457608 | tf_op jit(solution)/shard_map/ppermute | solution.py:217
  39.5 20.9 %collective-permute-start.8 = (bf16[10,160,256]{2,1,0:T(8,128)(2,1)S(1)}, bf16[10,160,256]{2,1,0:T(8,128)(2,1)S(1)}, u32[]{:S(2)}, u32[]{:S(2)}) collective-permute-start(bf16[10,160,256]{2,1,0:T(8,128)(2,1)S(1)} %collective-permute-done.7), channel_id=1, source_target_pairs={{24,16},{4,12},{25,17},{5,13},{26,18},{6,14},{27,19},{7,15}} | collective-permute-start | bytes 2457608 | tf_op jit(solution)/shard_map/ppermute | solution.py:222
  46.3 18.0 %copy-start = (bf16[10,160,256]{2,1,0:T(8,128)(2,1)}, bf16[10,160,256]{2,1,0:T(8,128)(2,1)S(1)}, u32[]{:S(2)}) copy-start(bf16[10,160,256]{2,1,0:T(8,128)(2,1)S(1)} %collective-permute-done.5.refs_5_) | copy-start | bytes 2457604
  46.3 14.2 %collective-permute-start.6 = (bf16[10,160,256]{2,1,0:T(8,128)(2,1)S(1)}, bf16[10,160,256]{2,1,0:T(8,128)(2,1)S(1)}, u32[]{:S(2)}, u32[]{:S(2)}) collective-permute-start(bf16[10,160,256]{2,1,0:T(8,128)(2,1)S(1)} %collective-permute-done.5.refs_5_), channel_id=1, source_target_pairs={{0,4},{8,12},{16,20},{1,5},{9,13},{17,21},{2,6},{10,14},{18,22},{3... | collective-permute-start | bytes 2457608 | tf_op jit(solution)/shard_map/ppermute | solution.py:228
  59.1 5.1 %copy-start.1 = (bf16[10,160,256]{2,1,0:T(8,128)(2,1)}, bf16[10,160,256]{2,1,0:T(8,128)(2,1)S(1)}, u32[]{:S(2)}) copy-start(bf16[10,160,256]{2,1,0:T(8,128)(2,1)S(1)} %collective-permute-done.2.refs_0_) | copy-start | bytes 2457604
  59.1 4.2 %collective-permute-start.3 = (bf16[10,160,256]{2,1,0:T(8,128)(2,1)S(1)}, bf16[10,160,256]{2,1,0:T(8,128)(2,1)S(1)}, u32[]{:S(2)}, u32[]{:S(2)}) collective-permute-start(bf16[10,160,256]{2,1,0:T(8,128)(2,1)S(1)} %collective-permute-done.2.refs_0_), channel_id=1, source_target_pairs={{12,8},{20,16},{28,24},{13,9},{21,17},{29,25},{14,10},{22,18},{30,... | collective-permute-start | bytes 2457608 | tf_op jit(solution)/shard_map/ppermute | solution.py:227
  60.4 3.8 %copy-start.2 = (bf16[10,160,256]{2,1,0:T(8,128)(2,1)}, bf16[10,160,256]{2,1,0:T(8,128)(2,1)S(1)}, u32[]{:S(2)}) copy-start(bf16[10,160,256]{2,1,0:T(8,128)(2,1)S(1)} %collective-permute-done.4.refs_3_) | copy-start | bytes 2457604
  60.5 3.8 %copy-start.3 = (bf16[10,160,256]{2,1,0:T(8,128)(2,1)}, bf16[10,160,256]{2,1,0:T(8,128)(2,1)S(1)}, u32[]{:S(2)}) copy-start(bf16[10,160,256]{2,1,0:T(8,128)(2,1)S(1)} %collective-permute-done.8.refs_6_) | copy-start | bytes 2457604
  60.5 2.9 %copy-start.4 = (bf16[10,160,256]{2,1,0:T(8,128)(2,1)}, bf16[10,160,256]{2,1,0:T(8,128)(2,1)S(1)}, u32[]{:S(2)}) copy-start(bf16[10,160,256]{2,1,0:T(8,128)(2,1)S(1)} %collective-permute-done.6.refs_4_) | copy-start | bytes 2457604
  63.4 0.9 %copy-start.5 = (bf16[10,160,256]{2,1,0:T(8,128)(2,1)}, bf16[10,160,256]{2,1,0:T(8,128)(2,1)S(1)}, u32[]{:S(2)}) copy-start(bf16[10,160,256]{2,1,0:T(8,128)(2,1)S(1)} %collective-permute-done.3.refs_1_) | copy-start | bytes 2457604

commit v17 on v16

--- a/solution.py
+++ b/solution.py
@@ -76,19 +76,27 @@
     split = rows // 2 + 1
     slices = [(fb_hbm, fb_ref), (rb_hbm, rb_ref), (own_hbm, own_ref), (par_hbm, par_ref),
               (ra_hbm, ra_ref), (fa_hbm, fa_ref), (routed_hbm, routed_ref)]
-    first = [pltpu.make_async_copy(w3_hbm, w3_ref, sems.at[0])]
-    for i, (src, dst) in enumerate(slices):
-        first.append(pltpu.make_async_copy(src.at[0:split], dst.at[0:split], sems.at[1 + i]))
+    received = [coef_ref[7 + i] > 0.5 for i in range(len(slices))]
     halo = below_hbm.shape[0] - 1
-    first.append(pltpu.make_async_copy(above_hbm.at[halo : halo + 1], fbuf.at[0:1], sems.at[8]))
-    first.append(pltpu.make_async_copy(frame_hbm, fbuf.at[1 : block + 1], sems.at[9]))
-    first.append(pltpu.make_async_copy(below_hbm.at[halo : halo + 1], fbuf.at[block + 1 :], sems.at[10]))
-    second = [
-        pltpu.make_async_copy(src.at[split:rows], dst.at[split:rows], sems.at[11 + i])
-        for i, (src, dst) in enumerate(slices)
+    fixed = [
+        pltpu.make_async_copy(w3_hbm, w3_ref, sems.at[0]),
+        pltpu.make_async_copy(above_hbm.at[halo : halo + 1], fbuf.at[0:1], sems.at[8]),
+        pltpu.make_async_copy(frame_hbm, fbuf.at[1 : block + 1], sems.at[9]),
+        pltpu.make_async_copy(below_hbm.at[halo : halo + 1], fbuf.at[block + 1 :], sems.at[10]),
     ]
-    for c in first + second:
+    first = [pltpu.make_async_copy(src.at[0:split], dst.at[0:split], sems.at[1 + i])
+             for i, (src, dst) in enumerate(slices)]
+    second = [pltpu.make_async_copy(src.at[split:rows], dst.at[split:rows], sems.at[11 + i])
+              for i, (src, dst) in enumerate(slices)]
+    for c in fixed:
         c.start()
+    for group in (first, second):
+        for flag, c in zip(received, group):
+            pl.when(flag)(c.start)
+    for flag, (src, dst) in zip(received, slices):
+        @pl.when(jnp.logical_not(flag))
+        def _():
+            dst[...] = jnp.zeros(dst.shape, dst.dtype)
     f32 = jnp.float32
     step = stack.shape[0]
 
@@ -108,15 +116,17 @@
     def emit(r0, n, value):
         out_ref[r0 : r0 + n] = value.astype(jnp.bfloat16)
 
-    for c in first:
+    for c in fixed:
         c.wait()
+    for flag, c in zip(received, first):
+        pl.when(flag)(c.wait)
     join(0, split)
     r0 = 0
     while r0 + step + 2 <= split:
         conv_chunk(mixed_buf, w3_ref, stack, r0, step, emit)
         r0 += step
-    for c in second:
-        c.wait()
+    for flag, c in zip(received, second):
+        pl.when(flag)(c.wait)
     join(split, rows - split)
     while r0 < block:
         n = min(step, block - r0)
@@ -216,16 +226,29 @@
 
     partner = lax.ppermute(second, "tm", [(i, i ^ 1) for i in range(count)])
     if count == 8:
-        from_behind = lax.ppermute(second, "tm", [(0, 2), (1, 3), (3, 5), (4, 6), (5, 7)])
-        from_ahead = lax.ppermute(second, "tm", [(2, 0), (3, 1), (4, 2), (6, 4), (7, 5)])
+        behind_pairs = [(0, 2), (1, 3), (3, 5), (4, 6), (5, 7)]
+        ahead_pairs = [(2, 0), (3, 1), (4, 2), (6, 4), (7, 5)]
+        routed_pairs = [(6, 4), (1, 3)]
         hop = lax.ppermute(second, "tm", [(2, 6), (5, 1)])
-        routed = lax.ppermute(hop, "tm", [(6, 4), (1, 3)])
+        routed = lax.ppermute(hop, "tm", routed_pairs)
     else:
-        from_behind = shifted(second, "tm", 2)
-        from_ahead = shifted(second, "tm", -2)
+        behind_pairs = [(i, i + 2) for i in range(count - 2)]
+        ahead_pairs = [(i + 2, i) for i in range(count - 2)]
+        routed_pairs = []
         routed = jnp.zeros_like(second)
-    relay_behind = lax.ppermute(from_behind, "tm", [(i + 1, i) for i in range(2, count, 2)])
-    relay_ahead = lax.ppermute(from_ahead, "tm", [(i, i + 1) for i in range(0, count - 2, 2)])
+    from_behind = lax.ppermute(second, "tm", behind_pairs)
+    from_ahead = lax.ppermute(second, "tm", ahead_pairs)
+    behind_relays = [(i + 1, i) for i in range(2, count, 2)]
+    ahead_relays = [(i, i + 1) for i in range(0, count - 2, 2)]
+    relay_behind = lax.ppermute(from_behind, "tm", behind_relays)
+    relay_ahead = lax.ppermute(from_ahead, "tm", ahead_relays)
+    every = [(i, i) for i in range(count)]
+    table = np.zeros((count, 7), np.float32)
+    for column, pairs in enumerate([behind_pairs, behind_relays, every, every, ahead_relays, ahead_pairs,
+                                    routed_pairs]):
+        for _, target in pairs:
+            table[target, column] = 1.0
+    coef = jnp.concatenate([coef, jnp.asarray(table)[t]])
     result = mix(coef, from_behind, relay_behind, second, partner, relay_ahead, from_ahead, routed,
                  from_above, frame, from_below, conv_frame)
     return result[None]

time: 71.5 us -> 72.6 us (1.015)
  the two profiles are of different devices: /device:TPU:22 before, /device:TPU:7 now
where the time goes in v17:
time: 72.6 us; the launch traced here: 72.2 us
  starting transfers between devices  27.7 us (38%)
  waiting for transfers between devices  18.9 us (26%)
  Pallas kernels  13.7 us (19%)
  local copies, waits for them, and re-layouts  5.34 us (7%)
  between operations  3.92 us (5%)
  other arithmetic  2.53 us (3%)
    ppermute x1, waiting for transfers between devices, shards(): from_ahead = lax.ppermute(second, 'tm', ahead_pairs)  14.7 us
    ppermute x1, starting transfers between devices, shards(): relay_behind = lax.ppermute(from_behind, 'tm', behind_relays)  13.6 us
    pallas_call x1, Pallas kernels, layers(): pl.pallas_call(layers_kernel, out_shape=jax.ShapeDtypeStruct((rows - 4, c...  7.66 us
    pallas_call x1, Pallas kernels, mix(): pl.pallas_call(mix_kernel, out_shape=jax.ShapeDtypeStruct((block, cols, c...  6.07 us
    ppermute x2, starting transfers between devices, shifted(): return lax.ppermute(value, axis, pairs)  4.51 us
    ppermute x1, starting transfers between devices, shards(): from_ahead = lax.ppermute(second, 'tm', ahead_pairs)  3.66 us
    ppermute x2, waiting for transfers between devices, shifted(): return lax.ppermute(value, axis, pairs)  2.56 us
    slice x2, local copies, waits for them, and re-layouts, shards(): up = jnp.concatenate([image[:3], frame[:1]], axis=0)  2.04 us
  transfers between devices with their start and end apart: 9, of which 3 were waited for; matrix products, arithmetic and copies ran while one was open for 5% of the time, Pallas kernels for 0%

profile of v17, /device:TPU:7, one launch (start us, length us, event | category | flops | bytes accessed | tf_op | source)
XLA Modules:
  0.0 72.2 jit_solution(17515319689593905696)
XLA Ops:
  0.0 0.9 %slice_bitcast_fusion.2 = (bf16[1,160,256]{2,1,0:T(8,128)(2,1)S(1)}, bf16[1,160,256]{2,1,0:T(8,128)(2,1)S(1)}) fusion(bf16[1,8,160,256]{3,2,1,0:T(8,128)(2,1)} %param.10), kind=kLoop, calls=%fused_computation.4 | loop fusion | bytes 327680 | tf_op jit(solution)/shard_map/slice | solution.py:205
  0.9 0.0 copy-start.6
  1.0 1.1 %slice_bitcast_fusion = (bf16[3,160,256]{2,1,0:T(8,128)(2,1)S(1)}, bf16[3,160,256]{2,1,0:T(8,128)(2,1)S(1)}) fusion(bf16[1,8,160,256]{3,2,1,0:T(8,128)(2,1)} %param.9), kind=kLoop, calls=%fused_computation.2 | loop fusion | bytes 983040 | tf_op jit(solution)/shard_map/slice | solution.py:205
  2.1 3.2 %collective-permute-start = (bf16[4,160,256]{2,1,0:T(8,128)(2,1)S(1)}, bf16[4,160,256]{2,1,0:T(8,128)(2,1)S(1)}, u32[]{:S(2)}, u32[]{:S(2)}) collective-permute-start(bf16[4,160,256]{2,1,0:T(8,128)(2,1)S(1)} %pad_maximum_fusion), channel_id=1, source_target_pairs={{0,1},{1,2},{2,3},{4,5},{5,6},{6,7},{8,9},{9,10},{10,11},{12,13},{... | collective-permute-start | bytes 983048 | tf_op jit(solution)/shard_map/ppermute | solution.py:16
  5.4 1.3 %collective-permute-start.1 = (bf16[4,160,256]{2,1,0:T(8,128)(2,1)S(1)}, bf16[4,160,256]{2,1,0:T(8,128)(2,1)S(1)}, u32[]{:S(2)}, u32[]{:S(2)}) collective-permute-start(bf16[4,160,256]{2,1,0:T(8,128)(2,1)S(1)} %pad_maximum_fusion.1), channel_id=1, source_target_pairs={{1,0},{2,1},{3,2},{5,4},{6,5},{7,6},{9,8},{10,9},{11,10},{13,12},{... | collective-permute-start | bytes 983048 | tf_op jit(solution)/shard_map/ppermute | solution.py:16
  8.0 0.0 copy-done.6
  8.0 0.6 fusion
  8.6 0.6 broadcast_divide_fusion
  9.2 0.1 slice.45
  9.2 0.6 fusion.1
  12.3 0.6 pad_add_fusion.bounds_ref
  12.9 0.1 pad_maximum_fusion.2
  13.0 0.0 collective-permute-done.above_ref.refs_7_
  13.0 0.0 copy-start.4
  13.0 2.6 %collective-permute-done.1.below_ref.refs_9_ = bf16[4,160,256]{2,1,0:T(8,128)(2,1)S(1)} collective-permute-done((bf16[4,160,256]{2,1,0:T(8,128)(2,1)S(1)}, bf16[4,160,256]{2,1,0:T(8,128)(2,1)S(1)}, u32[]{:S(2)}, u32[]{:S(2)}) %collective-permute-start.1) | collective-permute-done | bytes 327712 | tf_op jit(solution)/shard_map/ppermute | solution.py:16
  15.5 0.0 copy-done.4
  15.5 0.0 copy-start.5
  15.5 0.7 %copy-done.5 = bf16[4,160,256]{2,1,0:T(8,128)(2,1)} copy-done((bf16[4,160,256]{2,1,0:T(8,128)(2,1)}, bf16[4,160,256]{2,1,0:T(8,128)(2,1)S(1)}, u32[]{:S(2)}) %copy-start.5) | copy-done | bytes 327704
  16.3 7.7 %shard_map.91.refs_2_ = bf16[10,160,256]{2,1,0:T(8,128)(2,1)} custom-call(s32[2]{0:T(128)} %pad_add_fusion.bounds_ref, bf16[4,160,256]{2,1,0:T(8,128)(2,1)} %copy-done.4, bf16[8,160,256]{2,1,0:T(8,128)(2,1)} %bitcast.30, bf16[4,160,256]{2,1,0:T(8,128)(2,1)} %copy-done.5, bf16[3,3,256,256]{3,2,1,0:T(8,128)(2,1)} %w1_ref.1, bf16[3,3,256,256]{3,2,1,0:T(8,128)(2,1)} %w2_ref.1), custom_call_target="tpu_custom_call" | custom-call | flops 4152360960 | bytes 4653056 | tf_op jit(solution)/shard_map/pallas_call | solution.py:153
  23.9 1.6 %collective-permute-start.7 = (bf16[10,160,256]{2,1,0:T(8,128)(2,1)}, bf16[10,160,256]{2,1,0:T(8,128)(2,1)}, u32[]{:S(2)}, u32[]{:S(2)}) collective-permute-start(bf16[10,160,256]{2,1,0:T(8,128)(2,1)} %shard_map.91.refs_2_), channel_id=1, source_target_pairs={{8,24},{20,4},{9,25},{21,5},{10,26},{22,6},{11,27},{23,7}} | collective-permute-start | bytes 2457608 | tf_op jit(solution)/shard_map/ppermute | solution.py:232
  25.5 3.7 %collective-permute-start.5 = (bf16[10,160,256]{2,1,0:T(8,128)(2,1)}, bf16[10,160,256]{2,1,0:T(8,128)(2,1)S(1)}, u32[]{:S(2)}, u32[]{:S(2)}) collective-permute-start(bf16[10,160,256]{2,1,0:T(8,128)(2,1)} %shard_map.91.refs_2_), channel_id=1, source_target_pairs={{8,0},{12,4},{16,8},{24,16},{28,20},{9,1},{13,5},{17,9},{25,17},{2... | collective-permute-start | bytes 2457608 | tf_op jit(solution)/shard_map/ppermute | solution.py:240
  29.2 1.3 %collective-permute-start.2 = (bf16[10,160,256]{2,1,0:T(8,128)(2,1)}, bf16[10,160,256]{2,1,0:T(8,128)(2,1)S(1)}, u32[]{:S(2)}, u32[]{:S(2)}) collective-permute-start(bf16[10,160,256]{2,1,0:T(8,128)(2,1)} %shard_map.91.refs_2_), channel_id=1, source_target_pairs={{0,8},{4,12},{12,20},{16,24},{20,28},{1,9},{5,13},{13,21},{17,25},... | collective-permute-start | bytes 2457608 | tf_op jit(solution)/shard_map/ppermute | solution.py:239
  30.5 0.7 %collective-permute-start.4 = (bf16[10,160,256]{2,1,0:T(8,128)(2,1)}, bf16[10,160,256]{2,1,0:T(8,128)(2,1)S(1)}, u32[]{:S(2)}, u32[]{:S(2)}) collective-permute-start(bf16[10,160,256]{2,1,0:T(8,128)(2,1)} %shard_map.91.refs_2_), channel_id=1, source_target_pairs={{0,4},{4,0},{8,12},{12,8},{16,20},{20,16},{24,28},{28,24},{1,5},{5... | collective-permute-start | bytes 2457608 | tf_op jit(solution)/shard_map/ppermute | solution.py:227
  31.2 0.0 collective-permute-done.7
  31.2 0.7 collective-permute-start.8
  31.9 14.7 %collective-permute-done.5.refs_5_ = bf16[10,160,256]{2,1,0:T(8,128)(2,1)S(1)} collective-permute-done((bf16[10,160,256]{2,1,0:T(8,128)(2,1)}, bf16[10,160,256]{2,1,0:T(8,128)(2,1)S(1)}, u32[]{:S(2)}, u32[]{:S(2)}) %collective-permute-start.5) | collective-permute-done | bytes 819232 | tf_op jit(solution)/shard_map/ppermute | solution.py:240
  46.7 0.0 copy-start
  46.7 1.6 %collective-permute-start.6 = (bf16[10,160,256]{2,1,0:T(8,128)(2,1)S(1)}, bf16[10,160,256]{2,1,0:T(8,128)(2,1)}, u32[]{:S(2)}, u32[]{:S(2)}) collective-permute-start(bf16[10,160,256]{2,1,0:T(8,128)(2,1)S(1)} %collective-permute-done.5.refs_5_), channel_id=1, source_target_pairs={{0,4},{8,12},{16,20},{1,5},{9,13},{17,21},{2,6},{10,14},{18,22},{3... | collective-permute-start | bytes 2457608 | tf_op jit(solution)/shard_map/ppermute | solution.py:244
  48.2 1.6 %collective-permute-done.2.refs_0_ = bf16[10,160,256]{2,1,0:T(8,128)(2,1)S(1)} collective-permute-done((bf16[10,160,256]{2,1,0:T(8,128)(2,1)}, bf16[10,160,256]{2,1,0:T(8,128)(2,1)S(1)}, u32[]{:S(2)}, u32[]{:S(2)}) %collective-permute-start.2) | collective-permute-done | bytes 819232 | tf_op jit(solution)/shard_map/ppermute | solution.py:239
  49.9 0.0 copy-start.1
  49.9 13.6 %collective-permute-start.3 = (bf16[10,160,256]{2,1,0:T(8,128)(2,1)S(1)}, bf16[10,160,256]{2,1,0:T(8,128)(2,1)}, u32[]{:S(2)}, u32[]{:S(2)}) collective-permute-start(bf16[10,160,256]{2,1,0:T(8,128)(2,1)S(1)} %collective-permute-done.2.refs_0_), channel_id=1, source_target_pairs={{12,8},{20,16},{28,24},{13,9},{21,17},{29,25},{14,10},{22,18},{30,... | collective-permute-start | bytes 2457608 | tf_op jit(solution)/shard_map/ppermute | solution.py:243
  63.5 0.7 dynamic-slice_bitcast_fusion
  64.2 0.7 pad_maximum_fusion.3.coef_ref
  64.9 0.0 collective-permute-done.4.refs_3_
  64.9 0.0 copy-start.2
  64.9 0.0 collective-permute-done.8.refs_6_
  64.9 0.0 copy-start.3
  64.9 0.0 collective-permute-done.6.refs_4_
  64.9 0.0 collective-permute-done.3.refs_1_
  64.9 0.0 copy-done
  64.9 0.0 copy-done.1
  64.9 0.9 %copy-done.2 = bf16[10,160,256]{2,1,0:T(8,128)(2,1)} copy-done((bf16[10,160,256]{2,1,0:T(8,128)(2,1)}, bf16[10,160,256]{2,1,0:T(8,128)(2,1)S(1)}, u32[]{:S(2)}) %copy-start.2) | copy-done | bytes 819224
  65.8 0.3 copy-done.3
  66.1 6.1 %shard_map.92 = bf16[8,160,256]{2,1,0:T(8,128)(2,1)} custom-call(f32[14]{0:T(128)} %pad_maximum_fusion.3.coef_ref, bf16[10,160,256]{2,1,0:T(8,128)(2,1)} %copy-done.1, bf16[10,160,256]{2,1,0:T(8,128)(2,1)} %collective-permute-done.3.refs_1_, bf16[10,160,256]{2,1,0:T(8,128)(2,1)} %shard_map.91.refs_2_, bf16[10,160,256]{2,1,0:T(8,128)(2,1)} %copy-done.2, ...), custom_call_target="tpu_custom_call" | custom-call | flops 1509949440 | bytes 8552448 | tf_op jit(solution)/shard_map/pallas_call | solution.py:171
  (2 shorter events, 0.1 us)
Async XLA Ops:
  0.9 7.0 %copy-start.6 = (s32[1,5]{1,0:T(1,128)S(1)}, s32[1,5]{1,0:T(1,128)}, u32[]{:S(2)}) copy-start(s32[1,5]{1,0:T(1,128)} %param.13) | copy-start | bytes 64
  2.1 10.9 %collective-permute-start = (bf16[4,160,256]{2,1,0:T(8,128)(2,1)S(1)}, bf16[4,160,256]{2,1,0:T(8,128)(2,1)S(1)}, u32[]{:S(2)}, u32[]{:S(2)}) collective-permute-start(bf16[4,160,256]{2,1,0:T(8,128)(2,1)S(1)} %pad_maximum_fusion), channel_id=1, source_target_pairs={{0,1},{1,2},{2,3},{4,5},{5,6},{6,7},{8,9},{9,10},{10,11},{12,13},{... | collective-permute-start | bytes 983048 | tf_op jit(solution)/shard_map/ppermute | solution.py:16
  5.4 10.2 %collective-permute-start.1 = (bf16[4,160,256]{2,1,0:T(8,128)(2,1)S(1)}, bf16[4,160,256]{2,1,0:T(8,128)(2,1)S(1)}, u32[]{:S(2)}, u32[]{:S(2)}) collective-permute-start(bf16[4,160,256]{2,1,0:T(8,128)(2,1)S(1)} %pad_maximum_fusion.1), channel_id=1, source_target_pairs={{1,0},{2,1},{3,2},{5,4},{6,5},{7,6},{9,8},{10,9},{11,10},{13,12},{... | collective-permute-start | bytes 983048 | tf_op jit(solution)/shard_map/ppermute | solution.py:16
  13.0 2.6 %copy-start.4 = (bf16[4,160,256]{2,1,0:T(8,128)(2,1)}, bf16[4,160,256]{2,1,0:T(8,128)(2,1)S(1)}, u32[]{:S(2)}) copy-start(bf16[4,160,256]{2,1,0:T(8,128)(2,1)S(1)} %collective-permute-done.above_ref.refs_7_) | copy-start | bytes 983044
  15.5 0.7 %copy-start.5 = (bf16[4,160,256]{2,1,0:T(8,128)(2,1)}, bf16[4,160,256]{2,1,0:T(8,128)(2,1)S(1)}, u32[]{:S(2)}) copy-start(bf16[4,160,256]{2,1,0:T(8,128)(2,1)S(1)} %collective-permute-done.1.below_ref.refs_9_) | copy-start | bytes 983044
  23.9 7.3 %collective-permute-start.7 = (bf16[10,160,256]{2,1,0:T(8,128)(2,1)}, bf16[10,160,256]{2,1,0:T(8,128)(2,1)}, u32[]{:S(2)}, u32[]{:S(2)}) collective-permute-start(bf16[10,160,256]{2,1,0:T(8,128)(2,1)} %shard_map.91.refs_2_), channel_id=1, source_target_pairs={{8,24},{20,4},{9,25},{21,5},{10,26},{22,6},{11,27},{23,7}} | collective-permute-start | bytes 2457608 | tf_op jit(solution)/shard_map/ppermute | solution.py:232
  25.5 21.2 %collective-permute-start.5 = (bf16[10,160,256]{2,1,0:T(8,128)(2,1)}, bf16[10,160,256]{2,1,0:T(8,128)(2,1)S(1)}, u32[]{:S(2)}, u32[]{:S(2)}) collective-permute-start(bf16[10,160,256]{2,1,0:T(8,128)(2,1)} %shard_map.91.refs_2_), channel_id=1, source_target_pairs={{8,0},{12,4},{16,8},{24,16},{28,20},{9,1},{13,5},{17,9},{25,17},{2... | collective-permute-start | bytes 2457608 | tf_op jit(solution)/shard_map/ppermute | solution.py:240
  29.2 20.7 %collective-permute-start.2 = (bf16[10,160,256]{2,1,0:T(8,128)(2,1)}, bf16[10,160,256]{2,1,0:T(8,128)(2,1)S(1)}, u32[]{:S(2)}, u32[]{:S(2)}) collective-permute-start(bf16[10,160,256]{2,1,0:T(8,128)(2,1)} %shard_map.91.refs_2_), channel_id=1, source_target_pairs={{0,8},{4,12},{12,20},{16,24},{20,28},{1,9},{5,13},{13,21},{17,25},... | collective-permute-start | bytes 2457608 | tf_op jit(solution)/shard_map/ppermute | solution.py:239
  30.5 34.4 %collective-permute-start.4 = (bf16[10,160,256]{2,1,0:T(8,128)(2,1)}, bf16[10,160,256]{2,1,0:T(8,128)(2,1)S(1)}, u32[]{:S(2)}, u32[]{:S(2)}) collective-permute-start(bf16[10,160,256]{2,1,0:T(8,128)(2,1)} %shard_map.91.refs_2_), channel_id=1, source_target_pairs={{0,4},{4,0},{8,12},{12,8},{16,20},{20,16},{24,28},{28,24},{1,5},{5... | collective-permute-start | bytes 2457608 | tf_op jit(solution)/shard_map/ppermute | solution.py:227
  31.2 33.7 %collective-permute-start.8 = (bf16[10,160,256]{2,1,0:T(8,128)(2,1)}, bf16[10,160,256]{2,1,0:T(8,128)(2,1)S(1)}, u32[]{:S(2)}, u32[]{:S(2)}) collective-permute-start(bf16[10,160,256]{2,1,0:T(8,128)(2,1)} %collective-permute-done.7), channel_id=1, source_target_pairs={{24,16},{4,12},{25,17},{5,13},{26,18},{6,14},{27,19},{7,15}} | collective-permute-start | bytes 2457608 | tf_op jit(solution)/shard_map/ppermute | solution.py:233
  46.7 18.3 %copy-start = (bf16[10,160,256]{2,1,0:T(8,128)(2,1)}, bf16[10,160,256]{2,1,0:T(8,128)(2,1)S(1)}, u32[]{:S(2)}) copy-start(bf16[10,160,256]{2,1,0:T(8,128)(2,1)S(1)} %collective-permute-done.5.refs_5_) | copy-start | bytes 2457604
  46.7 18.2 %collective-permute-start.6 = (bf16[10,160,256]{2,1,0:T(8,128)(2,1)S(1)}, bf16[10,160,256]{2,1,0:T(8,128)(2,1)}, u32[]{:S(2)}, u32[]{:S(2)}) collective-permute-start(bf16[10,160,256]{2,1,0:T(8,128)(2,1)S(1)} %collective-permute-done.5.refs_5_), channel_id=1, source_target_pairs={{0,4},{8,12},{16,20},{1,5},{9,13},{17,21},{2,6},{10,14},{18,22},{3... | collective-permute-start | bytes 2457608 | tf_op jit(solution)/shard_map/ppermute | solution.py:244
  49.9 15.1 %copy-start.1 = (bf16[10,160,256]{2,1,0:T(8,128)(2,1)}, bf16[10,160,256]{2,1,0:T(8,128)(2,1)S(1)}, u32[]{:S(2)}) copy-start(bf16[10,160,256]{2,1,0:T(8,128)(2,1)S(1)} %collective-permute-done.2.refs_0_) | copy-start | bytes 2457604
  49.9 15.0 %collective-permute-start.3 = (bf16[10,160,256]{2,1,0:T(8,128)(2,1)S(1)}, bf16[10,160,256]{2,1,0:T(8,128)(2,1)}, u32[]{:S(2)}, u32[]{:S(2)}) collective-permute-start(bf16[10,160,256]{2,1,0:T(8,128)(2,1)S(1)} %collective-permute-done.2.refs_0_), channel_id=1, source_target_pairs={{12,8},{20,16},{28,24},{13,9},{21,17},{29,25},{14,10},{22,18},{30,... | collective-permute-start | bytes 2457608 | tf_op jit(solution)/shard_map/ppermute | solution.py:243
  64.9 0.9 %copy-start.2 = (bf16[10,160,256]{2,1,0:T(8,128)(2,1)}, bf16[10,160,256]{2,1,0:T(8,128)(2,1)S(1)}, u32[]{:S(2)}) copy-start(bf16[10,160,256]{2,1,0:T(8,128)(2,1)S(1)} %collective-permute-done.4.refs_3_) | copy-start | bytes 2457604
  64.9 1.2 %copy-start.3 = (bf16[10,160,256]{2,1,0:T(8,128)(2,1)}, bf16[10,160,256]{2,1,0:T(8,128)(2,1)S(1)}, u32[]{:S(2)}) copy-start(bf16[10,160,256]{2,1,0:T(8,128)(2,1)S(1)} %collective-permute-done.8.refs_6_) | copy-start | bytes 2457604

commit v18 on v13

--- a/solution.py
+++ b/solution.py
@@ -66,16 +66,12 @@
     conv_rows(first_buf, w2_ref, stack, rows1 - 2, emit_second)
 
 
-def mix_kernel(coef_ref, fb_ref, rb_ref, own_ref, par_ref, ra_ref, fa_ref, routed_ref,
-               above_ref, frame_ref, below_ref, w3_ref, out_ref, fbuf, mixed_buf, stack):
+def join_kernel(coef_ref, fb_ref, rb_ref, own_ref, par_ref, ra_ref, fa_ref, routed_ref, frame_ref,
+                mixed_ref, top_ref, bottom_ref):
+    f32 = jnp.float32
     block = frame_ref.shape[0]
-    fbuf[0:1] = above_ref[...]
-    fbuf[1 : block + 1] = frame_ref[...]
-    fbuf[block + 1 :] = below_ref[...]
-    f32 = jnp.float32
-    step = stack.shape[0]
-    for r0 in range(0, block + 2, step):
-        rows = pl.ds(r0, min(step, block + 2 - r0))
+    for r0 in range(0, block, 2):
+        rows = pl.ds(r0, 2)
         summed = (
             coef_ref[0] * fb_ref[rows].astype(f32)
             + coef_ref[1] * rb_ref[rows].astype(f32)
@@ -85,12 +81,33 @@
             + coef_ref[5] * fa_ref[rows].astype(f32)
             + coef_ref[6] * routed_ref[rows].astype(f32)
         )
-        mixed_buf[rows] = (summed * fbuf[rows].astype(f32)).astype(jnp.bfloat16)
-
+        mixed_ref[rows] = (summed * frame_ref[rows].astype(f32)).astype(jnp.bfloat16)
+    top_ref[...] = mixed_ref[0:1]
+    bottom_ref[...] = mixed_ref[block - 1 :]
+
+
+def interior_kernel(mixed_ref, w3_ref, out_ref, stack):
     def emit(r0, n, value):
         out_ref[r0 : r0 + n] = value.astype(jnp.bfloat16)
 
-    conv_rows(mixed_buf, w3_ref, stack, block, emit)
+    conv_rows(mixed_ref, w3_ref, stack, mixed_ref.shape[0] - 2, emit)
+
+
+def edges_kernel(above_ref, mixed_ref, below_ref, inner_ref, w3_ref, out_ref, ext, stack):
+    block = mixed_ref.shape[0]
+
+    def emit_at(row):
+        def emit(r0, n, value):
+            out_ref[row : row + 1] = value.astype(jnp.bfloat16)
+        return emit
+
+    ext[0:1] = above_ref[...]
+    ext[1:3] = mixed_ref[0:2]
+    conv_rows(ext, w3_ref, stack, 1, emit_at(0))
+    ext[0:2] = mixed_ref[block - 2 :]
+    ext[2:3] = below_ref[...]
+    conv_rows(ext, w3_ref, stack, 1, emit_at(block - 1))
+    out_ref[1 : block - 1] = inner_ref[...]
 
 
 def vmem():
@@ -122,20 +139,40 @@
     )(bounds, above, image, below, w1, w2)
 
 
-def mix(coef, fb, rb, own, par, ra, fa, routed, above, frame, below, w3):
+def join(coef, fb, rb, own, par, ra, fa, routed, frame):
     block, cols, c = frame.shape
-    flops = 2 * 9 * c * c * cols * block
+    row = jax.ShapeDtypeStruct((1, cols, c), jnp.bfloat16)
     return pl.pallas_call(
-        mix_kernel,
+        join_kernel,
+        out_shape=(jax.ShapeDtypeStruct((block, cols, c), jnp.bfloat16), row, row),
+        in_specs=[smem()] + [vmem()] * 8,
+        out_specs=(vmem(), vmem(), vmem()),
+        cost_estimate=pl.CostEstimate(flops=16 * block * cols * c, transcendentals=0,
+                                      bytes_accessed=18 * block * cols * c),
+    )(coef, fb, rb, own, par, ra, fa, routed, frame)
+
+
+def frame_conv(mixed, from_above, from_below, w3):
+    block, cols, c = mixed.shape
+    inner = pl.pallas_call(
+        interior_kernel,
+        out_shape=jax.ShapeDtypeStruct((block - 2, cols, c), jnp.bfloat16),
+        in_specs=[vmem()] * 2,
+        out_specs=vmem(),
+        scratch_shapes=[pltpu.VMEM((CHUNK, cols, 3 * c), jnp.bfloat16)],
+        cost_estimate=pl.CostEstimate(flops=2 * 9 * c * c * cols * (block - 2), transcendentals=0,
+                                      bytes_accessed=4 * block * cols * c + 2 * 9 * c * c),
+    )(mixed, w3)
+    return pl.pallas_call(
+        edges_kernel,
         out_shape=jax.ShapeDtypeStruct((block, cols, c), jnp.bfloat16),
-        in_specs=[smem()] + [vmem()] * 11,
+        in_specs=[vmem()] * 5,
         out_specs=vmem(),
-        scratch_shapes=[pltpu.VMEM((block + 2, cols, c), jnp.bfloat16),
-                        pltpu.VMEM((block + 2, cols, c), jnp.bfloat16),
-                        pltpu.VMEM((CHUNK, cols, 3 * c), jnp.bfloat16)],
-        cost_estimate=pl.CostEstimate(flops=flops, transcendentals=0,
-                                      bytes_accessed=18 * (block + 2) * cols * c + 2 * 9 * c * c),
-    )(coef, fb, rb, own, par, ra, fa, routed, above, frame, below, w3)
+        scratch_shapes=[pltpu.VMEM((3, cols, c), jnp.bfloat16),
+                        pltpu.VMEM((1, cols, 3 * c), jnp.bfloat16)],
+        cost_estimate=pl.CostEstimate(flops=2 * 9 * c * c * cols * 2, transcendentals=0,
+                                      bytes_accessed=4 * block * cols * c + 2 * 9 * c * c),
+    )(from_above, mixed, from_below, inner, w3)
 
 
 def shards(
@@ -154,10 +191,8 @@
     height = block * lax.axis_size("rows")
     row0 = lax.axis_index("rows") * block
 
-    image_above = shifted(image[block - 3 :], "rows", 1)
-    image_below = shifted(image[:3], "rows", -1)
-    frame_above = shifted(frame[block - 1 :], "rows", 1)
-    frame_below = shifted(frame[:1], "rows", -1)
+    from_above = shifted(image[block - 2 :], "rows", 1)
+    from_below = shifted(image[:2], "rows", -1)
 
     count = lax.axis_size("tm")
     t = lax.axis_index("tm")
@@ -172,10 +207,10 @@
     partner_weight = jnp.where(is_odd, weights[1], weights[3])
     routed_weight = jnp.where(is_odd, weights[4], weights[0])
     coef = jnp.concatenate([weights[:3], partner_weight[None], weights[3:], routed_weight[None]])
-    bounds = jnp.stack([2 - row0, height - row0 + 2]).astype(jnp.int32)
+    bounds = jnp.stack([1 - row0, height - row0 + 1]).astype(jnp.int32)
     coef, bounds, image = lax.optimization_barrier((coef, bounds, image))
 
-    second = layers(bounds, image_above, image, image_below, conv_first, conv_second)
+    second = layers(bounds, from_above, image, from_below, conv_first, conv_second)
 
     partner = lax.ppermute(second, "tm", [(i, i ^ 1) for i in range(count)])
     if count == 8:
@@ -189,8 +224,11 @@
         routed = jnp.zeros_like(second)
     relay_behind = lax.ppermute(from_behind, "tm", [(i + 1, i) for i in range(2, count, 2)])
     relay_ahead = lax.ppermute(from_ahead, "tm", [(i, i + 1) for i in range(0, count - 2, 2)])
-    result = mix(coef, from_behind, relay_behind, second, partner, relay_ahead, from_ahead, routed,
-                 frame_above, frame, frame_below, conv_frame)
+    mixed, top, bottom = join(coef, from_behind, relay_behind, second, partner, relay_ahead,
+                              from_ahead, routed, frame)
+    mixed_above = shifted(bottom, "rows", 1)
+    mixed_below = shifted(top, "rows", -1)
+    result = frame_conv(mixed, mixed_above, mixed_below, conv_frame)
     return result[None]
 
 

time: 82.8 us -> 75.9 us (0.917)
  waiting for transfers between devices: 36.7 us -> 25 us
  Pallas kernels: 13.9 us -> 18 us
  starting transfers between devices: 18.4 us -> 19.9 us
  local copies, waits for them, and re-layouts: 6.03 us -> 5.19 us
    ppermute x4, waiting for transfers between devices: 9.08 us -> 0.01 us  [shifted(): return lax.ppermute(value, axis, pairs)]
    pallas_call x1 -> x3, Pallas kernels: 6.32 us -> 11.3 us  [the longest x1 4.67 us: join(): pl.pallas_call(join_kernel, out_shape=(jax.ShapeDtypeStruct((block, cols,...]
    ppermute x1, waiting for transfers between devices: 0.01 us -> 2.63 us  [shards(): lax.ppermute(from_behind, 'tm', [(i + 1, i) for i in range(2, count, 2)])]
    ppermute x1, waiting for transfers between devices: 6.09 us -> 4.33 us  [shards(): lax.ppermute(second, 'tm', [(2, 0), (3, 1), (4, 2), (6, 4), (7, 5)])]
    ppermute x1, waiting for transfers between devices: 12.1 us -> 10.4 us  [shards(): lax.ppermute(second, 'tm', [(0, 2), (1, 3), (3, 5), (4, 6), (5, 7)])]
    ppermute x1, waiting for transfers between devices: 9.4 us -> 7.67 us  [shards(): hop = lax.ppermute(second, 'tm', [(2, 6), (5, 1)])]
    ppermute x4, starting transfers between devices: 10.1 us -> 11.7 us  [shifted(): return lax.ppermute(value, axis, pairs)]
    slice x2 -> x1, local copies, waits for them, and re-layouts: 2.03 us -> 1.02 us  [shards(): from_below = shifted(image[:2], 'rows', -1)]
  transfers between devices with their start and end apart: 11 -> 11, of which waited for: 5 -> 4; matrix products, arithmetic and copies ran while one was open for 6% -> 5% of each run, Pallas kernels for 0% -> 5%
where the time goes in v18:
time: 75.9 us; the launch traced here: 75.5 us
  waiting for transfers between devices  25 us (33%)
  starting transfers between devices  19.9 us (26%)
  Pallas kernels  18 us (24%)
  local copies, waits for them, and re-layouts  5.19 us (7%)
  between operations  4.01 us (5%)
  other arithmetic  3.29 us (4%)
    ppermute x4, starting transfers between devices, shifted(): return lax.ppermute(value, axis, pairs)  11.7 us
    ppermute x1, waiting for transfers between devices, shards(): lax.ppermute(second, 'tm', [(0, 2), (1, 3), (3, 5), (4, 6), (5, 7)])  10.4 us
    ppermute x1, waiting for transfers between devices, shards(): hop = lax.ppermute(second, 'tm', [(2, 6), (5, 1)])  7.67 us
    pallas_call x1, Pallas kernels, layers(): pl.pallas_call(layers_kernel, out_shape=jax.ShapeDtypeStruct((rows - 4, c...  6.69 us
    pallas_call x1, Pallas kernels, join(): pl.pallas_call(join_kernel, out_shape=(jax.ShapeDtypeStruct((block, cols,...  4.67 us
    ppermute x1, waiting for transfers between devices, shards(): lax.ppermute(second, 'tm', [(2, 0), (3, 1), (4, 2), (6, 4), (7, 5)])  4.33 us
    pallas_call x1, Pallas kernels, frame_conv(): pl.pallas_call(interior_kernel, out_shape=jax.ShapeDtypeStruct((block - 2...  3.6 us
    unnamed x20, local copies, waits for them, and re-layouts  3.43 us
  transfers between devices with their start and end apart: 11, of which 4 were waited for; matrix products, arithmetic and copies ran while one was open for 5% of the time, Pallas kernels for 5%

profile of v18, /device:TPU:22, one launch (start us, length us, event | category | flops | bytes accessed | tf_op | source)
XLA Modules:
  0.0 75.5 jit_solution(15150418892695071159)
XLA Ops:
  0.0 1.0 %slice_bitcast_fusion = (bf16[2,160,256]{2,1,0:T(8,128)(2,1)S(1)}, bf16[2,160,256]{2,1,0:T(8,128)(2,1)S(1)}) fusion(bf16[1,8,160,256]{3,2,1,0:T(8,128)(2,1)} %param.8), kind=kLoop, calls=%fused_computation | loop fusion | bytes 655360 | tf_op jit(solution)/shard_map/slice | solution.py:195
  1.0 2.4 %collective-permute-start.1 = (bf16[2,160,256]{2,1,0:T(8,128)(2,1)S(1)}, bf16[2,160,256]{2,1,0:T(8,128)(2,1)S(1)}, u32[]{:S(2)}, u32[]{:S(2)}) collective-permute-start(bf16[2,160,256]{2,1,0:T(8,128)(2,1)S(1)} %get-tuple-element.19), channel_id=1, source_target_pairs={{1,0},{2,1},{3,2},{5,4},{6,5},{7,6},{9,8},{10,9},{11,10},{13,12},{... | collective-permute-start | bytes 491528 | tf_op jit(solution)/shard_map/ppermute | solution.py:16
  3.4 3.5 %collective-permute-start = (bf16[2,160,256]{2,1,0:T(8,128)(2,1)S(1)}, bf16[2,160,256]{2,1,0:T(8,128)(2,1)S(1)}, u32[]{:S(2)}, u32[]{:S(2)}) collective-permute-start(bf16[2,160,256]{2,1,0:T(8,128)(2,1)S(1)} %get-tuple-element.20), channel_id=1, source_target_pairs={{0,1},{1,2},{2,3},{4,5},{5,6},{6,7},{8,9},{9,10},{10,11},{12,13},{... | collective-permute-start | bytes 491528 | tf_op jit(solution)/shard_map/ppermute | solution.py:16
  8.2 1.3 %fusion = (f32[]{:T(128)}, f32[5]{0:T(128)S(1)}) fusion(s32[1,5]{1,0:T(1,128)} %param.12, s32[]{:T(128)} %bitcast.22, s32[]{:T(128)} %bitcast.21, s32[]{:T(128)S(6)} %axis_index.23), kind=kLoop, calls=%fused_computation.6 | loop fusion | flops 39 | bytes 56 | tf_op jit(solution)/shard_map/reduce_sum | solution.py:205
  9.5 0.7 broadcast_divide_fusion
  10.2 0.7 fusion.1
  10.9 0.6 pad_add_fusion.bounds_ref
  11.5 0.1 slice.33
  14.1 0.7 pad_maximum_fusion.coef_ref
  14.8 0.0 collective-permute-done.1.below_ref
  14.8 0.0 copy-start.8
  14.8 0.0 collective-permute-done.above_ref
  14.8 0.7 copy-done.8
  15.4 0.0 copy-start.9
  15.4 0.7 copy-done.9
  16.1 6.7 %shard_map.82.own_ref = bf16[8,160,256]{2,1,0:T(8,128)(2,1)} custom-call(s32[2]{0:T(128)} %pad_add_fusion.bounds_ref, bf16[2,160,256]{2,1,0:T(8,128)(2,1)} %copy-done.9, bf16[8,160,256]{2,1,0:T(8,128)(2,1)} %bitcast.24, bf16[2,160,256]{2,1,0:T(8,128)(2,1)} %copy-done.8, bf16[3,3,256,256]{3,2,1,0:T(8,128)(2,1)} %w1_ref.1, bf16[3,3,256,256]{3,2,1,0:T(8,128)(2,1)} %w2_ref.1), custom_call_target="tpu_custom_call" | custom-call | flops 3397386240 | bytes 4325376 | tf_op jit(solution)/shard_map/pallas_call | solution.py:129
  22.8 1.3 %collective-permute-start.7 = (bf16[8,160,256]{2,1,0:T(8,128)(2,1)}, bf16[8,160,256]{2,1,0:T(8,128)(2,1)S(1)}, u32[]{:S(2)}, u32[]{:S(2)}) collective-permute-start(bf16[8,160,256]{2,1,0:T(8,128)(2,1)} %shard_map.82.own_ref), channel_id=1, source_target_pairs={{8,24},{20,4},{9,25},{21,5},{10,26},{22,6},{11,27},{23,7}} | collective-permute-start | bytes 1966088 | tf_op jit(solution)/shard_map/ppermute | solution.py:219
  24.1 1.9 %collective-permute-start.5 = (bf16[8,160,256]{2,1,0:T(8,128)(2,1)}, bf16[8,160,256]{2,1,0:T(8,128)(2,1)S(1)}, u32[]{:S(2)}, u32[]{:S(2)}) collective-permute-start(bf16[8,160,256]{2,1,0:T(8,128)(2,1)} %shard_map.82.own_ref), channel_id=1, source_target_pairs={{8,0},{12,4},{16,8},{24,16},{28,20},{9,1},{13,5},{17,9},{25,17},{2... | collective-permute-start | bytes 1966088 | tf_op jit(solution)/shard_map/ppermute | solution.py:218
  26.0 1.3 %collective-permute-start.2 = (bf16[8,160,256]{2,1,0:T(8,128)(2,1)}, bf16[8,160,256]{2,1,0:T(8,128)(2,1)S(1)}, u32[]{:S(2)}, u32[]{:S(2)}) collective-permute-start(bf16[8,160,256]{2,1,0:T(8,128)(2,1)} %shard_map.82.own_ref), channel_id=1, source_target_pairs={{0,8},{4,12},{12,20},{16,24},{20,28},{1,9},{5,13},{13,21},{17,25},... | collective-permute-start | bytes 1966088 | tf_op jit(solution)/shard_map/ppermute | solution.py:217
  27.3 0.5 collective-permute-start.4
  27.8 7.7 %collective-permute-done.7 = bf16[8,160,256]{2,1,0:T(8,128)(2,1)S(1)} collective-permute-done((bf16[8,160,256]{2,1,0:T(8,128)(2,1)}, bf16[8,160,256]{2,1,0:T(8,128)(2,1)S(1)}, u32[]{:S(2)}, u32[]{:S(2)}) %collective-permute-start.7) | collective-permute-done | bytes 655392 | tf_op jit(solution)/shard_map/ppermute | solution.py:219
  35.5 1.3 %collective-permute-start.8 = (bf16[8,160,256]{2,1,0:T(8,128)(2,1)S(1)}, bf16[8,160,256]{2,1,0:T(8,128)(2,1)S(1)}, u32[]{:S(2)}, u32[]{:S(2)}) collective-permute-start(bf16[8,160,256]{2,1,0:T(8,128)(2,1)S(1)} %collective-permute-done.7), channel_id=1, source_target_pairs={{24,16},{4,12},{25,17},{5,13},{26,18},{6,14},{27,19},{7,15}} | collective-permute-start | bytes 1966088 | tf_op jit(solution)/shard_map/ppermute | solution.py:220
  36.8 4.3 %collective-permute-done.5.fa_ref = bf16[8,160,256]{2,1,0:T(8,128)(2,1)S(1)} collective-permute-done((bf16[8,160,256]{2,1,0:T(8,128)(2,1)}, bf16[8,160,256]{2,1,0:T(8,128)(2,1)S(1)}, u32[]{:S(2)}, u32[]{:S(2)}) %collective-permute-start.5) | collective-permute-done | bytes 655392 | tf_op jit(solution)/shard_map/ppermute | solution.py:218
  41.1 0.7 collective-permute-start.6
  41.8 10.4 %collective-permute-done.2.fb_ref = bf16[8,160,256]{2,1,0:T(8,128)(2,1)S(1)} collective-permute-done((bf16[8,160,256]{2,1,0:T(8,128)(2,1)}, bf16[8,160,256]{2,1,0:T(8,128)(2,1)S(1)}, u32[]{:S(2)}, u32[]{:S(2)}) %collective-permute-start.2) | collective-permute-done | bytes 655392 | tf_op jit(solution)/shard_map/ppermute | solution.py:217
  52.2 1.3 %collective-permute-start.3 = (bf16[8,160,256]{2,1,0:T(8,128)(2,1)S(1)}, bf16[8,160,256]{2,1,0:T(8,128)(2,1)S(1)}, u32[]{:S(2)}, u32[]{:S(2)}) collective-permute-start(bf16[8,160,256]{2,1,0:T(8,128)(2,1)S(1)} %collective-permute-done.2.fb_ref), channel_id=1, source_target_pairs={{12,8},{20,16},{28,24},{13,9},{21,17},{29,25},{14,10},{22,18},{30,... | collective-permute-start | bytes 1966088 | tf_op jit(solution)/shard_map/ppermute | solution.py:225
  53.5 0.0 collective-permute-done.4.par_ref
  53.5 0.0 copy-start.2
  53.5 0.0 collective-permute-done.8.routed_ref
  53.5 0.0 copy-start.3
  53.5 0.0 collective-permute-done.6.ra_ref
  53.5 0.0 copy-start.4
  53.5 2.6 %collective-permute-done.3.rb_ref = bf16[8,160,256]{2,1,0:T(8,128)(2,1)S(1)} collective-permute-done((bf16[8,160,256]{2,1,0:T(8,128)(2,1)S(1)}, bf16[8,160,256]{2,1,0:T(8,128)(2,1)S(1)}, u32[]{:S(2)}, u32[]{:S(2)}) %collective-permute-start.3) | collective-permute-done | bytes 655392 | tf_op jit(solution)/shard_map/ppermute | solution.py:225
  56.2 0.8 %copy-done.5 = bf16[8,160,256]{2,1,0:T(8,128)(2,1)} copy-done((bf16[8,160,256]{2,1,0:T(8,128)(2,1)}, bf16[8,160,256]{2,1,0:T(8,128)(2,1)S(1)}, u32[]{:S(2)}) %copy-start.5) | copy-done | bytes 655384
  57.0 0.0 copy-done
  57.0 0.0 copy-done.1
  57.0 0.0 copy-done.2
  57.0 0.0 copy-done.3
  57.0 0.0 copy-done.4
  57.0 4.7 %shard_map.83 = (bf16[8,160,256]{2,1,0:T(8,128)(2,1)}, bf16[1,160,256]{2,1,0:T(8,128)(2,1)}, bf16[1,160,256]{2,1,0:T(8,128)(2,1)}) custom-call(f32[7]{0:T(128)} %pad_maximum_fusion.coef_ref, bf16[8,160,256]{2,1,0:T(8,128)(2,1)} %copy-done.1, bf16[8,160,256]{2,1,0:T(8,128)(2,1)} %copy-done.5, bf16[8,160,256]{2,1,0:T(8,128)(2,1)} %shard_map.82.own_ref, ...), custom_call_target="tpu_custom_call" | custom-call | flops 5242880 | bytes 5898240 | tf_op jit(solution)/shard_map/pallas_call | solution.py:145
  61.7 1.9 %collective-permute-start.9 = (bf16[1,160,256]{2,1,0:T(8,128)(2,1)}, bf16[1,160,256]{2,1,0:T(8,128)(2,1)S(1)}, u32[]{:S(2)}, u32[]{:S(2)}) collective-permute-start(bf16[1,160,256]{2,1,0:T(8,128)(2,1)} %get-tuple-element.14), channel_id=1, source_target_pairs={{0,1},{1,2},{2,3},{4,5},{5,6},{6,7},{8,9},{9,10},{10,11},{12,13},{... | collective-permute-start | bytes 245768 | tf_op jit(solution)/shard_map/ppermute | solution.py:16
  63.6 3.9 %collective-permute-start.10 = (bf16[1,160,256]{2,1,0:T(8,128)(2,1)}, bf16[1,160,256]{2,1,0:T(8,128)(2,1)S(1)}, u32[]{:S(2)}, u32[]{:S(2)}) collective-permute-start(bf16[1,160,256]{2,1,0:T(8,128)(2,1)} %get-tuple-element.16), channel_id=1, source_target_pairs={{1,0},{2,1},{3,2},{5,4},{6,5},{7,6},{9,8},{10,9},{11,10},{13,12},{... | collective-permute-start | bytes 245768 | tf_op jit(solution)/shard_map/ppermute | solution.py:16
  67.5 3.6 %shard_map.84.inner_ref = bf16[6,160,256]{2,1,0:T(8,128)(2,1)} custom-call(bf16[8,160,256]{2,1,0:T(8,128)(2,1)} %get-tuple-element.15.mixed_ref, bf16[3,3,256,256]{3,2,1,0:T(8,128)(2,1)} %w3_ref.3), custom_call_target="tpu_custom_call" | custom-call | flops 1132462080 | bytes 2490368 | tf_op jit(solution)/shard_map/pallas_call | solution.py:157
  71.1 0.0 collective-permute-done.9.above_ref
  71.1 0.0 collective-permute-done.10.below_ref
  71.1 0.6 copy-done.6
  71.8 0.6 copy-done.7
  72.4 3.1 %shard_map.85 = bf16[8,160,256]{2,1,0:T(8,128)(2,1)} custom-call(bf16[1,160,256]{2,1,0:T(8,128)(2,1)} %copy-done.6, bf16[8,160,256]{2,1,0:T(8,128)(2,1)} %get-tuple-element.15.mixed_ref, bf16[1,160,256]{2,1,0:T(8,128)(2,1)} %copy-done.7, bf16[6,160,256]{2,1,0:T(8,128)(2,1)} %shard_map.84.inner_ref, bf16[3,3,256,256]{3,2,1,0:T(8,128)(2,1)} %w3_ref.3), custom_call_target="tpu_custom_call" | custom-call | flops 377487360 | bytes 2490368 | tf_op jit(solution)/shard_map/pallas_call | solution.py:166
  (5 shorter events, 0.0 us)
Async XLA Ops:
  1.0 13.7 %collective-permute-start.1 = (bf16[2,160,256]{2,1,0:T(8,128)(2,1)S(1)}, bf16[2,160,256]{2,1,0:T(8,128)(2,1)S(1)}, u32[]{:S(2)}, u32[]{:S(2)}) collective-permute-start(bf16[2,160,256]{2,1,0:T(8,128)(2,1)S(1)} %get-tuple-element.19), channel_id=1, source_target_pairs={{1,0},{2,1},{3,2},{5,4},{6,5},{7,6},{9,8},{10,9},{11,10},{13,12},{... | collective-permute-start | bytes 491528 | tf_op jit(solution)/shard_map/ppermute | solution.py:16
  3.4 11.4 %collective-permute-start = (bf16[2,160,256]{2,1,0:T(8,128)(2,1)S(1)}, bf16[2,160,256]{2,1,0:T(8,128)(2,1)S(1)}, u32[]{:S(2)}, u32[]{:S(2)}) collective-permute-start(bf16[2,160,256]{2,1,0:T(8,128)(2,1)S(1)} %get-tuple-element.20), channel_id=1, source_target_pairs={{0,1},{1,2},{2,3},{4,5},{5,6},{6,7},{8,9},{9,10},{10,11},{12,13},{... | collective-permute-start | bytes 491528 | tf_op jit(solution)/shard_map/ppermute | solution.py:16
  14.8 0.7 copy-start.8
  15.4 0.7 copy-start.9
  22.8 12.7 %collective-permute-start.7 = (bf16[8,160,256]{2,1,0:T(8,128)(2,1)}, bf16[8,160,256]{2,1,0:T(8,128)(2,1)S(1)}, u32[]{:S(2)}, u32[]{:S(2)}) collective-permute-start(bf16[8,160,256]{2,1,0:T(8,128)(2,1)} %shard_map.82.own_ref), channel_id=1, source_target_pairs={{8,24},{20,4},{9,25},{21,5},{10,26},{22,6},{11,27},{23,7}} | collective-permute-start | bytes 1966088 | tf_op jit(solution)/shard_map/ppermute | solution.py:219
  24.1 17.0 %collective-permute-start.5 = (bf16[8,160,256]{2,1,0:T(8,128)(2,1)}, bf16[8,160,256]{2,1,0:T(8,128)(2,1)S(1)}, u32[]{:S(2)}, u32[]{:S(2)}) collective-permute-start(bf16[8,160,256]{2,1,0:T(8,128)(2,1)} %shard_map.82.own_ref), channel_id=1, source_target_pairs={{8,0},{12,4},{16,8},{24,16},{28,20},{9,1},{13,5},{17,9},{25,17},{2... | collective-permute-start | bytes 1966088 | tf_op jit(solution)/shard_map/ppermute | solution.py:218
  26.0 26.2 %collective-permute-start.2 = (bf16[8,160,256]{2,1,0:T(8,128)(2,1)}, bf16[8,160,256]{2,1,0:T(8,128)(2,1)S(1)}, u32[]{:S(2)}, u32[]{:S(2)}) collective-permute-start(bf16[8,160,256]{2,1,0:T(8,128)(2,1)} %shard_map.82.own_ref), channel_id=1, source_target_pairs={{0,8},{4,12},{12,20},{16,24},{20,28},{1,9},{5,13},{13,21},{17,25},... | collective-permute-start | bytes 1966088 | tf_op jit(solution)/shard_map/ppermute | solution.py:217
  27.3 26.2 %collective-permute-start.4 = (bf16[8,160,256]{2,1,0:T(8,128)(2,1)}, bf16[8,160,256]{2,1,0:T(8,128)(2,1)S(1)}, u32[]{:S(2)}, u32[]{:S(2)}) collective-permute-start(bf16[8,160,256]{2,1,0:T(8,128)(2,1)} %shard_map.82.own_ref), channel_id=1, source_target_pairs={{0,4},{4,0},{8,12},{12,8},{16,20},{20,16},{24,28},{28,24},{1,5},{5... | collective-permute-start | bytes 1966088 | tf_op jit(solution)/shard_map/ppermute | solution.py:215
  35.5 18.0 %collective-permute-start.8 = (bf16[8,160,256]{2,1,0:T(8,128)(2,1)S(1)}, bf16[8,160,256]{2,1,0:T(8,128)(2,1)S(1)}, u32[]{:S(2)}, u32[]{:S(2)}) collective-permute-start(bf16[8,160,256]{2,1,0:T(8,128)(2,1)S(1)} %collective-permute-done.7), channel_id=1, source_target_pairs={{24,16},{4,12},{25,17},{5,13},{26,18},{6,14},{27,19},{7,15}} | collective-permute-start | bytes 1966088 | tf_op jit(solution)/shard_map/ppermute | solution.py:220
  41.1 15.9 %copy-start = (bf16[8,160,256]{2,1,0:T(8,128)(2,1)}, bf16[8,160,256]{2,1,0:T(8,128)(2,1)S(1)}, u32[]{:S(2)}) copy-start(bf16[8,160,256]{2,1,0:T(8,128)(2,1)S(1)} %collective-permute-done.5.fa_ref) | copy-start | bytes 1966084
  41.1 12.4 %collective-permute-start.6 = (bf16[8,160,256]{2,1,0:T(8,128)(2,1)S(1)}, bf16[8,160,256]{2,1,0:T(8,128)(2,1)S(1)}, u32[]{:S(2)}, u32[]{:S(2)}) collective-permute-start(bf16[8,160,256]{2,1,0:T(8,128)(2,1)S(1)} %collective-permute-done.5.fa_ref), channel_id=1, source_target_pairs={{0,4},{8,12},{16,20},{1,5},{9,13},{17,21},{2,6},{10,14},{18,22},{3... | collective-permute-start | bytes 1966088 | tf_op jit(solution)/shard_map/ppermute | solution.py:226
  52.2 4.8 %copy-start.1 = (bf16[8,160,256]{2,1,0:T(8,128)(2,1)}, bf16[8,160,256]{2,1,0:T(8,128)(2,1)S(1)}, u32[]{:S(2)}) copy-start(bf16[8,160,256]{2,1,0:T(8,128)(2,1)S(1)} %collective-permute-done.2.fb_ref) | copy-start | bytes 1966084
  52.2 4.0 %collective-permute-start.3 = (bf16[8,160,256]{2,1,0:T(8,128)(2,1)S(1)}, bf16[8,160,256]{2,1,0:T(8,128)(2,1)S(1)}, u32[]{:S(2)}, u32[]{:S(2)}) collective-permute-start(bf16[8,160,256]{2,1,0:T(8,128)(2,1)S(1)} %collective-permute-done.2.fb_ref), channel_id=1, source_target_pairs={{12,8},{20,16},{28,24},{13,9},{21,17},{29,25},{14,10},{22,18},{30,... | collective-permute-start | bytes 1966088 | tf_op jit(solution)/shard_map/ppermute | solution.py:225
  53.5 3.5 %copy-start.2 = (bf16[8,160,256]{2,1,0:T(8,128)(2,1)}, bf16[8,160,256]{2,1,0:T(8,128)(2,1)S(1)}, u32[]{:S(2)}) copy-start(bf16[8,160,256]{2,1,0:T(8,128)(2,1)S(1)} %collective-permute-done.4.par_ref) | copy-start | bytes 1966084
  53.5 3.5 %copy-start.3 = (bf16[8,160,256]{2,1,0:T(8,128)(2,1)}, bf16[8,160,256]{2,1,0:T(8,128)(2,1)S(1)}, u32[]{:S(2)}) copy-start(bf16[8,160,256]{2,1,0:T(8,128)(2,1)S(1)} %collective-permute-done.8.routed_ref) | copy-start | bytes 1966084
  53.5 3.5 %copy-start.4 = (bf16[8,160,256]{2,1,0:T(8,128)(2,1)}, bf16[8,160,256]{2,1,0:T(8,128)(2,1)S(1)}, u32[]{:S(2)}) copy-start(bf16[8,160,256]{2,1,0:T(8,128)(2,1)S(1)} %collective-permute-done.6.ra_ref) | copy-start | bytes 1966084
  56.2 0.8 %copy-start.5 = (bf16[8,160,256]{2,1,0:T(8,128)(2,1)}, bf16[8,160,256]{2,1,0:T(8,128)(2,1)S(1)}, u32[]{:S(2)}) copy-start(bf16[8,160,256]{2,1,0:T(8,128)(2,1)S(1)} %collective-permute-done.3.rb_ref) | copy-start | bytes 1966084
  61.7 9.5 %collective-permute-start.9 = (bf16[1,160,256]{2,1,0:T(8,128)(2,1)}, bf16[1,160,256]{2,1,0:T(8,128)(2,1)S(1)}, u32[]{:S(2)}, u32[]{:S(2)}) collective-permute-start(bf16[1,160,256]{2,1,0:T(8,128)(2,1)} %get-tuple-element.14), channel_id=1, source_target_pairs={{0,1},{1,2},{2,3},{4,5},{5,6},{6,7},{8,9},{9,10},{10,11},{12,13},{... | collective-permute-start | bytes 245768 | tf_op jit(solution)/shard_map/ppermute | solution.py:16
  63.6 7.5 %collective-permute-start.10 = (bf16[1,160,256]{2,1,0:T(8,128)(2,1)}, bf16[1,160,256]{2,1,0:T(8,128)(2,1)S(1)}, u32[]{:S(2)}, u32[]{:S(2)}) collective-permute-start(bf16[1,160,256]{2,1,0:T(8,128)(2,1)} %get-tuple-element.16), channel_id=1, source_target_pairs={{1,0},{2,1},{3,2},{5,4},{6,5},{7,6},{9,8},{10,9},{11,10},{13,12},{... | collective-permute-start | bytes 245768 | tf_op jit(solution)/shard_map/ppermute | solution.py:16
  71.1 0.6 copy-start.6
  71.8 0.6 copy-start.7

commit v19 on v11

--- a/solution.py
+++ b/solution.py
@@ -66,7 +66,7 @@
     conv_rows(first_buf, w2_ref, stack, rows1 - 2, emit_second)
 
 
-def mix_kernel(coef_ref, fb_ref, rb_ref, own_ref, par_ref, ra_ref, fa_ref, routed_ref,
+def mix_kernel(coef_ref, fb_ref, fbo_ref, rb_ref, own_ref, par_ref, ra_ref, fa_ref, routed_ref,
                above_ref, frame_ref, below_ref, w3_ref, out_ref, fbuf, mixed_buf, stack):
     halo = below_ref.shape[0] - 1
     block = frame_ref.shape[0]
@@ -78,7 +78,7 @@
     for r0 in range(0, block + 2, step):
         rows = pl.ds(r0, min(step, block + 2 - r0))
         summed = (
-            coef_ref[0] * fb_ref[rows].astype(f32)
+            coef_ref[0] * (fb_ref[rows].astype(f32) + fbo_ref[rows].astype(f32))
             + coef_ref[1] * rb_ref[rows].astype(f32)
             + coef_ref[2] * own_ref[rows].astype(f32)
             + coef_ref[3] * par_ref[rows].astype(f32)
@@ -123,20 +123,20 @@
     )(bounds, above, image, below, w1, w2)
 
 
-def mix(coef, fb, rb, own, par, ra, fa, routed, above, frame, below, w3):
+def mix(coef, fb, fbo, rb, own, par, ra, fa, routed, above, frame, below, w3):
     block, cols, c = frame.shape
     flops = 2 * 9 * c * c * cols * block
     return pl.pallas_call(
         mix_kernel,
         out_shape=jax.ShapeDtypeStruct((block, cols, c), jnp.bfloat16),
-        in_specs=[smem()] + [vmem()] * 11,
+        in_specs=[smem()] + [vmem()] * 12,
         out_specs=vmem(),
         scratch_shapes=[pltpu.VMEM((block + 2, cols, c), jnp.bfloat16),
                         pltpu.VMEM((block + 2, cols, c), jnp.bfloat16),
                         pltpu.VMEM((CHUNK, cols, 3 * c), jnp.bfloat16)],
         cost_estimate=pl.CostEstimate(flops=flops, transcendentals=0,
                                       bytes_accessed=18 * (block + 2) * cols * c + 2 * 9 * c * c),
-    )(coef, fb, rb, own, par, ra, fa, routed, above, frame, below, w3)
+    )(coef, fb, fbo, rb, own, par, ra, fa, routed, above, frame, below, w3)
 
 
 def shards(
@@ -180,18 +180,20 @@
 
     partner = lax.ppermute(second, "tm", [(i, i ^ 1) for i in range(count)])
     if count == 8:
-        from_behind = lax.ppermute(second, "tm", [(0, 2), (1, 3), (3, 5), (4, 6), (5, 7)])
+        behind_pairs = [(0, 2), (1, 3), (3, 5), (4, 6), (5, 7)]
         from_ahead = lax.ppermute(second, "tm", [(2, 0), (3, 1), (4, 2), (6, 4), (7, 5)])
         hop = lax.ppermute(second, "tm", [(2, 6), (5, 1)])
         routed = lax.ppermute(hop, "tm", [(6, 4), (1, 3)])
     else:
-        from_behind = shifted(second, "tm", 2)
+        behind_pairs = [(i, i + 2) for i in range(count - 2)]
         from_ahead = shifted(second, "tm", -2)
         routed = jnp.zeros_like(second)
-    relay_behind = lax.ppermute(from_behind, "tm", [(i + 1, i) for i in range(2, count, 2)])
+    behind_even = lax.ppermute(second, "tm", [(a, b) for a, b in behind_pairs if b % 2 == 0])
+    behind_odd = lax.ppermute(second, "tm", [(a, b) for a, b in behind_pairs if b % 2 == 1])
+    relay_behind = lax.ppermute(behind_odd, "tm", [(i + 1, i) for i in range(2, count, 2)])
     relay_ahead = lax.ppermute(from_ahead, "tm", [(i, i + 1) for i in range(0, count - 2, 2)])
-    result = mix(coef, from_behind, relay_behind, second, partner, relay_ahead, from_ahead, routed,
-                 from_above, frame, from_below, conv_frame)
+    result = mix(coef, behind_even, behind_odd, relay_behind, second, partner, relay_ahead, from_ahead,
+                 routed, from_above, frame, from_below, conv_frame)
     return result[None]
 
 

time: 71.4 us -> 68.5 us (0.959)
  waiting for transfers between devices: 31.9 us -> 26.5 us
  local copies, waits for them, and re-layouts: 4.42 us -> 5.58 us
  starting transfers between devices: 13.7 us -> 14.8 us
    ppermute x2 -> x3, waiting for transfers between devices: 15 us -> 10.8 us  [the longest x1 10.8 us: shards(): lax.ppermute(second, 'tm', [(a, b) for a, b in behind_pairs if b % 2 == 0])]
    unnamed x18 -> x20, local copies, waits for them, and re-layouts: 1.65 us -> 2.8 us
    ppermute x1, waiting for transfers between devices: 9.85 us -> 8.74 us  [shards(): hop = lax.ppermute(second, 'tm', [(2, 6), (5, 1)])]
    ppermute x2 -> x3, starting transfers between devices: 2.57 us -> 3.29 us  [the longest x1 1.29 us: shards(): lax.ppermute(behind_odd, 'tm', [(i + 1, i) for i in range(2, count, 2)])]
  transfers between devices with their start and end apart: 9 -> 10, of which waited for: 5 -> 4; matrix products, arithmetic and copies ran while one was open for 5% -> 5% of each run, Pallas kernels for 0% -> 0%
where the time goes in v19:
time: 68.5 us; the launch traced here: 68.1 us
  waiting for transfers between devices  26.5 us (39%)
  starting transfers between devices  14.8 us (22%)
  Pallas kernels  14.5 us (21%)
  local copies, waits for them, and re-layouts  5.58 us (8%)
  between operations  4.03 us (6%)
  other arithmetic  2.62 us (4%)
    ppermute x1, waiting for transfers between devices, shards(): lax.ppermute(second, 'tm', [(a, b) for a, b in behind_pairs if b % 2 == 0])  10.8 us
    ppermute x1, waiting for transfers between devices, shards(): hop = lax.ppermute(second, 'tm', [(2, 6), (5, 1)])  8.74 us
    pallas_call x1, Pallas kernels, layers(): pl.pallas_call(layers_kernel, out_shape=jax.ShapeDtypeStruct((rows - 4, c...  7.65 us
    pallas_call x1, Pallas kernels, mix(): pl.pallas_call(mix_kernel, out_shape=jax.ShapeDtypeStruct((block, cols, c...  6.84 us
    ppermute x2, starting transfers between devices, shifted(): return lax.ppermute(value, axis, pairs)  5.84 us
    ppermute x1, waiting for transfers between devices, shards(): lax.ppermute(second, 'tm', [(2, 0), (3, 1), (4, 2), (6, 4), (7, 5)])  5.46 us
    unnamed x20, local copies, waits for them, and re-layouts  2.8 us
    slice x2, local copies, waits for them, and re-layouts, shards(): up = jnp.concatenate([image[:3], frame[:1]], axis=0)  2.04 us
  transfers between devices with their start and end apart: 10, of which 4 were waited for; matrix products, arithmetic and copies ran while one was open for 5% of the time, Pallas kernels for 0%

profile of v19, /device:TPU:22, one launch (start us, length us, event | category | flops | bytes accessed | tf_op | source)
XLA Modules:
  0.0 68.1 jit_solution(16434364826595774036)
XLA Ops:
  0.0 0.9 %slice_bitcast_fusion.2 = (bf16[1,160,256]{2,1,0:T(8,128)(2,1)S(1)}, bf16[1,160,256]{2,1,0:T(8,128)(2,1)S(1)}) fusion(bf16[1,8,160,256]{3,2,1,0:T(8,128)(2,1)} %param.9), kind=kLoop, calls=%fused_computation.4 | loop fusion | bytes 327680 | tf_op jit(solution)/shard_map/slice | solution.py:159
  0.9 0.0 copy-start.9
  1.0 1.1 %slice_bitcast_fusion = (bf16[3,160,256]{2,1,0:T(8,128)(2,1)S(1)}, bf16[3,160,256]{2,1,0:T(8,128)(2,1)S(1)}) fusion(bf16[1,8,160,256]{3,2,1,0:T(8,128)(2,1)} %param.8), kind=kLoop, calls=%fused_computation.2 | loop fusion | bytes 983040 | tf_op jit(solution)/shard_map/slice | solution.py:159
  2.1 3.5 %collective-permute-start = (bf16[4,160,256]{2,1,0:T(8,128)(2,1)S(1)}, bf16[4,160,256]{2,1,0:T(8,128)(2,1)S(1)}, u32[]{:S(2)}, u32[]{:S(2)}) collective-permute-start(bf16[4,160,256]{2,1,0:T(8,128)(2,1)S(1)} %pad_maximum_fusion), channel_id=1, source_target_pairs={{0,1},{1,2},{2,3},{4,5},{5,6},{6,7},{8,9},{9,10},{10,11},{12,13},{... | collective-permute-start | bytes 983048 | tf_op jit(solution)/shard_map/ppermute | solution.py:16
  5.6 2.4 %collective-permute-start.1 = (bf16[4,160,256]{2,1,0:T(8,128)(2,1)S(1)}, bf16[4,160,256]{2,1,0:T(8,128)(2,1)S(1)}, u32[]{:S(2)}, u32[]{:S(2)}) collective-permute-start(bf16[4,160,256]{2,1,0:T(8,128)(2,1)S(1)} %pad_maximum_fusion.1), channel_id=1, source_target_pairs={{1,0},{2,1},{3,2},{5,4},{6,5},{7,6},{9,8},{10,9},{11,10},{13,12},{... | collective-permute-start | bytes 983048 | tf_op jit(solution)/shard_map/ppermute | solution.py:16
  9.3 0.0 copy-done.9
  9.3 0.6 fusion
  9.9 0.6 broadcast_divide_fusion
  10.6 0.1 slice.45
  10.6 0.7 fusion.1
  13.8 0.6 pad_add_fusion.bounds_ref
  14.5 0.7 pad_maximum_fusion.2.coef_ref
  15.2 0.0 collective-permute-done.above_ref
  15.2 0.0 copy-start.7
  15.2 1.5 %collective-permute-done.1.below_ref = bf16[4,160,256]{2,1,0:T(8,128)(2,1)S(1)} collective-permute-done((bf16[4,160,256]{2,1,0:T(8,128)(2,1)S(1)}, bf16[4,160,256]{2,1,0:T(8,128)(2,1)S(1)}, u32[]{:S(2)}, u32[]{:S(2)}) %collective-permute-start.1) | collective-permute-done | bytes 327712 | tf_op jit(solution)/shard_map/ppermute | solution.py:16
  16.7 0.0 copy-done.7
  16.7 0.0 copy-start.8
  16.7 0.7 %copy-done.8 = bf16[4,160,256]{2,1,0:T(8,128)(2,1)} copy-done((bf16[4,160,256]{2,1,0:T(8,128)(2,1)}, bf16[4,160,256]{2,1,0:T(8,128)(2,1)S(1)}, u32[]{:S(2)}) %copy-start.8) | copy-done | bytes 327704
  17.4 7.7 %shard_map.82.own_ref = bf16[10,160,256]{2,1,0:T(8,128)(2,1)} custom-call(s32[2]{0:T(128)} %pad_add_fusion.bounds_ref, bf16[4,160,256]{2,1,0:T(8,128)(2,1)} %copy-done.7, bf16[8,160,256]{2,1,0:T(8,128)(2,1)} %bitcast.28, bf16[4,160,256]{2,1,0:T(8,128)(2,1)} %copy-done.8, bf16[3,3,256,256]{3,2,1,0:T(8,128)(2,1)} %w1_ref.1, bf16[3,3,256,256]{3,2,1,0:T(8,128)(2,1)} %w2_ref.1), custom_call_target="tpu_custom_call" | custom-call | flops 4152360960 | bytes 4653056 | tf_op jit(solution)/shard_map/pallas_call | solution.py:113
  25.1 1.3 %collective-permute-start.8 = (bf16[10,160,256]{2,1,0:T(8,128)(2,1)}, bf16[10,160,256]{2,1,0:T(8,128)(2,1)S(1)}, u32[]{:S(2)}, u32[]{:S(2)}) collective-permute-start(bf16[10,160,256]{2,1,0:T(8,128)(2,1)} %shard_map.82.own_ref), channel_id=1, source_target_pairs={{8,24},{20,4},{9,25},{21,5},{10,26},{22,6},{11,27},{23,7}} | collective-permute-start | bytes 2457608 | tf_op jit(solution)/shard_map/ppermute | solution.py:185
  26.4 1.9 %collective-permute-start.6 = (bf16[10,160,256]{2,1,0:T(8,128)(2,1)}, bf16[10,160,256]{2,1,0:T(8,128)(2,1)S(1)}, u32[]{:S(2)}, u32[]{:S(2)}) collective-permute-start(bf16[10,160,256]{2,1,0:T(8,128)(2,1)} %shard_map.82.own_ref), channel_id=1, source_target_pairs={{8,0},{12,4},{16,8},{24,16},{28,20},{9,1},{13,5},{17,9},{25,17},{2... | collective-permute-start | bytes 2457608 | tf_op jit(solution)/shard_map/ppermute | solution.py:184
  28.3 0.7 %collective-permute-start.3 = (bf16[10,160,256]{2,1,0:T(8,128)(2,1)}, bf16[10,160,256]{2,1,0:T(8,128)(2,1)S(1)}, u32[]{:S(2)}, u32[]{:S(2)}) collective-permute-start(bf16[10,160,256]{2,1,0:T(8,128)(2,1)} %shard_map.82.own_ref), channel_id=1, source_target_pairs={{4,12},{12,20},{20,28},{5,13},{13,21},{21,29},{6,14},{14,22},{22,3... | collective-permute-start | bytes 2457608 | tf_op jit(solution)/shard_map/ppermute | solution.py:192
  29.0 0.5 collective-permute-start.5
  29.5 1.3 %collective-permute-start.2 = (bf16[10,160,256]{2,1,0:T(8,128)(2,1)}, bf16[10,160,256]{2,1,0:T(8,128)(2,1)S(1)}, u32[]{:S(2)}, u32[]{:S(2)}) collective-permute-start(bf16[10,160,256]{2,1,0:T(8,128)(2,1)} %shard_map.82.own_ref), channel_id=1, source_target_pairs={{0,8},{16,24},{1,9},{17,25},{2,10},{18,26},{3,11},{19,27}} | collective-permute-start | bytes 2457608 | tf_op jit(solution)/shard_map/ppermute | solution.py:191
  30.8 8.7 %collective-permute-done.8 = bf16[10,160,256]{2,1,0:T(8,128)(2,1)S(1)} collective-permute-done((bf16[10,160,256]{2,1,0:T(8,128)(2,1)}, bf16[10,160,256]{2,1,0:T(8,128)(2,1)S(1)}, u32[]{:S(2)}, u32[]{:S(2)}) %collective-permute-start.8) | collective-permute-done | bytes 819232 | tf_op jit(solution)/shard_map/ppermute | solution.py:185
  39.5 1.3 %collective-permute-start.9 = (bf16[10,160,256]{2,1,0:T(8,128)(2,1)S(1)}, bf16[10,160,256]{2,1,0:T(8,128)(2,1)S(1)}, u32[]{:S(2)}, u32[]{:S(2)}) collective-permute-start(bf16[10,160,256]{2,1,0:T(8,128)(2,1)S(1)} %collective-permute-done.8), channel_id=1, source_target_pairs={{24,16},{4,12},{25,17},{5,13},{26,18},{6,14},{27,19},{7,15}} | collective-permute-start | bytes 2457608 | tf_op jit(solution)/shard_map/ppermute | solution.py:186
  40.8 5.5 %collective-permute-done.6.fa_ref = bf16[10,160,256]{2,1,0:T(8,128)(2,1)S(1)} collective-permute-done((bf16[10,160,256]{2,1,0:T(8,128)(2,1)}, bf16[10,160,256]{2,1,0:T(8,128)(2,1)S(1)}, u32[]{:S(2)}, u32[]{:S(2)}) %collective-permute-start.6) | collective-permute-done | bytes 819232 | tf_op jit(solution)/shard_map/ppermute | solution.py:184
  46.3 0.0 copy-start
  46.3 0.7 %collective-permute-start.7 = (bf16[10,160,256]{2,1,0:T(8,128)(2,1)S(1)}, bf16[10,160,256]{2,1,0:T(8,128)(2,1)S(1)}, u32[]{:S(2)}, u32[]{:S(2)}) collective-permute-start(bf16[10,160,256]{2,1,0:T(8,128)(2,1)S(1)} %collective-permute-done.6.fa_ref), channel_id=1, source_target_pairs={{0,4},{8,12},{16,20},{1,5},{9,13},{17,21},{2,6},{10,14},{18,22},{3... | collective-permute-start | bytes 2457608 | tf_op jit(solution)/shard_map/ppermute | solution.py:194
  47.0 0.0 collective-permute-done.3.fbo_ref
  47.0 0.0 copy-start.1
  47.0 1.3 %collective-permute-start.4 = (bf16[10,160,256]{2,1,0:T(8,128)(2,1)S(1)}, bf16[10,160,256]{2,1,0:T(8,128)(2,1)S(1)}, u32[]{:S(2)}, u32[]{:S(2)}) collective-permute-start(bf16[10,160,256]{2,1,0:T(8,128)(2,1)S(1)} %collective-permute-done.3.fbo_ref), channel_id=1, source_target_pairs={{12,8},{20,16},{28,24},{13,9},{21,17},{29,25},{14,10},{22,18},{30,... | collective-permute-start | bytes 2457608 | tf_op jit(solution)/shard_map/ppermute | solution.py:193
  48.3 0.0 collective-permute-done.5.par_ref
  48.3 0.0 copy-start.2
  48.4 10.8 %collective-permute-done.2.fb_ref = bf16[10,160,256]{2,1,0:T(8,128)(2,1)S(1)} collective-permute-done((bf16[10,160,256]{2,1,0:T(8,128)(2,1)}, bf16[10,160,256]{2,1,0:T(8,128)(2,1)S(1)}, u32[]{:S(2)}, u32[]{:S(2)}) %collective-permute-start.2) | collective-permute-done | bytes 819232 | tf_op jit(solution)/shard_map/ppermute | solution.py:191
  59.1 0.0 copy-start.3
  59.1 0.0 collective-permute-done.9.routed_ref
  59.2 0.0 collective-permute-done.7.ra_ref
  59.2 0.0 copy-start.5
  59.2 0.0 collective-permute-done.4.rb_ref
  59.2 0.9 %copy-done.4 = bf16[10,160,256]{2,1,0:T(8,128)(2,1)} copy-done((bf16[10,160,256]{2,1,0:T(8,128)(2,1)}, bf16[10,160,256]{2,1,0:T(8,128)(2,1)S(1)}, u32[]{:S(2)}) %copy-start.4) | copy-done | bytes 819224
  60.1 0.2 copy-done.5
  60.3 0.9 %copy-done.6 = bf16[10,160,256]{2,1,0:T(8,128)(2,1)} copy-done((bf16[10,160,256]{2,1,0:T(8,128)(2,1)}, bf16[10,160,256]{2,1,0:T(8,128)(2,1)S(1)}, u32[]{:S(2)}) %copy-start.6) | copy-done | bytes 819224
  61.2 0.0 copy-done
  61.2 0.0 copy-done.1
  61.2 0.0 copy-done.2
  61.2 0.0 copy-done.3
  61.2 6.8 %shard_map.83 = bf16[8,160,256]{2,1,0:T(8,128)(2,1)} custom-call(f32[7]{0:T(128)} %pad_maximum_fusion.2.coef_ref, bf16[10,160,256]{2,1,0:T(8,128)(2,1)} %copy-done.3, bf16[10,160,256]{2,1,0:T(8,128)(2,1)} %copy-done.1, bf16[10,160,256]{2,1,0:T(8,128)(2,1)} %copy-done.6, bf16[10,160,256]{2,1,0:T(8,128)(2,1)} %shard_map.82.own_ref, ...), custom_call_target="tpu_custom_call" | custom-call | flops 1509949440 | bytes 8552448 | tf_op jit(solution)/shard_map/pallas_call | solution.py:129
  (4 shorter events, 0.1 us)
Async XLA Ops:
  0.9 8.4 %copy-start.9 = (s32[1,5]{1,0:T(1,128)S(1)}, s32[1,5]{1,0:T(1,128)}, u32[]{:S(2)}) copy-start(s32[1,5]{1,0:T(1,128)} %param.12) | copy-start | bytes 64
  2.1 13.1 %collective-permute-start = (bf16[4,160,256]{2,1,0:T(8,128)(2,1)S(1)}, bf16[4,160,256]{2,1,0:T(8,128)(2,1)S(1)}, u32[]{:S(2)}, u32[]{:S(2)}) collective-permute-start(bf16[4,160,256]{2,1,0:T(8,128)(2,1)S(1)} %pad_maximum_fusion), channel_id=1, source_target_pairs={{0,1},{1,2},{2,3},{4,5},{5,6},{6,7},{8,9},{9,10},{10,11},{12,13},{... | collective-permute-start | bytes 983048 | tf_op jit(solution)/shard_map/ppermute | solution.py:16
  5.6 11.1 %collective-permute-start.1 = (bf16[4,160,256]{2,1,0:T(8,128)(2,1)S(1)}, bf16[4,160,256]{2,1,0:T(8,128)(2,1)S(1)}, u32[]{:S(2)}, u32[]{:S(2)}) collective-permute-start(bf16[4,160,256]{2,1,0:T(8,128)(2,1)S(1)} %pad_maximum_fusion.1), channel_id=1, source_target_pairs={{1,0},{2,1},{3,2},{5,4},{6,5},{7,6},{9,8},{10,9},{11,10},{13,12},{... | collective-permute-start | bytes 983048 | tf_op jit(solution)/shard_map/ppermute | solution.py:16
  15.2 1.5 %copy-start.7 = (bf16[4,160,256]{2,1,0:T(8,128)(2,1)}, bf16[4,160,256]{2,1,0:T(8,128)(2,1)S(1)}, u32[]{:S(2)}) copy-start(bf16[4,160,256]{2,1,0:T(8,128)(2,1)S(1)} %collective-permute-done.above_ref) | copy-start | bytes 983044
  16.7 0.7 %copy-start.8 = (bf16[4,160,256]{2,1,0:T(8,128)(2,1)}, bf16[4,160,256]{2,1,0:T(8,128)(2,1)S(1)}, u32[]{:S(2)}) copy-start(bf16[4,160,256]{2,1,0:T(8,128)(2,1)S(1)} %collective-permute-done.1.below_ref) | copy-start | bytes 983044
  25.1 14.4 %collective-permute-start.8 = (bf16[10,160,256]{2,1,0:T(8,128)(2,1)}, bf16[10,160,256]{2,1,0:T(8,128)(2,1)S(1)}, u32[]{:S(2)}, u32[]{:S(2)}) collective-permute-start(bf16[10,160,256]{2,1,0:T(8,128)(2,1)} %shard_map.82.own_ref), channel_id=1, source_target_pairs={{8,24},{20,4},{9,25},{21,5},{10,26},{22,6},{11,27},{23,7}} | collective-permute-start | bytes 2457608 | tf_op jit(solution)/shard_map/ppermute | solution.py:185
  26.4 19.9 %collective-permute-start.6 = (bf16[10,160,256]{2,1,0:T(8,128)(2,1)}, bf16[10,160,256]{2,1,0:T(8,128)(2,1)S(1)}, u32[]{:S(2)}, u32[]{:S(2)}) collective-permute-start(bf16[10,160,256]{2,1,0:T(8,128)(2,1)} %shard_map.82.own_ref), channel_id=1, source_target_pairs={{8,0},{12,4},{16,8},{24,16},{28,20},{9,1},{13,5},{17,9},{25,17},{2... | collective-permute-start | bytes 2457608 | tf_op jit(solution)/shard_map/ppermute | solution.py:184
  28.3 18.7 %collective-permute-start.3 = (bf16[10,160,256]{2,1,0:T(8,128)(2,1)}, bf16[10,160,256]{2,1,0:T(8,128)(2,1)S(1)}, u32[]{:S(2)}, u32[]{:S(2)}) collective-permute-start(bf16[10,160,256]{2,1,0:T(8,128)(2,1)} %shard_map.82.own_ref), channel_id=1, source_target_pairs={{4,12},{12,20},{20,28},{5,13},{13,21},{21,29},{6,14},{14,22},{22,3... | collective-permute-start | bytes 2457608 | tf_op jit(solution)/shard_map/ppermute | solution.py:192
  29.0 19.3 %collective-permute-start.5 = (bf16[10,160,256]{2,1,0:T(8,128)(2,1)}, bf16[10,160,256]{2,1,0:T(8,128)(2,1)S(1)}, u32[]{:S(2)}, u32[]{:S(2)}) collective-permute-start(bf16[10,160,256]{2,1,0:T(8,128)(2,1)} %shard_map.82.own_ref), channel_id=1, source_target_pairs={{0,4},{4,0},{8,12},{12,8},{16,20},{20,16},{24,28},{28,24},{1,5},{5... | collective-permute-start | bytes 2457608 | tf_op jit(solution)/shard_map/ppermute | solution.py:181
  29.5 29.7 %collective-permute-start.2 = (bf16[10,160,256]{2,1,0:T(8,128)(2,1)}, bf16[10,160,256]{2,1,0:T(8,128)(2,1)S(1)}, u32[]{:S(2)}, u32[]{:S(2)}) collective-permute-start(bf16[10,160,256]{2,1,0:T(8,128)(2,1)} %shard_map.82.own_ref), channel_id=1, source_target_pairs={{0,8},{16,24},{1,9},{17,25},{2,10},{18,26},{3,11},{19,27}} | collective-permute-start | bytes 2457608 | tf_op jit(solution)/shard_map/ppermute | solution.py:191
  39.5 19.6 %collective-permute-start.9 = (bf16[10,160,256]{2,1,0:T(8,128)(2,1)S(1)}, bf16[10,160,256]{2,1,0:T(8,128)(2,1)S(1)}, u32[]{:S(2)}, u32[]{:S(2)}) collective-permute-start(bf16[10,160,256]{2,1,0:T(8,128)(2,1)S(1)} %collective-permute-done.8), channel_id=1, source_target_pairs={{24,16},{4,12},{25,17},{5,13},{26,18},{6,14},{27,19},{7,15}} | collective-permute-start | bytes 2457608 | tf_op jit(solution)/shard_map/ppermute | solution.py:186
  46.3 14.9 %copy-start = (bf16[10,160,256]{2,1,0:T(8,128)(2,1)}, bf16[10,160,256]{2,1,0:T(8,128)(2,1)S(1)}, u32[]{:S(2)}) copy-start(bf16[10,160,256]{2,1,0:T(8,128)(2,1)S(1)} %collective-permute-done.6.fa_ref) | copy-start | bytes 2457604
  46.3 12.8 %collective-permute-start.7 = (bf16[10,160,256]{2,1,0:T(8,128)(2,1)S(1)}, bf16[10,160,256]{2,1,0:T(8,128)(2,1)S(1)}, u32[]{:S(2)}, u32[]{:S(2)}) collective-permute-start(bf16[10,160,256]{2,1,0:T(8,128)(2,1)S(1)} %collective-permute-done.6.fa_ref), channel_id=1, source_target_pairs={{0,4},{8,12},{16,20},{1,5},{9,13},{17,21},{2,6},{10,14},{18,22},{3... | collective-permute-start | bytes 2457608 | tf_op jit(solution)/shard_map/ppermute | solution.py:194
  47.0 14.2 %copy-start.1 = (bf16[10,160,256]{2,1,0:T(8,128)(2,1)}, bf16[10,160,256]{2,1,0:T(8,128)(2,1)S(1)}, u32[]{:S(2)}) copy-start(bf16[10,160,256]{2,1,0:T(8,128)(2,1)S(1)} %collective-permute-done.3.fbo_ref) | copy-start | bytes 2457604
  47.0 12.1 %collective-permute-start.4 = (bf16[10,160,256]{2,1,0:T(8,128)(2,1)S(1)}, bf16[10,160,256]{2,1,0:T(8,128)(2,1)S(1)}, u32[]{:S(2)}, u32[]{:S(2)}) collective-permute-start(bf16[10,160,256]{2,1,0:T(8,128)(2,1)S(1)} %collective-permute-done.3.fbo_ref), channel_id=1, source_target_pairs={{12,8},{20,16},{28,24},{13,9},{21,17},{29,25},{14,10},{22,18},{30,... | collective-permute-start | bytes 2457608 | tf_op jit(solution)/shard_map/ppermute | solution.py:193
  48.3 12.9 %copy-start.2 = (bf16[10,160,256]{2,1,0:T(8,128)(2,1)}, bf16[10,160,256]{2,1,0:T(8,128)(2,1)S(1)}, u32[]{:S(2)}) copy-start(bf16[10,160,256]{2,1,0:T(8,128)(2,1)S(1)} %collective-permute-done.5.par_ref) | copy-start | bytes 2457604
  59.1 2.1 %copy-start.3 = (bf16[10,160,256]{2,1,0:T(8,128)(2,1)}, bf16[10,160,256]{2,1,0:T(8,128)(2,1)S(1)}, u32[]{:S(2)}) copy-start(bf16[10,160,256]{2,1,0:T(8,128)(2,1)S(1)} %collective-permute-done.2.fb_ref) | copy-start | bytes 2457604
  59.1 0.9 %copy-start.4 = (bf16[10,160,256]{2,1,0:T(8,128)(2,1)}, bf16[10,160,256]{2,1,0:T(8,128)(2,1)S(1)}, u32[]{:S(2)}) copy-start(bf16[10,160,256]{2,1,0:T(8,128)(2,1)S(1)} %collective-permute-done.9.routed_ref) | copy-start | bytes 2457604
  59.2 1.2 %copy-start.5 = (bf16[10,160,256]{2,1,0:T(8,128)(2,1)}, bf16[10,160,256]{2,1,0:T(8,128)(2,1)S(1)}, u32[]{:S(2)}) copy-start(bf16[10,160,256]{2,1,0:T(8,128)(2,1)S(1)} %collective-permute-done.7.ra_ref) | copy-start | bytes 2457604
  60.3 0.9 %copy-start.6 = (bf16[10,160,256]{2,1,0:T(8,128)(2,1)}, bf16[10,160,256]{2,1,0:T(8,128)(2,1)S(1)}, u32[]{:S(2)}) copy-start(bf16[10,160,256]{2,1,0:T(8,128)(2,1)S(1)} %collective-permute-done.4.rb_ref) | copy-start | bytes 2457604

commit v20 on v19

--- a/solution.py
+++ b/solution.py
@@ -66,7 +66,7 @@
     conv_rows(first_buf, w2_ref, stack, rows1 - 2, emit_second)
 
 
-def mix_kernel(coef_ref, fb_ref, fbo_ref, rb_ref, own_ref, par_ref, ra_ref, fa_ref, routed_ref,
+def mix_kernel(coef_ref, fb_ref, fbo_ref, rb_ref, own_ref, par_ref, ra_ref, fa_ref, fao_ref, routed_ref,
                above_ref, frame_ref, below_ref, w3_ref, out_ref, fbuf, mixed_buf, stack):
     halo = below_ref.shape[0] - 1
     block = frame_ref.shape[0]
@@ -83,7 +83,7 @@
             + coef_ref[2] * own_ref[rows].astype(f32)
             + coef_ref[3] * par_ref[rows].astype(f32)
             + coef_ref[4] * ra_ref[rows].astype(f32)
-            + coef_ref[5] * fa_ref[rows].astype(f32)
+            + coef_ref[5] * (fa_ref[rows].astype(f32) + fao_ref[rows].astype(f32))
             + coef_ref[6] * routed_ref[rows].astype(f32)
         )
         mixed_buf[rows] = (summed * fbuf[rows].astype(f32)).astype(jnp.bfloat16)
@@ -123,20 +123,20 @@
     )(bounds, above, image, below, w1, w2)
 
 
-def mix(coef, fb, fbo, rb, own, par, ra, fa, routed, above, frame, below, w3):
+def mix(coef, fb, fbo, rb, own, par, ra, fa, fao, routed, above, frame, below, w3):
     block, cols, c = frame.shape
     flops = 2 * 9 * c * c * cols * block
     return pl.pallas_call(
         mix_kernel,
         out_shape=jax.ShapeDtypeStruct((block, cols, c), jnp.bfloat16),
-        in_specs=[smem()] + [vmem()] * 12,
+        in_specs=[smem()] + [vmem()] * 13,
         out_specs=vmem(),
         scratch_shapes=[pltpu.VMEM((block + 2, cols, c), jnp.bfloat16),
                         pltpu.VMEM((block + 2, cols, c), jnp.bfloat16),
                         pltpu.VMEM((CHUNK, cols, 3 * c), jnp.bfloat16)],
         cost_estimate=pl.CostEstimate(flops=flops, transcendentals=0,
                                       bytes_accessed=18 * (block + 2) * cols * c + 2 * 9 * c * c),
-    )(coef, fb, fbo, rb, own, par, ra, fa, routed, above, frame, below, w3)
+    )(coef, fb, fbo, rb, own, par, ra, fa, fao, routed, above, frame, below, w3)
 
 
 def shards(
@@ -181,19 +181,21 @@
     partner = lax.ppermute(second, "tm", [(i, i ^ 1) for i in range(count)])
     if count == 8:
         behind_pairs = [(0, 2), (1, 3), (3, 5), (4, 6), (5, 7)]
-        from_ahead = lax.ppermute(second, "tm", [(2, 0), (3, 1), (4, 2), (6, 4), (7, 5)])
+        ahead_pairs = [(2, 0), (3, 1), (4, 2), (6, 4), (7, 5)]
         hop = lax.ppermute(second, "tm", [(2, 6), (5, 1)])
         routed = lax.ppermute(hop, "tm", [(6, 4), (1, 3)])
     else:
         behind_pairs = [(i, i + 2) for i in range(count - 2)]
-        from_ahead = shifted(second, "tm", -2)
+        ahead_pairs = [(i + 2, i) for i in range(count - 2)]
         routed = jnp.zeros_like(second)
     behind_even = lax.ppermute(second, "tm", [(a, b) for a, b in behind_pairs if b % 2 == 0])
     behind_odd = lax.ppermute(second, "tm", [(a, b) for a, b in behind_pairs if b % 2 == 1])
     relay_behind = lax.ppermute(behind_odd, "tm", [(i + 1, i) for i in range(2, count, 2)])
-    relay_ahead = lax.ppermute(from_ahead, "tm", [(i, i + 1) for i in range(0, count - 2, 2)])
-    result = mix(coef, behind_even, behind_odd, relay_behind, second, partner, relay_ahead, from_ahead,
-                 routed, from_above, frame, from_below, conv_frame)
+    ahead_even = lax.ppermute(second, "tm", [(a, b) for a, b in ahead_pairs if b % 2 == 0])
+    ahead_odd = lax.ppermute(second, "tm", [(a, b) for a, b in ahead_pairs if b % 2 == 1])
+    relay_ahead = lax.ppermute(ahead_even, "tm", [(i, i + 1) for i in range(0, count - 2, 2)])
+    result = mix(coef, behind_even, behind_odd, relay_behind, second, partner, relay_ahead, ahead_even,
+                 ahead_odd, routed, from_above, frame, from_below, conv_frame)
     return result[None]
 
 

time: 68.5 us -> 71.6 us (1.045)
  the two profiles are of different devices: /device:TPU:22 before, /device:TPU:1 now
where the time goes in v20:
time: 71.6 us; the launch traced here: 71.2 us
  waiting for transfers between devices  27.5 us (38%)
  starting transfers between devices  16.8 us (23%)
  Pallas kernels  14.8 us (21%)
  local copies, waits for them, and re-layouts  5.6 us (8%)
  between operations  4.12 us (6%)
  other arithmetic  2.45 us (3%)
    ppermute x1, waiting for transfers between devices, shards(): routed = lax.ppermute(hop, 'tm', [(6, 4), (1, 3)])  14.9 us
    pallas_call x1, Pallas kernels, layers(): pl.pallas_call(layers_kernel, out_shape=jax.ShapeDtypeStruct((rows - 4, c...  7.65 us
    pallas_call x1, Pallas kernels, mix(): pl.pallas_call(mix_kernel, out_shape=jax.ShapeDtypeStruct((block, cols, c...  7.13 us
    ppermute x1, waiting for transfers between devices, shards(): hop = lax.ppermute(second, 'tm', [(2, 6), (5, 1)])  6.1 us
    ppermute x2, starting transfers between devices, shifted(): return lax.ppermute(value, axis, pairs)  5.34 us
    ppermute x1, waiting for transfers between devices, shards(): lax.ppermute(second, 'tm', [(a, b) for a, b in ahead_pairs if b % 2 == 1])  4.6 us
    ppermute x1, starting transfers between devices, shards(): lax.ppermute(second, 'tm', [(a, b) for a, b in behind_pairs if b % 2 == 1])  4.08 us
    unnamed x22, local copies, waits for them, and re-layouts  2.82 us
  transfers between devices with their start and end apart: 11, of which 4 were waited for; matrix products, arithmetic and copies ran while one was open for 4% of the time, Pallas kernels for 0%

profile of v20, /device:TPU:1, one launch (start us, length us, event | category | flops | bytes accessed | tf_op | source)
XLA Modules:
  0.0 71.2 jit_solution(706036610878474086)
XLA Ops:
  0.0 0.9 %slice_bitcast_fusion.2 = (bf16[1,160,256]{2,1,0:T(8,128)(2,1)S(1)}, bf16[1,160,256]{2,1,0:T(8,128)(2,1)S(1)}) fusion(bf16[1,8,160,256]{3,2,1,0:T(8,128)(2,1)} %param.9), kind=kLoop, calls=%fused_computation.4 | loop fusion | bytes 327680 | tf_op jit(solution)/shard_map/slice | solution.py:159
  0.9 0.0 copy-start.10
  1.0 1.1 %slice_bitcast_fusion = (bf16[3,160,256]{2,1,0:T(8,128)(2,1)S(1)}, bf16[3,160,256]{2,1,0:T(8,128)(2,1)S(1)}) fusion(bf16[1,8,160,256]{3,2,1,0:T(8,128)(2,1)} %param.8), kind=kLoop, calls=%fused_computation.2 | loop fusion | bytes 983040 | tf_op jit(solution)/shard_map/slice | solution.py:159
  2.1 4.0 %collective-permute-start = (bf16[4,160,256]{2,1,0:T(8,128)(2,1)S(1)}, bf16[4,160,256]{2,1,0:T(8,128)(2,1)S(1)}, u32[]{:S(2)}, u32[]{:S(2)}) collective-permute-start(bf16[4,160,256]{2,1,0:T(8,128)(2,1)S(1)} %pad_maximum_fusion), channel_id=1, source_target_pairs={{0,1},{1,2},{2,3},{4,5},{5,6},{6,7},{8,9},{9,10},{10,11},{12,13},{... | collective-permute-start | bytes 983048 | tf_op jit(solution)/shard_map/ppermute | solution.py:16
  6.2 1.3 %collective-permute-start.1 = (bf16[4,160,256]{2,1,0:T(8,128)(2,1)S(1)}, bf16[4,160,256]{2,1,0:T(8,128)(2,1)S(1)}, u32[]{:S(2)}, u32[]{:S(2)}) collective-permute-start(bf16[4,160,256]{2,1,0:T(8,128)(2,1)S(1)} %pad_maximum_fusion.1), channel_id=1, source_target_pairs={{1,0},{2,1},{3,2},{5,4},{6,5},{7,6},{9,8},{10,9},{11,10},{13,12},{... | collective-permute-start | bytes 983048 | tf_op jit(solution)/shard_map/ppermute | solution.py:16
  8.8 0.0 copy-done.10
  8.8 0.6 fusion
  9.4 0.6 broadcast_divide_fusion
  10.0 0.1 slice.45
  10.1 0.7 fusion.1
  13.3 0.6 pad_add_fusion.bounds_ref
  13.9 0.6 pad_maximum_fusion.2.coef_ref
  14.5 0.0 collective-permute-done.above_ref
  14.5 1.8 %collective-permute-done.1.below_ref = bf16[4,160,256]{2,1,0:T(8,128)(2,1)S(1)} collective-permute-done((bf16[4,160,256]{2,1,0:T(8,128)(2,1)S(1)}, bf16[4,160,256]{2,1,0:T(8,128)(2,1)S(1)}, u32[]{:S(2)}, u32[]{:S(2)}) %collective-permute-start.1) | collective-permute-done | bytes 327712 | tf_op jit(solution)/shard_map/ppermute | solution.py:16
  16.3 0.0 copy-done.8
  16.4 0.7 %copy-done.9 = bf16[4,160,256]{2,1,0:T(8,128)(2,1)} copy-done((bf16[4,160,256]{2,1,0:T(8,128)(2,1)}, bf16[4,160,256]{2,1,0:T(8,128)(2,1)S(1)}, u32[]{:S(2)}) %copy-start.9) | copy-done | bytes 327704
  17.1 7.6 %shard_map.82.own_ref = bf16[10,160,256]{2,1,0:T(8,128)(2,1)} custom-call(s32[2]{0:T(128)} %pad_add_fusion.bounds_ref, bf16[4,160,256]{2,1,0:T(8,128)(2,1)} %copy-done.8, bf16[8,160,256]{2,1,0:T(8,128)(2,1)} %bitcast.28, bf16[4,160,256]{2,1,0:T(8,128)(2,1)} %copy-done.9, bf16[3,3,256,256]{3,2,1,0:T(8,128)(2,1)} %w1_ref.1, bf16[3,3,256,256]{3,2,1,0:T(8,128)(2,1)} %w2_ref.1), custom_call_target="tpu_custom_call" | custom-call | flops 4152360960 | bytes 4653056 | tf_op jit(solution)/shard_map/pallas_call | solution.py:113
  24.7 1.3 %collective-permute-start.9 = (bf16[10,160,256]{2,1,0:T(8,128)(2,1)}, bf16[10,160,256]{2,1,0:T(8,128)(2,1)S(1)}, u32[]{:S(2)}, u32[]{:S(2)}) collective-permute-start(bf16[10,160,256]{2,1,0:T(8,128)(2,1)} %shard_map.82.own_ref), channel_id=1, source_target_pairs={{8,24},{20,4},{9,25},{21,5},{10,26},{22,6},{11,27},{23,7}} | collective-permute-start | bytes 2457608 | tf_op jit(solution)/shard_map/ppermute | solution.py:185
  26.0 1.3 %collective-permute-start.8 = (bf16[10,160,256]{2,1,0:T(8,128)(2,1)}, bf16[10,160,256]{2,1,0:T(8,128)(2,1)S(1)}, u32[]{:S(2)}, u32[]{:S(2)}) collective-permute-start(bf16[10,160,256]{2,1,0:T(8,128)(2,1)} %shard_map.82.own_ref), channel_id=1, source_target_pairs={{12,4},{28,20},{13,5},{29,21},{14,6},{30,22},{15,7},{31,23}} | collective-permute-start | bytes 2457608 | tf_op jit(solution)/shard_map/ppermute | solution.py:195
  27.3 0.7 %collective-permute-start.6 = (bf16[10,160,256]{2,1,0:T(8,128)(2,1)}, bf16[10,160,256]{2,1,0:T(8,128)(2,1)S(1)}, u32[]{:S(2)}, u32[]{:S(2)}) collective-permute-start(bf16[10,160,256]{2,1,0:T(8,128)(2,1)} %shard_map.82.own_ref), channel_id=1, source_target_pairs={{8,0},{16,8},{24,16},{9,1},{17,9},{25,17},{10,2},{18,10},{26,18},{... | collective-permute-start | bytes 2457608 | tf_op jit(solution)/shard_map/ppermute | solution.py:194
  28.1 4.1 %collective-permute-start.3 = (bf16[10,160,256]{2,1,0:T(8,128)(2,1)}, bf16[10,160,256]{2,1,0:T(8,128)(2,1)S(1)}, u32[]{:S(2)}, u32[]{:S(2)}) collective-permute-start(bf16[10,160,256]{2,1,0:T(8,128)(2,1)} %shard_map.82.own_ref), channel_id=1, source_target_pairs={{4,12},{12,20},{20,28},{5,13},{13,21},{21,29},{6,14},{14,22},{22,3... | collective-permute-start | bytes 2457608 | tf_op jit(solution)/shard_map/ppermute | solution.py:192
  32.1 0.1 collective-permute-start.5
  32.2 6.1 %collective-permute-done.9 = bf16[10,160,256]{2,1,0:T(8,128)(2,1)S(1)} collective-permute-done((bf16[10,160,256]{2,1,0:T(8,128)(2,1)}, bf16[10,160,256]{2,1,0:T(8,128)(2,1)S(1)}, u32[]{:S(2)}, u32[]{:S(2)}) %collective-permute-start.9) | collective-permute-done | bytes 819232 | tf_op jit(solution)/shard_map/ppermute | solution.py:185
  38.3 0.7 collective-permute-start.2
  39.0 4.6 %collective-permute-done.8.fao_ref = bf16[10,160,256]{2,1,0:T(8,128)(2,1)S(1)} collective-permute-done((bf16[10,160,256]{2,1,0:T(8,128)(2,1)}, bf16[10,160,256]{2,1,0:T(8,128)(2,1)S(1)}, u32[]{:S(2)}, u32[]{:S(2)}) %collective-permute-start.8) | collective-permute-done | bytes 819232 | tf_op jit(solution)/shard_map/ppermute | solution.py:195
  43.6 1.3 %collective-permute-start.10 = (bf16[10,160,256]{2,1,0:T(8,128)(2,1)S(1)}, bf16[10,160,256]{2,1,0:T(8,128)(2,1)S(1)}, u32[]{:S(2)}, u32[]{:S(2)}) collective-permute-start(bf16[10,160,256]{2,1,0:T(8,128)(2,1)S(1)} %collective-permute-done.9), channel_id=1, source_target_pairs={{24,16},{4,12},{25,17},{5,13},{26,18},{6,14},{27,19},{7,15}} | collective-permute-start | bytes 2457608 | tf_op jit(solution)/shard_map/ppermute | solution.py:186
  45.0 0.0 collective-permute-done.6.fa_ref
  45.0 0.0 copy-start.1
  45.0 1.3 %collective-permute-start.7 = (bf16[10,160,256]{2,1,0:T(8,128)(2,1)S(1)}, bf16[10,160,256]{2,1,0:T(8,128)(2,1)S(1)}, u32[]{:S(2)}, u32[]{:S(2)}) collective-permute-start(bf16[10,160,256]{2,1,0:T(8,128)(2,1)S(1)} %collective-permute-done.6.fa_ref), channel_id=1, source_target_pairs={{0,4},{8,12},{16,20},{1,5},{9,13},{17,21},{2,6},{10,14},{18,22},{3... | collective-permute-start | bytes 2457608 | tf_op jit(solution)/shard_map/ppermute | solution.py:196
  46.3 0.0 collective-permute-done.3.fbo_ref
  46.3 0.0 copy-start.2
  46.3 0.7 %collective-permute-start.4 = (bf16[10,160,256]{2,1,0:T(8,128)(2,1)S(1)}, bf16[10,160,256]{2,1,0:T(8,128)(2,1)S(1)}, u32[]{:S(2)}, u32[]{:S(2)}) collective-permute-start(bf16[10,160,256]{2,1,0:T(8,128)(2,1)S(1)} %collective-permute-done.3.fbo_ref), channel_id=1, source_target_pairs={{12,8},{20,16},{28,24},{13,9},{21,17},{29,25},{14,10},{22,18},{30,... | collective-permute-start | bytes 2457608 | tf_op jit(solution)/shard_map/ppermute | solution.py:193
  47.0 0.0 collective-permute-done.5.par_ref
  47.0 0.0 copy-start.3
  47.1 0.0 collective-permute-done.2.fb_ref
  47.1 0.0 copy-start.4
  47.1 14.9 %collective-permute-done.10.routed_ref = bf16[10,160,256]{2,1,0:T(8,128)(2,1)S(1)} collective-permute-done((bf16[10,160,256]{2,1,0:T(8,128)(2,1)S(1)}, bf16[10,160,256]{2,1,0:T(8,128)(2,1)S(1)}, u32[]{:S(2)}, u32[]{:S(2)}) %collective-permute-start.10) | collective-permute-done | bytes 819232 | tf_op jit(solution)/shard_map/ppermute | solution.py:186
  62.0 0.0 collective-permute-done.7.ra_ref
  62.0 0.0 collective-permute-done.4.rb_ref
  62.0 0.0 copy-done.4
  62.0 0.9 %copy-done.5 = bf16[10,160,256]{2,1,0:T(8,128)(2,1)} copy-done((bf16[10,160,256]{2,1,0:T(8,128)(2,1)}, bf16[10,160,256]{2,1,0:T(8,128)(2,1)S(1)}, u32[]{:S(2)}) %copy-start.5) | copy-done | bytes 819224
  62.9 0.3 copy-done.6
  63.2 0.9 %copy-done.7 = bf16[10,160,256]{2,1,0:T(8,128)(2,1)} copy-done((bf16[10,160,256]{2,1,0:T(8,128)(2,1)}, bf16[10,160,256]{2,1,0:T(8,128)(2,1)S(1)}, u32[]{:S(2)}) %copy-start.7) | copy-done | bytes 819224
  64.1 0.0 copy-done
  64.1 0.0 copy-done.1
  64.1 0.0 copy-done.2
  64.1 0.0 copy-done.3
  64.1 7.1 %shard_map.83 = bf16[8,160,256]{2,1,0:T(8,128)(2,1)} custom-call(f32[7]{0:T(128)} %pad_maximum_fusion.2.coef_ref, bf16[10,160,256]{2,1,0:T(8,128)(2,1)} %copy-done.4, bf16[10,160,256]{2,1,0:T(8,128)(2,1)} %copy-done.2, bf16[10,160,256]{2,1,0:T(8,128)(2,1)} %copy-done.7, bf16[10,160,256]{2,1,0:T(8,128)(2,1)} %shard_map.82.own_ref, ...), custom_call_target="tpu_custom_call" | custom-call | flops 1509949440 | bytes 8552448 | tf_op jit(solution)/shard_map/pallas_call | solution.py:129
  (8 shorter events, 0.1 us)
Async XLA Ops:
  0.9 7.9 %copy-start.10 = (s32[1,5]{1,0:T(1,128)S(1)}, s32[1,5]{1,0:T(1,128)}, u32[]{:S(2)}) copy-start(s32[1,5]{1,0:T(1,128)} %param.12) | copy-start | bytes 64
  2.1 12.4 %collective-permute-start = (bf16[4,160,256]{2,1,0:T(8,128)(2,1)S(1)}, bf16[4,160,256]{2,1,0:T(8,128)(2,1)S(1)}, u32[]{:S(2)}, u32[]{:S(2)}) collective-permute-start(bf16[4,160,256]{2,1,0:T(8,128)(2,1)S(1)} %pad_maximum_fusion), channel_id=1, source_target_pairs={{0,1},{1,2},{2,3},{4,5},{5,6},{6,7},{8,9},{9,10},{10,11},{12,13},{... | collective-permute-start | bytes 983048 | tf_op jit(solution)/shard_map/ppermute | solution.py:16
  6.2 10.2 %collective-permute-start.1 = (bf16[4,160,256]{2,1,0:T(8,128)(2,1)S(1)}, bf16[4,160,256]{2,1,0:T(8,128)(2,1)S(1)}, u32[]{:S(2)}, u32[]{:S(2)}) collective-permute-start(bf16[4,160,256]{2,1,0:T(8,128)(2,1)S(1)} %pad_maximum_fusion.1), channel_id=1, source_target_pairs={{1,0},{2,1},{3,2},{5,4},{6,5},{7,6},{9,8},{10,9},{11,10},{13,12},{... | collective-permute-start | bytes 983048 | tf_op jit(solution)/shard_map/ppermute | solution.py:16
  14.5 1.8 %copy-start.8 = (bf16[4,160,256]{2,1,0:T(8,128)(2,1)}, bf16[4,160,256]{2,1,0:T(8,128)(2,1)S(1)}, u32[]{:S(2)}) copy-start(bf16[4,160,256]{2,1,0:T(8,128)(2,1)S(1)} %collective-permute-done.above_ref) | copy-start | bytes 983044
  16.4 0.7 %copy-start.9 = (bf16[4,160,256]{2,1,0:T(8,128)(2,1)}, bf16[4,160,256]{2,1,0:T(8,128)(2,1)S(1)}, u32[]{:S(2)}) copy-start(bf16[4,160,256]{2,1,0:T(8,128)(2,1)S(1)} %collective-permute-done.1.below_ref) | copy-start | bytes 983044
  24.7 13.6 %collective-permute-start.9 = (bf16[10,160,256]{2,1,0:T(8,128)(2,1)}, bf16[10,160,256]{2,1,0:T(8,128)(2,1)S(1)}, u32[]{:S(2)}, u32[]{:S(2)}) collective-permute-start(bf16[10,160,256]{2,1,0:T(8,128)(2,1)} %shard_map.82.own_ref), channel_id=1, source_target_pairs={{8,24},{20,4},{9,25},{21,5},{10,26},{22,6},{11,27},{23,7}} | collective-permute-start | bytes 2457608 | tf_op jit(solution)/shard_map/ppermute | solution.py:185
  26.0 17.6 %collective-permute-start.8 = (bf16[10,160,256]{2,1,0:T(8,128)(2,1)}, bf16[10,160,256]{2,1,0:T(8,128)(2,1)S(1)}, u32[]{:S(2)}, u32[]{:S(2)}) collective-permute-start(bf16[10,160,256]{2,1,0:T(8,128)(2,1)} %shard_map.82.own_ref), channel_id=1, source_target_pairs={{12,4},{28,20},{13,5},{29,21},{14,6},{30,22},{15,7},{31,23}} | collective-permute-start | bytes 2457608 | tf_op jit(solution)/shard_map/ppermute | solution.py:195
  27.3 17.6 %collective-permute-start.6 = (bf16[10,160,256]{2,1,0:T(8,128)(2,1)}, bf16[10,160,256]{2,1,0:T(8,128)(2,1)S(1)}, u32[]{:S(2)}, u32[]{:S(2)}) collective-permute-start(bf16[10,160,256]{2,1,0:T(8,128)(2,1)} %shard_map.82.own_ref), channel_id=1, source_target_pairs={{8,0},{16,8},{24,16},{9,1},{17,9},{25,17},{10,2},{18,10},{26,18},{... | collective-permute-start | bytes 2457608 | tf_op jit(solution)/shard_map/ppermute | solution.py:194
  28.1 18.2 %collective-permute-start.3 = (bf16[10,160,256]{2,1,0:T(8,128)(2,1)}, bf16[10,160,256]{2,1,0:T(8,128)(2,1)S(1)}, u32[]{:S(2)}, u32[]{:S(2)}) collective-permute-start(bf16[10,160,256]{2,1,0:T(8,128)(2,1)} %shard_map.82.own_ref), channel_id=1, source_target_pairs={{4,12},{12,20},{20,28},{5,13},{13,21},{21,29},{6,14},{14,22},{22,3... | collective-permute-start | bytes 2457608 | tf_op jit(solution)/shard_map/ppermute | solution.py:192
  32.1 14.9 %collective-permute-start.5 = (bf16[10,160,256]{2,1,0:T(8,128)(2,1)}, bf16[10,160,256]{2,1,0:T(8,128)(2,1)S(1)}, u32[]{:S(2)}, u32[]{:S(2)}) collective-permute-start(bf16[10,160,256]{2,1,0:T(8,128)(2,1)} %shard_map.82.own_ref), channel_id=1, source_target_pairs={{0,4},{4,0},{8,12},{12,8},{16,20},{20,16},{24,28},{28,24},{1,5},{5... | collective-permute-start | bytes 2457608 | tf_op jit(solution)/shard_map/ppermute | solution.py:181
  38.3 8.7 %collective-permute-start.2 = (bf16[10,160,256]{2,1,0:T(8,128)(2,1)}, bf16[10,160,256]{2,1,0:T(8,128)(2,1)S(1)}, u32[]{:S(2)}, u32[]{:S(2)}) collective-permute-start(bf16[10,160,256]{2,1,0:T(8,128)(2,1)} %shard_map.82.own_ref), channel_id=1, source_target_pairs={{0,8},{16,24},{1,9},{17,25},{2,10},{18,26},{3,11},{19,27}} | collective-permute-start | bytes 2457608 | tf_op jit(solution)/shard_map/ppermute | solution.py:191
  43.6 20.4 %copy-start = (bf16[10,160,256]{2,1,0:T(8,128)(2,1)}, bf16[10,160,256]{2,1,0:T(8,128)(2,1)S(1)}, u32[]{:S(2)}) copy-start(bf16[10,160,256]{2,1,0:T(8,128)(2,1)S(1)} %collective-permute-done.8.fao_ref) | copy-start | bytes 2457604
  43.6 18.4 %collective-permute-start.10 = (bf16[10,160,256]{2,1,0:T(8,128)(2,1)S(1)}, bf16[10,160,256]{2,1,0:T(8,128)(2,1)S(1)}, u32[]{:S(2)}, u32[]{:S(2)}) collective-permute-start(bf16[10,160,256]{2,1,0:T(8,128)(2,1)S(1)} %collective-permute-done.9), channel_id=1, source_target_pairs={{24,16},{4,12},{25,17},{5,13},{26,18},{6,14},{27,19},{7,15}} | collective-permute-start | bytes 2457608 | tf_op jit(solution)/shard_map/ppermute | solution.py:186
  45.0 19.1 %copy-start.1 = (bf16[10,160,256]{2,1,0:T(8,128)(2,1)}, bf16[10,160,256]{2,1,0:T(8,128)(2,1)S(1)}, u32[]{:S(2)}) copy-start(bf16[10,160,256]{2,1,0:T(8,128)(2,1)S(1)} %collective-permute-done.6.fa_ref) | copy-start | bytes 2457604
  45.0 17.0 %collective-permute-start.7 = (bf16[10,160,256]{2,1,0:T(8,128)(2,1)S(1)}, bf16[10,160,256]{2,1,0:T(8,128)(2,1)S(1)}, u32[]{:S(2)}, u32[]{:S(2)}) collective-permute-start(bf16[10,160,256]{2,1,0:T(8,128)(2,1)S(1)} %collective-permute-done.6.fa_ref), channel_id=1, source_target_pairs={{0,4},{8,12},{16,20},{1,5},{9,13},{17,21},{2,6},{10,14},{18,22},{3... | collective-permute-start | bytes 2457608 | tf_op jit(solution)/shard_map/ppermute | solution.py:196
  46.3 17.8 %copy-start.2 = (bf16[10,160,256]{2,1,0:T(8,128)(2,1)}, bf16[10,160,256]{2,1,0:T(8,128)(2,1)S(1)}, u32[]{:S(2)}) copy-start(bf16[10,160,256]{2,1,0:T(8,128)(2,1)S(1)} %collective-permute-done.3.fbo_ref) | copy-start | bytes 2457604
  46.3 15.7 %collective-permute-start.4 = (bf16[10,160,256]{2,1,0:T(8,128)(2,1)S(1)}, bf16[10,160,256]{2,1,0:T(8,128)(2,1)S(1)}, u32[]{:S(2)}, u32[]{:S(2)}) collective-permute-start(bf16[10,160,256]{2,1,0:T(8,128)(2,1)S(1)} %collective-permute-done.3.fbo_ref), channel_id=1, source_target_pairs={{12,8},{20,16},{28,24},{13,9},{21,17},{29,25},{14,10},{22,18},{30,... | collective-permute-start | bytes 2457608 | tf_op jit(solution)/shard_map/ppermute | solution.py:193
  47.0 17.0 %copy-start.3 = (bf16[10,160,256]{2,1,0:T(8,128)(2,1)}, bf16[10,160,256]{2,1,0:T(8,128)(2,1)S(1)}, u32[]{:S(2)}) copy-start(bf16[10,160,256]{2,1,0:T(8,128)(2,1)S(1)} %collective-permute-done.5.par_ref) | copy-start | bytes 2457604
  47.1 15.0 %copy-start.4 = (bf16[10,160,256]{2,1,0:T(8,128)(2,1)}, bf16[10,160,256]{2,1,0:T(8,128)(2,1)S(1)}, u32[]{:S(2)}) copy-start(bf16[10,160,256]{2,1,0:T(8,128)(2,1)S(1)} %collective-permute-done.2.fb_ref) | copy-start | bytes 2457604
  62.0 0.9 %copy-start.5 = (bf16[10,160,256]{2,1,0:T(8,128)(2,1)}, bf16[10,160,256]{2,1,0:T(8,128)(2,1)S(1)}, u32[]{:S(2)}) copy-start(bf16[10,160,256]{2,1,0:T(8,128)(2,1)S(1)} %collective-permute-done.10.routed_ref) | copy-start | bytes 2457604
  62.0 1.2 %copy-start.6 = (bf16[10,160,256]{2,1,0:T(8,128)(2,1)}, bf16[10,160,256]{2,1,0:T(8,128)(2,1)S(1)}, u32[]{:S(2)}) copy-start(bf16[10,160,256]{2,1,0:T(8,128)(2,1)S(1)} %collective-permute-done.7.ra_ref) | copy-start | bytes 2457604
  63.2 0.9 %copy-start.7 = (bf16[10,160,256]{2,1,0:T(8,128)(2,1)}, bf16[10,160,256]{2,1,0:T(8,128)(2,1)S(1)}, u32[]{:S(2)}) copy-start(bf16[10,160,256]{2,1,0:T(8,128)(2,1)S(1)} %collective-permute-done.4.rb_ref) | copy-start | bytes 2457604

commit v21 on v19

--- a/solution.py
+++ b/solution.py
@@ -18,7 +18,9 @@
 
 def gelu(v):
     c = np.float32(np.sqrt(2 / np.pi))
-    return v * (0.5 * (1.0 + jnp.tanh(c * (v + 0.044715 * (v * v * v)))))
+    k = np.float32(np.sqrt(2 / np.pi) * 0.044715)
+    h = 0.5 * v
+    return h + h * jnp.tanh(v * (c + k * (v * v)))
 
 
 def conv_rows(src_ref, w_ref, stack, rows_out, emit):

time: 68.5 us -> 68.5 us (level)
  no operation moved by 1% of the time
where the time goes in v21:
time: 68.5 us; the launch traced here: 68.1 us
  waiting for transfers between devices  26.5 us (39%)
  starting transfers between devices  14.8 us (22%)
  Pallas kernels  14.5 us (21%)
  local copies, waits for them, and re-layouts  5.58 us (8%)
  between operations  4.03 us (6%)
  other arithmetic  2.62 us (4%)
    ppermute x1, waiting for transfers between devices, shards(): lax.ppermute(second, 'tm', [(a, b) for a, b in behind_pairs if b % 2 == 0])  10.8 us
    ppermute x1, waiting for transfers between devices, shards(): hop = lax.ppermute(second, 'tm', [(2, 6), (5, 1)])  8.74 us
    pallas_call x1, Pallas kernels, layers(): pl.pallas_call(layers_kernel, out_shape=jax.ShapeDtypeStruct((rows - 4, c...  7.67 us
    pallas_call x1, Pallas kernels, mix(): pl.pallas_call(mix_kernel, out_shape=jax.ShapeDtypeStruct((block, cols, c...  6.83 us
    ppermute x2, starting transfers between devices, shifted(): return lax.ppermute(value, axis, pairs)  5.84 us
    ppermute x1, waiting for transfers between devices, shards(): lax.ppermute(second, 'tm', [(2, 0), (3, 1), (4, 2), (6, 4), (7, 5)])  5.46 us
    unnamed x20, local copies, waits for them, and re-layouts  2.8 us
    slice x2, local copies, waits for them, and re-layouts, shards(): up = jnp.concatenate([image[:3], frame[:1]], axis=0)  2.04 us
  transfers between devices with their start and end apart: 10, of which 4 were waited for; matrix products, arithmetic and copies ran while one was open for 5% of the time, Pallas kernels for 0%

profile of v21, /device:TPU:22, one launch (start us, length us, event | category | flops | bytes accessed | tf_op | source)
XLA Modules:
  0.0 68.1 jit_solution(8647488933545434108)
XLA Ops:
  0.0 0.9 %slice_bitcast_fusion.2 = (bf16[1,160,256]{2,1,0:T(8,128)(2,1)S(1)}, bf16[1,160,256]{2,1,0:T(8,128)(2,1)S(1)}) fusion(bf16[1,8,160,256]{3,2,1,0:T(8,128)(2,1)} %param.9), kind=kLoop, calls=%fused_computation.4 | loop fusion | bytes 327680 | tf_op jit(solution)/shard_map/slice | solution.py:161
  0.9 0.0 copy-start.9
  1.0 1.1 %slice_bitcast_fusion = (bf16[3,160,256]{2,1,0:T(8,128)(2,1)S(1)}, bf16[3,160,256]{2,1,0:T(8,128)(2,1)S(1)}) fusion(bf16[1,8,160,256]{3,2,1,0:T(8,128)(2,1)} %param.8), kind=kLoop, calls=%fused_computation.2 | loop fusion | bytes 983040 | tf_op jit(solution)/shard_map/slice | solution.py:161
  2.1 3.5 %collective-permute-start = (bf16[4,160,256]{2,1,0:T(8,128)(2,1)S(1)}, bf16[4,160,256]{2,1,0:T(8,128)(2,1)S(1)}, u32[]{:S(2)}, u32[]{:S(2)}) collective-permute-start(bf16[4,160,256]{2,1,0:T(8,128)(2,1)S(1)} %pad_maximum_fusion), channel_id=1, source_target_pairs={{0,1},{1,2},{2,3},{4,5},{5,6},{6,7},{8,9},{9,10},{10,11},{12,13},{... | collective-permute-start | bytes 983048 | tf_op jit(solution)/shard_map/ppermute | solution.py:16
  5.6 2.4 %collective-permute-start.1 = (bf16[4,160,256]{2,1,0:T(8,128)(2,1)S(1)}, bf16[4,160,256]{2,1,0:T(8,128)(2,1)S(1)}, u32[]{:S(2)}, u32[]{:S(2)}) collective-permute-start(bf16[4,160,256]{2,1,0:T(8,128)(2,1)S(1)} %pad_maximum_fusion.1), channel_id=1, source_target_pairs={{1,0},{2,1},{3,2},{5,4},{6,5},{7,6},{9,8},{10,9},{11,10},{13,12},{... | collective-permute-start | bytes 983048 | tf_op jit(solution)/shard_map/ppermute | solution.py:16
  9.3 0.0 copy-done.9
  9.3 0.6 fusion
  9.9 0.6 broadcast_divide_fusion
  10.6 0.1 slice.45
  10.6 0.7 fusion.1
  13.8 0.6 pad_add_fusion.bounds_ref
  14.5 0.7 pad_maximum_fusion.2.coef_ref
  15.2 0.0 collective-permute-done.above_ref
  15.2 0.0 copy-start.7
  15.2 1.5 %collective-permute-done.1.below_ref = bf16[4,160,256]{2,1,0:T(8,128)(2,1)S(1)} collective-permute-done((bf16[4,160,256]{2,1,0:T(8,128)(2,1)S(1)}, bf16[4,160,256]{2,1,0:T(8,128)(2,1)S(1)}, u32[]{:S(2)}, u32[]{:S(2)}) %collective-permute-start.1) | collective-permute-done | bytes 327712 | tf_op jit(solution)/shard_map/ppermute | solution.py:16
  16.7 0.0 copy-done.7
  16.7 0.0 copy-start.8
  16.7 0.7 %copy-done.8 = bf16[4,160,256]{2,1,0:T(8,128)(2,1)} copy-done((bf16[4,160,256]{2,1,0:T(8,128)(2,1)}, bf16[4,160,256]{2,1,0:T(8,128)(2,1)S(1)}, u32[]{:S(2)}) %copy-start.8) | copy-done | bytes 327704
  17.4 7.7 %shard_map.82.own_ref = bf16[10,160,256]{2,1,0:T(8,128)(2,1)} custom-call(s32[2]{0:T(128)} %pad_add_fusion.bounds_ref, bf16[4,160,256]{2,1,0:T(8,128)(2,1)} %copy-done.7, bf16[8,160,256]{2,1,0:T(8,128)(2,1)} %bitcast.28, bf16[4,160,256]{2,1,0:T(8,128)(2,1)} %copy-done.8, bf16[3,3,256,256]{3,2,1,0:T(8,128)(2,1)} %w1_ref.1, bf16[3,3,256,256]{3,2,1,0:T(8,128)(2,1)} %w2_ref.1), custom_call_target="tpu_custom_call" | custom-call | flops 4152360960 | bytes 4653056 | tf_op jit(solution)/shard_map/pallas_call | solution.py:115
  25.1 1.3 %collective-permute-start.8 = (bf16[10,160,256]{2,1,0:T(8,128)(2,1)}, bf16[10,160,256]{2,1,0:T(8,128)(2,1)S(1)}, u32[]{:S(2)}, u32[]{:S(2)}) collective-permute-start(bf16[10,160,256]{2,1,0:T(8,128)(2,1)} %shard_map.82.own_ref), channel_id=1, source_target_pairs={{8,24},{20,4},{9,25},{21,5},{10,26},{22,6},{11,27},{23,7}} | collective-permute-start | bytes 2457608 | tf_op jit(solution)/shard_map/ppermute | solution.py:187
  26.4 1.9 %collective-permute-start.6 = (bf16[10,160,256]{2,1,0:T(8,128)(2,1)}, bf16[10,160,256]{2,1,0:T(8,128)(2,1)S(1)}, u32[]{:S(2)}, u32[]{:S(2)}) collective-permute-start(bf16[10,160,256]{2,1,0:T(8,128)(2,1)} %shard_map.82.own_ref), channel_id=1, source_target_pairs={{8,0},{12,4},{16,8},{24,16},{28,20},{9,1},{13,5},{17,9},{25,17},{2... | collective-permute-start | bytes 2457608 | tf_op jit(solution)/shard_map/ppermute | solution.py:186
  28.3 0.7 %collective-permute-start.3 = (bf16[10,160,256]{2,1,0:T(8,128)(2,1)}, bf16[10,160,256]{2,1,0:T(8,128)(2,1)S(1)}, u32[]{:S(2)}, u32[]{:S(2)}) collective-permute-start(bf16[10,160,256]{2,1,0:T(8,128)(2,1)} %shard_map.82.own_ref), channel_id=1, source_target_pairs={{4,12},{12,20},{20,28},{5,13},{13,21},{21,29},{6,14},{14,22},{22,3... | collective-permute-start | bytes 2457608 | tf_op jit(solution)/shard_map/ppermute | solution.py:194
  29.0 0.5 collective-permute-start.5
  29.5 1.3 %collective-permute-start.2 = (bf16[10,160,256]{2,1,0:T(8,128)(2,1)}, bf16[10,160,256]{2,1,0:T(8,128)(2,1)S(1)}, u32[]{:S(2)}, u32[]{:S(2)}) collective-permute-start(bf16[10,160,256]{2,1,0:T(8,128)(2,1)} %shard_map.82.own_ref), channel_id=1, source_target_pairs={{0,8},{16,24},{1,9},{17,25},{2,10},{18,26},{3,11},{19,27}} | collective-permute-start | bytes 2457608 | tf_op jit(solution)/shard_map/ppermute | solution.py:193
  30.8 8.7 %collective-permute-done.8 = bf16[10,160,256]{2,1,0:T(8,128)(2,1)S(1)} collective-permute-done((bf16[10,160,256]{2,1,0:T(8,128)(2,1)}, bf16[10,160,256]{2,1,0:T(8,128)(2,1)S(1)}, u32[]{:S(2)}, u32[]{:S(2)}) %collective-permute-start.8) | collective-permute-done | bytes 819232 | tf_op jit(solution)/shard_map/ppermute | solution.py:187
  39.5 1.3 %collective-permute-start.9 = (bf16[10,160,256]{2,1,0:T(8,128)(2,1)S(1)}, bf16[10,160,256]{2,1,0:T(8,128)(2,1)S(1)}, u32[]{:S(2)}, u32[]{:S(2)}) collective-permute-start(bf16[10,160,256]{2,1,0:T(8,128)(2,1)S(1)} %collective-permute-done.8), channel_id=1, source_target_pairs={{24,16},{4,12},{25,17},{5,13},{26,18},{6,14},{27,19},{7,15}} | collective-permute-start | bytes 2457608 | tf_op jit(solution)/shard_map/ppermute | solution.py:188
  40.9 5.5 %collective-permute-done.6.fa_ref = bf16[10,160,256]{2,1,0:T(8,128)(2,1)S(1)} collective-permute-done((bf16[10,160,256]{2,1,0:T(8,128)(2,1)}, bf16[10,160,256]{2,1,0:T(8,128)(2,1)S(1)}, u32[]{:S(2)}, u32[]{:S(2)}) %collective-permute-start.6) | collective-permute-done | bytes 819232 | tf_op jit(solution)/shard_map/ppermute | solution.py:186
  46.3 0.0 copy-start
  46.3 0.7 %collective-permute-start.7 = (bf16[10,160,256]{2,1,0:T(8,128)(2,1)S(1)}, bf16[10,160,256]{2,1,0:T(8,128)(2,1)S(1)}, u32[]{:S(2)}, u32[]{:S(2)}) collective-permute-start(bf16[10,160,256]{2,1,0:T(8,128)(2,1)S(1)} %collective-permute-done.6.fa_ref), channel_id=1, source_target_pairs={{0,4},{8,12},{16,20},{1,5},{9,13},{17,21},{2,6},{10,14},{18,22},{3... | collective-permute-start | bytes 2457608 | tf_op jit(solution)/shard_map/ppermute | solution.py:196
  47.0 0.0 collective-permute-done.3.fbo_ref
  47.0 0.0 copy-start.1
  47.1 1.3 %collective-permute-start.4 = (bf16[10,160,256]{2,1,0:T(8,128)(2,1)S(1)}, bf16[10,160,256]{2,1,0:T(8,128)(2,1)S(1)}, u32[]{:S(2)}, u32[]{:S(2)}) collective-permute-start(bf16[10,160,256]{2,1,0:T(8,128)(2,1)S(1)} %collective-permute-done.3.fbo_ref), channel_id=1, source_target_pairs={{12,8},{20,16},{28,24},{13,9},{21,17},{29,25},{14,10},{22,18},{30,... | collective-permute-start | bytes 2457608 | tf_op jit(solution)/shard_map/ppermute | solution.py:195
  48.4 0.0 collective-permute-done.5.par_ref
  48.4 0.0 copy-start.2
  48.4 10.8 %collective-permute-done.2.fb_ref = bf16[10,160,256]{2,1,0:T(8,128)(2,1)S(1)} collective-permute-done((bf16[10,160,256]{2,1,0:T(8,128)(2,1)}, bf16[10,160,256]{2,1,0:T(8,128)(2,1)S(1)}, u32[]{:S(2)}, u32[]{:S(2)}) %collective-permute-start.2) | collective-permute-done | bytes 819232 | tf_op jit(solution)/shard_map/ppermute | solution.py:193
  59.2 0.0 copy-start.3
  59.2 0.0 collective-permute-done.9.routed_ref
  59.2 0.0 collective-permute-done.7.ra_ref
  59.2 0.0 copy-start.5
  59.2 0.0 collective-permute-done.4.rb_ref
  59.2 0.9 %copy-done.4 = bf16[10,160,256]{2,1,0:T(8,128)(2,1)} copy-done((bf16[10,160,256]{2,1,0:T(8,128)(2,1)}, bf16[10,160,256]{2,1,0:T(8,128)(2,1)S(1)}, u32[]{:S(2)}) %copy-start.4) | copy-done | bytes 819224
  60.1 0.2 copy-done.5
  60.3 0.9 %copy-done.6 = bf16[10,160,256]{2,1,0:T(8,128)(2,1)} copy-done((bf16[10,160,256]{2,1,0:T(8,128)(2,1)}, bf16[10,160,256]{2,1,0:T(8,128)(2,1)S(1)}, u32[]{:S(2)}) %copy-start.6) | copy-done | bytes 819224
  61.2 0.0 copy-done
  61.3 0.0 copy-done.1
  61.3 0.0 copy-done.2
  61.3 0.0 copy-done.3
  61.3 6.8 %shard_map.83 = bf16[8,160,256]{2,1,0:T(8,128)(2,1)} custom-call(f32[7]{0:T(128)} %pad_maximum_fusion.2.coef_ref, bf16[10,160,256]{2,1,0:T(8,128)(2,1)} %copy-done.3, bf16[10,160,256]{2,1,0:T(8,128)(2,1)} %copy-done.1, bf16[10,160,256]{2,1,0:T(8,128)(2,1)} %copy-done.6, bf16[10,160,256]{2,1,0:T(8,128)(2,1)} %shard_map.82.own_ref, ...), custom_call_target="tpu_custom_call" | custom-call | flops 1509949440 | bytes 8552448 | tf_op jit(solution)/shard_map/pallas_call | solution.py:131
  (4 shorter events, 0.1 us)
Async XLA Ops:
  0.9 8.4 %copy-start.9 = (s32[1,5]{1,0:T(1,128)S(1)}, s32[1,5]{1,0:T(1,128)}, u32[]{:S(2)}) copy-start(s32[1,5]{1,0:T(1,128)} %param.12) | copy-start | bytes 64
  2.1 13.1 %collective-permute-start = (bf16[4,160,256]{2,1,0:T(8,128)(2,1)S(1)}, bf16[4,160,256]{2,1,0:T(8,128)(2,1)S(1)}, u32[]{:S(2)}, u32[]{:S(2)}) collective-permute-start(bf16[4,160,256]{2,1,0:T(8,128)(2,1)S(1)} %pad_maximum_fusion), channel_id=1, source_target_pairs={{0,1},{1,2},{2,3},{4,5},{5,6},{6,7},{8,9},{9,10},{10,11},{12,13},{... | collective-permute-start | bytes 983048 | tf_op jit(solution)/shard_map/ppermute | solution.py:16
  5.6 11.1 %collective-permute-start.1 = (bf16[4,160,256]{2,1,0:T(8,128)(2,1)S(1)}, bf16[4,160,256]{2,1,0:T(8,128)(2,1)S(1)}, u32[]{:S(2)}, u32[]{:S(2)}) collective-permute-start(bf16[4,160,256]{2,1,0:T(8,128)(2,1)S(1)} %pad_maximum_fusion.1), channel_id=1, source_target_pairs={{1,0},{2,1},{3,2},{5,4},{6,5},{7,6},{9,8},{10,9},{11,10},{13,12},{... | collective-permute-start | bytes 983048 | tf_op jit(solution)/shard_map/ppermute | solution.py:16
  15.2 1.5 %copy-start.7 = (bf16[4,160,256]{2,1,0:T(8,128)(2,1)}, bf16[4,160,256]{2,1,0:T(8,128)(2,1)S(1)}, u32[]{:S(2)}) copy-start(bf16[4,160,256]{2,1,0:T(8,128)(2,1)S(1)} %collective-permute-done.above_ref) | copy-start | bytes 983044
  16.7 0.7 %copy-start.8 = (bf16[4,160,256]{2,1,0:T(8,128)(2,1)}, bf16[4,160,256]{2,1,0:T(8,128)(2,1)S(1)}, u32[]{:S(2)}) copy-start(bf16[4,160,256]{2,1,0:T(8,128)(2,1)S(1)} %collective-permute-done.1.below_ref) | copy-start | bytes 983044
  25.1 14.4 %collective-permute-start.8 = (bf16[10,160,256]{2,1,0:T(8,128)(2,1)}, bf16[10,160,256]{2,1,0:T(8,128)(2,1)S(1)}, u32[]{:S(2)}, u32[]{:S(2)}) collective-permute-start(bf16[10,160,256]{2,1,0:T(8,128)(2,1)} %shard_map.82.own_ref), channel_id=1, source_target_pairs={{8,24},{20,4},{9,25},{21,5},{10,26},{22,6},{11,27},{23,7}} | collective-permute-start | bytes 2457608 | tf_op jit(solution)/shard_map/ppermute | solution.py:187
  26.4 19.9 %collective-permute-start.6 = (bf16[10,160,256]{2,1,0:T(8,128)(2,1)}, bf16[10,160,256]{2,1,0:T(8,128)(2,1)S(1)}, u32[]{:S(2)}, u32[]{:S(2)}) collective-permute-start(bf16[10,160,256]{2,1,0:T(8,128)(2,1)} %shard_map.82.own_ref), channel_id=1, source_target_pairs={{8,0},{12,4},{16,8},{24,16},{28,20},{9,1},{13,5},{17,9},{25,17},{2... | collective-permute-start | bytes 2457608 | tf_op jit(solution)/shard_map/ppermute | solution.py:186
  28.3 18.8 %collective-permute-start.3 = (bf16[10,160,256]{2,1,0:T(8,128)(2,1)}, bf16[10,160,256]{2,1,0:T(8,128)(2,1)S(1)}, u32[]{:S(2)}, u32[]{:S(2)}) collective-permute-start(bf16[10,160,256]{2,1,0:T(8,128)(2,1)} %shard_map.82.own_ref), channel_id=1, source_target_pairs={{4,12},{12,20},{20,28},{5,13},{13,21},{21,29},{6,14},{14,22},{22,3... | collective-permute-start | bytes 2457608 | tf_op jit(solution)/shard_map/ppermute | solution.py:194
  29.0 19.4 %collective-permute-start.5 = (bf16[10,160,256]{2,1,0:T(8,128)(2,1)}, bf16[10,160,256]{2,1,0:T(8,128)(2,1)S(1)}, u32[]{:S(2)}, u32[]{:S(2)}) collective-permute-start(bf16[10,160,256]{2,1,0:T(8,128)(2,1)} %shard_map.82.own_ref), channel_id=1, source_target_pairs={{0,4},{4,0},{8,12},{12,8},{16,20},{20,16},{24,28},{28,24},{1,5},{5... | collective-permute-start | bytes 2457608 | tf_op jit(solution)/shard_map/ppermute | solution.py:183
  29.5 29.7 %collective-permute-start.2 = (bf16[10,160,256]{2,1,0:T(8,128)(2,1)}, bf16[10,160,256]{2,1,0:T(8,128)(2,1)S(1)}, u32[]{:S(2)}, u32[]{:S(2)}) collective-permute-start(bf16[10,160,256]{2,1,0:T(8,128)(2,1)} %shard_map.82.own_ref), channel_id=1, source_target_pairs={{0,8},{16,24},{1,9},{17,25},{2,10},{18,26},{3,11},{19,27}} | collective-permute-start | bytes 2457608 | tf_op jit(solution)/shard_map/ppermute | solution.py:193
  39.5 19.6 %collective-permute-start.9 = (bf16[10,160,256]{2,1,0:T(8,128)(2,1)S(1)}, bf16[10,160,256]{2,1,0:T(8,128)(2,1)S(1)}, u32[]{:S(2)}, u32[]{:S(2)}) collective-permute-start(bf16[10,160,256]{2,1,0:T(8,128)(2,1)S(1)} %collective-permute-done.8), channel_id=1, source_target_pairs={{24,16},{4,12},{25,17},{5,13},{26,18},{6,14},{27,19},{7,15}} | collective-permute-start | bytes 2457608 | tf_op jit(solution)/shard_map/ppermute | solution.py:188
  46.3 14.9 %copy-start = (bf16[10,160,256]{2,1,0:T(8,128)(2,1)}, bf16[10,160,256]{2,1,0:T(8,128)(2,1)S(1)}, u32[]{:S(2)}) copy-start(bf16[10,160,256]{2,1,0:T(8,128)(2,1)S(1)} %collective-permute-done.6.fa_ref) | copy-start | bytes 2457604
  46.3 12.8 %collective-permute-start.7 = (bf16[10,160,256]{2,1,0:T(8,128)(2,1)S(1)}, bf16[10,160,256]{2,1,0:T(8,128)(2,1)S(1)}, u32[]{:S(2)}, u32[]{:S(2)}) collective-permute-start(bf16[10,160,256]{2,1,0:T(8,128)(2,1)S(1)} %collective-permute-done.6.fa_ref), channel_id=1, source_target_pairs={{0,4},{8,12},{16,20},{1,5},{9,13},{17,21},{2,6},{10,14},{18,22},{3... | collective-permute-start | bytes 2457608 | tf_op jit(solution)/shard_map/ppermute | solution.py:196
  47.0 14.2 %copy-start.1 = (bf16[10,160,256]{2,1,0:T(8,128)(2,1)}, bf16[10,160,256]{2,1,0:T(8,128)(2,1)S(1)}, u32[]{:S(2)}) copy-start(bf16[10,160,256]{2,1,0:T(8,128)(2,1)S(1)} %collective-permute-done.3.fbo_ref) | copy-start | bytes 2457604
  47.1 12.1 %collective-permute-start.4 = (bf16[10,160,256]{2,1,0:T(8,128)(2,1)S(1)}, bf16[10,160,256]{2,1,0:T(8,128)(2,1)S(1)}, u32[]{:S(2)}, u32[]{:S(2)}) collective-permute-start(bf16[10,160,256]{2,1,0:T(8,128)(2,1)S(1)} %collective-permute-done.3.fbo_ref), channel_id=1, source_target_pairs={{12,8},{20,16},{28,24},{13,9},{21,17},{29,25},{14,10},{22,18},{30,... | collective-permute-start | bytes 2457608 | tf_op jit(solution)/shard_map/ppermute | solution.py:195
  48.4 12.9 %copy-start.2 = (bf16[10,160,256]{2,1,0:T(8,128)(2,1)}, bf16[10,160,256]{2,1,0:T(8,128)(2,1)S(1)}, u32[]{:S(2)}) copy-start(bf16[10,160,256]{2,1,0:T(8,128)(2,1)S(1)} %collective-permute-done.5.par_ref) | copy-start | bytes 2457604
  59.2 2.1 %copy-start.3 = (bf16[10,160,256]{2,1,0:T(8,128)(2,1)}, bf16[10,160,256]{2,1,0:T(8,128)(2,1)S(1)}, u32[]{:S(2)}) copy-start(bf16[10,160,256]{2,1,0:T(8,128)(2,1)S(1)} %collective-permute-done.2.fb_ref) | copy-start | bytes 2457604
  59.2 0.9 %copy-start.4 = (bf16[10,160,256]{2,1,0:T(8,128)(2,1)}, bf16[10,160,256]{2,1,0:T(8,128)(2,1)S(1)}, u32[]{:S(2)}) copy-start(bf16[10,160,256]{2,1,0:T(8,128)(2,1)S(1)} %collective-permute-done.9.routed_ref) | copy-start | bytes 2457604
  59.2 1.2 %copy-start.5 = (bf16[10,160,256]{2,1,0:T(8,128)(2,1)}, bf16[10,160,256]{2,1,0:T(8,128)(2,1)S(1)}, u32[]{:S(2)}) copy-start(bf16[10,160,256]{2,1,0:T(8,128)(2,1)S(1)} %collective-permute-done.7.ra_ref) | copy-start | bytes 2457604
  60.3 0.9 %copy-start.6 = (bf16[10,160,256]{2,1,0:T(8,128)(2,1)}, bf16[10,160,256]{2,1,0:T(8,128)(2,1)S(1)}, u32[]{:S(2)}) copy-start(bf16[10,160,256]{2,1,0:T(8,128)(2,1)S(1)} %collective-permute-done.4.rb_ref) | copy-start | bytes 2457604

commit v22 on v21

--- a/solution.py
+++ b/solution.py
@@ -135,7 +135,7 @@
         out_specs=vmem(),
         scratch_shapes=[pltpu.VMEM((block + 2, cols, c), jnp.bfloat16),
                         pltpu.VMEM((block + 2, cols, c), jnp.bfloat16),
-                        pltpu.VMEM((CHUNK, cols, 3 * c), jnp.bfloat16)],
+                        pltpu.VMEM((2 * CHUNK, cols, 3 * c), jnp.bfloat16)],
         cost_estimate=pl.CostEstimate(flops=flops, transcendentals=0,
                                       bytes_accessed=18 * (block + 2) * cols * c + 2 * 9 * c * c),
     )(coef, fb, fbo, rb, own, par, ra, fa, routed, above, frame, below, w3)

time: 68.5 us -> 68.5 us (level)
  no operation moved by 1% of the time
where the time goes in v22:
time: 68.5 us; the launch traced here: 68.1 us
  waiting for transfers between devices  26.5 us (39%)
  starting transfers between devices  14.8 us (22%)
  Pallas kernels  14.5 us (21%)
  local copies, waits for them, and re-layouts  5.58 us (8%)
  between operations  4.03 us (6%)
  other arithmetic  2.62 us (4%)
    ppermute x1, waiting for transfers between devices, shards(): lax.ppermute(second, 'tm', [(a, b) for a, b in behind_pairs if b % 2 == 0])  10.8 us
    ppermute x1, waiting for transfers between devices, shards(): hop = lax.ppermute(second, 'tm', [(2, 6), (5, 1)])  8.74 us
    pallas_call x1, Pallas kernels, layers(): pl.pallas_call(layers_kernel, out_shape=jax.ShapeDtypeStruct((rows - 4, c...  7.67 us
    pallas_call x1, Pallas kernels, mix(): pl.pallas_call(mix_kernel, out_shape=jax.ShapeDtypeStruct((block, cols, c...  6.81 us
    ppermute x2, starting transfers between devices, shifted(): return lax.ppermute(value, axis, pairs)  5.84 us
    ppermute x1, waiting for transfers between devices, shards(): lax.ppermute(second, 'tm', [(2, 0), (3, 1), (4, 2), (6, 4), (7, 5)])  5.46 us
    unnamed x20, local copies, waits for them, and re-layouts  2.8 us
    slice x2, local copies, waits for them, and re-layouts, shards(): up = jnp.concatenate([image[:3], frame[:1]], axis=0)  2.04 us
  transfers between devices with their start and end apart: 10, of which 4 were waited for; matrix products, arithmetic and copies ran while one was open for 5% of the time, Pallas kernels for 0%

profile of v22, /device:TPU:22, one launch (start us, length us, event | category | flops | bytes accessed | tf_op | source)
XLA Modules:
  0.0 68.1 jit_solution(6190201655743828533)
XLA Ops:
  0.0 0.9 %slice_bitcast_fusion.2 = (bf16[1,160,256]{2,1,0:T(8,128)(2,1)S(1)}, bf16[1,160,256]{2,1,0:T(8,128)(2,1)S(1)}) fusion(bf16[1,8,160,256]{3,2,1,0:T(8,128)(2,1)} %param.9), kind=kLoop, calls=%fused_computation.4 | loop fusion | bytes 327680 | tf_op jit(solution)/shard_map/slice | solution.py:161
  0.9 0.0 copy-start.9
  1.0 1.1 %slice_bitcast_fusion = (bf16[3,160,256]{2,1,0:T(8,128)(2,1)S(1)}, bf16[3,160,256]{2,1,0:T(8,128)(2,1)S(1)}) fusion(bf16[1,8,160,256]{3,2,1,0:T(8,128)(2,1)} %param.8), kind=kLoop, calls=%fused_computation.2 | loop fusion | bytes 983040 | tf_op jit(solution)/shard_map/slice | solution.py:161
  2.1 3.5 %collective-permute-start = (bf16[4,160,256]{2,1,0:T(8,128)(2,1)S(1)}, bf16[4,160,256]{2,1,0:T(8,128)(2,1)S(1)}, u32[]{:S(2)}, u32[]{:S(2)}) collective-permute-start(bf16[4,160,256]{2,1,0:T(8,128)(2,1)S(1)} %pad_maximum_fusion), channel_id=1, source_target_pairs={{0,1},{1,2},{2,3},{4,5},{5,6},{6,7},{8,9},{9,10},{10,11},{12,13},{... | collective-permute-start | bytes 983048 | tf_op jit(solution)/shard_map/ppermute | solution.py:16
  5.6 2.4 %collective-permute-start.1 = (bf16[4,160,256]{2,1,0:T(8,128)(2,1)S(1)}, bf16[4,160,256]{2,1,0:T(8,128)(2,1)S(1)}, u32[]{:S(2)}, u32[]{:S(2)}) collective-permute-start(bf16[4,160,256]{2,1,0:T(8,128)(2,1)S(1)} %pad_maximum_fusion.1), channel_id=1, source_target_pairs={{1,0},{2,1},{3,2},{5,4},{6,5},{7,6},{9,8},{10,9},{11,10},{13,12},{... | collective-permute-start | bytes 983048 | tf_op jit(solution)/shard_map/ppermute | solution.py:16
  9.3 0.0 copy-done.9
  9.3 0.6 fusion
  9.9 0.6 broadcast_divide_fusion
  10.6 0.1 slice.45
  10.6 0.7 fusion.1
  13.8 0.6 pad_add_fusion.bounds_ref
  14.5 0.7 pad_maximum_fusion.2.coef_ref
  15.2 0.0 collective-permute-done.above_ref
  15.2 0.0 copy-start.7
  15.2 1.5 %collective-permute-done.1.below_ref = bf16[4,160,256]{2,1,0:T(8,128)(2,1)S(1)} collective-permute-done((bf16[4,160,256]{2,1,0:T(8,128)(2,1)S(1)}, bf16[4,160,256]{2,1,0:T(8,128)(2,1)S(1)}, u32[]{:S(2)}, u32[]{:S(2)}) %collective-permute-start.1) | collective-permute-done | bytes 327712 | tf_op jit(solution)/shard_map/ppermute | solution.py:16
  16.7 0.0 copy-done.7
  16.7 0.0 copy-start.8
  16.7 0.7 %copy-done.8 = bf16[4,160,256]{2,1,0:T(8,128)(2,1)} copy-done((bf16[4,160,256]{2,1,0:T(8,128)(2,1)}, bf16[4,160,256]{2,1,0:T(8,128)(2,1)S(1)}, u32[]{:S(2)}) %copy-start.8) | copy-done | bytes 327704
  17.4 7.7 %shard_map.82.own_ref = bf16[10,160,256]{2,1,0:T(8,128)(2,1)} custom-call(s32[2]{0:T(128)} %pad_add_fusion.bounds_ref, bf16[4,160,256]{2,1,0:T(8,128)(2,1)} %copy-done.7, bf16[8,160,256]{2,1,0:T(8,128)(2,1)} %bitcast.28, bf16[4,160,256]{2,1,0:T(8,128)(2,1)} %copy-done.8, bf16[3,3,256,256]{3,2,1,0:T(8,128)(2,1)} %w1_ref.1, bf16[3,3,256,256]{3,2,1,0:T(8,128)(2,1)} %w2_ref.1), custom_call_target="tpu_custom_call" | custom-call | flops 4152360960 | bytes 4653056 | tf_op jit(solution)/shard_map/pallas_call | solution.py:115
  25.1 1.3 %collective-permute-start.8 = (bf16[10,160,256]{2,1,0:T(8,128)(2,1)}, bf16[10,160,256]{2,1,0:T(8,128)(2,1)S(1)}, u32[]{:S(2)}, u32[]{:S(2)}) collective-permute-start(bf16[10,160,256]{2,1,0:T(8,128)(2,1)} %shard_map.82.own_ref), channel_id=1, source_target_pairs={{8,24},{20,4},{9,25},{21,5},{10,26},{22,6},{11,27},{23,7}} | collective-permute-start | bytes 2457608 | tf_op jit(solution)/shard_map/ppermute | solution.py:187
  26.4 1.9 %collective-permute-start.6 = (bf16[10,160,256]{2,1,0:T(8,128)(2,1)}, bf16[10,160,256]{2,1,0:T(8,128)(2,1)S(1)}, u32[]{:S(2)}, u32[]{:S(2)}) collective-permute-start(bf16[10,160,256]{2,1,0:T(8,128)(2,1)} %shard_map.82.own_ref), channel_id=1, source_target_pairs={{8,0},{12,4},{16,8},{24,16},{28,20},{9,1},{13,5},{17,9},{25,17},{2... | collective-permute-start | bytes 2457608 | tf_op jit(solution)/shard_map/ppermute | solution.py:186
  28.3 0.7 %collective-permute-start.3 = (bf16[10,160,256]{2,1,0:T(8,128)(2,1)}, bf16[10,160,256]{2,1,0:T(8,128)(2,1)S(1)}, u32[]{:S(2)}, u32[]{:S(2)}) collective-permute-start(bf16[10,160,256]{2,1,0:T(8,128)(2,1)} %shard_map.82.own_ref), channel_id=1, source_target_pairs={{4,12},{12,20},{20,28},{5,13},{13,21},{21,29},{6,14},{14,22},{22,3... | collective-permute-start | bytes 2457608 | tf_op jit(solution)/shard_map/ppermute | solution.py:194
  29.0 0.5 collective-permute-start.5
  29.5 1.3 %collective-permute-start.2 = (bf16[10,160,256]{2,1,0:T(8,128)(2,1)}, bf16[10,160,256]{2,1,0:T(8,128)(2,1)S(1)}, u32[]{:S(2)}, u32[]{:S(2)}) collective-permute-start(bf16[10,160,256]{2,1,0:T(8,128)(2,1)} %shard_map.82.own_ref), channel_id=1, source_target_pairs={{0,8},{16,24},{1,9},{17,25},{2,10},{18,26},{3,11},{19,27}} | collective-permute-start | bytes 2457608 | tf_op jit(solution)/shard_map/ppermute | solution.py:193
  30.8 8.7 %collective-permute-done.8 = bf16[10,160,256]{2,1,0:T(8,128)(2,1)S(1)} collective-permute-done((bf16[10,160,256]{2,1,0:T(8,128)(2,1)}, bf16[10,160,256]{2,1,0:T(8,128)(2,1)S(1)}, u32[]{:S(2)}, u32[]{:S(2)}) %collective-permute-start.8) | collective-permute-done | bytes 819232 | tf_op jit(solution)/shard_map/ppermute | solution.py:187
  39.5 1.3 %collective-permute-start.9 = (bf16[10,160,256]{2,1,0:T(8,128)(2,1)S(1)}, bf16[10,160,256]{2,1,0:T(8,128)(2,1)S(1)}, u32[]{:S(2)}, u32[]{:S(2)}) collective-permute-start(bf16[10,160,256]{2,1,0:T(8,128)(2,1)S(1)} %collective-permute-done.8), channel_id=1, source_target_pairs={{24,16},{4,12},{25,17},{5,13},{26,18},{6,14},{27,19},{7,15}} | collective-permute-start | bytes 2457608 | tf_op jit(solution)/shard_map/ppermute | solution.py:188
  40.9 5.5 %collective-permute-done.6.fa_ref = bf16[10,160,256]{2,1,0:T(8,128)(2,1)S(1)} collective-permute-done((bf16[10,160,256]{2,1,0:T(8,128)(2,1)}, bf16[10,160,256]{2,1,0:T(8,128)(2,1)S(1)}, u32[]{:S(2)}, u32[]{:S(2)}) %collective-permute-start.6) | collective-permute-done | bytes 819232 | tf_op jit(solution)/shard_map/ppermute | solution.py:186
  46.3 0.0 copy-start
  46.3 0.7 %collective-permute-start.7 = (bf16[10,160,256]{2,1,0:T(8,128)(2,1)S(1)}, bf16[10,160,256]{2,1,0:T(8,128)(2,1)S(1)}, u32[]{:S(2)}, u32[]{:S(2)}) collective-permute-start(bf16[10,160,256]{2,1,0:T(8,128)(2,1)S(1)} %collective-permute-done.6.fa_ref), channel_id=1, source_target_pairs={{0,4},{8,12},{16,20},{1,5},{9,13},{17,21},{2,6},{10,14},{18,22},{3... | collective-permute-start | bytes 2457608 | tf_op jit(solution)/shard_map/ppermute | solution.py:196
  47.0 0.0 collective-permute-done.3.fbo_ref
  47.0 0.0 copy-start.1
  47.1 1.3 %collective-permute-start.4 = (bf16[10,160,256]{2,1,0:T(8,128)(2,1)S(1)}, bf16[10,160,256]{2,1,0:T(8,128)(2,1)S(1)}, u32[]{:S(2)}, u32[]{:S(2)}) collective-permute-start(bf16[10,160,256]{2,1,0:T(8,128)(2,1)S(1)} %collective-permute-done.3.fbo_ref), channel_id=1, source_target_pairs={{12,8},{20,16},{28,24},{13,9},{21,17},{29,25},{14,10},{22,18},{30,... | collective-permute-start | bytes 2457608 | tf_op jit(solution)/shard_map/ppermute | solution.py:195
  48.4 0.0 collective-permute-done.5.par_ref
  48.4 0.0 copy-start.2
  48.4 10.8 %collective-permute-done.2.fb_ref = bf16[10,160,256]{2,1,0:T(8,128)(2,1)S(1)} collective-permute-done((bf16[10,160,256]{2,1,0:T(8,128)(2,1)}, bf16[10,160,256]{2,1,0:T(8,128)(2,1)S(1)}, u32[]{:S(2)}, u32[]{:S(2)}) %collective-permute-start.2) | collective-permute-done | bytes 819232 | tf_op jit(solution)/shard_map/ppermute | solution.py:193
  59.2 0.0 copy-start.3
  59.2 0.0 collective-permute-done.9.routed_ref
  59.2 0.0 collective-permute-done.7.ra_ref
  59.2 0.0 copy-start.5
  59.2 0.0 collective-permute-done.4.rb_ref
  59.2 0.9 %copy-done.4 = bf16[10,160,256]{2,1,0:T(8,128)(2,1)} copy-done((bf16[10,160,256]{2,1,0:T(8,128)(2,1)}, bf16[10,160,256]{2,1,0:T(8,128)(2,1)S(1)}, u32[]{:S(2)}) %copy-start.4) | copy-done | bytes 819224
  60.1 0.2 copy-done.5
  60.3 0.9 %copy-done.6 = bf16[10,160,256]{2,1,0:T(8,128)(2,1)} copy-done((bf16[10,160,256]{2,1,0:T(8,128)(2,1)}, bf16[10,160,256]{2,1,0:T(8,128)(2,1)S(1)}, u32[]{:S(2)}) %copy-start.6) | copy-done | bytes 819224
  61.2 0.0 copy-done
  61.3 0.0 copy-done.1
  61.3 0.0 copy-done.2
  61.3 0.0 copy-done.3
  61.3 6.8 %shard_map.83 = bf16[8,160,256]{2,1,0:T(8,128)(2,1)} custom-call(f32[7]{0:T(128)} %pad_maximum_fusion.2.coef_ref, bf16[10,160,256]{2,1,0:T(8,128)(2,1)} %copy-done.3, bf16[10,160,256]{2,1,0:T(8,128)(2,1)} %copy-done.1, bf16[10,160,256]{2,1,0:T(8,128)(2,1)} %copy-done.6, bf16[10,160,256]{2,1,0:T(8,128)(2,1)} %shard_map.82.own_ref, ...), custom_call_target="tpu_custom_call" | custom-call | flops 1509949440 | bytes 8552448 | tf_op jit(solution)/shard_map/pallas_call | solution.py:131
  (4 shorter events, 0.1 us)
Async XLA Ops:
  0.9 8.4 %copy-start.9 = (s32[1,5]{1,0:T(1,128)S(1)}, s32[1,5]{1,0:T(1,128)}, u32[]{:S(2)}) copy-start(s32[1,5]{1,0:T(1,128)} %param.12) | copy-start | bytes 64
  2.1 13.1 %collective-permute-start = (bf16[4,160,256]{2,1,0:T(8,128)(2,1)S(1)}, bf16[4,160,256]{2,1,0:T(8,128)(2,1)S(1)}, u32[]{:S(2)}, u32[]{:S(2)}) collective-permute-start(bf16[4,160,256]{2,1,0:T(8,128)(2,1)S(1)} %pad_maximum_fusion), channel_id=1, source_target_pairs={{0,1},{1,2},{2,3},{4,5},{5,6},{6,7},{8,9},{9,10},{10,11},{12,13},{... | collective-permute-start | bytes 983048 | tf_op jit(solution)/shard_map/ppermute | solution.py:16
  5.6 11.1 %collective-permute-start.1 = (bf16[4,160,256]{2,1,0:T(8,128)(2,1)S(1)}, bf16[4,160,256]{2,1,0:T(8,128)(2,1)S(1)}, u32[]{:S(2)}, u32[]{:S(2)}) collective-permute-start(bf16[4,160,256]{2,1,0:T(8,128)(2,1)S(1)} %pad_maximum_fusion.1), channel_id=1, source_target_pairs={{1,0},{2,1},{3,2},{5,4},{6,5},{7,6},{9,8},{10,9},{11,10},{13,12},{... | collective-permute-start | bytes 983048 | tf_op jit(solution)/shard_map/ppermute | solution.py:16
  15.2 1.5 %copy-start.7 = (bf16[4,160,256]{2,1,0:T(8,128)(2,1)}, bf16[4,160,256]{2,1,0:T(8,128)(2,1)S(1)}, u32[]{:S(2)}) copy-start(bf16[4,160,256]{2,1,0:T(8,128)(2,1)S(1)} %collective-permute-done.above_ref) | copy-start | bytes 983044
  16.7 0.7 %copy-start.8 = (bf16[4,160,256]{2,1,0:T(8,128)(2,1)}, bf16[4,160,256]{2,1,0:T(8,128)(2,1)S(1)}, u32[]{:S(2)}) copy-start(bf16[4,160,256]{2,1,0:T(8,128)(2,1)S(1)} %collective-permute-done.1.below_ref) | copy-start | bytes 983044
  25.1 14.4 %collective-permute-start.8 = (bf16[10,160,256]{2,1,0:T(8,128)(2,1)}, bf16[10,160,256]{2,1,0:T(8,128)(2,1)S(1)}, u32[]{:S(2)}, u32[]{:S(2)}) collective-permute-start(bf16[10,160,256]{2,1,0:T(8,128)(2,1)} %shard_map.82.own_ref), channel_id=1, source_target_pairs={{8,24},{20,4},{9,25},{21,5},{10,26},{22,6},{11,27},{23,7}} | collective-permute-start | bytes 2457608 | tf_op jit(solution)/shard_map/ppermute | solution.py:187
  26.4 19.9 %collective-permute-start.6 = (bf16[10,160,256]{2,1,0:T(8,128)(2,1)}, bf16[10,160,256]{2,1,0:T(8,128)(2,1)S(1)}, u32[]{:S(2)}, u32[]{:S(2)}) collective-permute-start(bf16[10,160,256]{2,1,0:T(8,128)(2,1)} %shard_map.82.own_ref), channel_id=1, source_target_pairs={{8,0},{12,4},{16,8},{24,16},{28,20},{9,1},{13,5},{17,9},{25,17},{2... | collective-permute-start | bytes 2457608 | tf_op jit(solution)/shard_map/ppermute | solution.py:186
  28.3 18.8 %collective-permute-start.3 = (bf16[10,160,256]{2,1,0:T(8,128)(2,1)}, bf16[10,160,256]{2,1,0:T(8,128)(2,1)S(1)}, u32[]{:S(2)}, u32[]{:S(2)}) collective-permute-start(bf16[10,160,256]{2,1,0:T(8,128)(2,1)} %shard_map.82.own_ref), channel_id=1, source_target_pairs={{4,12},{12,20},{20,28},{5,13},{13,21},{21,29},{6,14},{14,22},{22,3... | collective-permute-start | bytes 2457608 | tf_op jit(solution)/shard_map/ppermute | solution.py:194
  29.0 19.4 %collective-permute-start.5 = (bf16[10,160,256]{2,1,0:T(8,128)(2,1)}, bf16[10,160,256]{2,1,0:T(8,128)(2,1)S(1)}, u32[]{:S(2)}, u32[]{:S(2)}) collective-permute-start(bf16[10,160,256]{2,1,0:T(8,128)(2,1)} %shard_map.82.own_ref), channel_id=1, source_target_pairs={{0,4},{4,0},{8,12},{12,8},{16,20},{20,16},{24,28},{28,24},{1,5},{5... | collective-permute-start | bytes 2457608 | tf_op jit(solution)/shard_map/ppermute | solution.py:183
  29.5 29.7 %collective-permute-start.2 = (bf16[10,160,256]{2,1,0:T(8,128)(2,1)}, bf16[10,160,256]{2,1,0:T(8,128)(2,1)S(1)}, u32[]{:S(2)}, u32[]{:S(2)}) collective-permute-start(bf16[10,160,256]{2,1,0:T(8,128)(2,1)} %shard_map.82.own_ref), channel_id=1, source_target_pairs={{0,8},{16,24},{1,9},{17,25},{2,10},{18,26},{3,11},{19,27}} | collective-permute-start | bytes 2457608 | tf_op jit(solution)/shard_map/ppermute | solution.py:193
  39.5 19.6 %collective-permute-start.9 = (bf16[10,160,256]{2,1,0:T(8,128)(2,1)S(1)}, bf16[10,160,256]{2,1,0:T(8,128)(2,1)S(1)}, u32[]{:S(2)}, u32[]{:S(2)}) collective-permute-start(bf16[10,160,256]{2,1,0:T(8,128)(2,1)S(1)} %collective-permute-done.8), channel_id=1, source_target_pairs={{24,16},{4,12},{25,17},{5,13},{26,18},{6,14},{27,19},{7,15}} | collective-permute-start | bytes 2457608 | tf_op jit(solution)/shard_map/ppermute | solution.py:188
  46.3 14.9 %copy-start = (bf16[10,160,256]{2,1,0:T(8,128)(2,1)}, bf16[10,160,256]{2,1,0:T(8,128)(2,1)S(1)}, u32[]{:S(2)}) copy-start(bf16[10,160,256]{2,1,0:T(8,128)(2,1)S(1)} %collective-permute-done.6.fa_ref) | copy-start | bytes 2457604
  46.3 12.8 %collective-permute-start.7 = (bf16[10,160,256]{2,1,0:T(8,128)(2,1)S(1)}, bf16[10,160,256]{2,1,0:T(8,128)(2,1)S(1)}, u32[]{:S(2)}, u32[]{:S(2)}) collective-permute-start(bf16[10,160,256]{2,1,0:T(8,128)(2,1)S(1)} %collective-permute-done.6.fa_ref), channel_id=1, source_target_pairs={{0,4},{8,12},{16,20},{1,5},{9,13},{17,21},{2,6},{10,14},{18,22},{3... | collective-permute-start | bytes 2457608 | tf_op jit(solution)/shard_map/ppermute | solution.py:196
  47.0 14.2 %copy-start.1 = (bf16[10,160,256]{2,1,0:T(8,128)(2,1)}, bf16[10,160,256]{2,1,0:T(8,128)(2,1)S(1)}, u32[]{:S(2)}) copy-start(bf16[10,160,256]{2,1,0:T(8,128)(2,1)S(1)} %collective-permute-done.3.fbo_ref) | copy-start | bytes 2457604
  47.1 12.1 %collective-permute-start.4 = (bf16[10,160,256]{2,1,0:T(8,128)(2,1)S(1)}, bf16[10,160,256]{2,1,0:T(8,128)(2,1)S(1)}, u32[]{:S(2)}, u32[]{:S(2)}) collective-permute-start(bf16[10,160,256]{2,1,0:T(8,128)(2,1)S(1)} %collective-permute-done.3.fbo_ref), channel_id=1, source_target_pairs={{12,8},{20,16},{28,24},{13,9},{21,17},{29,25},{14,10},{22,18},{30,... | collective-permute-start | bytes 2457608 | tf_op jit(solution)/shard_map/ppermute | solution.py:195
  48.4 12.9 %copy-start.2 = (bf16[10,160,256]{2,1,0:T(8,128)(2,1)}, bf16[10,160,256]{2,1,0:T(8,128)(2,1)S(1)}, u32[]{:S(2)}) copy-start(bf16[10,160,256]{2,1,0:T(8,128)(2,1)S(1)} %collective-permute-done.5.par_ref) | copy-start | bytes 2457604
  59.2 2.1 %copy-start.3 = (bf16[10,160,256]{2,1,0:T(8,128)(2,1)}, bf16[10,160,256]{2,1,0:T(8,128)(2,1)S(1)}, u32[]{:S(2)}) copy-start(bf16[10,160,256]{2,1,0:T(8,128)(2,1)S(1)} %collective-permute-done.2.fb_ref) | copy-start | bytes 2457604
  59.2 0.9 %copy-start.4 = (bf16[10,160,256]{2,1,0:T(8,128)(2,1)}, bf16[10,160,256]{2,1,0:T(8,128)(2,1)S(1)}, u32[]{:S(2)}) copy-start(bf16[10,160,256]{2,1,0:T(8,128)(2,1)S(1)} %collective-permute-done.9.routed_ref) | copy-start | bytes 2457604
  59.2 1.2 %copy-start.5 = (bf16[10,160,256]{2,1,0:T(8,128)(2,1)}, bf16[10,160,256]{2,1,0:T(8,128)(2,1)S(1)}, u32[]{:S(2)}) copy-start(bf16[10,160,256]{2,1,0:T(8,128)(2,1)S(1)} %collective-permute-done.7.ra_ref) | copy-start | bytes 2457604
  60.3 0.9 %copy-start.6 = (bf16[10,160,256]{2,1,0:T(8,128)(2,1)}, bf16[10,160,256]{2,1,0:T(8,128)(2,1)S(1)}, u32[]{:S(2)}) copy-start(bf16[10,160,256]{2,1,0:T(8,128)(2,1)S(1)} %collective-permute-done.4.rb_ref) | copy-start | bytes 2457604

commit v23 on v21

--- a/solution.py
+++ b/solution.py
@@ -80,7 +80,8 @@
     for r0 in range(0, block + 2, step):
         rows = pl.ds(r0, min(step, block + 2 - r0))
         summed = (
-            coef_ref[0] * (fb_ref[rows].astype(f32) + fbo_ref[rows].astype(f32))
+            coef_ref[7] * fb_ref[rows].astype(f32)
+            + coef_ref[0] * fbo_ref[rows].astype(f32)
             + coef_ref[1] * rb_ref[rows].astype(f32)
             + coef_ref[2] * own_ref[rows].astype(f32)
             + coef_ref[3] * par_ref[rows].astype(f32)
@@ -174,7 +175,9 @@
     is_odd = (t % 2) == 1
     partner_weight = jnp.where(is_odd, weights[1], weights[3])
     routed_weight = jnp.where(is_odd, weights[4], weights[0])
-    coef = jnp.concatenate([weights[:3], partner_weight[None], weights[3:], routed_weight[None]])
+    mixed_weight = jnp.where(is_odd, weights[4], weights[0])
+    coef = jnp.concatenate([weights[:3], partner_weight[None], weights[3:], routed_weight[None],
+                            mixed_weight[None]])
     bounds = jnp.stack([2 - row0, height - row0 + 2]).astype(jnp.int32)
     coef, bounds, image = lax.optimization_barrier((coef, bounds, image))
 
@@ -183,14 +186,16 @@
     partner = lax.ppermute(second, "tm", [(i, i ^ 1) for i in range(count)])
     if count == 8:
         behind_pairs = [(0, 2), (1, 3), (3, 5), (4, 6), (5, 7)]
-        from_ahead = lax.ppermute(second, "tm", [(2, 0), (3, 1), (4, 2), (6, 4), (7, 5)])
+        ahead_pairs = [(2, 0), (3, 1), (4, 2), (6, 4), (7, 5)]
         hop = lax.ppermute(second, "tm", [(2, 6), (5, 1)])
         routed = lax.ppermute(hop, "tm", [(6, 4), (1, 3)])
     else:
         behind_pairs = [(i, i + 2) for i in range(count - 2)]
-        from_ahead = shifted(second, "tm", -2)
+        ahead_pairs = [(i + 2, i) for i in range(count - 2)]
         routed = jnp.zeros_like(second)
-    behind_even = lax.ppermute(second, "tm", [(a, b) for a, b in behind_pairs if b % 2 == 0])
+    behind_even = lax.ppermute(second, "tm", [(a, b) for a, b in behind_pairs if b % 2 == 0]
+                               + [(a, b) for a, b in ahead_pairs if b % 2 == 1])
+    from_ahead = lax.ppermute(second, "tm", [(a, b) for a, b in ahead_pairs if b % 2 == 0])
     behind_odd = lax.ppermute(second, "tm", [(a, b) for a, b in behind_pairs if b % 2 == 1])
     relay_behind = lax.ppermute(behind_odd, "tm", [(i + 1, i) for i in range(2, count, 2)])
     relay_ahead = lax.ppermute(from_ahead, "tm", [(i, i + 1) for i in range(0, count - 2, 2)])

time: 68.5 us -> 68.8 us (level)
  the two profiles are of different devices: /device:TPU:22 before, /device:TPU:1 now
where the time goes in v23:
time: 68.8 us; the launch traced here: 68.4 us
  waiting for transfers between devices  27 us (39%)
  starting transfers between devices  14.6 us (21%)
  Pallas kernels  14.6 us (21%)
  local copies, waits for them, and re-layouts  6.26 us (9%)
  between operations  4.06 us (6%)
  other arithmetic  1.92 us (3%)
    ppermute x1, waiting for transfers between devices, shards(): lax.ppermute(second, 'tm', [(a, b) for a, b in behind_pairs if b % 2 == 0...  17.7 us
    pallas_call x1, Pallas kernels, layers(): pl.pallas_call(layers_kernel, out_shape=jax.ShapeDtypeStruct((rows - 4, c...  7.67 us
    ppermute x1, waiting for transfers between devices, shards(): hop = lax.ppermute(second, 'tm', [(2, 6), (5, 1)])  7.6 us
    pallas_call x1, Pallas kernels, mix(): pl.pallas_call(mix_kernel, out_shape=jax.ShapeDtypeStruct((block, cols, c...  6.89 us
    ppermute x2, starting transfers between devices, shifted(): return lax.ppermute(value, axis, pairs)  5.34 us
    unnamed x20, local copies, waits for them, and re-layouts  2.8 us
    ppermute x1, starting transfers between devices, shards(): lax.ppermute(second, 'tm', [(a, b) for a, b in behind_pairs if b % 2 == 1])  2.58 us
    slice x2, local copies, waits for them, and re-layouts, shards(): up = jnp.concatenate([image[:3], frame[:1]], axis=0)  2.04 us
  transfers between devices with their start and end apart: 10, of which 3 were waited for; matrix products, arithmetic and copies ran while one was open for 5% of the time, Pallas kernels for 0%

profile of v23, /device:TPU:1, one launch (start us, length us, event | category | flops | bytes accessed | tf_op | source)
XLA Modules:
  0.0 68.4 jit_solution(11031501122776534466)
XLA Ops:
  0.0 0.9 %slice_bitcast_fusion.2 = (bf16[1,160,256]{2,1,0:T(8,128)(2,1)S(1)}, bf16[1,160,256]{2,1,0:T(8,128)(2,1)S(1)}) fusion(bf16[1,8,160,256]{3,2,1,0:T(8,128)(2,1)} %param.9), kind=kLoop, calls=%fused_computation.4 | loop fusion | bytes 327680 | tf_op jit(solution)/shard_map/slice | solution.py:162
  0.9 0.0 copy-start.9
  1.0 1.1 %slice_bitcast_fusion = (bf16[3,160,256]{2,1,0:T(8,128)(2,1)S(1)}, bf16[3,160,256]{2,1,0:T(8,128)(2,1)S(1)}) fusion(bf16[1,8,160,256]{3,2,1,0:T(8,128)(2,1)} %param.8), kind=kLoop, calls=%fused_computation.2 | loop fusion | bytes 983040 | tf_op jit(solution)/shard_map/slice | solution.py:162
  2.1 4.0 %collective-permute-start = (bf16[4,160,256]{2,1,0:T(8,128)(2,1)S(1)}, bf16[4,160,256]{2,1,0:T(8,128)(2,1)S(1)}, u32[]{:S(2)}, u32[]{:S(2)}) collective-permute-start(bf16[4,160,256]{2,1,0:T(8,128)(2,1)S(1)} %pad_maximum_fusion), channel_id=1, source_target_pairs={{0,1},{1,2},{2,3},{4,5},{5,6},{6,7},{8,9},{9,10},{10,11},{12,13},{... | collective-permute-start | bytes 983048 | tf_op jit(solution)/shard_map/ppermute | solution.py:16
  6.2 1.3 %collective-permute-start.1 = (bf16[4,160,256]{2,1,0:T(8,128)(2,1)S(1)}, bf16[4,160,256]{2,1,0:T(8,128)(2,1)S(1)}, u32[]{:S(2)}, u32[]{:S(2)}) collective-permute-start(bf16[4,160,256]{2,1,0:T(8,128)(2,1)S(1)} %pad_maximum_fusion.1), channel_id=1, source_target_pairs={{1,0},{2,1},{3,2},{5,4},{6,5},{7,6},{9,8},{10,9},{11,10},{13,12},{... | collective-permute-start | bytes 983048 | tf_op jit(solution)/shard_map/ppermute | solution.py:16
  8.8 0.0 copy-done.9
  8.8 0.6 fusion
  9.4 0.6 broadcast_divide_fusion
  10.1 0.1 slice.47
  10.2 0.7 fusion.1
  13.4 0.7 concatenate.9.coef_ref
  14.1 0.6 pad_add_fusion.bounds_ref
  14.6 0.0 collective-permute-done.above_ref
  14.6 0.0 copy-start.7
  14.6 1.7 %collective-permute-done.1.below_ref = bf16[4,160,256]{2,1,0:T(8,128)(2,1)S(1)} collective-permute-done((bf16[4,160,256]{2,1,0:T(8,128)(2,1)S(1)}, bf16[4,160,256]{2,1,0:T(8,128)(2,1)S(1)}, u32[]{:S(2)}, u32[]{:S(2)}) %collective-permute-start.1) | collective-permute-done | bytes 327712 | tf_op jit(solution)/shard_map/ppermute | solution.py:16
  16.3 0.0 copy-done.7
  16.4 0.0 copy-start.8
  16.4 0.7 %copy-done.8 = bf16[4,160,256]{2,1,0:T(8,128)(2,1)} copy-done((bf16[4,160,256]{2,1,0:T(8,128)(2,1)}, bf16[4,160,256]{2,1,0:T(8,128)(2,1)S(1)}, u32[]{:S(2)}) %copy-start.8) | copy-done | bytes 327704
  17.1 7.7 %shard_map.82.own_ref = bf16[10,160,256]{2,1,0:T(8,128)(2,1)} custom-call(s32[2]{0:T(128)} %pad_add_fusion.bounds_ref, bf16[4,160,256]{2,1,0:T(8,128)(2,1)} %copy-done.7, bf16[8,160,256]{2,1,0:T(8,128)(2,1)} %bitcast.28, bf16[4,160,256]{2,1,0:T(8,128)(2,1)} %copy-done.8, bf16[3,3,256,256]{3,2,1,0:T(8,128)(2,1)} %w1_ref.1, bf16[3,3,256,256]{3,2,1,0:T(8,128)(2,1)} %w2_ref.1), custom_call_target="tpu_custom_call" | custom-call | flops 4152360960 | bytes 4653056 | tf_op jit(solution)/shard_map/pallas_call | solution.py:116
  24.7 1.3 %collective-permute-start.8 = (bf16[10,160,256]{2,1,0:T(8,128)(2,1)}, bf16[10,160,256]{2,1,0:T(8,128)(2,1)S(1)}, u32[]{:S(2)}, u32[]{:S(2)}) collective-permute-start(bf16[10,160,256]{2,1,0:T(8,128)(2,1)} %shard_map.82.own_ref), channel_id=1, source_target_pairs={{8,24},{20,4},{9,25},{21,5},{10,26},{22,6},{11,27},{23,7}} | collective-permute-start | bytes 2457608 | tf_op jit(solution)/shard_map/ppermute | solution.py:190
  26.0 0.7 %collective-permute-start.6 = (bf16[10,160,256]{2,1,0:T(8,128)(2,1)}, bf16[10,160,256]{2,1,0:T(8,128)(2,1)S(1)}, u32[]{:S(2)}, u32[]{:S(2)}) collective-permute-start(bf16[10,160,256]{2,1,0:T(8,128)(2,1)} %shard_map.82.own_ref), channel_id=1, source_target_pairs={{8,0},{16,8},{24,16},{9,1},{17,9},{25,17},{10,2},{18,10},{26,18},{... | collective-permute-start | bytes 2457608 | tf_op jit(solution)/shard_map/ppermute | solution.py:198
  26.8 2.6 %collective-permute-start.3 = (bf16[10,160,256]{2,1,0:T(8,128)(2,1)}, bf16[10,160,256]{2,1,0:T(8,128)(2,1)S(1)}, u32[]{:S(2)}, u32[]{:S(2)}) collective-permute-start(bf16[10,160,256]{2,1,0:T(8,128)(2,1)} %shard_map.82.own_ref), channel_id=1, source_target_pairs={{4,12},{12,20},{20,28},{5,13},{13,21},{21,29},{6,14},{14,22},{22,3... | collective-permute-start | bytes 2457608 | tf_op jit(solution)/shard_map/ppermute | solution.py:199
  29.3 0.1 collective-permute-start.5
  29.4 1.3 %collective-permute-start.2 = (bf16[10,160,256]{2,1,0:T(8,128)(2,1)}, bf16[10,160,256]{2,1,0:T(8,128)(2,1)S(1)}, u32[]{:S(2)}, u32[]{:S(2)}) collective-permute-start(bf16[10,160,256]{2,1,0:T(8,128)(2,1)} %shard_map.82.own_ref), channel_id=1, source_target_pairs={{0,8},{16,24},{12,4},{28,20},{1,9},{17,25},{13,5},{29,21},{2,10},{... | collective-permute-start | bytes 2457608 | tf_op jit(solution)/shard_map/ppermute | solution.py:196
  30.7 7.6 %collective-permute-done.8 = bf16[10,160,256]{2,1,0:T(8,128)(2,1)S(1)} collective-permute-done((bf16[10,160,256]{2,1,0:T(8,128)(2,1)}, bf16[10,160,256]{2,1,0:T(8,128)(2,1)S(1)}, u32[]{:S(2)}, u32[]{:S(2)}) %collective-permute-start.8) | collective-permute-done | bytes 819232 | tf_op jit(solution)/shard_map/ppermute | solution.py:190
  38.3 1.3 %collective-permute-start.9 = (bf16[10,160,256]{2,1,0:T(8,128)(2,1)S(1)}, bf16[10,160,256]{2,1,0:T(8,128)(2,1)S(1)}, u32[]{:S(2)}, u32[]{:S(2)}) collective-permute-start(bf16[10,160,256]{2,1,0:T(8,128)(2,1)S(1)} %collective-permute-done.8), channel_id=1, source_target_pairs={{24,16},{4,12},{25,17},{5,13},{26,18},{6,14},{27,19},{7,15}} | collective-permute-start | bytes 2457608 | tf_op jit(solution)/shard_map/ppermute | solution.py:191
  39.7 0.0 collective-permute-done.6.fa_ref
  39.7 0.0 copy-start
  39.7 1.3 %collective-permute-start.7 = (bf16[10,160,256]{2,1,0:T(8,128)(2,1)S(1)}, bf16[10,160,256]{2,1,0:T(8,128)(2,1)S(1)}, u32[]{:S(2)}, u32[]{:S(2)}) collective-permute-start(bf16[10,160,256]{2,1,0:T(8,128)(2,1)S(1)} %collective-permute-done.6.fa_ref), channel_id=1, source_target_pairs={{0,4},{8,12},{16,20},{1,5},{9,13},{17,21},{2,6},{10,14},{18,22},{3... | collective-permute-start | bytes 2457608 | tf_op jit(solution)/shard_map/ppermute | solution.py:201
  41.0 0.0 collective-permute-done.3.fbo_ref
  41.0 0.0 copy-start.1
  41.0 0.7 %collective-permute-start.4 = (bf16[10,160,256]{2,1,0:T(8,128)(2,1)S(1)}, bf16[10,160,256]{2,1,0:T(8,128)(2,1)S(1)}, u32[]{:S(2)}, u32[]{:S(2)}) collective-permute-start(bf16[10,160,256]{2,1,0:T(8,128)(2,1)S(1)} %collective-permute-done.3.fbo_ref), channel_id=1, source_target_pairs={{12,8},{20,16},{28,24},{13,9},{21,17},{29,25},{14,10},{22,18},{30,... | collective-permute-start | bytes 2457608 | tf_op jit(solution)/shard_map/ppermute | solution.py:200
  41.7 0.0 collective-permute-done.5.par_ref
  41.7 0.0 copy-start.2
  41.7 17.7 %collective-permute-done.2.fb_ref = bf16[10,160,256]{2,1,0:T(8,128)(2,1)S(1)} collective-permute-done((bf16[10,160,256]{2,1,0:T(8,128)(2,1)}, bf16[10,160,256]{2,1,0:T(8,128)(2,1)S(1)}, u32[]{:S(2)}, u32[]{:S(2)}) %collective-permute-start.2) | collective-permute-done | bytes 819232 | tf_op jit(solution)/shard_map/ppermute | solution.py:196
  59.5 0.0 copy-start.3
  59.5 0.0 collective-permute-done.9.routed_ref
  59.5 0.0 collective-permute-done.7.ra_ref
  59.5 0.0 copy-start.5
  59.5 0.0 collective-permute-done.4.rb_ref
  59.5 0.9 %copy-done.4 = bf16[10,160,256]{2,1,0:T(8,128)(2,1)} copy-done((bf16[10,160,256]{2,1,0:T(8,128)(2,1)}, bf16[10,160,256]{2,1,0:T(8,128)(2,1)S(1)}, u32[]{:S(2)}) %copy-start.4) | copy-done | bytes 819224
  60.4 0.2 copy-done.5
  60.6 0.9 %copy-done.6 = bf16[10,160,256]{2,1,0:T(8,128)(2,1)} copy-done((bf16[10,160,256]{2,1,0:T(8,128)(2,1)}, bf16[10,160,256]{2,1,0:T(8,128)(2,1)S(1)}, u32[]{:S(2)}) %copy-start.6) | copy-done | bytes 819224
  61.5 0.0 copy-done
  61.5 0.0 copy-done.1
  61.5 0.0 copy-done.2
  61.5 0.0 copy-done.3
  61.6 6.9 %shard_map.83 = bf16[8,160,256]{2,1,0:T(8,128)(2,1)} custom-call(f32[8]{0:T(128)} %concatenate.9.coef_ref, bf16[10,160,256]{2,1,0:T(8,128)(2,1)} %copy-done.3, bf16[10,160,256]{2,1,0:T(8,128)(2,1)} %copy-done.1, bf16[10,160,256]{2,1,0:T(8,128)(2,1)} %copy-done.6, bf16[10,160,256]{2,1,0:T(8,128)(2,1)} %shard_map.82.own_ref, bf16[10,160,256]{2,1,0:T(8,128)(2,1)} %copy-done.2, ...), custom_call_target="tpu_custom_call" | custom-call | flops 1509949440 | bytes 8552448 | tf_op jit(solution)/shard_map/pallas_call | solution.py:132
  (4 shorter events, 0.1 us)
Async XLA Ops:
  0.9 7.9 %copy-start.9 = (s32[1,5]{1,0:T(1,128)S(1)}, s32[1,5]{1,0:T(1,128)}, u32[]{:S(2)}) copy-start(s32[1,5]{1,0:T(1,128)} %param.12) | copy-start | bytes 64
  2.1 12.5 %collective-permute-start = (bf16[4,160,256]{2,1,0:T(8,128)(2,1)S(1)}, bf16[4,160,256]{2,1,0:T(8,128)(2,1)S(1)}, u32[]{:S(2)}, u32[]{:S(2)}) collective-permute-start(bf16[4,160,256]{2,1,0:T(8,128)(2,1)S(1)} %pad_maximum_fusion), channel_id=1, source_target_pairs={{0,1},{1,2},{2,3},{4,5},{5,6},{6,7},{8,9},{9,10},{10,11},{12,13},{... | collective-permute-start | bytes 983048 | tf_op jit(solution)/shard_map/ppermute | solution.py:16
  6.2 10.2 %collective-permute-start.1 = (bf16[4,160,256]{2,1,0:T(8,128)(2,1)S(1)}, bf16[4,160,256]{2,1,0:T(8,128)(2,1)S(1)}, u32[]{:S(2)}, u32[]{:S(2)}) collective-permute-start(bf16[4,160,256]{2,1,0:T(8,128)(2,1)S(1)} %pad_maximum_fusion.1), channel_id=1, source_target_pairs={{1,0},{2,1},{3,2},{5,4},{6,5},{7,6},{9,8},{10,9},{11,10},{13,12},{... | collective-permute-start | bytes 983048 | tf_op jit(solution)/shard_map/ppermute | solution.py:16
  14.6 1.7 %copy-start.7 = (bf16[4,160,256]{2,1,0:T(8,128)(2,1)}, bf16[4,160,256]{2,1,0:T(8,128)(2,1)S(1)}, u32[]{:S(2)}) copy-start(bf16[4,160,256]{2,1,0:T(8,128)(2,1)S(1)} %collective-permute-done.above_ref) | copy-start | bytes 983044
  16.4 0.7 %copy-start.8 = (bf16[4,160,256]{2,1,0:T(8,128)(2,1)}, bf16[4,160,256]{2,1,0:T(8,128)(2,1)S(1)}, u32[]{:S(2)}) copy-start(bf16[4,160,256]{2,1,0:T(8,128)(2,1)S(1)} %collective-permute-done.1.below_ref) | copy-start | bytes 983044
  24.7 13.6 %collective-permute-start.8 = (bf16[10,160,256]{2,1,0:T(8,128)(2,1)}, bf16[10,160,256]{2,1,0:T(8,128)(2,1)S(1)}, u32[]{:S(2)}, u32[]{:S(2)}) collective-permute-start(bf16[10,160,256]{2,1,0:T(8,128)(2,1)} %shard_map.82.own_ref), channel_id=1, source_target_pairs={{8,24},{20,4},{9,25},{21,5},{10,26},{22,6},{11,27},{23,7}} | collective-permute-start | bytes 2457608 | tf_op jit(solution)/shard_map/ppermute | solution.py:190
  26.0 13.6 %collective-permute-start.6 = (bf16[10,160,256]{2,1,0:T(8,128)(2,1)}, bf16[10,160,256]{2,1,0:T(8,128)(2,1)S(1)}, u32[]{:S(2)}, u32[]{:S(2)}) collective-permute-start(bf16[10,160,256]{2,1,0:T(8,128)(2,1)} %shard_map.82.own_ref), channel_id=1, source_target_pairs={{8,0},{16,8},{24,16},{9,1},{17,9},{25,17},{10,2},{18,10},{26,18},{... | collective-permute-start | bytes 2457608 | tf_op jit(solution)/shard_map/ppermute | solution.py:198
  26.8 14.2 %collective-permute-start.3 = (bf16[10,160,256]{2,1,0:T(8,128)(2,1)}, bf16[10,160,256]{2,1,0:T(8,128)(2,1)S(1)}, u32[]{:S(2)}, u32[]{:S(2)}) collective-permute-start(bf16[10,160,256]{2,1,0:T(8,128)(2,1)} %shard_map.82.own_ref), channel_id=1, source_target_pairs={{4,12},{12,20},{20,28},{5,13},{13,21},{21,29},{6,14},{14,22},{22,3... | collective-permute-start | bytes 2457608 | tf_op jit(solution)/shard_map/ppermute | solution.py:199
  29.3 12.4 %collective-permute-start.5 = (bf16[10,160,256]{2,1,0:T(8,128)(2,1)}, bf16[10,160,256]{2,1,0:T(8,128)(2,1)S(1)}, u32[]{:S(2)}, u32[]{:S(2)}) collective-permute-start(bf16[10,160,256]{2,1,0:T(8,128)(2,1)} %shard_map.82.own_ref), channel_id=1, source_target_pairs={{0,4},{4,0},{8,12},{12,8},{16,20},{20,16},{24,28},{28,24},{1,5},{5... | collective-permute-start | bytes 2457608 | tf_op jit(solution)/shard_map/ppermute | solution.py:186
  29.4 30.0 %collective-permute-start.2 = (bf16[10,160,256]{2,1,0:T(8,128)(2,1)}, bf16[10,160,256]{2,1,0:T(8,128)(2,1)S(1)}, u32[]{:S(2)}, u32[]{:S(2)}) collective-permute-start(bf16[10,160,256]{2,1,0:T(8,128)(2,1)} %shard_map.82.own_ref), channel_id=1, source_target_pairs={{0,8},{16,24},{12,4},{28,20},{1,9},{17,25},{13,5},{29,21},{2,10},{... | collective-permute-start | bytes 2457608 | tf_op jit(solution)/shard_map/ppermute | solution.py:196
  38.3 21.1 %collective-permute-start.9 = (bf16[10,160,256]{2,1,0:T(8,128)(2,1)S(1)}, bf16[10,160,256]{2,1,0:T(8,128)(2,1)S(1)}, u32[]{:S(2)}, u32[]{:S(2)}) collective-permute-start(bf16[10,160,256]{2,1,0:T(8,128)(2,1)S(1)} %collective-permute-done.8), channel_id=1, source_target_pairs={{24,16},{4,12},{25,17},{5,13},{26,18},{6,14},{27,19},{7,15}} | collective-permute-start | bytes 2457608 | tf_op jit(solution)/shard_map/ppermute | solution.py:191
  39.7 21.9 %copy-start = (bf16[10,160,256]{2,1,0:T(8,128)(2,1)}, bf16[10,160,256]{2,1,0:T(8,128)(2,1)S(1)}, u32[]{:S(2)}) copy-start(bf16[10,160,256]{2,1,0:T(8,128)(2,1)S(1)} %collective-permute-done.6.fa_ref) | copy-start | bytes 2457604
  39.7 19.8 %collective-permute-start.7 = (bf16[10,160,256]{2,1,0:T(8,128)(2,1)S(1)}, bf16[10,160,256]{2,1,0:T(8,128)(2,1)S(1)}, u32[]{:S(2)}, u32[]{:S(2)}) collective-permute-start(bf16[10,160,256]{2,1,0:T(8,128)(2,1)S(1)} %collective-permute-done.6.fa_ref), channel_id=1, source_target_pairs={{0,4},{8,12},{16,20},{1,5},{9,13},{17,21},{2,6},{10,14},{18,22},{3... | collective-permute-start | bytes 2457608 | tf_op jit(solution)/shard_map/ppermute | solution.py:201
  41.0 20.5 %copy-start.1 = (bf16[10,160,256]{2,1,0:T(8,128)(2,1)}, bf16[10,160,256]{2,1,0:T(8,128)(2,1)S(1)}, u32[]{:S(2)}) copy-start(bf16[10,160,256]{2,1,0:T(8,128)(2,1)S(1)} %collective-permute-done.3.fbo_ref) | copy-start | bytes 2457604
  41.0 18.5 %collective-permute-start.4 = (bf16[10,160,256]{2,1,0:T(8,128)(2,1)S(1)}, bf16[10,160,256]{2,1,0:T(8,128)(2,1)S(1)}, u32[]{:S(2)}, u32[]{:S(2)}) collective-permute-start(bf16[10,160,256]{2,1,0:T(8,128)(2,1)S(1)} %collective-permute-done.3.fbo_ref), channel_id=1, source_target_pairs={{12,8},{20,16},{28,24},{13,9},{21,17},{29,25},{14,10},{22,18},{30,... | collective-permute-start | bytes 2457608 | tf_op jit(solution)/shard_map/ppermute | solution.py:200
  41.7 19.8 %copy-start.2 = (bf16[10,160,256]{2,1,0:T(8,128)(2,1)}, bf16[10,160,256]{2,1,0:T(8,128)(2,1)S(1)}, u32[]{:S(2)}) copy-start(bf16[10,160,256]{2,1,0:T(8,128)(2,1)S(1)} %collective-permute-done.5.par_ref) | copy-start | bytes 2457604
  59.5 2.1 %copy-start.3 = (bf16[10,160,256]{2,1,0:T(8,128)(2,1)}, bf16[10,160,256]{2,1,0:T(8,128)(2,1)S(1)}, u32[]{:S(2)}) copy-start(bf16[10,160,256]{2,1,0:T(8,128)(2,1)S(1)} %collective-permute-done.2.fb_ref) | copy-start | bytes 2457604
  59.5 0.9 %copy-start.4 = (bf16[10,160,256]{2,1,0:T(8,128)(2,1)}, bf16[10,160,256]{2,1,0:T(8,128)(2,1)S(1)}, u32[]{:S(2)}) copy-start(bf16[10,160,256]{2,1,0:T(8,128)(2,1)S(1)} %collective-permute-done.9.routed_ref) | copy-start | bytes 2457604
  59.5 1.2 %copy-start.5 = (bf16[10,160,256]{2,1,0:T(8,128)(2,1)}, bf16[10,160,256]{2,1,0:T(8,128)(2,1)S(1)}, u32[]{:S(2)}) copy-start(bf16[10,160,256]{2,1,0:T(8,128)(2,1)S(1)} %collective-permute-done.7.ra_ref) | copy-start | bytes 2457604
  60.6 0.9 %copy-start.6 = (bf16[10,160,256]{2,1,0:T(8,128)(2,1)}, bf16[10,160,256]{2,1,0:T(8,128)(2,1)S(1)}, u32[]{:S(2)}) copy-start(bf16[10,160,256]{2,1,0:T(8,128)(2,1)S(1)} %collective-permute-done.4.rb_ref) | copy-start | bytes 2457604

commit v24 on v21

--- a/solution.py
+++ b/solution.py
@@ -80,11 +80,10 @@
     for r0 in range(0, block + 2, step):
         rows = pl.ds(r0, min(step, block + 2 - r0))
         summed = (
-            coef_ref[0] * (fb_ref[rows].astype(f32) + fbo_ref[rows].astype(f32))
-            + coef_ref[1] * rb_ref[rows].astype(f32)
+            coef_ref[0] * (fb_ref[rows] + fbo_ref[rows]).astype(f32)
+            + coef_ref[7] * (rb_ref[rows] + ra_ref[rows]).astype(f32)
             + coef_ref[2] * own_ref[rows].astype(f32)
             + coef_ref[3] * par_ref[rows].astype(f32)
-            + coef_ref[4] * ra_ref[rows].astype(f32)
             + coef_ref[5] * fa_ref[rows].astype(f32)
             + coef_ref[6] * routed_ref[rows].astype(f32)
         )
@@ -174,7 +173,9 @@
     is_odd = (t % 2) == 1
     partner_weight = jnp.where(is_odd, weights[1], weights[3])
     routed_weight = jnp.where(is_odd, weights[4], weights[0])
-    coef = jnp.concatenate([weights[:3], partner_weight[None], weights[3:], routed_weight[None]])
+    relay_weight = jnp.where(is_odd, weights[3], weights[1])
+    coef = jnp.concatenate([weights[:3], partner_weight[None], weights[3:], routed_weight[None],
+                            relay_weight[None]])
     bounds = jnp.stack([2 - row0, height - row0 + 2]).astype(jnp.int32)
     coef, bounds, image = lax.optimization_barrier((coef, bounds, image))
 

time: 68.5 us -> 69.5 us (1.015)
  between operations: 4.03 us -> 5.4 us
  waiting for transfers between devices: 26.5 us -> 25.2 us
  local copies, waits for them, and re-layouts: 5.58 us -> 6.79 us
  other arithmetic: 2.62 us -> 1.92 us
  starting transfers between devices: 14.8 us -> 15.5 us
    ppermute x2, waiting for transfers between devices: 1.53 us -> 0.19 us  [shifted(): return lax.ppermute(value, axis, pairs)]
where the time goes in v24:
time: 69.5 us; the launch traced here: 69 us
  waiting for transfers between devices  25.2 us (36%)
  starting transfers between devices  15.5 us (22%)
  Pallas kernels  14.3 us (21%)
  local copies, waits for them, and re-layouts  6.79 us (10%)
  between operations  5.4 us (8%)
  other arithmetic  1.92 us (3%)
    ppermute x1, waiting for transfers between devices, shards(): lax.ppermute(second, 'tm', [(a, b) for a, b in behind_pairs if b % 2 == 0])  10.8 us
    ppermute x1, waiting for transfers between devices, shards(): hop = lax.ppermute(second, 'tm', [(2, 6), (5, 1)])  8.12 us
    pallas_call x1, Pallas kernels, layers(): pl.pallas_call(layers_kernel, out_shape=jax.ShapeDtypeStruct((rows - 4, c...  7.67 us
    pallas_call x1, Pallas kernels, mix(): pl.pallas_call(mix_kernel, out_shape=jax.ShapeDtypeStruct((block, cols, c...  6.61 us
    ppermute x1, waiting for transfers between devices, shards(): lax.ppermute(second, 'tm', [(2, 0), (3, 1), (4, 2), (6, 4), (7, 5)])  6.09 us
    ppermute x2, starting transfers between devices, shifted(): return lax.ppermute(value, axis, pairs)  5.84 us
    unnamed x20, local copies, waits for them, and re-layouts  3.34 us
    slice x2, local copies, waits for them, and re-layouts, shards(): up = jnp.concatenate([image[:3], frame[:1]], axis=0)  2.04 us
  transfers between devices with their start and end apart: 10, of which 4 were waited for; matrix products, arithmetic and copies ran while one was open for 5% of the time, Pallas kernels for 0%

profile of v24, /device:TPU:22, one launch (start us, length us, event | category | flops | bytes accessed | tf_op | source)
XLA Modules:
  0.0 69.0 jit_solution(8856714173217099378)
XLA Ops:
  0.0 0.9 %slice_bitcast_fusion.2 = (bf16[1,160,256]{2,1,0:T(8,128)(2,1)S(1)}, bf16[1,160,256]{2,1,0:T(8,128)(2,1)S(1)}) fusion(bf16[1,8,160,256]{3,2,1,0:T(8,128)(2,1)} %param.9), kind=kLoop, calls=%fused_computation.4 | loop fusion | bytes 327680 | tf_op jit(solution)/shard_map/slice | solution.py:160
  0.9 0.0 copy-start.9
  1.0 1.1 %slice_bitcast_fusion = (bf16[3,160,256]{2,1,0:T(8,128)(2,1)S(1)}, bf16[3,160,256]{2,1,0:T(8,128)(2,1)S(1)}) fusion(bf16[1,8,160,256]{3,2,1,0:T(8,128)(2,1)} %param.8), kind=kLoop, calls=%fused_computation.2 | loop fusion | bytes 983040 | tf_op jit(solution)/shard_map/slice | solution.py:160
  2.1 3.5 %collective-permute-start = (bf16[4,160,256]{2,1,0:T(8,128)(2,1)S(1)}, bf16[4,160,256]{2,1,0:T(8,128)(2,1)S(1)}, u32[]{:S(2)}, u32[]{:S(2)}) collective-permute-start(bf16[4,160,256]{2,1,0:T(8,128)(2,1)S(1)} %pad_maximum_fusion), channel_id=1, source_target_pairs={{0,1},{1,2},{2,3},{4,5},{5,6},{6,7},{8,9},{9,10},{10,11},{12,13},{... | collective-permute-start | bytes 983048 | tf_op jit(solution)/shard_map/ppermute | solution.py:16
  5.6 2.4 %collective-permute-start.1 = (bf16[4,160,256]{2,1,0:T(8,128)(2,1)S(1)}, bf16[4,160,256]{2,1,0:T(8,128)(2,1)S(1)}, u32[]{:S(2)}, u32[]{:S(2)}) collective-permute-start(bf16[4,160,256]{2,1,0:T(8,128)(2,1)S(1)} %pad_maximum_fusion.1), channel_id=1, source_target_pairs={{1,0},{2,1},{3,2},{5,4},{6,5},{7,6},{9,8},{10,9},{11,10},{13,12},{... | collective-permute-start | bytes 983048 | tf_op jit(solution)/shard_map/ppermute | solution.py:16
  9.3 0.0 copy-done.9
  9.3 0.6 fusion
  9.9 0.6 broadcast_divide_fusion
  10.6 0.1 slice.47
  10.7 0.7 fusion.1
  15.2 0.7 concatenate.9.coef_ref
  15.9 0.6 pad_add_fusion.bounds_ref
  16.5 0.0 collective-permute-done.above_ref
  16.5 0.0 copy-start.7
  16.5 0.2 collective-permute-done.1.below_ref
  16.7 0.5 copy-done.7
  17.2 0.0 copy-start.8
  17.2 0.7 %copy-done.8 = bf16[4,160,256]{2,1,0:T(8,128)(2,1)} copy-done((bf16[4,160,256]{2,1,0:T(8,128)(2,1)}, bf16[4,160,256]{2,1,0:T(8,128)(2,1)S(1)}, u32[]{:S(2)}) %copy-start.8) | copy-done | bytes 327704
  18.0 7.7 %shard_map.82.own_ref = bf16[10,160,256]{2,1,0:T(8,128)(2,1)} custom-call(s32[2]{0:T(128)} %pad_add_fusion.bounds_ref, bf16[4,160,256]{2,1,0:T(8,128)(2,1)} %copy-done.7, bf16[8,160,256]{2,1,0:T(8,128)(2,1)} %bitcast.29, bf16[4,160,256]{2,1,0:T(8,128)(2,1)} %copy-done.8, bf16[3,3,256,256]{3,2,1,0:T(8,128)(2,1)} %w1_ref.1, bf16[3,3,256,256]{3,2,1,0:T(8,128)(2,1)} %w2_ref.1), custom_call_target="tpu_custom_call" | custom-call | flops 4152360960 | bytes 4653056 | tf_op jit(solution)/shard_map/pallas_call | solution.py:114
  25.6 1.3 %collective-permute-start.8 = (bf16[10,160,256]{2,1,0:T(8,128)(2,1)}, bf16[10,160,256]{2,1,0:T(8,128)(2,1)S(1)}, u32[]{:S(2)}, u32[]{:S(2)}) collective-permute-start(bf16[10,160,256]{2,1,0:T(8,128)(2,1)} %shard_map.82.own_ref), channel_id=1, source_target_pairs={{8,24},{20,4},{9,25},{21,5},{10,26},{22,6},{11,27},{23,7}} | collective-permute-start | bytes 2457608 | tf_op jit(solution)/shard_map/ppermute | solution.py:188
  26.9 1.9 %collective-permute-start.6 = (bf16[10,160,256]{2,1,0:T(8,128)(2,1)}, bf16[10,160,256]{2,1,0:T(8,128)(2,1)S(1)}, u32[]{:S(2)}, u32[]{:S(2)}) collective-permute-start(bf16[10,160,256]{2,1,0:T(8,128)(2,1)} %shard_map.82.own_ref), channel_id=1, source_target_pairs={{8,0},{12,4},{16,8},{24,16},{28,20},{9,1},{13,5},{17,9},{25,17},{2... | collective-permute-start | bytes 2457608 | tf_op jit(solution)/shard_map/ppermute | solution.py:187
  28.8 0.7 %collective-permute-start.3 = (bf16[10,160,256]{2,1,0:T(8,128)(2,1)}, bf16[10,160,256]{2,1,0:T(8,128)(2,1)S(1)}, u32[]{:S(2)}, u32[]{:S(2)}) collective-permute-start(bf16[10,160,256]{2,1,0:T(8,128)(2,1)} %shard_map.82.own_ref), channel_id=1, source_target_pairs={{4,12},{12,20},{20,28},{5,13},{13,21},{21,29},{6,14},{14,22},{22,3... | collective-permute-start | bytes 2457608 | tf_op jit(solution)/shard_map/ppermute | solution.py:195
  29.6 1.1 %collective-permute-start.5 = (bf16[10,160,256]{2,1,0:T(8,128)(2,1)}, bf16[10,160,256]{2,1,0:T(8,128)(2,1)S(1)}, u32[]{:S(2)}, u32[]{:S(2)}) collective-permute-start(bf16[10,160,256]{2,1,0:T(8,128)(2,1)} %shard_map.82.own_ref), channel_id=1, source_target_pairs={{0,4},{4,0},{8,12},{12,8},{16,20},{20,16},{24,28},{28,24},{1,5},{5... | collective-permute-start | bytes 2457608 | tf_op jit(solution)/shard_map/ppermute | solution.py:184
  30.7 1.3 %collective-permute-start.2 = (bf16[10,160,256]{2,1,0:T(8,128)(2,1)}, bf16[10,160,256]{2,1,0:T(8,128)(2,1)S(1)}, u32[]{:S(2)}, u32[]{:S(2)}) collective-permute-start(bf16[10,160,256]{2,1,0:T(8,128)(2,1)} %shard_map.82.own_ref), channel_id=1, source_target_pairs={{0,8},{16,24},{1,9},{17,25},{2,10},{18,26},{3,11},{19,27}} | collective-permute-start | bytes 2457608 | tf_op jit(solution)/shard_map/ppermute | solution.py:194
  31.9 8.1 %collective-permute-done.8 = bf16[10,160,256]{2,1,0:T(8,128)(2,1)S(1)} collective-permute-done((bf16[10,160,256]{2,1,0:T(8,128)(2,1)}, bf16[10,160,256]{2,1,0:T(8,128)(2,1)S(1)}, u32[]{:S(2)}, u32[]{:S(2)}) %collective-permute-start.8) | collective-permute-done | bytes 819232 | tf_op jit(solution)/shard_map/ppermute | solution.py:188
  40.1 1.3 %collective-permute-start.9 = (bf16[10,160,256]{2,1,0:T(8,128)(2,1)S(1)}, bf16[10,160,256]{2,1,0:T(8,128)(2,1)S(1)}, u32[]{:S(2)}, u32[]{:S(2)}) collective-permute-start(bf16[10,160,256]{2,1,0:T(8,128)(2,1)S(1)} %collective-permute-done.8), channel_id=1, source_target_pairs={{24,16},{4,12},{25,17},{5,13},{26,18},{6,14},{27,19},{7,15}} | collective-permute-start | bytes 2457608 | tf_op jit(solution)/shard_map/ppermute | solution.py:189
  41.4 6.1 %collective-permute-done.6.fa_ref = bf16[10,160,256]{2,1,0:T(8,128)(2,1)S(1)} collective-permute-done((bf16[10,160,256]{2,1,0:T(8,128)(2,1)}, bf16[10,160,256]{2,1,0:T(8,128)(2,1)S(1)}, u32[]{:S(2)}, u32[]{:S(2)}) %collective-permute-start.6) | collective-permute-done | bytes 819232 | tf_op jit(solution)/shard_map/ppermute | solution.py:187
  47.5 0.0 copy-start
  47.5 0.7 %collective-permute-start.7 = (bf16[10,160,256]{2,1,0:T(8,128)(2,1)S(1)}, bf16[10,160,256]{2,1,0:T(8,128)(2,1)S(1)}, u32[]{:S(2)}, u32[]{:S(2)}) collective-permute-start(bf16[10,160,256]{2,1,0:T(8,128)(2,1)S(1)} %collective-permute-done.6.fa_ref), channel_id=1, source_target_pairs={{0,4},{8,12},{16,20},{1,5},{9,13},{17,21},{2,6},{10,14},{18,22},{3... | collective-permute-start | bytes 2457608 | tf_op jit(solution)/shard_map/ppermute | solution.py:197
  48.2 0.0 collective-permute-done.3.fbo_ref
  48.2 0.0 copy-start.1
  48.2 1.3 %collective-permute-start.4 = (bf16[10,160,256]{2,1,0:T(8,128)(2,1)S(1)}, bf16[10,160,256]{2,1,0:T(8,128)(2,1)S(1)}, u32[]{:S(2)}, u32[]{:S(2)}) collective-permute-start(bf16[10,160,256]{2,1,0:T(8,128)(2,1)S(1)} %collective-permute-done.3.fbo_ref), channel_id=1, source_target_pairs={{12,8},{20,16},{28,24},{13,9},{21,17},{29,25},{14,10},{22,18},{30,... | collective-permute-start | bytes 2457608 | tf_op jit(solution)/shard_map/ppermute | solution.py:196
  49.5 0.0 collective-permute-done.5.par_ref
  49.5 0.0 copy-start.2
  49.5 10.8 %collective-permute-done.2.fb_ref = bf16[10,160,256]{2,1,0:T(8,128)(2,1)S(1)} collective-permute-done((bf16[10,160,256]{2,1,0:T(8,128)(2,1)}, bf16[10,160,256]{2,1,0:T(8,128)(2,1)S(1)}, u32[]{:S(2)}, u32[]{:S(2)}) %collective-permute-start.2) | collective-permute-done | bytes 819232 | tf_op jit(solution)/shard_map/ppermute | solution.py:194
  60.3 0.0 copy-start.3
  60.3 0.0 collective-permute-done.9.routed_ref
  60.3 0.0 collective-permute-done.7.ra_ref
  60.3 0.0 copy-start.5
  60.3 0.0 collective-permute-done.4.rb_ref
  60.4 0.9 %copy-done.4 = bf16[10,160,256]{2,1,0:T(8,128)(2,1)} copy-done((bf16[10,160,256]{2,1,0:T(8,128)(2,1)}, bf16[10,160,256]{2,1,0:T(8,128)(2,1)S(1)}, u32[]{:S(2)}) %copy-start.4) | copy-done | bytes 819224
  61.3 0.2 copy-done.5
  61.5 0.9 %copy-done.6 = bf16[10,160,256]{2,1,0:T(8,128)(2,1)} copy-done((bf16[10,160,256]{2,1,0:T(8,128)(2,1)}, bf16[10,160,256]{2,1,0:T(8,128)(2,1)S(1)}, u32[]{:S(2)}) %copy-start.6) | copy-done | bytes 819224
  62.4 0.0 copy-done
  62.4 0.0 copy-done.1
  62.4 0.0 copy-done.2
  62.4 0.0 copy-done.3
  62.4 6.6 %shard_map.83 = bf16[8,160,256]{2,1,0:T(8,128)(2,1)} custom-call(f32[8]{0:T(128)} %concatenate.9.coef_ref, bf16[10,160,256]{2,1,0:T(8,128)(2,1)} %copy-done.3, bf16[10,160,256]{2,1,0:T(8,128)(2,1)} %copy-done.1, bf16[10,160,256]{2,1,0:T(8,128)(2,1)} %copy-done.6, bf16[10,160,256]{2,1,0:T(8,128)(2,1)} %shard_map.82.own_ref, bf16[10,160,256]{2,1,0:T(8,128)(2,1)} %copy-done.2, ...), custom_call_target="tpu_custom_call" | custom-call | flops 1509949440 | bytes 8552448 | tf_op jit(solution)/shard_map/pallas_call | solution.py:130
  (4 shorter events, 0.1 us)
Async XLA Ops:
  0.9 8.4 %copy-start.9 = (s32[1,5]{1,0:T(1,128)S(1)}, s32[1,5]{1,0:T(1,128)}, u32[]{:S(2)}) copy-start(s32[1,5]{1,0:T(1,128)} %param.12) | copy-start | bytes 64
  2.1 14.4 %collective-permute-start = (bf16[4,160,256]{2,1,0:T(8,128)(2,1)S(1)}, bf16[4,160,256]{2,1,0:T(8,128)(2,1)S(1)}, u32[]{:S(2)}, u32[]{:S(2)}) collective-permute-start(bf16[4,160,256]{2,1,0:T(8,128)(2,1)S(1)} %pad_maximum_fusion), channel_id=1, source_target_pairs={{0,1},{1,2},{2,3},{4,5},{5,6},{6,7},{8,9},{9,10},{10,11},{12,13},{... | collective-permute-start | bytes 983048 | tf_op jit(solution)/shard_map/ppermute | solution.py:16
  5.6 11.1 %collective-permute-start.1 = (bf16[4,160,256]{2,1,0:T(8,128)(2,1)S(1)}, bf16[4,160,256]{2,1,0:T(8,128)(2,1)S(1)}, u32[]{:S(2)}, u32[]{:S(2)}) collective-permute-start(bf16[4,160,256]{2,1,0:T(8,128)(2,1)S(1)} %pad_maximum_fusion.1), channel_id=1, source_target_pairs={{1,0},{2,1},{3,2},{5,4},{6,5},{7,6},{9,8},{10,9},{11,10},{13,12},{... | collective-permute-start | bytes 983048 | tf_op jit(solution)/shard_map/ppermute | solution.py:16
  16.5 0.7 %copy-start.7 = (bf16[4,160,256]{2,1,0:T(8,128)(2,1)}, bf16[4,160,256]{2,1,0:T(8,128)(2,1)S(1)}, u32[]{:S(2)}) copy-start(bf16[4,160,256]{2,1,0:T(8,128)(2,1)S(1)} %collective-permute-done.above_ref) | copy-start | bytes 983044
  17.2 0.7 %copy-start.8 = (bf16[4,160,256]{2,1,0:T(8,128)(2,1)}, bf16[4,160,256]{2,1,0:T(8,128)(2,1)S(1)}, u32[]{:S(2)}) copy-start(bf16[4,160,256]{2,1,0:T(8,128)(2,1)S(1)} %collective-permute-done.1.below_ref) | copy-start | bytes 983044
  25.6 14.4 %collective-permute-start.8 = (bf16[10,160,256]{2,1,0:T(8,128)(2,1)}, bf16[10,160,256]{2,1,0:T(8,128)(2,1)S(1)}, u32[]{:S(2)}, u32[]{:S(2)}) collective-permute-start(bf16[10,160,256]{2,1,0:T(8,128)(2,1)} %shard_map.82.own_ref), channel_id=1, source_target_pairs={{8,24},{20,4},{9,25},{21,5},{10,26},{22,6},{11,27},{23,7}} | collective-permute-start | bytes 2457608 | tf_op jit(solution)/shard_map/ppermute | solution.py:188
  26.9 20.6 %collective-permute-start.6 = (bf16[10,160,256]{2,1,0:T(8,128)(2,1)}, bf16[10,160,256]{2,1,0:T(8,128)(2,1)S(1)}, u32[]{:S(2)}, u32[]{:S(2)}) collective-permute-start(bf16[10,160,256]{2,1,0:T(8,128)(2,1)} %shard_map.82.own_ref), channel_id=1, source_target_pairs={{8,0},{12,4},{16,8},{24,16},{28,20},{9,1},{13,5},{17,9},{25,17},{2... | collective-permute-start | bytes 2457608 | tf_op jit(solution)/shard_map/ppermute | solution.py:187
  28.8 19.4 %collective-permute-start.3 = (bf16[10,160,256]{2,1,0:T(8,128)(2,1)}, bf16[10,160,256]{2,1,0:T(8,128)(2,1)S(1)}, u32[]{:S(2)}, u32[]{:S(2)}) collective-permute-start(bf16[10,160,256]{2,1,0:T(8,128)(2,1)} %shard_map.82.own_ref), channel_id=1, source_target_pairs={{4,12},{12,20},{20,28},{5,13},{13,21},{21,29},{6,14},{14,22},{22,3... | collective-permute-start | bytes 2457608 | tf_op jit(solution)/shard_map/ppermute | solution.py:195
  29.6 20.0 %collective-permute-start.5 = (bf16[10,160,256]{2,1,0:T(8,128)(2,1)}, bf16[10,160,256]{2,1,0:T(8,128)(2,1)S(1)}, u32[]{:S(2)}, u32[]{:S(2)}) collective-permute-start(bf16[10,160,256]{2,1,0:T(8,128)(2,1)} %shard_map.82.own_ref), channel_id=1, source_target_pairs={{0,4},{4,0},{8,12},{12,8},{16,20},{20,16},{24,28},{28,24},{1,5},{5... | collective-permute-start | bytes 2457608 | tf_op jit(solution)/shard_map/ppermute | solution.py:184
  30.7 29.7 %collective-permute-start.2 = (bf16[10,160,256]{2,1,0:T(8,128)(2,1)}, bf16[10,160,256]{2,1,0:T(8,128)(2,1)S(1)}, u32[]{:S(2)}, u32[]{:S(2)}) collective-permute-start(bf16[10,160,256]{2,1,0:T(8,128)(2,1)} %shard_map.82.own_ref), channel_id=1, source_target_pairs={{0,8},{16,24},{1,9},{17,25},{2,10},{18,26},{3,11},{19,27}} | collective-permute-start | bytes 2457608 | tf_op jit(solution)/shard_map/ppermute | solution.py:194
  40.1 20.3 %collective-permute-start.9 = (bf16[10,160,256]{2,1,0:T(8,128)(2,1)S(1)}, bf16[10,160,256]{2,1,0:T(8,128)(2,1)S(1)}, u32[]{:S(2)}, u32[]{:S(2)}) collective-permute-start(bf16[10,160,256]{2,1,0:T(8,128)(2,1)S(1)} %collective-permute-done.8), channel_id=1, source_target_pairs={{24,16},{4,12},{25,17},{5,13},{26,18},{6,14},{27,19},{7,15}} | collective-permute-start | bytes 2457608 | tf_op jit(solution)/shard_map/ppermute | solution.py:189
  47.5 14.9 %copy-start = (bf16[10,160,256]{2,1,0:T(8,128)(2,1)}, bf16[10,160,256]{2,1,0:T(8,128)(2,1)S(1)}, u32[]{:S(2)}) copy-start(bf16[10,160,256]{2,1,0:T(8,128)(2,1)S(1)} %collective-permute-done.6.fa_ref) | copy-start | bytes 2457604
  47.5 12.8 %collective-permute-start.7 = (bf16[10,160,256]{2,1,0:T(8,128)(2,1)S(1)}, bf16[10,160,256]{2,1,0:T(8,128)(2,1)S(1)}, u32[]{:S(2)}, u32[]{:S(2)}) collective-permute-start(bf16[10,160,256]{2,1,0:T(8,128)(2,1)S(1)} %collective-permute-done.6.fa_ref), channel_id=1, source_target_pairs={{0,4},{8,12},{16,20},{1,5},{9,13},{17,21},{2,6},{10,14},{18,22},{3... | collective-permute-start | bytes 2457608 | tf_op jit(solution)/shard_map/ppermute | solution.py:197
  48.2 14.2 %copy-start.1 = (bf16[10,160,256]{2,1,0:T(8,128)(2,1)}, bf16[10,160,256]{2,1,0:T(8,128)(2,1)S(1)}, u32[]{:S(2)}) copy-start(bf16[10,160,256]{2,1,0:T(8,128)(2,1)S(1)} %collective-permute-done.3.fbo_ref) | copy-start | bytes 2457604
  48.2 12.1 %collective-permute-start.4 = (bf16[10,160,256]{2,1,0:T(8,128)(2,1)S(1)}, bf16[10,160,256]{2,1,0:T(8,128)(2,1)S(1)}, u32[]{:S(2)}, u32[]{:S(2)}) collective-permute-start(bf16[10,160,256]{2,1,0:T(8,128)(2,1)S(1)} %collective-permute-done.3.fbo_ref), channel_id=1, source_target_pairs={{12,8},{20,16},{28,24},{13,9},{21,17},{29,25},{14,10},{22,18},{30,... | collective-permute-start | bytes 2457608 | tf_op jit(solution)/shard_map/ppermute | solution.py:196
  49.5 12.9 %copy-start.2 = (bf16[10,160,256]{2,1,0:T(8,128)(2,1)}, bf16[10,160,256]{2,1,0:T(8,128)(2,1)S(1)}, u32[]{:S(2)}) copy-start(bf16[10,160,256]{2,1,0:T(8,128)(2,1)S(1)} %collective-permute-done.5.par_ref) | copy-start | bytes 2457604
  60.3 2.1 %copy-start.3 = (bf16[10,160,256]{2,1,0:T(8,128)(2,1)}, bf16[10,160,256]{2,1,0:T(8,128)(2,1)S(1)}, u32[]{:S(2)}) copy-start(bf16[10,160,256]{2,1,0:T(8,128)(2,1)S(1)} %collective-permute-done.2.fb_ref) | copy-start | bytes 2457604
  60.3 0.9 %copy-start.4 = (bf16[10,160,256]{2,1,0:T(8,128)(2,1)}, bf16[10,160,256]{2,1,0:T(8,128)(2,1)S(1)}, u32[]{:S(2)}) copy-start(bf16[10,160,256]{2,1,0:T(8,128)(2,1)S(1)} %collective-permute-done.9.routed_ref) | copy-start | bytes 2457604
  60.3 1.2 %copy-start.5 = (bf16[10,160,256]{2,1,0:T(8,128)(2,1)}, bf16[10,160,256]{2,1,0:T(8,128)(2,1)S(1)}, u32[]{:S(2)}) copy-start(bf16[10,160,256]{2,1,0:T(8,128)(2,1)S(1)} %collective-permute-done.7.ra_ref) | copy-start | bytes 2457604
  61.5 0.9 %copy-start.6 = (bf16[10,160,256]{2,1,0:T(8,128)(2,1)}, bf16[10,160,256]{2,1,0:T(8,128)(2,1)S(1)}, u32[]{:S(2)}) copy-start(bf16[10,160,256]{2,1,0:T(8,128)(2,1)S(1)} %collective-permute-done.4.rb_ref) | copy-start | bytes 2457604

commit v25 on v21

--- a/solution.py
+++ b/solution.py
@@ -46,13 +46,19 @@
         r0 += n
 
 
-def layers_kernel(bounds_ref, above_ref, image_ref, below_ref, w1_ref, w2_ref, out_ref, xbuf,
-                  first_buf, stack):
-    halo = below_ref.shape[0] - 1
-    block = image_ref.shape[0]
-    xbuf[0:halo] = above_ref[0:halo]
-    xbuf[halo : halo + block] = image_ref[...]
-    xbuf[halo + block :] = below_ref[0:halo]
+def layers_kernel(bounds_ref, above_hbm, image_hbm, below_hbm, w1_ref, w2_ref, out_ref, xbuf,
+                  first_buf, stack, sems):
+    halo = below_hbm.shape[0] - 1
+    block = image_hbm.shape[0]
+    copies = [
+        pltpu.make_async_copy(above_hbm.at[0:halo], xbuf.at[0:halo], sems.at[0]),
+        pltpu.make_async_copy(image_hbm, xbuf.at[halo : halo + block], sems.at[1]),
+        pltpu.make_async_copy(below_hbm.at[0:halo], xbuf.at[halo + block :], sems.at[2]),
+    ]
+    for c in copies:
+        c.start()
+    for c in copies:
+        c.wait()
     rows1 = block + 2 * halo - 2
 
     def emit_first(r0, n, value):
@@ -115,11 +121,12 @@
     return pl.pallas_call(
         layers_kernel,
         out_shape=jax.ShapeDtypeStruct((rows - 4, cols, c), jnp.bfloat16),
-        in_specs=[smem()] + [vmem()] * 5,
+        in_specs=[smem()] + [pl.BlockSpec(memory_space=pl.ANY)] * 3 + [vmem()] * 2,
         out_specs=vmem(),
         scratch_shapes=[pltpu.VMEM((rows, cols, c), jnp.bfloat16),
                         pltpu.VMEM((rows - 2, cols, c), jnp.bfloat16),
-                        pltpu.VMEM((CHUNK, cols, 3 * c), jnp.bfloat16)],
+                        pltpu.VMEM((CHUNK, cols, 3 * c), jnp.bfloat16),
+                        pltpu.SemaphoreType.DMA((3,))],
         cost_estimate=pl.CostEstimate(flops=flops, transcendentals=2 * rows * cols * c,
                                       bytes_accessed=4 * rows * cols * c + 4 * 9 * c * c),
     )(bounds, above, image, below, w1, w2)

time: 68.5 us -> 69.5 us (1.015)
  Pallas kernels: 14.5 us -> 15.4 us
    pallas_call x1, Pallas kernels: 7.67 us -> 8.58 us  [layers(): pl.pallas_call(layers_kernel, out_shape=jax.ShapeDtypeStruct((rows - 4, c...]
where the time goes in v25:
time: 69.5 us; the launch traced here: 69 us
  waiting for transfers between devices  26.5 us (38%)
  Pallas kernels  15.4 us (22%)
  starting transfers between devices  14.8 us (21%)
  local copies, waits for them, and re-layouts  5.58 us (8%)
  between operations  4.04 us (6%)
  other arithmetic  2.62 us (4%)
    ppermute x1, waiting for transfers between devices, shards(): lax.ppermute(second, 'tm', [(a, b) for a, b in behind_pairs if b % 2 == 0])  10.8 us
    ppermute x1, waiting for transfers between devices, shards(): hop = lax.ppermute(second, 'tm', [(2, 6), (5, 1)])  8.74 us
    pallas_call x1, Pallas kernels, layers(): pl.pallas_call(layers_kernel, out_shape=jax.ShapeDtypeStruct((rows - 4, c...  8.58 us
    pallas_call x1, Pallas kernels, mix(): pl.pallas_call(mix_kernel, out_shape=jax.ShapeDtypeStruct((block, cols, c...  6.84 us
    ppermute x2, starting transfers between devices, shifted(): return lax.ppermute(value, axis, pairs)  5.84 us
    ppermute x1, waiting for transfers between devices, shards(): lax.ppermute(second, 'tm', [(2, 0), (3, 1), (4, 2), (6, 4), (7, 5)])  5.46 us
    unnamed x20, local copies, waits for them, and re-layouts  2.8 us
    slice x2, local copies, waits for them, and re-layouts, shards(): up = jnp.concatenate([image[:3], frame[:1]], axis=0)  2.04 us
  transfers between devices with their start and end apart: 10, of which 4 were waited for; matrix products, arithmetic and copies ran while one was open for 5% of the time, Pallas kernels for 0%

profile of v25, /device:TPU:22, one launch (start us, length us, event | category | flops | bytes accessed | tf_op | source)
XLA Modules:
  0.0 69.0 jit_solution(9268495944143515229)
XLA Ops:
  0.0 0.9 %slice_bitcast_fusion.2 = (bf16[1,160,256]{2,1,0:T(8,128)(2,1)S(1)}, bf16[1,160,256]{2,1,0:T(8,128)(2,1)S(1)}) fusion(bf16[1,8,160,256]{3,2,1,0:T(8,128)(2,1)} %param.9), kind=kLoop, calls=%fused_computation.4 | loop fusion | bytes 327680 | tf_op jit(solution)/shard_map/slice | solution.py:168
  0.9 0.0 copy-start.9
  1.0 1.1 %slice_bitcast_fusion = (bf16[3,160,256]{2,1,0:T(8,128)(2,1)S(1)}, bf16[3,160,256]{2,1,0:T(8,128)(2,1)S(1)}) fusion(bf16[1,8,160,256]{3,2,1,0:T(8,128)(2,1)} %param.8), kind=kLoop, calls=%fused_computation.2 | loop fusion | bytes 983040 | tf_op jit(solution)/shard_map/slice | solution.py:168
  2.1 3.5 %collective-permute-start = (bf16[4,160,256]{2,1,0:T(8,128)(2,1)S(1)}, bf16[4,160,256]{2,1,0:T(8,128)(2,1)S(1)}, u32[]{:S(2)}, u32[]{:S(2)}) collective-permute-start(bf16[4,160,256]{2,1,0:T(8,128)(2,1)S(1)} %pad_maximum_fusion), channel_id=1, source_target_pairs={{0,1},{1,2},{2,3},{4,5},{5,6},{6,7},{8,9},{9,10},{10,11},{12,13},{... | collective-permute-start | bytes 983048 | tf_op jit(solution)/shard_map/ppermute | solution.py:16
  5.6 2.4 %collective-permute-start.1 = (bf16[4,160,256]{2,1,0:T(8,128)(2,1)S(1)}, bf16[4,160,256]{2,1,0:T(8,128)(2,1)S(1)}, u32[]{:S(2)}, u32[]{:S(2)}) collective-permute-start(bf16[4,160,256]{2,1,0:T(8,128)(2,1)S(1)} %pad_maximum_fusion.1), channel_id=1, source_target_pairs={{1,0},{2,1},{3,2},{5,4},{6,5},{7,6},{9,8},{10,9},{11,10},{13,12},{... | collective-permute-start | bytes 983048 | tf_op jit(solution)/shard_map/ppermute | solution.py:16
  9.3 0.0 copy-done.9
  9.3 0.6 fusion
  9.9 0.6 broadcast_divide_fusion
  10.6 0.1 slice.45
  10.6 0.7 fusion.1
  13.8 0.6 pad_add_fusion.bounds_ref
  14.5 0.7 pad_maximum_fusion.2.coef_ref
  15.2 0.0 collective-permute-done.above_hbm.above_ref
  15.2 0.0 copy-start.7
  15.2 1.5 %collective-permute-done.1.below_hbm.below_ref = bf16[4,160,256]{2,1,0:T(8,128)(2,1)S(1)} collective-permute-done((bf16[4,160,256]{2,1,0:T(8,128)(2,1)S(1)}, bf16[4,160,256]{2,1,0:T(8,128)(2,1)S(1)}, u32[]{:S(2)}, u32[]{:S(2)}) %collective-permute-start.1) | collective-permute-done | bytes 327712 | tf_op jit(solution)/shard_map/ppermute | solution.py:16
  16.7 0.0 copy-done.7
  16.7 0.0 copy-start.8
  16.7 0.7 %copy-done.8 = bf16[4,160,256]{2,1,0:T(8,128)(2,1)} copy-done((bf16[4,160,256]{2,1,0:T(8,128)(2,1)}, bf16[4,160,256]{2,1,0:T(8,128)(2,1)S(1)}, u32[]{:S(2)}) %copy-start.8) | copy-done | bytes 327704
  17.4 8.6 %shard_map.82.own_ref = bf16[10,160,256]{2,1,0:T(8,128)(2,1)} custom-call(s32[2]{0:T(128)} %pad_add_fusion.bounds_ref, bf16[4,160,256]{2,1,0:T(8,128)(2,1)} %copy-done.7, bf16[8,160,256]{2,1,0:T(8,128)(2,1)} %bitcast.28, bf16[4,160,256]{2,1,0:T(8,128)(2,1)} %copy-done.8, bf16[3,3,256,256]{3,2,1,0:T(8,128)(2,1)} %w1_ref.1, bf16[3,3,256,256]{3,2,1,0:T(8,128)(2,1)} %w2_ref.1), custom_call_target="tpu_custom_call" | custom-call | flops 4152360960 | bytes 4653056 | tf_op jit(solution)/shard_map/pallas_call | solution.py:121
  26.0 1.3 %collective-permute-start.8 = (bf16[10,160,256]{2,1,0:T(8,128)(2,1)}, bf16[10,160,256]{2,1,0:T(8,128)(2,1)S(1)}, u32[]{:S(2)}, u32[]{:S(2)}) collective-permute-start(bf16[10,160,256]{2,1,0:T(8,128)(2,1)} %shard_map.82.own_ref), channel_id=1, source_target_pairs={{8,24},{20,4},{9,25},{21,5},{10,26},{22,6},{11,27},{23,7}} | collective-permute-start | bytes 2457608 | tf_op jit(solution)/shard_map/ppermute | solution.py:194
  27.3 1.9 %collective-permute-start.6 = (bf16[10,160,256]{2,1,0:T(8,128)(2,1)}, bf16[10,160,256]{2,1,0:T(8,128)(2,1)S(1)}, u32[]{:S(2)}, u32[]{:S(2)}) collective-permute-start(bf16[10,160,256]{2,1,0:T(8,128)(2,1)} %shard_map.82.own_ref), channel_id=1, source_target_pairs={{8,0},{12,4},{16,8},{24,16},{28,20},{9,1},{13,5},{17,9},{25,17},{2... | collective-permute-start | bytes 2457608 | tf_op jit(solution)/shard_map/ppermute | solution.py:193
  29.2 0.7 %collective-permute-start.3 = (bf16[10,160,256]{2,1,0:T(8,128)(2,1)}, bf16[10,160,256]{2,1,0:T(8,128)(2,1)S(1)}, u32[]{:S(2)}, u32[]{:S(2)}) collective-permute-start(bf16[10,160,256]{2,1,0:T(8,128)(2,1)} %shard_map.82.own_ref), channel_id=1, source_target_pairs={{4,12},{12,20},{20,28},{5,13},{13,21},{21,29},{6,14},{14,22},{22,3... | collective-permute-start | bytes 2457608 | tf_op jit(solution)/shard_map/ppermute | solution.py:201
  29.9 0.5 collective-permute-start.5
  30.4 1.3 %collective-permute-start.2 = (bf16[10,160,256]{2,1,0:T(8,128)(2,1)}, bf16[10,160,256]{2,1,0:T(8,128)(2,1)S(1)}, u32[]{:S(2)}, u32[]{:S(2)}) collective-permute-start(bf16[10,160,256]{2,1,0:T(8,128)(2,1)} %shard_map.82.own_ref), channel_id=1, source_target_pairs={{0,8},{16,24},{1,9},{17,25},{2,10},{18,26},{3,11},{19,27}} | collective-permute-start | bytes 2457608 | tf_op jit(solution)/shard_map/ppermute | solution.py:200
  31.7 8.7 %collective-permute-done.8 = bf16[10,160,256]{2,1,0:T(8,128)(2,1)S(1)} collective-permute-done((bf16[10,160,256]{2,1,0:T(8,128)(2,1)}, bf16[10,160,256]{2,1,0:T(8,128)(2,1)S(1)}, u32[]{:S(2)}, u32[]{:S(2)}) %collective-permute-start.8) | collective-permute-done | bytes 819232 | tf_op jit(solution)/shard_map/ppermute | solution.py:194
  40.5 1.3 %collective-permute-start.9 = (bf16[10,160,256]{2,1,0:T(8,128)(2,1)S(1)}, bf16[10,160,256]{2,1,0:T(8,128)(2,1)S(1)}, u32[]{:S(2)}, u32[]{:S(2)}) collective-permute-start(bf16[10,160,256]{2,1,0:T(8,128)(2,1)S(1)} %collective-permute-done.8), channel_id=1, source_target_pairs={{24,16},{4,12},{25,17},{5,13},{26,18},{6,14},{27,19},{7,15}} | collective-permute-start | bytes 2457608 | tf_op jit(solution)/shard_map/ppermute | solution.py:195
  41.8 5.5 %collective-permute-done.6.fa_ref = bf16[10,160,256]{2,1,0:T(8,128)(2,1)S(1)} collective-permute-done((bf16[10,160,256]{2,1,0:T(8,128)(2,1)}, bf16[10,160,256]{2,1,0:T(8,128)(2,1)S(1)}, u32[]{:S(2)}, u32[]{:S(2)}) %collective-permute-start.6) | collective-permute-done | bytes 819232 | tf_op jit(solution)/shard_map/ppermute | solution.py:193
  47.3 0.0 copy-start
  47.3 0.7 %collective-permute-start.7 = (bf16[10,160,256]{2,1,0:T(8,128)(2,1)S(1)}, bf16[10,160,256]{2,1,0:T(8,128)(2,1)S(1)}, u32[]{:S(2)}, u32[]{:S(2)}) collective-permute-start(bf16[10,160,256]{2,1,0:T(8,128)(2,1)S(1)} %collective-permute-done.6.fa_ref), channel_id=1, source_target_pairs={{0,4},{8,12},{16,20},{1,5},{9,13},{17,21},{2,6},{10,14},{18,22},{3... | collective-permute-start | bytes 2457608 | tf_op jit(solution)/shard_map/ppermute | solution.py:203
  48.0 0.0 collective-permute-done.3.fbo_ref
  48.0 0.0 copy-start.1
  48.0 1.3 %collective-permute-start.4 = (bf16[10,160,256]{2,1,0:T(8,128)(2,1)S(1)}, bf16[10,160,256]{2,1,0:T(8,128)(2,1)S(1)}, u32[]{:S(2)}, u32[]{:S(2)}) collective-permute-start(bf16[10,160,256]{2,1,0:T(8,128)(2,1)S(1)} %collective-permute-done.3.fbo_ref), channel_id=1, source_target_pairs={{12,8},{20,16},{28,24},{13,9},{21,17},{29,25},{14,10},{22,18},{30,... | collective-permute-start | bytes 2457608 | tf_op jit(solution)/shard_map/ppermute | solution.py:202
  49.3 0.0 collective-permute-done.5.par_ref
  49.3 0.0 copy-start.2
  49.3 10.8 %collective-permute-done.2.fb_ref = bf16[10,160,256]{2,1,0:T(8,128)(2,1)S(1)} collective-permute-done((bf16[10,160,256]{2,1,0:T(8,128)(2,1)}, bf16[10,160,256]{2,1,0:T(8,128)(2,1)S(1)}, u32[]{:S(2)}, u32[]{:S(2)}) %collective-permute-start.2) | collective-permute-done | bytes 819232 | tf_op jit(solution)/shard_map/ppermute | solution.py:200
  60.1 0.0 copy-start.3
  60.1 0.0 collective-permute-done.9.routed_ref
  60.1 0.0 collective-permute-done.7.ra_ref
  60.1 0.0 copy-start.5
  60.1 0.0 collective-permute-done.4.rb_ref
  60.1 0.9 %copy-done.4 = bf16[10,160,256]{2,1,0:T(8,128)(2,1)} copy-done((bf16[10,160,256]{2,1,0:T(8,128)(2,1)}, bf16[10,160,256]{2,1,0:T(8,128)(2,1)S(1)}, u32[]{:S(2)}) %copy-start.4) | copy-done | bytes 819224
  61.0 0.2 copy-done.5
  61.3 0.9 %copy-done.6 = bf16[10,160,256]{2,1,0:T(8,128)(2,1)} copy-done((bf16[10,160,256]{2,1,0:T(8,128)(2,1)}, bf16[10,160,256]{2,1,0:T(8,128)(2,1)S(1)}, u32[]{:S(2)}) %copy-start.6) | copy-done | bytes 819224
  62.2 0.0 copy-done
  62.2 0.0 copy-done.1
  62.2 0.0 copy-done.2
  62.2 0.0 copy-done.3
  62.2 6.8 %shard_map.83 = bf16[8,160,256]{2,1,0:T(8,128)(2,1)} custom-call(f32[7]{0:T(128)} %pad_maximum_fusion.2.coef_ref, bf16[10,160,256]{2,1,0:T(8,128)(2,1)} %copy-done.3, bf16[10,160,256]{2,1,0:T(8,128)(2,1)} %copy-done.1, bf16[10,160,256]{2,1,0:T(8,128)(2,1)} %copy-done.6, bf16[10,160,256]{2,1,0:T(8,128)(2,1)} %shard_map.82.own_ref, ...), custom_call_target="tpu_custom_call" | custom-call | flops 1509949440 | bytes 8552448 | tf_op jit(solution)/shard_map/pallas_call | solution.py:138
  (4 shorter events, 0.1 us)
Async XLA Ops:
  0.9 8.4 %copy-start.9 = (s32[1,5]{1,0:T(1,128)S(1)}, s32[1,5]{1,0:T(1,128)}, u32[]{:S(2)}) copy-start(s32[1,5]{1,0:T(1,128)} %param.12) | copy-start | bytes 64
  2.1 13.1 %collective-permute-start = (bf16[4,160,256]{2,1,0:T(8,128)(2,1)S(1)}, bf16[4,160,256]{2,1,0:T(8,128)(2,1)S(1)}, u32[]{:S(2)}, u32[]{:S(2)}) collective-permute-start(bf16[4,160,256]{2,1,0:T(8,128)(2,1)S(1)} %pad_maximum_fusion), channel_id=1, source_target_pairs={{0,1},{1,2},{2,3},{4,5},{5,6},{6,7},{8,9},{9,10},{10,11},{12,13},{... | collective-permute-start | bytes 983048 | tf_op jit(solution)/shard_map/ppermute | solution.py:16
  5.6 11.1 %collective-permute-start.1 = (bf16[4,160,256]{2,1,0:T(8,128)(2,1)S(1)}, bf16[4,160,256]{2,1,0:T(8,128)(2,1)S(1)}, u32[]{:S(2)}, u32[]{:S(2)}) collective-permute-start(bf16[4,160,256]{2,1,0:T(8,128)(2,1)S(1)} %pad_maximum_fusion.1), channel_id=1, source_target_pairs={{1,0},{2,1},{3,2},{5,4},{6,5},{7,6},{9,8},{10,9},{11,10},{13,12},{... | collective-permute-start | bytes 983048 | tf_op jit(solution)/shard_map/ppermute | solution.py:16
  15.2 1.5 %copy-start.7 = (bf16[4,160,256]{2,1,0:T(8,128)(2,1)}, bf16[4,160,256]{2,1,0:T(8,128)(2,1)S(1)}, u32[]{:S(2)}) copy-start(bf16[4,160,256]{2,1,0:T(8,128)(2,1)S(1)} %collective-permute-done.above_hbm.above_ref) | copy-start | bytes 983044
  16.7 0.7 %copy-start.8 = (bf16[4,160,256]{2,1,0:T(8,128)(2,1)}, bf16[4,160,256]{2,1,0:T(8,128)(2,1)S(1)}, u32[]{:S(2)}) copy-start(bf16[4,160,256]{2,1,0:T(8,128)(2,1)S(1)} %collective-permute-done.1.below_hbm.below_ref) | copy-start | bytes 983044
  26.0 14.4 %collective-permute-start.8 = (bf16[10,160,256]{2,1,0:T(8,128)(2,1)}, bf16[10,160,256]{2,1,0:T(8,128)(2,1)S(1)}, u32[]{:S(2)}, u32[]{:S(2)}) collective-permute-start(bf16[10,160,256]{2,1,0:T(8,128)(2,1)} %shard_map.82.own_ref), channel_id=1, source_target_pairs={{8,24},{20,4},{9,25},{21,5},{10,26},{22,6},{11,27},{23,7}} | collective-permute-start | bytes 2457608 | tf_op jit(solution)/shard_map/ppermute | solution.py:194
  27.3 19.9 %collective-permute-start.6 = (bf16[10,160,256]{2,1,0:T(8,128)(2,1)}, bf16[10,160,256]{2,1,0:T(8,128)(2,1)S(1)}, u32[]{:S(2)}, u32[]{:S(2)}) collective-permute-start(bf16[10,160,256]{2,1,0:T(8,128)(2,1)} %shard_map.82.own_ref), channel_id=1, source_target_pairs={{8,0},{12,4},{16,8},{24,16},{28,20},{9,1},{13,5},{17,9},{25,17},{2... | collective-permute-start | bytes 2457608 | tf_op jit(solution)/shard_map/ppermute | solution.py:193
  29.2 18.8 %collective-permute-start.3 = (bf16[10,160,256]{2,1,0:T(8,128)(2,1)}, bf16[10,160,256]{2,1,0:T(8,128)(2,1)S(1)}, u32[]{:S(2)}, u32[]{:S(2)}) collective-permute-start(bf16[10,160,256]{2,1,0:T(8,128)(2,1)} %shard_map.82.own_ref), channel_id=1, source_target_pairs={{4,12},{12,20},{20,28},{5,13},{13,21},{21,29},{6,14},{14,22},{22,3... | collective-permute-start | bytes 2457608 | tf_op jit(solution)/shard_map/ppermute | solution.py:201
  29.9 19.4 %collective-permute-start.5 = (bf16[10,160,256]{2,1,0:T(8,128)(2,1)}, bf16[10,160,256]{2,1,0:T(8,128)(2,1)S(1)}, u32[]{:S(2)}, u32[]{:S(2)}) collective-permute-start(bf16[10,160,256]{2,1,0:T(8,128)(2,1)} %shard_map.82.own_ref), channel_id=1, source_target_pairs={{0,4},{4,0},{8,12},{12,8},{16,20},{20,16},{24,28},{28,24},{1,5},{5... | collective-permute-start | bytes 2457608 | tf_op jit(solution)/shard_map/ppermute | solution.py:190
  30.4 29.7 %collective-permute-start.2 = (bf16[10,160,256]{2,1,0:T(8,128)(2,1)}, bf16[10,160,256]{2,1,0:T(8,128)(2,1)S(1)}, u32[]{:S(2)}, u32[]{:S(2)}) collective-permute-start(bf16[10,160,256]{2,1,0:T(8,128)(2,1)} %shard_map.82.own_ref), channel_id=1, source_target_pairs={{0,8},{16,24},{1,9},{17,25},{2,10},{18,26},{3,11},{19,27}} | collective-permute-start | bytes 2457608 | tf_op jit(solution)/shard_map/ppermute | solution.py:200
  40.5 19.6 %collective-permute-start.9 = (bf16[10,160,256]{2,1,0:T(8,128)(2,1)S(1)}, bf16[10,160,256]{2,1,0:T(8,128)(2,1)S(1)}, u32[]{:S(2)}, u32[]{:S(2)}) collective-permute-start(bf16[10,160,256]{2,1,0:T(8,128)(2,1)S(1)} %collective-permute-done.8), channel_id=1, source_target_pairs={{24,16},{4,12},{25,17},{5,13},{26,18},{6,14},{27,19},{7,15}} | collective-permute-start | bytes 2457608 | tf_op jit(solution)/shard_map/ppermute | solution.py:195
  47.3 14.9 %copy-start = (bf16[10,160,256]{2,1,0:T(8,128)(2,1)}, bf16[10,160,256]{2,1,0:T(8,128)(2,1)S(1)}, u32[]{:S(2)}) copy-start(bf16[10,160,256]{2,1,0:T(8,128)(2,1)S(1)} %collective-permute-done.6.fa_ref) | copy-start | bytes 2457604
  47.3 12.8 %collective-permute-start.7 = (bf16[10,160,256]{2,1,0:T(8,128)(2,1)S(1)}, bf16[10,160,256]{2,1,0:T(8,128)(2,1)S(1)}, u32[]{:S(2)}, u32[]{:S(2)}) collective-permute-start(bf16[10,160,256]{2,1,0:T(8,128)(2,1)S(1)} %collective-permute-done.6.fa_ref), channel_id=1, source_target_pairs={{0,4},{8,12},{16,20},{1,5},{9,13},{17,21},{2,6},{10,14},{18,22},{3... | collective-permute-start | bytes 2457608 | tf_op jit(solution)/shard_map/ppermute | solution.py:203
  48.0 14.2 %copy-start.1 = (bf16[10,160,256]{2,1,0:T(8,128)(2,1)}, bf16[10,160,256]{2,1,0:T(8,128)(2,1)S(1)}, u32[]{:S(2)}) copy-start(bf16[10,160,256]{2,1,0:T(8,128)(2,1)S(1)} %collective-permute-done.3.fbo_ref) | copy-start | bytes 2457604
  48.0 12.1 %collective-permute-start.4 = (bf16[10,160,256]{2,1,0:T(8,128)(2,1)S(1)}, bf16[10,160,256]{2,1,0:T(8,128)(2,1)S(1)}, u32[]{:S(2)}, u32[]{:S(2)}) collective-permute-start(bf16[10,160,256]{2,1,0:T(8,128)(2,1)S(1)} %collective-permute-done.3.fbo_ref), channel_id=1, source_target_pairs={{12,8},{20,16},{28,24},{13,9},{21,17},{29,25},{14,10},{22,18},{30,... | collective-permute-start | bytes 2457608 | tf_op jit(solution)/shard_map/ppermute | solution.py:202
  49.3 12.9 %copy-start.2 = (bf16[10,160,256]{2,1,0:T(8,128)(2,1)}, bf16[10,160,256]{2,1,0:T(8,128)(2,1)S(1)}, u32[]{:S(2)}) copy-start(bf16[10,160,256]{2,1,0:T(8,128)(2,1)S(1)} %collective-permute-done.5.par_ref) | copy-start | bytes 2457604
  60.1 2.1 %copy-start.3 = (bf16[10,160,256]{2,1,0:T(8,128)(2,1)}, bf16[10,160,256]{2,1,0:T(8,128)(2,1)S(1)}, u32[]{:S(2)}) copy-start(bf16[10,160,256]{2,1,0:T(8,128)(2,1)S(1)} %collective-permute-done.2.fb_ref) | copy-start | bytes 2457604
  60.1 0.9 %copy-start.4 = (bf16[10,160,256]{2,1,0:T(8,128)(2,1)}, bf16[10,160,256]{2,1,0:T(8,128)(2,1)S(1)}, u32[]{:S(2)}) copy-start(bf16[10,160,256]{2,1,0:T(8,128)(2,1)S(1)} %collective-permute-done.9.routed_ref) | copy-start | bytes 2457604
  60.1 1.2 %copy-start.5 = (bf16[10,160,256]{2,1,0:T(8,128)(2,1)}, bf16[10,160,256]{2,1,0:T(8,128)(2,1)S(1)}, u32[]{:S(2)}) copy-start(bf16[10,160,256]{2,1,0:T(8,128)(2,1)S(1)} %collective-permute-done.7.ra_ref) | copy-start | bytes 2457604
  61.3 0.9 %copy-start.6 = (bf16[10,160,256]{2,1,0:T(8,128)(2,1)}, bf16[10,160,256]{2,1,0:T(8,128)(2,1)S(1)}, u32[]{:S(2)}) copy-start(bf16[10,160,256]{2,1,0:T(8,128)(2,1)S(1)} %collective-permute-done.4.rb_ref) | copy-start | bytes 2457604

commit v26 on v21

--- a/solution.py
+++ b/solution.py
@@ -119,7 +119,7 @@
         out_specs=vmem(),
         scratch_shapes=[pltpu.VMEM((rows, cols, c), jnp.bfloat16),
                         pltpu.VMEM((rows - 2, cols, c), jnp.bfloat16),
-                        pltpu.VMEM((CHUNK, cols, 3 * c), jnp.bfloat16)],
+                        pltpu.VMEM((1, cols, 3 * c), jnp.bfloat16)],
         cost_estimate=pl.CostEstimate(flops=flops, transcendentals=2 * rows * cols * c,
                                       bytes_accessed=4 * rows * cols * c + 4 * 9 * c * c),
     )(bounds, above, image, below, w1, w2)

time: 68.5 us -> 68.4 us (level)
  no operation moved by 1% of the time
where the time goes in v26:
time: 68.4 us; the launch traced here: 68 us
  waiting for transfers between devices  26.5 us (39%)
  starting transfers between devices  14.8 us (22%)
  Pallas kernels  14.4 us (21%)
  local copies, waits for them, and re-layouts  5.58 us (8%)
  between operations  4.03 us (6%)
  other arithmetic  2.62 us (4%)
    ppermute x1, waiting for transfers between devices, shards(): lax.ppermute(second, 'tm', [(a, b) for a, b in behind_pairs if b % 2 == 0])  10.8 us
    ppermute x1, waiting for transfers between devices, shards(): hop = lax.ppermute(second, 'tm', [(2, 6), (5, 1)])  8.74 us
    pallas_call x1, Pallas kernels, layers(): pl.pallas_call(layers_kernel, out_shape=jax.ShapeDtypeStruct((rows - 4, c...  7.54 us
    pallas_call x1, Pallas kernels, mix(): pl.pallas_call(mix_kernel, out_shape=jax.ShapeDtypeStruct((block, cols, c...  6.83 us
    ppermute x2, starting transfers between devices, shifted(): return lax.ppermute(value, axis, pairs)  5.84 us
    ppermute x1, waiting for transfers between devices, shards(): lax.ppermute(second, 'tm', [(2, 0), (3, 1), (4, 2), (6, 4), (7, 5)])  5.46 us
    unnamed x20, local copies, waits for them, and re-layouts  2.8 us
    slice x2, local copies, waits for them, and re-layouts, shards(): up = jnp.concatenate([image[:3], frame[:1]], axis=0)  2.04 us
  transfers between devices with their start and end apart: 10, of which 4 were waited for; matrix products, arithmetic and copies ran while one was open for 5% of the time, Pallas kernels for 0%

profile of v26, /device:TPU:22, one launch (start us, length us, event | category | flops | bytes accessed | tf_op | source)
XLA Modules:
  0.0 68.0 jit_solution(13836632495574437284)
XLA Ops:
  0.0 0.9 %slice_bitcast_fusion.2 = (bf16[1,160,256]{2,1,0:T(8,128)(2,1)S(1)}, bf16[1,160,256]{2,1,0:T(8,128)(2,1)S(1)}) fusion(bf16[1,8,160,256]{3,2,1,0:T(8,128)(2,1)} %param.9), kind=kLoop, calls=%fused_computation.4 | loop fusion | bytes 327680 | tf_op jit(solution)/shard_map/slice | solution.py:161
  0.9 0.0 copy-start.9
  1.0 1.1 %slice_bitcast_fusion = (bf16[3,160,256]{2,1,0:T(8,128)(2,1)S(1)}, bf16[3,160,256]{2,1,0:T(8,128)(2,1)S(1)}) fusion(bf16[1,8,160,256]{3,2,1,0:T(8,128)(2,1)} %param.8), kind=kLoop, calls=%fused_computation.2 | loop fusion | bytes 983040 | tf_op jit(solution)/shard_map/slice | solution.py:161
  2.1 3.5 %collective-permute-start = (bf16[4,160,256]{2,1,0:T(8,128)(2,1)S(1)}, bf16[4,160,256]{2,1,0:T(8,128)(2,1)S(1)}, u32[]{:S(2)}, u32[]{:S(2)}) collective-permute-start(bf16[4,160,256]{2,1,0:T(8,128)(2,1)S(1)} %pad_maximum_fusion), channel_id=1, source_target_pairs={{0,1},{1,2},{2,3},{4,5},{5,6},{6,7},{8,9},{9,10},{10,11},{12,13},{... | collective-permute-start | bytes 983048 | tf_op jit(solution)/shard_map/ppermute | solution.py:16
  5.6 2.4 %collective-permute-start.1 = (bf16[4,160,256]{2,1,0:T(8,128)(2,1)S(1)}, bf16[4,160,256]{2,1,0:T(8,128)(2,1)S(1)}, u32[]{:S(2)}, u32[]{:S(2)}) collective-permute-start(bf16[4,160,256]{2,1,0:T(8,128)(2,1)S(1)} %pad_maximum_fusion.1), channel_id=1, source_target_pairs={{1,0},{2,1},{3,2},{5,4},{6,5},{7,6},{9,8},{10,9},{11,10},{13,12},{... | collective-permute-start | bytes 983048 | tf_op jit(solution)/shard_map/ppermute | solution.py:16
  9.3 0.0 copy-done.9
  9.3 0.6 fusion
  9.9 0.6 broadcast_divide_fusion
  10.6 0.1 slice.45
  10.6 0.7 fusion.1
  13.8 0.6 pad_add_fusion.bounds_ref
  14.5 0.7 pad_maximum_fusion.2.coef_ref
  15.2 0.0 collective-permute-done.above_ref
  15.2 0.0 copy-start.7
  15.2 1.5 %collective-permute-done.1.below_ref = bf16[4,160,256]{2,1,0:T(8,128)(2,1)S(1)} collective-permute-done((bf16[4,160,256]{2,1,0:T(8,128)(2,1)S(1)}, bf16[4,160,256]{2,1,0:T(8,128)(2,1)S(1)}, u32[]{:S(2)}, u32[]{:S(2)}) %collective-permute-start.1) | collective-permute-done | bytes 327712 | tf_op jit(solution)/shard_map/ppermute | solution.py:16
  16.7 0.0 copy-done.7
  16.7 0.0 copy-start.8
  16.7 0.7 %copy-done.8 = bf16[4,160,256]{2,1,0:T(8,128)(2,1)} copy-done((bf16[4,160,256]{2,1,0:T(8,128)(2,1)}, bf16[4,160,256]{2,1,0:T(8,128)(2,1)S(1)}, u32[]{:S(2)}) %copy-start.8) | copy-done | bytes 327704
  17.4 7.5 %shard_map.82.own_ref = bf16[10,160,256]{2,1,0:T(8,128)(2,1)} custom-call(s32[2]{0:T(128)} %pad_add_fusion.bounds_ref, bf16[4,160,256]{2,1,0:T(8,128)(2,1)} %copy-done.7, bf16[8,160,256]{2,1,0:T(8,128)(2,1)} %bitcast.28, bf16[4,160,256]{2,1,0:T(8,128)(2,1)} %copy-done.8, bf16[3,3,256,256]{3,2,1,0:T(8,128)(2,1)} %w1_ref.1, bf16[3,3,256,256]{3,2,1,0:T(8,128)(2,1)} %w2_ref.1), custom_call_target="tpu_custom_call" | custom-call | flops 4152360960 | bytes 4653056 | tf_op jit(solution)/shard_map/pallas_call | solution.py:115
  25.0 1.3 %collective-permute-start.8 = (bf16[10,160,256]{2,1,0:T(8,128)(2,1)}, bf16[10,160,256]{2,1,0:T(8,128)(2,1)S(1)}, u32[]{:S(2)}, u32[]{:S(2)}) collective-permute-start(bf16[10,160,256]{2,1,0:T(8,128)(2,1)} %shard_map.82.own_ref), channel_id=1, source_target_pairs={{8,24},{20,4},{9,25},{21,5},{10,26},{22,6},{11,27},{23,7}} | collective-permute-start | bytes 2457608 | tf_op jit(solution)/shard_map/ppermute | solution.py:187
  26.3 1.9 %collective-permute-start.6 = (bf16[10,160,256]{2,1,0:T(8,128)(2,1)}, bf16[10,160,256]{2,1,0:T(8,128)(2,1)S(1)}, u32[]{:S(2)}, u32[]{:S(2)}) collective-permute-start(bf16[10,160,256]{2,1,0:T(8,128)(2,1)} %shard_map.82.own_ref), channel_id=1, source_target_pairs={{8,0},{12,4},{16,8},{24,16},{28,20},{9,1},{13,5},{17,9},{25,17},{2... | collective-permute-start | bytes 2457608 | tf_op jit(solution)/shard_map/ppermute | solution.py:186
  28.2 0.7 %collective-permute-start.3 = (bf16[10,160,256]{2,1,0:T(8,128)(2,1)}, bf16[10,160,256]{2,1,0:T(8,128)(2,1)S(1)}, u32[]{:S(2)}, u32[]{:S(2)}) collective-permute-start(bf16[10,160,256]{2,1,0:T(8,128)(2,1)} %shard_map.82.own_ref), channel_id=1, source_target_pairs={{4,12},{12,20},{20,28},{5,13},{13,21},{21,29},{6,14},{14,22},{22,3... | collective-permute-start | bytes 2457608 | tf_op jit(solution)/shard_map/ppermute | solution.py:194
  28.9 0.5 collective-permute-start.5
  29.4 1.3 %collective-permute-start.2 = (bf16[10,160,256]{2,1,0:T(8,128)(2,1)}, bf16[10,160,256]{2,1,0:T(8,128)(2,1)S(1)}, u32[]{:S(2)}, u32[]{:S(2)}) collective-permute-start(bf16[10,160,256]{2,1,0:T(8,128)(2,1)} %shard_map.82.own_ref), channel_id=1, source_target_pairs={{0,8},{16,24},{1,9},{17,25},{2,10},{18,26},{3,11},{19,27}} | collective-permute-start | bytes 2457608 | tf_op jit(solution)/shard_map/ppermute | solution.py:193
  30.7 8.7 %collective-permute-done.8 = bf16[10,160,256]{2,1,0:T(8,128)(2,1)S(1)} collective-permute-done((bf16[10,160,256]{2,1,0:T(8,128)(2,1)}, bf16[10,160,256]{2,1,0:T(8,128)(2,1)S(1)}, u32[]{:S(2)}, u32[]{:S(2)}) %collective-permute-start.8) | collective-permute-done | bytes 819232 | tf_op jit(solution)/shard_map/ppermute | solution.py:187
  39.4 1.3 %collective-permute-start.9 = (bf16[10,160,256]{2,1,0:T(8,128)(2,1)S(1)}, bf16[10,160,256]{2,1,0:T(8,128)(2,1)S(1)}, u32[]{:S(2)}, u32[]{:S(2)}) collective-permute-start(bf16[10,160,256]{2,1,0:T(8,128)(2,1)S(1)} %collective-permute-done.8), channel_id=1, source_target_pairs={{24,16},{4,12},{25,17},{5,13},{26,18},{6,14},{27,19},{7,15}} | collective-permute-start | bytes 2457608 | tf_op jit(solution)/shard_map/ppermute | solution.py:188
  40.7 5.5 %collective-permute-done.6.fa_ref = bf16[10,160,256]{2,1,0:T(8,128)(2,1)S(1)} collective-permute-done((bf16[10,160,256]{2,1,0:T(8,128)(2,1)}, bf16[10,160,256]{2,1,0:T(8,128)(2,1)S(1)}, u32[]{:S(2)}, u32[]{:S(2)}) %collective-permute-start.6) | collective-permute-done | bytes 819232 | tf_op jit(solution)/shard_map/ppermute | solution.py:186
  46.2 0.0 copy-start
  46.2 0.7 %collective-permute-start.7 = (bf16[10,160,256]{2,1,0:T(8,128)(2,1)S(1)}, bf16[10,160,256]{2,1,0:T(8,128)(2,1)S(1)}, u32[]{:S(2)}, u32[]{:S(2)}) collective-permute-start(bf16[10,160,256]{2,1,0:T(8,128)(2,1)S(1)} %collective-permute-done.6.fa_ref), channel_id=1, source_target_pairs={{0,4},{8,12},{16,20},{1,5},{9,13},{17,21},{2,6},{10,14},{18,22},{3... | collective-permute-start | bytes 2457608 | tf_op jit(solution)/shard_map/ppermute | solution.py:196
  46.9 0.0 collective-permute-done.3.fbo_ref
  46.9 0.0 copy-start.1
  46.9 1.3 %collective-permute-start.4 = (bf16[10,160,256]{2,1,0:T(8,128)(2,1)S(1)}, bf16[10,160,256]{2,1,0:T(8,128)(2,1)S(1)}, u32[]{:S(2)}, u32[]{:S(2)}) collective-permute-start(bf16[10,160,256]{2,1,0:T(8,128)(2,1)S(1)} %collective-permute-done.3.fbo_ref), channel_id=1, source_target_pairs={{12,8},{20,16},{28,24},{13,9},{21,17},{29,25},{14,10},{22,18},{30,... | collective-permute-start | bytes 2457608 | tf_op jit(solution)/shard_map/ppermute | solution.py:195
  48.2 0.0 collective-permute-done.5.par_ref
  48.2 0.0 copy-start.2
  48.3 10.8 %collective-permute-done.2.fb_ref = bf16[10,160,256]{2,1,0:T(8,128)(2,1)S(1)} collective-permute-done((bf16[10,160,256]{2,1,0:T(8,128)(2,1)}, bf16[10,160,256]{2,1,0:T(8,128)(2,1)S(1)}, u32[]{:S(2)}, u32[]{:S(2)}) %collective-permute-start.2) | collective-permute-done | bytes 819232 | tf_op jit(solution)/shard_map/ppermute | solution.py:193
  59.0 0.0 copy-start.3
  59.0 0.0 collective-permute-done.9.routed_ref
  59.0 0.0 collective-permute-done.7.ra_ref
  59.0 0.0 copy-start.5
  59.1 0.0 collective-permute-done.4.rb_ref
  59.1 0.9 %copy-done.4 = bf16[10,160,256]{2,1,0:T(8,128)(2,1)} copy-done((bf16[10,160,256]{2,1,0:T(8,128)(2,1)}, bf16[10,160,256]{2,1,0:T(8,128)(2,1)S(1)}, u32[]{:S(2)}) %copy-start.4) | copy-done | bytes 819224
  60.0 0.2 copy-done.5
  60.2 0.9 %copy-done.6 = bf16[10,160,256]{2,1,0:T(8,128)(2,1)} copy-done((bf16[10,160,256]{2,1,0:T(8,128)(2,1)}, bf16[10,160,256]{2,1,0:T(8,128)(2,1)S(1)}, u32[]{:S(2)}) %copy-start.6) | copy-done | bytes 819224
  61.1 0.0 copy-done
  61.1 0.0 copy-done.1
  61.1 0.0 copy-done.2
  61.1 0.0 copy-done.3
  61.1 6.8 %shard_map.83 = bf16[8,160,256]{2,1,0:T(8,128)(2,1)} custom-call(f32[7]{0:T(128)} %pad_maximum_fusion.2.coef_ref, bf16[10,160,256]{2,1,0:T(8,128)(2,1)} %copy-done.3, bf16[10,160,256]{2,1,0:T(8,128)(2,1)} %copy-done.1, bf16[10,160,256]{2,1,0:T(8,128)(2,1)} %copy-done.6, bf16[10,160,256]{2,1,0:T(8,128)(2,1)} %shard_map.82.own_ref, ...), custom_call_target="tpu_custom_call" | custom-call | flops 1509949440 | bytes 8552448 | tf_op jit(solution)/shard_map/pallas_call | solution.py:131
  (4 shorter events, 0.1 us)
Async XLA Ops:
  0.9 8.4 %copy-start.9 = (s32[1,5]{1,0:T(1,128)S(1)}, s32[1,5]{1,0:T(1,128)}, u32[]{:S(2)}) copy-start(s32[1,5]{1,0:T(1,128)} %param.12) | copy-start | bytes 64
  2.1 13.1 %collective-permute-start = (bf16[4,160,256]{2,1,0:T(8,128)(2,1)S(1)}, bf16[4,160,256]{2,1,0:T(8,128)(2,1)S(1)}, u32[]{:S(2)}, u32[]{:S(2)}) collective-permute-start(bf16[4,160,256]{2,1,0:T(8,128)(2,1)S(1)} %pad_maximum_fusion), channel_id=1, source_target_pairs={{0,1},{1,2},{2,3},{4,5},{5,6},{6,7},{8,9},{9,10},{10,11},{12,13},{... | collective-permute-start | bytes 983048 | tf_op jit(solution)/shard_map/ppermute | solution.py:16
  5.6 11.1 %collective-permute-start.1 = (bf16[4,160,256]{2,1,0:T(8,128)(2,1)S(1)}, bf16[4,160,256]{2,1,0:T(8,128)(2,1)S(1)}, u32[]{:S(2)}, u32[]{:S(2)}) collective-permute-start(bf16[4,160,256]{2,1,0:T(8,128)(2,1)S(1)} %pad_maximum_fusion.1), channel_id=1, source_target_pairs={{1,0},{2,1},{3,2},{5,4},{6,5},{7,6},{9,8},{10,9},{11,10},{13,12},{... | collective-permute-start | bytes 983048 | tf_op jit(solution)/shard_map/ppermute | solution.py:16
  15.2 1.5 %copy-start.7 = (bf16[4,160,256]{2,1,0:T(8,128)(2,1)}, bf16[4,160,256]{2,1,0:T(8,128)(2,1)S(1)}, u32[]{:S(2)}) copy-start(bf16[4,160,256]{2,1,0:T(8,128)(2,1)S(1)} %collective-permute-done.above_ref) | copy-start | bytes 983044
  16.7 0.7 %copy-start.8 = (bf16[4,160,256]{2,1,0:T(8,128)(2,1)}, bf16[4,160,256]{2,1,0:T(8,128)(2,1)S(1)}, u32[]{:S(2)}) copy-start(bf16[4,160,256]{2,1,0:T(8,128)(2,1)S(1)} %collective-permute-done.1.below_ref) | copy-start | bytes 983044
  25.0 14.4 %collective-permute-start.8 = (bf16[10,160,256]{2,1,0:T(8,128)(2,1)}, bf16[10,160,256]{2,1,0:T(8,128)(2,1)S(1)}, u32[]{:S(2)}, u32[]{:S(2)}) collective-permute-start(bf16[10,160,256]{2,1,0:T(8,128)(2,1)} %shard_map.82.own_ref), channel_id=1, source_target_pairs={{8,24},{20,4},{9,25},{21,5},{10,26},{22,6},{11,27},{23,7}} | collective-permute-start | bytes 2457608 | tf_op jit(solution)/shard_map/ppermute | solution.py:187
  26.3 19.9 %collective-permute-start.6 = (bf16[10,160,256]{2,1,0:T(8,128)(2,1)}, bf16[10,160,256]{2,1,0:T(8,128)(2,1)S(1)}, u32[]{:S(2)}, u32[]{:S(2)}) collective-permute-start(bf16[10,160,256]{2,1,0:T(8,128)(2,1)} %shard_map.82.own_ref), channel_id=1, source_target_pairs={{8,0},{12,4},{16,8},{24,16},{28,20},{9,1},{13,5},{17,9},{25,17},{2... | collective-permute-start | bytes 2457608 | tf_op jit(solution)/shard_map/ppermute | solution.py:186
  28.2 18.7 %collective-permute-start.3 = (bf16[10,160,256]{2,1,0:T(8,128)(2,1)}, bf16[10,160,256]{2,1,0:T(8,128)(2,1)S(1)}, u32[]{:S(2)}, u32[]{:S(2)}) collective-permute-start(bf16[10,160,256]{2,1,0:T(8,128)(2,1)} %shard_map.82.own_ref), channel_id=1, source_target_pairs={{4,12},{12,20},{20,28},{5,13},{13,21},{21,29},{6,14},{14,22},{22,3... | collective-permute-start | bytes 2457608 | tf_op jit(solution)/shard_map/ppermute | solution.py:194
  28.9 19.3 %collective-permute-start.5 = (bf16[10,160,256]{2,1,0:T(8,128)(2,1)}, bf16[10,160,256]{2,1,0:T(8,128)(2,1)S(1)}, u32[]{:S(2)}, u32[]{:S(2)}) collective-permute-start(bf16[10,160,256]{2,1,0:T(8,128)(2,1)} %shard_map.82.own_ref), channel_id=1, source_target_pairs={{0,4},{4,0},{8,12},{12,8},{16,20},{20,16},{24,28},{28,24},{1,5},{5... | collective-permute-start | bytes 2457608 | tf_op jit(solution)/shard_map/ppermute | solution.py:183
  29.4 29.7 %collective-permute-start.2 = (bf16[10,160,256]{2,1,0:T(8,128)(2,1)}, bf16[10,160,256]{2,1,0:T(8,128)(2,1)S(1)}, u32[]{:S(2)}, u32[]{:S(2)}) collective-permute-start(bf16[10,160,256]{2,1,0:T(8,128)(2,1)} %shard_map.82.own_ref), channel_id=1, source_target_pairs={{0,8},{16,24},{1,9},{17,25},{2,10},{18,26},{3,11},{19,27}} | collective-permute-start | bytes 2457608 | tf_op jit(solution)/shard_map/ppermute | solution.py:193
  39.4 19.6 %collective-permute-start.9 = (bf16[10,160,256]{2,1,0:T(8,128)(2,1)S(1)}, bf16[10,160,256]{2,1,0:T(8,128)(2,1)S(1)}, u32[]{:S(2)}, u32[]{:S(2)}) collective-permute-start(bf16[10,160,256]{2,1,0:T(8,128)(2,1)S(1)} %collective-permute-done.8), channel_id=1, source_target_pairs={{24,16},{4,12},{25,17},{5,13},{26,18},{6,14},{27,19},{7,15}} | collective-permute-start | bytes 2457608 | tf_op jit(solution)/shard_map/ppermute | solution.py:188
  46.2 14.9 %copy-start = (bf16[10,160,256]{2,1,0:T(8,128)(2,1)}, bf16[10,160,256]{2,1,0:T(8,128)(2,1)S(1)}, u32[]{:S(2)}) copy-start(bf16[10,160,256]{2,1,0:T(8,128)(2,1)S(1)} %collective-permute-done.6.fa_ref) | copy-start | bytes 2457604
  46.2 12.8 %collective-permute-start.7 = (bf16[10,160,256]{2,1,0:T(8,128)(2,1)S(1)}, bf16[10,160,256]{2,1,0:T(8,128)(2,1)S(1)}, u32[]{:S(2)}, u32[]{:S(2)}) collective-permute-start(bf16[10,160,256]{2,1,0:T(8,128)(2,1)S(1)} %collective-permute-done.6.fa_ref), channel_id=1, source_target_pairs={{0,4},{8,12},{16,20},{1,5},{9,13},{17,21},{2,6},{10,14},{18,22},{3... | collective-permute-start | bytes 2457608 | tf_op jit(solution)/shard_map/ppermute | solution.py:196
  46.9 14.2 %copy-start.1 = (bf16[10,160,256]{2,1,0:T(8,128)(2,1)}, bf16[10,160,256]{2,1,0:T(8,128)(2,1)S(1)}, u32[]{:S(2)}) copy-start(bf16[10,160,256]{2,1,0:T(8,128)(2,1)S(1)} %collective-permute-done.3.fbo_ref) | copy-start | bytes 2457604
  46.9 12.1 %collective-permute-start.4 = (bf16[10,160,256]{2,1,0:T(8,128)(2,1)S(1)}, bf16[10,160,256]{2,1,0:T(8,128)(2,1)S(1)}, u32[]{:S(2)}, u32[]{:S(2)}) collective-permute-start(bf16[10,160,256]{2,1,0:T(8,128)(2,1)S(1)} %collective-permute-done.3.fbo_ref), channel_id=1, source_target_pairs={{12,8},{20,16},{28,24},{13,9},{21,17},{29,25},{14,10},{22,18},{30,... | collective-permute-start | bytes 2457608 | tf_op jit(solution)/shard_map/ppermute | solution.py:195
  48.2 12.9 %copy-start.2 = (bf16[10,160,256]{2,1,0:T(8,128)(2,1)}, bf16[10,160,256]{2,1,0:T(8,128)(2,1)S(1)}, u32[]{:S(2)}) copy-start(bf16[10,160,256]{2,1,0:T(8,128)(2,1)S(1)} %collective-permute-done.5.par_ref) | copy-start | bytes 2457604
  59.0 2.1 %copy-start.3 = (bf16[10,160,256]{2,1,0:T(8,128)(2,1)}, bf16[10,160,256]{2,1,0:T(8,128)(2,1)S(1)}, u32[]{:S(2)}) copy-start(bf16[10,160,256]{2,1,0:T(8,128)(2,1)S(1)} %collective-permute-done.2.fb_ref) | copy-start | bytes 2457604
  59.0 0.9 %copy-start.4 = (bf16[10,160,256]{2,1,0:T(8,128)(2,1)}, bf16[10,160,256]{2,1,0:T(8,128)(2,1)S(1)}, u32[]{:S(2)}) copy-start(bf16[10,160,256]{2,1,0:T(8,128)(2,1)S(1)} %collective-permute-done.9.routed_ref) | copy-start | bytes 2457604
  59.0 1.2 %copy-start.5 = (bf16[10,160,256]{2,1,0:T(8,128)(2,1)}, bf16[10,160,256]{2,1,0:T(8,128)(2,1)S(1)}, u32[]{:S(2)}) copy-start(bf16[10,160,256]{2,1,0:T(8,128)(2,1)S(1)} %collective-permute-done.7.ra_ref) | copy-start | bytes 2457604
  60.2 0.9 %copy-start.6 = (bf16[10,160,256]{2,1,0:T(8,128)(2,1)}, bf16[10,160,256]{2,1,0:T(8,128)(2,1)S(1)}, u32[]{:S(2)}) copy-start(bf16[10,160,256]{2,1,0:T(8,128)(2,1)S(1)} %collective-permute-done.4.rb_ref) | copy-start | bytes 2457604

commit v27 on v22

--- a/solution.py
+++ b/solution.py
@@ -135,7 +135,7 @@
         out_specs=vmem(),
         scratch_shapes=[pltpu.VMEM((block + 2, cols, c), jnp.bfloat16),
                         pltpu.VMEM((block + 2, cols, c), jnp.bfloat16),
-                        pltpu.VMEM((2 * CHUNK, cols, 3 * c), jnp.bfloat16)],
+                        pltpu.VMEM((1, cols, 3 * c), jnp.bfloat16)],
         cost_estimate=pl.CostEstimate(flops=flops, transcendentals=0,
                                       bytes_accessed=18 * (block + 2) * cols * c + 2 * 9 * c * c),
     )(coef, fb, fbo, rb, own, par, ra, fa, routed, above, frame, below, w3)

time: 68.5 us -> 68.6 us (level)
  no operation moved by 1% of the time
where the time goes in v27:
time: 68.6 us; the launch traced here: 68.2 us
  waiting for transfers between devices  26.5 us (39%)
  starting transfers between devices  14.8 us (22%)
  Pallas kernels  14.6 us (21%)
  local copies, waits for them, and re-layouts  5.58 us (8%)
  between operations  4.03 us (6%)
  other arithmetic  2.62 us (4%)
    ppermute x1, waiting for transfers between devices, shards(): lax.ppermute(second, 'tm', [(a, b) for a, b in behind_pairs if b % 2 == 0])  10.8 us
    ppermute x1, waiting for transfers between devices, shards(): hop = lax.ppermute(second, 'tm', [(2, 6), (5, 1)])  8.74 us
    pallas_call x1, Pallas kernels, layers(): pl.pallas_call(layers_kernel, out_shape=jax.ShapeDtypeStruct((rows - 4, c...  7.67 us
    pallas_call x1, Pallas kernels, mix(): pl.pallas_call(mix_kernel, out_shape=jax.ShapeDtypeStruct((block, cols, c...  6.93 us
    ppermute x2, starting transfers between devices, shifted(): return lax.ppermute(value, axis, pairs)  5.84 us
    ppermute x1, waiting for transfers between devices, shards(): lax.ppermute(second, 'tm', [(2, 0), (3, 1), (4, 2), (6, 4), (7, 5)])  5.46 us
    unnamed x20, local copies, waits for them, and re-layouts  2.8 us
    slice x2, local copies, waits for them, and re-layouts, shards(): up = jnp.concatenate([image[:3], frame[:1]], axis=0)  2.04 us
  transfers between devices with their start and end apart: 10, of which 4 were waited for; matrix products, arithmetic and copies ran while one was open for 5% of the time, Pallas kernels for 0%

profile of v27, /device:TPU:22, one launch (start us, length us, event | category | flops | bytes accessed | tf_op | source)
XLA Modules:
  0.0 68.2 jit_solution(7852939522644929319)
XLA Ops:
  0.0 0.9 %slice_bitcast_fusion.2 = (bf16[1,160,256]{2,1,0:T(8,128)(2,1)S(1)}, bf16[1,160,256]{2,1,0:T(8,128)(2,1)S(1)}) fusion(bf16[1,8,160,256]{3,2,1,0:T(8,128)(2,1)} %param.9), kind=kLoop, calls=%fused_computation.4 | loop fusion | bytes 327680 | tf_op jit(solution)/shard_map/slice | solution.py:161
  0.9 0.0 copy-start.9
  1.0 1.1 %slice_bitcast_fusion = (bf16[3,160,256]{2,1,0:T(8,128)(2,1)S(1)}, bf16[3,160,256]{2,1,0:T(8,128)(2,1)S(1)}) fusion(bf16[1,8,160,256]{3,2,1,0:T(8,128)(2,1)} %param.8), kind=kLoop, calls=%fused_computation.2 | loop fusion | bytes 983040 | tf_op jit(solution)/shard_map/slice | solution.py:161
  2.1 3.5 %collective-permute-start = (bf16[4,160,256]{2,1,0:T(8,128)(2,1)S(1)}, bf16[4,160,256]{2,1,0:T(8,128)(2,1)S(1)}, u32[]{:S(2)}, u32[]{:S(2)}) collective-permute-start(bf16[4,160,256]{2,1,0:T(8,128)(2,1)S(1)} %pad_maximum_fusion), channel_id=1, source_target_pairs={{0,1},{1,2},{2,3},{4,5},{5,6},{6,7},{8,9},{9,10},{10,11},{12,13},{... | collective-permute-start | bytes 983048 | tf_op jit(solution)/shard_map/ppermute | solution.py:16
  5.6 2.4 %collective-permute-start.1 = (bf16[4,160,256]{2,1,0:T(8,128)(2,1)S(1)}, bf16[4,160,256]{2,1,0:T(8,128)(2,1)S(1)}, u32[]{:S(2)}, u32[]{:S(2)}) collective-permute-start(bf16[4,160,256]{2,1,0:T(8,128)(2,1)S(1)} %pad_maximum_fusion.1), channel_id=1, source_target_pairs={{1,0},{2,1},{3,2},{5,4},{6,5},{7,6},{9,8},{10,9},{11,10},{13,12},{... | collective-permute-start | bytes 983048 | tf_op jit(solution)/shard_map/ppermute | solution.py:16
  9.3 0.0 copy-done.9
  9.3 0.6 fusion
  9.9 0.6 broadcast_divide_fusion
  10.6 0.1 slice.45
  10.6 0.7 fusion.1
  13.8 0.6 pad_add_fusion.bounds_ref
  14.5 0.7 pad_maximum_fusion.2.coef_ref
  15.2 0.0 collective-permute-done.above_ref
  15.2 0.0 copy-start.7
  15.2 1.5 %collective-permute-done.1.below_ref = bf16[4,160,256]{2,1,0:T(8,128)(2,1)S(1)} collective-permute-done((bf16[4,160,256]{2,1,0:T(8,128)(2,1)S(1)}, bf16[4,160,256]{2,1,0:T(8,128)(2,1)S(1)}, u32[]{:S(2)}, u32[]{:S(2)}) %collective-permute-start.1) | collective-permute-done | bytes 327712 | tf_op jit(solution)/shard_map/ppermute | solution.py:16
  16.7 0.0 copy-done.7
  16.7 0.0 copy-start.8
  16.7 0.7 %copy-done.8 = bf16[4,160,256]{2,1,0:T(8,128)(2,1)} copy-done((bf16[4,160,256]{2,1,0:T(8,128)(2,1)}, bf16[4,160,256]{2,1,0:T(8,128)(2,1)S(1)}, u32[]{:S(2)}) %copy-start.8) | copy-done | bytes 327704
  17.4 7.7 %shard_map.82.own_ref = bf16[10,160,256]{2,1,0:T(8,128)(2,1)} custom-call(s32[2]{0:T(128)} %pad_add_fusion.bounds_ref, bf16[4,160,256]{2,1,0:T(8,128)(2,1)} %copy-done.7, bf16[8,160,256]{2,1,0:T(8,128)(2,1)} %bitcast.28, bf16[4,160,256]{2,1,0:T(8,128)(2,1)} %copy-done.8, bf16[3,3,256,256]{3,2,1,0:T(8,128)(2,1)} %w1_ref.1, bf16[3,3,256,256]{3,2,1,0:T(8,128)(2,1)} %w2_ref.1), custom_call_target="tpu_custom_call" | custom-call | flops 4152360960 | bytes 4653056 | tf_op jit(solution)/shard_map/pallas_call | solution.py:115
  25.1 1.3 %collective-permute-start.8 = (bf16[10,160,256]{2,1,0:T(8,128)(2,1)}, bf16[10,160,256]{2,1,0:T(8,128)(2,1)S(1)}, u32[]{:S(2)}, u32[]{:S(2)}) collective-permute-start(bf16[10,160,256]{2,1,0:T(8,128)(2,1)} %shard_map.82.own_ref), channel_id=1, source_target_pairs={{8,24},{20,4},{9,25},{21,5},{10,26},{22,6},{11,27},{23,7}} | collective-permute-start | bytes 2457608 | tf_op jit(solution)/shard_map/ppermute | solution.py:187
  26.4 1.9 %collective-permute-start.6 = (bf16[10,160,256]{2,1,0:T(8,128)(2,1)}, bf16[10,160,256]{2,1,0:T(8,128)(2,1)S(1)}, u32[]{:S(2)}, u32[]{:S(2)}) collective-permute-start(bf16[10,160,256]{2,1,0:T(8,128)(2,1)} %shard_map.82.own_ref), channel_id=1, source_target_pairs={{8,0},{12,4},{16,8},{24,16},{28,20},{9,1},{13,5},{17,9},{25,17},{2... | collective-permute-start | bytes 2457608 | tf_op jit(solution)/shard_map/ppermute | solution.py:186
  28.3 0.7 %collective-permute-start.3 = (bf16[10,160,256]{2,1,0:T(8,128)(2,1)}, bf16[10,160,256]{2,1,0:T(8,128)(2,1)S(1)}, u32[]{:S(2)}, u32[]{:S(2)}) collective-permute-start(bf16[10,160,256]{2,1,0:T(8,128)(2,1)} %shard_map.82.own_ref), channel_id=1, source_target_pairs={{4,12},{12,20},{20,28},{5,13},{13,21},{21,29},{6,14},{14,22},{22,3... | collective-permute-start | bytes 2457608 | tf_op jit(solution)/shard_map/ppermute | solution.py:194
  29.0 0.5 collective-permute-start.5
  29.5 1.3 %collective-permute-start.2 = (bf16[10,160,256]{2,1,0:T(8,128)(2,1)}, bf16[10,160,256]{2,1,0:T(8,128)(2,1)S(1)}, u32[]{:S(2)}, u32[]{:S(2)}) collective-permute-start(bf16[10,160,256]{2,1,0:T(8,128)(2,1)} %shard_map.82.own_ref), channel_id=1, source_target_pairs={{0,8},{16,24},{1,9},{17,25},{2,10},{18,26},{3,11},{19,27}} | collective-permute-start | bytes 2457608 | tf_op jit(solution)/shard_map/ppermute | solution.py:193
  30.8 8.7 %collective-permute-done.8 = bf16[10,160,256]{2,1,0:T(8,128)(2,1)S(1)} collective-permute-done((bf16[10,160,256]{2,1,0:T(8,128)(2,1)}, bf16[10,160,256]{2,1,0:T(8,128)(2,1)S(1)}, u32[]{:S(2)}, u32[]{:S(2)}) %collective-permute-start.8) | collective-permute-done | bytes 819232 | tf_op jit(solution)/shard_map/ppermute | solution.py:187
  39.5 1.3 %collective-permute-start.9 = (bf16[10,160,256]{2,1,0:T(8,128)(2,1)S(1)}, bf16[10,160,256]{2,1,0:T(8,128)(2,1)S(1)}, u32[]{:S(2)}, u32[]{:S(2)}) collective-permute-start(bf16[10,160,256]{2,1,0:T(8,128)(2,1)S(1)} %collective-permute-done.8), channel_id=1, source_target_pairs={{24,16},{4,12},{25,17},{5,13},{26,18},{6,14},{27,19},{7,15}} | collective-permute-start | bytes 2457608 | tf_op jit(solution)/shard_map/ppermute | solution.py:188
  40.9 5.5 %collective-permute-done.6.fa_ref = bf16[10,160,256]{2,1,0:T(8,128)(2,1)S(1)} collective-permute-done((bf16[10,160,256]{2,1,0:T(8,128)(2,1)}, bf16[10,160,256]{2,1,0:T(8,128)(2,1)S(1)}, u32[]{:S(2)}, u32[]{:S(2)}) %collective-permute-start.6) | collective-permute-done | bytes 819232 | tf_op jit(solution)/shard_map/ppermute | solution.py:186
  46.3 0.0 copy-start
  46.3 0.7 %collective-permute-start.7 = (bf16[10,160,256]{2,1,0:T(8,128)(2,1)S(1)}, bf16[10,160,256]{2,1,0:T(8,128)(2,1)S(1)}, u32[]{:S(2)}, u32[]{:S(2)}) collective-permute-start(bf16[10,160,256]{2,1,0:T(8,128)(2,1)S(1)} %collective-permute-done.6.fa_ref), channel_id=1, source_target_pairs={{0,4},{8,12},{16,20},{1,5},{9,13},{17,21},{2,6},{10,14},{18,22},{3... | collective-permute-start | bytes 2457608 | tf_op jit(solution)/shard_map/ppermute | solution.py:196
  47.0 0.0 collective-permute-done.3.fbo_ref
  47.0 0.0 copy-start.1
  47.1 1.3 %collective-permute-start.4 = (bf16[10,160,256]{2,1,0:T(8,128)(2,1)S(1)}, bf16[10,160,256]{2,1,0:T(8,128)(2,1)S(1)}, u32[]{:S(2)}, u32[]{:S(2)}) collective-permute-start(bf16[10,160,256]{2,1,0:T(8,128)(2,1)S(1)} %collective-permute-done.3.fbo_ref), channel_id=1, source_target_pairs={{12,8},{20,16},{28,24},{13,9},{21,17},{29,25},{14,10},{22,18},{30,... | collective-permute-start | bytes 2457608 | tf_op jit(solution)/shard_map/ppermute | solution.py:195
  48.4 0.0 collective-permute-done.5.par_ref
  48.4 0.0 copy-start.2
  48.4 10.8 %collective-permute-done.2.fb_ref = bf16[10,160,256]{2,1,0:T(8,128)(2,1)S(1)} collective-permute-done((bf16[10,160,256]{2,1,0:T(8,128)(2,1)}, bf16[10,160,256]{2,1,0:T(8,128)(2,1)S(1)}, u32[]{:S(2)}, u32[]{:S(2)}) %collective-permute-start.2) | collective-permute-done | bytes 819232 | tf_op jit(solution)/shard_map/ppermute | solution.py:193
  59.2 0.0 copy-start.3
  59.2 0.0 collective-permute-done.9.routed_ref
  59.2 0.0 collective-permute-done.7.ra_ref
  59.2 0.0 copy-start.5
  59.2 0.0 collective-permute-done.4.rb_ref
  59.2 0.9 %copy-done.4 = bf16[10,160,256]{2,1,0:T(8,128)(2,1)} copy-done((bf16[10,160,256]{2,1,0:T(8,128)(2,1)}, bf16[10,160,256]{2,1,0:T(8,128)(2,1)S(1)}, u32[]{:S(2)}) %copy-start.4) | copy-done | bytes 819224
  60.1 0.2 copy-done.5
  60.3 0.9 %copy-done.6 = bf16[10,160,256]{2,1,0:T(8,128)(2,1)} copy-done((bf16[10,160,256]{2,1,0:T(8,128)(2,1)}, bf16[10,160,256]{2,1,0:T(8,128)(2,1)S(1)}, u32[]{:S(2)}) %copy-start.6) | copy-done | bytes 819224
  61.2 0.0 copy-done
  61.3 0.0 copy-done.1
  61.3 0.0 copy-done.2
  61.3 0.0 copy-done.3
  61.3 6.9 %shard_map.83 = bf16[8,160,256]{2,1,0:T(8,128)(2,1)} custom-call(f32[7]{0:T(128)} %pad_maximum_fusion.2.coef_ref, bf16[10,160,256]{2,1,0:T(8,128)(2,1)} %copy-done.3, bf16[10,160,256]{2,1,0:T(8,128)(2,1)} %copy-done.1, bf16[10,160,256]{2,1,0:T(8,128)(2,1)} %copy-done.6, bf16[10,160,256]{2,1,0:T(8,128)(2,1)} %shard_map.82.own_ref, ...), custom_call_target="tpu_custom_call" | custom-call | flops 1509949440 | bytes 8552448 | tf_op jit(solution)/shard_map/pallas_call | solution.py:131
  (4 shorter events, 0.1 us)
Async XLA Ops:
  0.9 8.4 %copy-start.9 = (s32[1,5]{1,0:T(1,128)S(1)}, s32[1,5]{1,0:T(1,128)}, u32[]{:S(2)}) copy-start(s32[1,5]{1,0:T(1,128)} %param.12) | copy-start | bytes 64
  2.1 13.1 %collective-permute-start = (bf16[4,160,256]{2,1,0:T(8,128)(2,1)S(1)}, bf16[4,160,256]{2,1,0:T(8,128)(2,1)S(1)}, u32[]{:S(2)}, u32[]{:S(2)}) collective-permute-start(bf16[4,160,256]{2,1,0:T(8,128)(2,1)S(1)} %pad_maximum_fusion), channel_id=1, source_target_pairs={{0,1},{1,2},{2,3},{4,5},{5,6},{6,7},{8,9},{9,10},{10,11},{12,13},{... | collective-permute-start | bytes 983048 | tf_op jit(solution)/shard_map/ppermute | solution.py:16
  5.6 11.1 %collective-permute-start.1 = (bf16[4,160,256]{2,1,0:T(8,128)(2,1)S(1)}, bf16[4,160,256]{2,1,0:T(8,128)(2,1)S(1)}, u32[]{:S(2)}, u32[]{:S(2)}) collective-permute-start(bf16[4,160,256]{2,1,0:T(8,128)(2,1)S(1)} %pad_maximum_fusion.1), channel_id=1, source_target_pairs={{1,0},{2,1},{3,2},{5,4},{6,5},{7,6},{9,8},{10,9},{11,10},{13,12},{... | collective-permute-start | bytes 983048 | tf_op jit(solution)/shard_map/ppermute | solution.py:16
  15.2 1.5 %copy-start.7 = (bf16[4,160,256]{2,1,0:T(8,128)(2,1)}, bf16[4,160,256]{2,1,0:T(8,128)(2,1)S(1)}, u32[]{:S(2)}) copy-start(bf16[4,160,256]{2,1,0:T(8,128)(2,1)S(1)} %collective-permute-done.above_ref) | copy-start | bytes 983044
  16.7 0.7 %copy-start.8 = (bf16[4,160,256]{2,1,0:T(8,128)(2,1)}, bf16[4,160,256]{2,1,0:T(8,128)(2,1)S(1)}, u32[]{:S(2)}) copy-start(bf16[4,160,256]{2,1,0:T(8,128)(2,1)S(1)} %collective-permute-done.1.below_ref) | copy-start | bytes 983044
  25.1 14.4 %collective-permute-start.8 = (bf16[10,160,256]{2,1,0:T(8,128)(2,1)}, bf16[10,160,256]{2,1,0:T(8,128)(2,1)S(1)}, u32[]{:S(2)}, u32[]{:S(2)}) collective-permute-start(bf16[10,160,256]{2,1,0:T(8,128)(2,1)} %shard_map.82.own_ref), channel_id=1, source_target_pairs={{8,24},{20,4},{9,25},{21,5},{10,26},{22,6},{11,27},{23,7}} | collective-permute-start | bytes 2457608 | tf_op jit(solution)/shard_map/ppermute | solution.py:187
  26.4 19.9 %collective-permute-start.6 = (bf16[10,160,256]{2,1,0:T(8,128)(2,1)}, bf16[10,160,256]{2,1,0:T(8,128)(2,1)S(1)}, u32[]{:S(2)}, u32[]{:S(2)}) collective-permute-start(bf16[10,160,256]{2,1,0:T(8,128)(2,1)} %shard_map.82.own_ref), channel_id=1, source_target_pairs={{8,0},{12,4},{16,8},{24,16},{28,20},{9,1},{13,5},{17,9},{25,17},{2... | collective-permute-start | bytes 2457608 | tf_op jit(solution)/shard_map/ppermute | solution.py:186
  28.3 18.8 %collective-permute-start.3 = (bf16[10,160,256]{2,1,0:T(8,128)(2,1)}, bf16[10,160,256]{2,1,0:T(8,128)(2,1)S(1)}, u32[]{:S(2)}, u32[]{:S(2)}) collective-permute-start(bf16[10,160,256]{2,1,0:T(8,128)(2,1)} %shard_map.82.own_ref), channel_id=1, source_target_pairs={{4,12},{12,20},{20,28},{5,13},{13,21},{21,29},{6,14},{14,22},{22,3... | collective-permute-start | bytes 2457608 | tf_op jit(solution)/shard_map/ppermute | solution.py:194
  29.0 19.4 %collective-permute-start.5 = (bf16[10,160,256]{2,1,0:T(8,128)(2,1)}, bf16[10,160,256]{2,1,0:T(8,128)(2,1)S(1)}, u32[]{:S(2)}, u32[]{:S(2)}) collective-permute-start(bf16[10,160,256]{2,1,0:T(8,128)(2,1)} %shard_map.82.own_ref), channel_id=1, source_target_pairs={{0,4},{4,0},{8,12},{12,8},{16,20},{20,16},{24,28},{28,24},{1,5},{5... | collective-permute-start | bytes 2457608 | tf_op jit(solution)/shard_map/ppermute | solution.py:183
  29.5 29.7 %collective-permute-start.2 = (bf16[10,160,256]{2,1,0:T(8,128)(2,1)}, bf16[10,160,256]{2,1,0:T(8,128)(2,1)S(1)}, u32[]{:S(2)}, u32[]{:S(2)}) collective-permute-start(bf16[10,160,256]{2,1,0:T(8,128)(2,1)} %shard_map.82.own_ref), channel_id=1, source_target_pairs={{0,8},{16,24},{1,9},{17,25},{2,10},{18,26},{3,11},{19,27}} | collective-permute-start | bytes 2457608 | tf_op jit(solution)/shard_map/ppermute | solution.py:193
  39.5 19.6 %collective-permute-start.9 = (bf16[10,160,256]{2,1,0:T(8,128)(2,1)S(1)}, bf16[10,160,256]{2,1,0:T(8,128)(2,1)S(1)}, u32[]{:S(2)}, u32[]{:S(2)}) collective-permute-start(bf16[10,160,256]{2,1,0:T(8,128)(2,1)S(1)} %collective-permute-done.8), channel_id=1, source_target_pairs={{24,16},{4,12},{25,17},{5,13},{26,18},{6,14},{27,19},{7,15}} | collective-permute-start | bytes 2457608 | tf_op jit(solution)/shard_map/ppermute | solution.py:188
  46.3 14.9 %copy-start = (bf16[10,160,256]{2,1,0:T(8,128)(2,1)}, bf16[10,160,256]{2,1,0:T(8,128)(2,1)S(1)}, u32[]{:S(2)}) copy-start(bf16[10,160,256]{2,1,0:T(8,128)(2,1)S(1)} %collective-permute-done.6.fa_ref) | copy-start | bytes 2457604
  46.3 12.8 %collective-permute-start.7 = (bf16[10,160,256]{2,1,0:T(8,128)(2,1)S(1)}, bf16[10,160,256]{2,1,0:T(8,128)(2,1)S(1)}, u32[]{:S(2)}, u32[]{:S(2)}) collective-permute-start(bf16[10,160,256]{2,1,0:T(8,128)(2,1)S(1)} %collective-permute-done.6.fa_ref), channel_id=1, source_target_pairs={{0,4},{8,12},{16,20},{1,5},{9,13},{17,21},{2,6},{10,14},{18,22},{3... | collective-permute-start | bytes 2457608 | tf_op jit(solution)/shard_map/ppermute | solution.py:196
  47.0 14.2 %copy-start.1 = (bf16[10,160,256]{2,1,0:T(8,128)(2,1)}, bf16[10,160,256]{2,1,0:T(8,128)(2,1)S(1)}, u32[]{:S(2)}) copy-start(bf16[10,160,256]{2,1,0:T(8,128)(2,1)S(1)} %collective-permute-done.3.fbo_ref) | copy-start | bytes 2457604
  47.1 12.1 %collective-permute-start.4 = (bf16[10,160,256]{2,1,0:T(8,128)(2,1)S(1)}, bf16[10,160,256]{2,1,0:T(8,128)(2,1)S(1)}, u32[]{:S(2)}, u32[]{:S(2)}) collective-permute-start(bf16[10,160,256]{2,1,0:T(8,128)(2,1)S(1)} %collective-permute-done.3.fbo_ref), channel_id=1, source_target_pairs={{12,8},{20,16},{28,24},{13,9},{21,17},{29,25},{14,10},{22,18},{30,... | collective-permute-start | bytes 2457608 | tf_op jit(solution)/shard_map/ppermute | solution.py:195
  48.4 12.9 %copy-start.2 = (bf16[10,160,256]{2,1,0:T(8,128)(2,1)}, bf16[10,160,256]{2,1,0:T(8,128)(2,1)S(1)}, u32[]{:S(2)}) copy-start(bf16[10,160,256]{2,1,0:T(8,128)(2,1)S(1)} %collective-permute-done.5.par_ref) | copy-start | bytes 2457604
  59.2 2.1 %copy-start.3 = (bf16[10,160,256]{2,1,0:T(8,128)(2,1)}, bf16[10,160,256]{2,1,0:T(8,128)(2,1)S(1)}, u32[]{:S(2)}) copy-start(bf16[10,160,256]{2,1,0:T(8,128)(2,1)S(1)} %collective-permute-done.2.fb_ref) | copy-start | bytes 2457604
  59.2 0.9 %copy-start.4 = (bf16[10,160,256]{2,1,0:T(8,128)(2,1)}, bf16[10,160,256]{2,1,0:T(8,128)(2,1)S(1)}, u32[]{:S(2)}) copy-start(bf16[10,160,256]{2,1,0:T(8,128)(2,1)S(1)} %collective-permute-done.9.routed_ref) | copy-start | bytes 2457604
  59.2 1.2 %copy-start.5 = (bf16[10,160,256]{2,1,0:T(8,128)(2,1)}, bf16[10,160,256]{2,1,0:T(8,128)(2,1)S(1)}, u32[]{:S(2)}) copy-start(bf16[10,160,256]{2,1,0:T(8,128)(2,1)S(1)} %collective-permute-done.7.ra_ref) | copy-start | bytes 2457604
  60.3 0.9 %copy-start.6 = (bf16[10,160,256]{2,1,0:T(8,128)(2,1)}, bf16[10,160,256]{2,1,0:T(8,128)(2,1)S(1)}, u32[]{:S(2)}) copy-start(bf16[10,160,256]{2,1,0:T(8,128)(2,1)S(1)} %collective-permute-done.4.rb_ref) | copy-start | bytes 2457604
